TPU v7x, 32 devices: a whole 2x2x4 slice. The times are simulated.
32 devices in a mesh: dp: 8 (over z, x), mp: 4 (over y, core).
Axes of the slice: x: 2, y: 2, z: 4, core: 2. Of those that a mesh axis runs over, the one named last changes fastest.
Arguments:
- tokens: bfloat16 [4096, 2048], P('dp'), may hold values from -6 to 6
- cotangent: bfloat16 [4096, 2048], P('dp'), may hold values from -6 to 6
- doc_ids: int32 [4096], P('dp'), may hold values from 0 to 1, as said below
- row_ids: int32 [8], P('dp'), may hold values from 0 to 2, as said below
- offsets: int32 [8], P('dp'), may hold values from 0 to 1536, as said below
- w_query: bfloat16 [2048, 2048], P(None, 'mp'), may hold values from -0.125 to 0.125
- w_key: bfloat16 [2048, 2048], P(None, 'mp'), may hold values from -0.125 to 0.125
- w_value: bfloat16 [2048, 2048], P(None, 'mp'), may hold values from -0.125 to 0.125
- w_output: bfloat16 [2048, 2048], P('mp'), may hold values from -0.125 to 0.125
- w_gate: bfloat16 [2048, 8192], P(None, 'mp'), may hold values from -0.125 to 0.125
- w_up: bfloat16 [2048, 8192], P(None, 'mp'), may hold values from -0.125 to 0.125
- w_down: bfloat16 [8192, 2048], P('mp'), may hold values from -0.0625 to 0.0625
- gain_query: float32 [16, 128], P('mp'), may hold values from 0.1 to 1.9
- gain_key: float32 [16, 128], P('mp'), may hold values from 0.1 to 1.9
- gain_attn: float32 [16, 128], replicated, may hold values from 0.1 to 1.9
- gain_mlp: float32 [16, 128], replicated, may hold values from 0.1 to 1.9
Outputs:
- output: bfloat16 [4096, 2048], P('dp')
- grad_tokens: bfloat16 [4096, 2048], P('dp')
- grad_w_query: float32 [2048, 2048], P('dp', 'mp')
- grad_w_key: float32 [2048, 2048], P('dp', 'mp')
- grad_w_value: float32 [2048, 2048], P('dp', 'mp')
- grad_w_output: float32 [2048, 2048], P('mp', 'dp')
- grad_w_gate: float32 [2048, 8192], P('dp', 'mp')
- grad_w_up: float32 [2048, 8192], P('dp', 'mp')
- grad_w_down: float32 [8192, 2048], P('mp', 'dp')
- grad_gain_query: float32 [16, 128], P('mp', 'dp')
- grad_gain_key: float32 [16, 128], P('mp', 'dp')
- grad_gain_attn: float32 [16, 128], P(None, 'dp')
- grad_gain_mlp: float32 [16, 128], P(None, 'dp')
Inputs may be any that keep to these rules, and one draw needn't show every extreme that they name: Index i of dp holds 512 consecutive tokens of row row_ids[i]. Rows 0 and 1 have 1024 tokens, row 2 has 2048, and every block of 512 tokens of every row is held by exactly one index. offsets[i] is the position in its row of the first token of index i; it is a multiple of 512. `doc_ids`: within a row, the document number is 0 at the row's first position and never falls; from one position to the next it rises by 0 or 1. The last position of row 2 has the largest number.
All inputs are finite; a program needn't handle non-finite values.
Results may differ from a plain program's by a relative error of at most 0.025.
Values may be sent and summed in bfloat16 or wider, within the bound.
A program may use at most 192 MiB of HBM per device.

v0:
```python
import math

import jax
import jax.numpy as jnp
from jax import lax
from jax.sharding import PartitionSpec as P

epsilon = 1e-06
rope_base = 500000.0
masked_score = -1e30


def rope_tables(positions, head_width):
    freqs = rope_base ** (-jnp.arange(0, head_width // 2, dtype=jnp.float32) * 2.0 / head_width)
    angles = positions.astype(jnp.float32)[:, None] * freqs[None, :]
    return (jnp.cos(angles)[:, None, :], jnp.sin(angles)[:, None, :])


def rotate(values, cosines, sines):
    half = values.shape[-1] // 2
    first = values[..., :half]
    second = values[..., half:]
    return jnp.concatenate(
        [first * cosines - second * sines, second * cosines + first * sines], axis=-1
    )


def norm_back(grad_normed, normed, factor):
    return factor * (grad_normed - normed * jnp.mean(grad_normed * normed, axis=-1, keepdims=True))


def on_device(
    tokens,
    cotangent,
    doc_ids,
    row_ids,
    offsets,
    w_query,
    w_key,
    w_value,
    w_output,
    w_gate,
    w_up,
    w_down,
    gain_query,
    gain_key,
    gain_attn,
    gain_mlp,
):
    f32 = jnp.float32
    bf16 = jnp.bfloat16
    row_count = tokens.shape[0]
    model_width = tokens.shape[1]
    heads_here = gain_query.shape[0]
    head_width = gain_query.shape[1]
    local_width = heads_here * head_width
    groups = lax.axis_size("dp")
    key_rows = row_count * groups
    block_rows = min(key_rows, row_count * max(1, 512 // row_count))
    block_count = key_rows // block_rows
    score_scale = 1.0 / math.sqrt(head_width)
    positions = offsets[0] + jnp.arange(row_count, dtype=jnp.int32)
    labels = row_ids[0] * key_rows + doc_ids
    cosines, sines = rope_tables(positions, head_width)
    q_raw = jnp.dot(tokens, w_query, preferred_element_type=f32)
    k_raw = jnp.dot(tokens, w_key, preferred_element_type=f32)
    v_raw = jnp.dot(tokens, w_value, preferred_element_type=f32)
    squares = lax.psum(
        jnp.stack([jnp.sum(q_raw * q_raw, axis=1), jnp.sum(k_raw * k_raw, axis=1)]), "mp"
    )
    q_factor = lax.rsqrt(squares[0] / model_width + epsilon)[:, None]
    k_factor = lax.rsqrt(squares[1] / model_width + epsilon)[:, None]
    g_query = gain_query.reshape(local_width)
    g_key = gain_key.reshape(local_width)
    q_normed = q_raw * q_factor
    k_normed = k_raw * k_factor
    queries = rotate(
        (q_normed * g_query).reshape(row_count, heads_here, head_width), cosines, sines
    ).astype(bf16)
    keys_low = rotate(
        (k_normed * g_key).reshape(row_count, heads_here, head_width), cosines, sines
    ).astype(bf16)
    values_low = v_raw.astype(bf16)
    all_keys, all_values, all_labels, all_positions = (
        lax.all_gather(keys_low.reshape(row_count, local_width), "dp", axis=0, tiled=True),
        lax.all_gather(values_low, "dp", axis=0, tiled=True),
        lax.all_gather(labels, "dp", axis=0, tiled=True),
        lax.all_gather(positions, "dp", axis=0, tiled=True),
    )
    key_blocks = all_keys.reshape(block_count, block_rows, heads_here, head_width)
    value_blocks = all_values.reshape(block_count, block_rows, heads_here, head_width)
    label_blocks = all_labels.reshape(block_count, block_rows)
    position_blocks = all_positions.reshape(block_count, block_rows)
    scanned = (key_blocks, value_blocks, label_blocks, position_blocks)
    low_label = jnp.min(labels)
    high_label = jnp.max(labels)

    def scores_of(key_block, label_block, position_block):
        scores = (
            jnp.einsum("qhd,khd->hqk", queries, key_block, preferred_element_type=f32) * score_scale
        )
        allowed = (labels[:, None] == label_block[None, :]) & (
            positions[:, None] >= position_block[None, :]
        )
        return (scores, allowed[None])

    def touches(label_block):
        return (jnp.max(label_block) >= low_label) & (jnp.min(label_block) <= high_label)

    def max_step(carry, blocks_in):
        key_block, value_block, label_block, position_block = blocks_in

        def max_live_block(state):
            running, totals = state
            scores, allowed = scores_of(key_block, label_block, position_block)
            highest = jnp.maximum(
                running, jnp.max(jnp.where(allowed, scores, masked_score), axis=2)
            )
            weights = jnp.where(allowed, jnp.exp(scores - highest[:, :, None]), 0.0)
            return (highest, totals * jnp.exp(running - highest) + jnp.sum(weights, axis=2))

        return (lax.cond(touches(label_block), max_live_block, lambda state: state, carry), None)

    start_state = (
        jnp.full((heads_here, row_count), masked_score, f32),
        jnp.zeros((heads_here, row_count), f32),
    )
    (running_max, running_total), _ = lax.scan(max_step, start_state, scanned)
    log_total = running_max + jnp.log(running_total)

    def value_step(accum, blocks_in):
        key_block, value_block, label_block, position_block = blocks_in

        def value_live_block(current):
            scores, allowed = scores_of(key_block, label_block, position_block)
            probs_low = jnp.where(allowed, jnp.exp(scores - log_total[:, :, None]), 0.0).astype(
                bf16
            )
            return current + jnp.einsum(
                "hqk,khd->qhd", probs_low, value_block, preferred_element_type=f32
            )

        return (
            lax.cond(touches(label_block), value_live_block, lambda current: current, accum),
            None,
        )

    attended, _ = lax.scan(value_step, jnp.zeros((row_count, heads_here, head_width), f32), scanned)
    attended_low = attended.reshape(row_count, local_width).astype(bf16)
    attn_sum = lax.psum(
        jnp.dot(attended_low, w_output, preferred_element_type=f32).astype(jnp.bfloat16), "mp"
    ).astype(jnp.float32)
    attn_factor = lax.rsqrt(jnp.mean(attn_sum * attn_sum, axis=1, keepdims=True) + epsilon)
    attn_normed = attn_sum * attn_factor
    g_attn = gain_attn.reshape(model_width)
    hidden = tokens.astype(f32) + attn_normed * g_attn
    hidden_low = hidden.astype(bf16)
    gate_val = jnp.dot(hidden_low, w_gate, preferred_element_type=f32)
    up_val = jnp.dot(hidden_low, w_up, preferred_element_type=f32)
    sigmoid_gate = jax.nn.sigmoid(gate_val)
    silu_gate = gate_val * sigmoid_gate
    act_low = (silu_gate * up_val).astype(bf16)
    mlp_sum = lax.psum(
        jnp.dot(act_low, w_down, preferred_element_type=f32).astype(jnp.bfloat16), "mp"
    ).astype(jnp.float32)
    mlp_factor = lax.rsqrt(jnp.mean(mlp_sum * mlp_sum, axis=1, keepdims=True) + epsilon)
    mlp_normed = mlp_sum * mlp_factor
    g_mlp = gain_mlp.reshape(model_width)
    output = (hidden + mlp_normed * g_mlp).astype(bf16)
    grad_out = cotangent.astype(f32)
    grad_gain_mlp = jnp.sum(grad_out * mlp_normed, axis=0)
    grad_mlp = norm_back(grad_out * g_mlp, mlp_normed, mlp_factor).astype(bf16)
    grad_w_down = jnp.einsum("tf,td->fd", act_low, grad_mlp, preferred_element_type=f32)
    grad_act = jnp.einsum("td,fd->tf", grad_mlp, w_down, preferred_element_type=f32)
    slope = sigmoid_gate * (1.0 + gate_val * (1.0 - sigmoid_gate))
    grad_gate = (grad_act * up_val * slope).astype(bf16)
    grad_up = (grad_act * silu_gate).astype(bf16)
    branch_grad = jnp.einsum(
        "tf,df->td", grad_gate, w_gate, preferred_element_type=f32
    ) + jnp.einsum("tf,df->td", grad_up, w_up, preferred_element_type=f32)
    grad_hidden = grad_out + lax.psum(branch_grad.astype(jnp.bfloat16), "mp").astype(jnp.float32)
    grad_gain_attn = jnp.sum(grad_hidden * attn_normed, axis=0)
    grad_attn = norm_back(grad_hidden * g_attn, attn_normed, attn_factor).astype(bf16)
    grad_w_output = jnp.einsum("tc,td->cd", attended_low, grad_attn, preferred_element_type=f32)
    grad_attended = (
        jnp.einsum("td,cd->tc", grad_attn, w_output, preferred_element_type=f32)
        .astype(bf16)
        .reshape(row_count, heads_here, head_width)
    )
    delta = jnp.sum(grad_attended.astype(f32) * attended, axis=2).T

    def grad_step(grad_q, blocks_in):
        key_block, value_block, label_block, position_block = blocks_in

        def grad_live_block(current):
            scores, allowed = scores_of(key_block, label_block, position_block)
            probs = jnp.where(allowed, jnp.exp(scores - log_total[:, :, None]), 0.0)
            grad_probs = jnp.einsum(
                "qhd,khd->hqk", grad_attended, value_block, preferred_element_type=f32
            )
            grad_scores = (probs * (grad_probs - delta[:, :, None])).astype(bf16)
            value_term = jnp.einsum(
                "hqk,qhd->khd", probs.astype(bf16), grad_attended, preferred_element_type=f32
            )
            key_term = jnp.einsum("hqk,qhd->khd", grad_scores, queries, preferred_element_type=f32)
            updated = current + jnp.einsum(
                "hqk,khd->qhd", grad_scores, key_block, preferred_element_type=f32
            )
            return (updated, (key_term, value_term))

        def skip_block(current):
            nothing = jnp.zeros((block_rows, heads_here, head_width), f32)
            return (current, (nothing, nothing))

        return lax.cond(touches(label_block), grad_live_block, skip_block, grad_q)

    grad_queries, (key_terms, value_terms) = lax.scan(
        grad_step, jnp.zeros((row_count, heads_here, head_width), f32), scanned
    )
    grad_keys, grad_values = (
        lax.psum_scatter(
            (key_terms.reshape(key_rows, local_width) * score_scale).astype(jnp.bfloat16),
            "dp",
            scatter_dimension=0,
            tiled=True,
        ).astype(jnp.float32),
        lax.psum_scatter(
            value_terms.reshape(key_rows, local_width).astype(jnp.bfloat16),
            "dp",
            scatter_dimension=0,
            tiled=True,
        ).astype(jnp.float32),
    )
    grad_values_low = grad_values.astype(bf16)
    back_q = rotate(grad_queries * score_scale, cosines, -sines).reshape(row_count, local_width)
    back_k = rotate(grad_keys.reshape(row_count, heads_here, head_width), cosines, -sines).reshape(
        row_count, local_width
    )
    grad_gain_query = jnp.sum(back_q * q_normed, axis=0).reshape(heads_here, head_width)
    grad_gain_key = jnp.sum(back_k * k_normed, axis=0).reshape(heads_here, head_width)
    scaled_q = back_q * g_query
    scaled_k = back_k * g_key
    inner = lax.psum(
        jnp.stack([jnp.sum(scaled_q * q_normed, axis=1), jnp.sum(scaled_k * k_normed, axis=1)]),
        "mp",
    )
    grad_q_raw = (q_factor * (scaled_q - q_normed * inner[0][:, None] / model_width)).astype(bf16)
    grad_k_raw = (k_factor * (scaled_k - k_normed * inner[1][:, None] / model_width)).astype(bf16)
    input_term = (
        jnp.einsum("tc,dc->td", grad_q_raw, w_query, preferred_element_type=f32)
        + jnp.einsum("tc,dc->td", grad_k_raw, w_key, preferred_element_type=f32)
        + jnp.einsum("tc,dc->td", grad_values_low, w_value, preferred_element_type=f32)
    )
    grad_tokens = (
        grad_hidden + lax.psum(input_term.astype(jnp.bfloat16), "mp").astype(jnp.float32)
    ).astype(bf16)
    local_w_query = jnp.einsum("td,tc->dc", tokens, grad_q_raw, preferred_element_type=f32)
    local_w_key = jnp.einsum("td,tc->dc", tokens, grad_k_raw, preferred_element_type=f32)
    local_w_value = jnp.einsum("td,tc->dc", tokens, grad_values_low, preferred_element_type=f32)
    local_w_gate = jnp.einsum("td,tf->df", hidden_low, grad_gate, preferred_element_type=f32)
    local_w_up = jnp.einsum("td,tf->df", hidden_low, grad_up, preferred_element_type=f32)
    grad_w_query, grad_w_key, grad_w_value, grad_w_gate, grad_w_up = (
        lax.psum_scatter(
            local_w_query.astype(jnp.bfloat16), "dp", scatter_dimension=0, tiled=True
        ).astype(jnp.float32),
        lax.psum_scatter(
            local_w_key.astype(jnp.bfloat16), "dp", scatter_dimension=0, tiled=True
        ).astype(jnp.float32),
        lax.psum_scatter(
            local_w_value.astype(jnp.bfloat16), "dp", scatter_dimension=0, tiled=True
        ).astype(jnp.float32),
        lax.psum_scatter(
            local_w_gate.astype(jnp.bfloat16), "dp", scatter_dimension=0, tiled=True
        ).astype(jnp.float32),
        lax.psum_scatter(
            local_w_up.astype(jnp.bfloat16), "dp", scatter_dimension=0, tiled=True
        ).astype(jnp.float32),
    )
    summed_out, summed_down, summed_gq, summed_gk, summed_ga, summed_gm = (
        lax.psum_scatter(
            grad_w_output.astype(jnp.bfloat16), "dp", scatter_dimension=1, tiled=True
        ).astype(jnp.float32),
        lax.psum_scatter(
            grad_w_down.astype(jnp.bfloat16), "dp", scatter_dimension=1, tiled=True
        ).astype(jnp.float32),
        lax.psum_scatter(
            grad_gain_query.astype(jnp.bfloat16), "dp", scatter_dimension=1, tiled=True
        ).astype(jnp.float32),
        lax.psum_scatter(
            grad_gain_key.astype(jnp.bfloat16), "dp", scatter_dimension=1, tiled=True
        ).astype(jnp.float32),
        lax.psum_scatter(
            grad_gain_attn.reshape(gain_attn.shape).astype(jnp.bfloat16),
            "dp",
            scatter_dimension=1,
            tiled=True,
        ).astype(jnp.float32),
        lax.psum_scatter(
            grad_gain_mlp.reshape(gain_mlp.shape).astype(jnp.bfloat16),
            "dp",
            scatter_dimension=1,
            tiled=True,
        ).astype(jnp.float32),
    )
    return (
        output,
        grad_tokens,
        grad_w_query,
        grad_w_key,
        grad_w_value,
        summed_out,
        grad_w_gate,
        grad_w_up,
        summed_down,
        summed_gq,
        summed_gk,
        summed_ga,
        summed_gm,
    )


def solution(mesh):
    return jax.shard_map(
        on_device,
        mesh=mesh,
        in_specs=(
            P("dp", None),
            P("dp", None),
            P("dp"),
            P("dp"),
            P("dp"),
            P(None, "mp"),
            P(None, "mp"),
            P(None, "mp"),
            P("mp", None),
            P(None, "mp"),
            P(None, "mp"),
            P("mp", None),
            P("mp", None),
            P("mp", None),
            P(),
            P(),
        ),
        out_specs=(
            P("dp", None),
            P("dp", None),
            P("dp", "mp"),
            P("dp", "mp"),
            P("dp", "mp"),
            P("mp", "dp"),
            P("dp", "mp"),
            P("dp", "mp"),
            P("mp", "dp"),
            P("mp", "dp"),
            P("mp", "dp"),
            P(None, "dp"),
            P(None, "dp"),
        ),
        check_vma=False,
    )
```

profile of v0, /device:TPU:0, one launch (start us, length us, event | category | flops | bytes accessed | tf_op | source)
XLA Modules:
  0.0 1814.0 jit_solution(2751500297274127159)
XLA Ops:
  7.2 4.4 convolution_convert_fusion.10
  12.4 3.7 multiply_reduce_fusion.4
  18.5 8.4 psum.42
  31.7 26.8 %all-gather.1 = s32[8,1,512]{2,1,0:T(1,128)S(1)} all-gather(s32[1,1,512]{2,1,0:T(1,128)S(1)} %bitcast.265), channel_id=1, replica_groups=mesh['dp'=8,'mp'=4] {'dp'}, dimensions={0}, use_global_device_ids=true | all-gather | bytes 18432 | tf_op jit(solution)/shard_map/all_gather | solution.py:88
  59.1 26.8 %all-gather = s32[8,1,512]{2,1,0:T(1,128)S(1)} all-gather(s32[1,1,512]{2,1,0:T(1,128)S(1)} %bitcast.224), channel_id=1, replica_groups=mesh['dp'=8,'mp'=4] {'dp'}, dimensions={0}, use_global_device_ids=true | all-gather | bytes 18432 | tf_op jit(solution)/shard_map/all_gather | solution.py:87
  88.3 6.9 reshape.414
  95.2 5.5 copy.69
  100.6 63.7 %all-gather.5.cloned.1.call-done = bf16[4096,512]{0,1:T(8,128)(2,1)} async-done(((bf16[512,512]{0,1:T(8,128)(2,1)}), bf16[4096,512]{0,1:T(8,128)(2,1)}) %all-gather.5.cloned.1.call-update) | async-done | bytes 4194320 | tf_op jit(solution)/shard_map/all_gather | solution.py:85
  164.3 6.4 copy.94
  170.7 7.9 copy.67
  178.6 33.7 %while.45 = (s32[]{:T(128)}, f32[4,512]{1,0:T(4,128)S(1)}, f32[4,512]{1,0:T(4,128)S(1)}, s32[8,512]{1,0:T(8,128)S(1)}, s32[]{:T(128)}, /*index=5*/s32[]{:T(128)}...) while((s32[]{:T(128)}, f32[4,512]{1,0:T(4,128)S(1)}, ...), condition=%wide.region_12.13_spmd.clone, body=%wide.region_5.12_spmd.clone.sunk | while | flops 276567552 | bytes 10353443 | solution.py:128
  181.9 3.8 conditional.9
  202.0 3.8 conditional.9
  213.4 36.4 %while.46 = (s32[]{:T(128)}, f32[512,4,128]{2,0,1:T(8,128)}, s32[8,512]{1,0:T(8,128)S(1)}, s32[]{:T(128)}, s32[]{:T(128)}, /*index=5*/s32[512]{0:T(512)S(1)}, s3...) while((s32[]{:T(128)}, f32[512,4,128]{2,0,1:T(8,128)}, ...), condition=%wide.region_18.19_spmd.clone, body=%wide.region_13.18_spmd.clone.sunk | while | flops 542115328 | bytes 4226323 | solution.py:148
  216.7 5.2 conditional.10
  217.6 4.3 fusion.17
  238.2 5.2 conditional.10
  239.1 4.2 fusion.17
  251.4 4.4 convolution_convert_fusion.8
  256.0 67.5 %all-reduce.5.cloned.1.call-done = bf16[512,2048]{1,0:T(8,128)(2,1)} async-done(((bf16[512,2048]{1,0:T(8,128)(2,1)}), bf16[512,2048]{1,0:T(8,128)(2,1)}) %all-reduce.5.cloned.1.call-update) | async-done | bytes 2097168 | tf_op jit(solution)/shard_map/psum | solution.py:150
  329.1 7.7 fusion.95
  336.9 6.5 multiply_convert_fusion.3
  344.7 5.7 convolution_convert_fusion.7
  350.7 51.4 %all-reduce.7.cloned.1.call-done = bf16[512,2048]{1,0:T(8,128)(2,1)} async-done(((bf16[512,2048]{1,0:T(8,128)(2,1)}), bf16[512,2048]{1,0:T(8,128)(2,1)}) %all-reduce.7.cloned.1.call-update) | async-done | bytes 2097168 | tf_op jit(solution)/shard_map/psum | solution.py:163
  404.3 3.5 fusion.73
  407.9 11.7 multiply_convert_fusion.1
  419.6 7.8 fusion.96
  427.4 9.4 add_convert_fusion.2
  437.3 51.1 %all-reduce.9.cloned.1.call-done = bf16[512,2048]{1,0:T(8,128)(2,1)} async-done(((bf16[512,2048]{1,0:T(8,128)(2,1)}), bf16[512,2048]{1,0:T(8,128)(2,1)}) %all-reduce.9.cloned.1.call-update) | async-done | bytes 2097168 | tf_op jit(solution)/shard_map/psum | solution.py:181
  488.5 4.5 fusion.67
  493.2 6.0 fusion.66
  506.5 57.7 %while.47 = (s32[]{:T(128)}, f32[512,4,128]{2,0,1:T(8,128)}, f32[8,512,4,128]{3,1,2,0:T(8,128)}, bf16[8,512,4,128]{3,1,2,0:T(8,128)(2,1)}, s32[8,512]{1,0:T(8,12...) while((s32[]{:T(128)}, f32[512,4,128]{2,0,1:T(8,128)}, ...), condition=%wide.region_32.33_spmd.clone, body=%wide.region_27.32_spmd.clone.sunk | while | flops 1353713152 | bytes 40157576 | solution.py:217
  509.9 9.7 conditional.11
  543.5 9.7 conditional.11
  564.2 6.6 multiply_convert_fusion
  570.8 8.0 copy.77
  578.8 6.4 copy.95
  585.3 8.0 copy.78
  593.3 6.4 copy.96
  601.3 4.4 convolution_convert_fusion.3
  608.5 84.4 %reduce-scatter.22.cloned.1.call-done = bf16[512,512]{0,1:T(8,128)(2,1)} async-done(((bf16[4096,512]{0,1:T(8,128)(2,1)}), bf16[512,512]{0,1:T(8,128)(2,1)}) %reduce-scatter.22.cloned.1.call-update) | async-done | bytes 524304 | tf_op jit(solution)/shard_map/reduce_scatter | solution.py:221
  698.9 6.9 psum.46
  713.4 4.9 fusion.97
  719.3 65.5 %reduce-scatter.24.cloned.1.call-done = bf16[512,512]{0,1:T(8,128)(2,1)} async-done(((bf16[4096,512]{0,1:T(8,128)(2,1)}), bf16[512,512]{0,1:T(8,128)(2,1)}) %reduce-scatter.24.cloned.1.call-update) | async-done | bytes 524304 | tf_op jit(solution)/shard_map/reduce_scatter | solution.py:227
  784.8 6.9 add_convert_fusion.1
  791.7 4.2 fusion.78
  796.0 4.2 fusion.76
  800.3 4.2 fusion.77
  804.6 11.0 convolution_convert_fusion
  815.9 10.0 convolution_convert_fusion.1
  826.0 10.0 convolution_convert_fusion.2
  836.1 5.4 reduce-scatter.46.cloned.1.call-done
  842.9 54.6 %reduce-scatter.44.cloned.1.call-done = bf16[16,16]{1,0:T(8,128)(2,1)} async-done(((bf16[128,16]{1,0:T(8,128)(2,1)}), bf16[16,16]{1,0:T(8,128)(2,1)}) %reduce-scatter.44.cloned.1.call-update) | async-done | bytes 528
  898.9 70.1 %reduce-scatter.32.cloned.1.call-done = bf16[512,256]{1,0:T(8,128)(2,1)} async-done(((bf16[512,2048]{1,0:T(8,128)(2,1)}), bf16[512,256]{1,0:T(8,128)(2,1)}) %reduce-scatter.32.cloned.1.call-update) | async-done | bytes 262160 | tf_op jit(solution)/shard_map/reduce_scatter | solution.py:280
  970.8 54.8 %reduce-scatter.42.cloned.1.call-done = bf16[16,4]{1,0:T(8,128)(2,1)} async-done(((bf16[128,4]{1,0:T(8,128)(2,1)}), bf16[16,4]{1,0:T(8,128)(2,1)}) %reduce-scatter.42.cloned.1.call-update) | async-done | bytes 144
  1026.9 55.1 %reduce-scatter.40.cloned.1.call-done = bf16[16,4]{1,0:T(8,128)(2,1)} async-done(((bf16[128,4]{1,0:T(8,128)(2,1)}), bf16[16,4]{1,0:T(8,128)(2,1)}) %reduce-scatter.40.cloned.1.call-update) | async-done | bytes 144
  1083.3 52.2 %all-reduce.11.cloned.1.call-done = bf16[512,2048]{1,0:T(8,128)(2,1)} async-done(((bf16[512,2048]{1,0:T(8,128)(2,1)}), bf16[512,2048]{1,0:T(8,128)(2,1)}) %all-reduce.11.cloned.1.call-update) | async-done | bytes 2097168 | tf_op jit(solution)/shard_map/psum | solution.py:255
  1135.5 5.6 add_convert_fusion
  1141.1 65.9 %reduce-scatter.30.cloned.1.call-done = bf16[256,512]{0,1:T(8,128)(2,1)} async-done(((bf16[2048,512]{0,1:T(8,128)(2,1)}), bf16[256,512]{0,1:T(8,128)(2,1)}) %reduce-scatter.30.cloned.1.call-update) | async-done | bytes 262160 | tf_op jit(solution)/shard_map/reduce_scatter | solution.py:269
  1208.9 69.3 %reduce-scatter.26.cloned.1.call-done = bf16[256,512]{0,1:T(8,128)(2,1)} async-done(((bf16[2048,512]{0,1:T(8,128)(2,1)}), bf16[256,512]{0,1:T(8,128)(2,1)}) %reduce-scatter.26.cloned.1.call-update) | async-done | bytes 262160 | tf_op jit(solution)/shard_map/reduce_scatter | solution.py:263
  1280.1 68.6 %reduce-scatter.28.cloned.1.call-done = bf16[256,512]{0,1:T(8,128)(2,1)} async-done(((bf16[2048,512]{0,1:T(8,128)(2,1)}), bf16[256,512]{0,1:T(8,128)(2,1)}) %reduce-scatter.28.cloned.1.call-update) | async-done | bytes 262160 | tf_op jit(solution)/shard_map/reduce_scatter | solution.py:266
  1350.6 150.0 %reduce-scatter.38.cloned.1.call-done = bf16[2048,256]{1,0:T(8,128)(2,1)} async-done(((bf16[2048,2048]{1,0:T(8,128)(2,1)}), bf16[2048,256]{1,0:T(8,128)(2,1)}) %reduce-scatter.38.cloned.1.call-update) | async-done | bytes 1048592 | tf_op jit(solution)/shard_map/reduce_scatter | solution.py:283
  1503.3 149.3 %reduce-scatter.36.cloned.1.call-done = bf16[256,2048]{1,0:T(8,128)(2,1)} async-done(((bf16[2048,2048]{1,0:T(8,128)(2,1)}), bf16[256,2048]{1,0:T(8,128)(2,1)}) %reduce-scatter.36.cloned.1.call-update) | async-done | bytes 1048592 | tf_op jit(solution)/shard_map/reduce_scatter | solution.py:275
  1655.4 148.9 %reduce-scatter.34.cloned.1.call-done = bf16[256,2048]{1,0:T(8,128)(2,1)} async-done(((bf16[2048,2048]{1,0:T(8,128)(2,1)}), bf16[256,2048]{1,0:T(8,128)(2,1)}) %reduce-scatter.34.cloned.1.call-update) | async-done | bytes 1048592 | tf_op jit(solution)/shard_map/reduce_scatter | solution.py:272
  (322 shorter events, 127.8 us)
Async XLA Ops:
  7.2 8.9 copy-start
  7.2 81.1 %all-gather.7.cloned.1.call-start = ((), (), s32[]{:S(2)}) async-start(), calls=%async_computation.14 | async-start | bytes 4718592 | tf_op jit(solution)/shard_map/all_gather | solution.py:86
  11.7 152.6 %all-gather.5.cloned.1.call-start = ((), (), s32[]{:S(2)}) async-start(), calls=%async_computation.13 | async-start | bytes 4718592 | tf_op jit(solution)/shard_map/all_gather | solution.py:85
  12.4 3.7 copy-start.13
  16.1 13.5 copy-start.9
  16.1 12.0 copy-start.30
  16.1 13.4 copy-start.32
  26.9 2.9 copy-start.26
  26.9 2.8 copy-start.28
  28.1 2.9 copy-start.19
  28.1 30.3 %copy-start.34 = (s32[512]{0:T(512)S(1)}, s32[512]{0:T(512)}, u32[]{:S(2)}) copy-start(s32[512]{0:T(512)} %param.30) | copy-start | bytes 6148
  31.0 292.5 %all-reduce.5.cloned.1.call-start = ((), (), s32[]{:S(2)}) async-start(), calls=%async_computation.15 | async-start | bytes 4194304 | tf_op jit(solution)/shard_map/psum | solution.py:150
  251.3 74.3 %copy-start.21 = (bf16[512,4,128]{0,2,1:T(8,128)(2,1)}, bf16[512,4,128]{0,2,1:T(8,128)(2,1)S(1)}, u32[]{:S(2)}) copy-start(bf16[512,4,128]{0,2,1:T(8,128)(2,1)S(1)} %copy.70) | copy-start | bytes 1572868
  251.3 74.3 %copy-start.24 = (f32[16,128]{1,0:T(8,128)S(1)}, f32[16,128]{1,0:T(8,128)}, u32[]{:S(2)}) copy-start(f32[16,128]{1,0:T(8,128)} %param.42) | copy-start | bytes 24580
  255.8 146.3 %all-reduce.7.cloned.1.call-start = ((), (), s32[]{:S(2)}) async-start(), calls=%async_computation.16 | async-start | bytes 4194304 | tf_op jit(solution)/shard_map/psum | solution.py:163
  325.6 11.2 slice-start.2
  329.1 7.8 copy-start.17
  329.1 7.8 slice-start.3
  329.1 15.6 slice-start
  336.9 6.5 copy-start.37
  336.9 7.8 slice-start.1
  343.4 1.3 copy-start.36
  350.4 53.9 %copy-start.25 = (f32[16,128]{1,0:T(8,128)S(1)}, f32[16,128]{1,0:T(8,128)}, u32[]{:S(2)}) copy-start(f32[16,128]{1,0:T(8,128)} %param.43) | copy-start | bytes 24580
  350.5 138.0 %all-reduce.9.cloned.1.call-start = ((), (), s32[]{:S(2)}) async-start(), calls=%async_computation.17 | async-start | bytes 4194304 | tf_op jit(solution)/shard_map/psum | solution.py:181
  402.1 5.8 copy-start.5
  402.1 5.8 copy-start.8
  419.6 7.8 copy-start.38
  419.6 7.8 copy-start.39
  436.8 256.1 %reduce-scatter.22.cloned.1.call-start = ((), (), s32[]{:S(2)}) async-start(), calls=%async_computation.18 | async-start | bytes 4718592 | tf_op jit(solution)/shard_map/reduce_scatter | solution.py:221
  488.5 4.5 copy-start.4
  488.5 4.5 copy-start.6
  488.5 4.7 copy-start.7
  493.2 7.3 copy-start.35
  499.2 1.3 copy-start.18
  515.1 1.2 copy-start.1
  518.6 1.0 copy-start.2
  548.8 1.2 copy-start.1
  552.3 1.0 copy-start.2
  585.2 199.5 %reduce-scatter.24.cloned.1.call-start = ((), (), s32[]{:S(2)}) async-start(), calls=%async_computation.19 | async-start | bytes 4718592 | tf_op jit(solution)/shard_map/reduce_scatter | solution.py:227
  599.7 241.8 %reduce-scatter.46.cloned.1.call-start = ((), (), s32[]{:S(2)}) async-start(), calls=%async_computation.31 | async-start | bytes 36864
  600.5 297.1 %reduce-scatter.44.cloned.1.call-start = ((), (), s32[]{:S(2)}) async-start(), calls=%async_computation.30 | async-start | bytes 36864
  601.2 4.5 copy-start.3
  601.3 367.7 %reduce-scatter.32.cloned.1.call-start = ((), (), s32[]{:S(2)}) async-start(), calls=%async_computation.24 | async-start | bytes 2359296 | tf_op jit(solution)/shard_map/reduce_scatter | solution.py:280
  605.7 88.3 %copy-start.20 = (f32[512,64]{0,1:T(8,128)S(1)}, f32[512,64]{0,1:T(8,128)}, u32[]{:S(2)}) copy-start(f32[512,64]{0,1:T(8,128)} %copy-done.19) | copy-start | bytes 393220
  605.7 88.3 %copy-start.23 = (f32[512,64]{0,1:T(8,128)S(1)}, f32[512,64]{0,1:T(8,128)}, u32[]{:S(2)}) copy-start(f32[512,64]{0,1:T(8,128)} %get-tuple-element.872) | copy-start | bytes 393220
  605.7 419.8 %reduce-scatter.42.cloned.1.call-start = ((), (), s32[]{:S(2)}) async-start(), calls=%async_computation.29 | async-start | bytes 36864
  694.1 1.5 copy-start.11
  694.1 1.5 copy-start.29
  694.1 1.5 copy-start.31
  694.4 2.9 copy-start.10
  694.4 2.9 copy-start.27
  694.4 2.9 copy-start.33
  707.5 5.8 copy-start.14
  710.0 3.4 copy-start.16
  713.3 368.7 %reduce-scatter.40.cloned.1.call-start = ((), (), s32[]{:S(2)}) async-start(), calls=%async_computation.28 | async-start | bytes 36864
  719.0 416.5 %all-reduce.11.cloned.1.call-start = ((), (), s32[]{:S(2)}) async-start(), calls=%async_computation.20 | async-start | bytes 4194304 | tf_op jit(solution)/shard_map/psum | solution.py:255
  784.8 6.9 copy-start.22
  791.7 415.4 %reduce-scatter.30.cloned.1.call-start = ((), (), s32[]{:S(2)}) async-start(), calls=%async_computation.23 | async-start | bytes 2359296 | tf_op jit(solution)/shard_map/reduce_scatter | solution.py:269
  796.0 4.4 copy-start.15
  796.0 482.2 %reduce-scatter.26.cloned.1.call-start = ((), (), s32[]{:S(2)}) async-start(), calls=%async_computation.21 | async-start | bytes 2359296 | tf_op jit(solution)/shard_map/reduce_scatter | solution.py:263
  800.3 548.4 %reduce-scatter.28.cloned.1.call-start = ((), (), s32[]{:S(2)}) async-start(), calls=%async_computation.22 | async-start | bytes 2359296 | tf_op jit(solution)/shard_map/reduce_scatter | solution.py:266
  804.6 696.0 %reduce-scatter.38.cloned.1.call-start = ((), (), s32[]{:S(2)}) async-start(), calls=%async_computation.27 | async-start | bytes 9437184 | tf_op jit(solution)/shard_map/reduce_scatter | solution.py:283
  815.6 836.9 %reduce-scatter.36.cloned.1.call-start = ((), (), s32[]{:S(2)}) async-start(), calls=%async_computation.26 | async-start | bytes 9437184 | tf_op jit(solution)/shard_map/reduce_scatter | solution.py:275
  826.0 978.3 %reduce-scatter.34.cloned.1.call-start = ((), (), s32[]{:S(2)}) async-start(), calls=%async_computation.25 | async-start | bytes 9437184 | tf_op jit(solution)/shard_map/reduce_scatter | solution.py:272
  (1 other events, 1.0 us)
Sparse Core Ops, SparseCore 0:
  11.8 76.4 all-gather.6
  90.9 73.3 all-gather.4
  255.9 67.5 all-reduce.4
  350.6 51.4 all-reduce.6
  437.0 51.4 all-reduce.8
  585.4 107.4 reduce-scatter.21
  696.5 88.2 reduce-scatter.23
  788.2 53.2 reduce-scatter.45
  845.0 52.5 reduce-scatter.43
  901.9 67.0 reduce-scatter.31
  973.0 52.4 reduce-scatter.41
  1029.4 52.5 reduce-scatter.39
  1085.0 50.4 all-reduce.10
  1138.9 68.0 reduce-scatter.29
  1211.0 67.2 reduce-scatter.25
  1281.6 67.0 reduce-scatter.27
  1352.2 148.3 reduce-scatter.37
  1504.5 148.0 reduce-scatter.35
  1656.2 148.0 reduce-scatter.33
where the time goes:
time: 1820 us; the launch traced here: 1810 us
  waiting for transfers between devices  1330 us (73%)
  matrix products  157 us (9%)
  local copies, waits for them, and re-layouts  89.6 us (5%)
  other arithmetic  86.4 us (5%)
  blocking collectives  68.8 us (4%)
  loops' own time  63.2 us (3%)
    unnamed x23, waiting for transfers between devices  170 us
    reduce_scatter x1, waiting for transfers between devices, on_device(): lax.psum_scatter(grad_w_down.astype(jnp.bfloat16), 'dp', scatter_dimensio...  150 us
    reduce_scatter x1, waiting for transfers between devices, on_device(): lax.psum_scatter(local_w_up.astype(jnp.bfloat16), 'dp', scatter_dimension...  149 us
    reduce_scatter x1, waiting for transfers between devices, on_device(): lax.psum_scatter(local_w_gate.astype(jnp.bfloat16), 'dp', scatter_dimensi...  149 us
    reduce_scatter x1, waiting for transfers between devices, on_device(): lax.psum_scatter((key_terms.reshape(key_rows, local_width) * score_scale)...  84.4 us
    reduce_scatter x1, waiting for transfers between devices, on_device(): lax.psum_scatter(grad_w_output.astype(jnp.bfloat16), 'dp', scatter_dimens...  70.1 us
    reduce_scatter x1, waiting for transfers between devices, on_device(): lax.psum_scatter(local_w_query.astype(jnp.bfloat16), 'dp', scatter_dimens...  69.3 us
    reduce_scatter x1, waiting for transfers between devices, on_device(): lax.psum_scatter(local_w_key.astype(jnp.bfloat16), 'dp', scatter_dimensio...  68.6 us
  transfers between devices with their start and end apart: 19, of which 19 were waited for; matrix products, arithmetic and copies ran while one was open for 8% of the time, Pallas kernels for 0%

commit v1 on v0

--- a/solution.py
+++ b/solution.py
@@ -1,8 +1,11 @@
+import functools
 import math
 
 import jax
 import jax.numpy as jnp
 from jax import lax
+from jax.experimental import pallas as pl
+from jax.experimental.pallas import tpu as pltpu
 from jax.sharding import PartitionSpec as P
 
 epsilon = 1e-06
@@ -29,7 +32,7 @@
     return factor * (grad_normed - normed * jnp.mean(grad_normed * normed, axis=-1, keepdims=True))
 
 
-def on_device(
+def on_device_general(
     tokens,
     cotangent,
     doc_ids,
@@ -319,9 +322,512 @@
     )
 
 
+line = 4
+pair = 2
+low_score = -1e30
+start_max = -1e20
+
+
+def line_shift(value, step):
+    moves = [
+        (z * pair + x, ((z + step) % line) * pair + x) for z in range(line) for x in range(pair)
+    ]
+    return lax.ppermute(value, "dp", moves)
+
+
+def line_send(value, moves):
+    return lax.ppermute(
+        value, "dp", [(a * pair + x, b * pair + x) for a, b in moves for x in range(pair)]
+    )
+
+
+def x_swap(value):
+    return lax.ppermute(value, "dp", [(i, i ^ 1) for i in range(line * pair)])
+
+
+def core_swap(value):
+    return lax.ppermute(value, "mp", [(i, i ^ 1) for i in range(4)])
+
+
+def y_swap(value):
+    return lax.ppermute(value, "mp", [(i, i ^ 2) for i in range(4)])
+
+
+def token_sum(value):
+    half = value.shape[1] // 2
+    arrived = core_swap(value)
+    value = value + jnp.concatenate([arrived[:, half:], arrived[:, :half]], axis=1)
+    return value + y_swap(value)
+
+
+def reduce_own_rows(partial_low):
+    f32 = jnp.float32
+    half = partial_low.shape[0] // 2
+    arrived = core_swap(partial_low[half:])
+    chip_sum = (partial_low[:half].astype(f32) + arrived.astype(f32)).astype(jnp.bfloat16)
+    return chip_sum.astype(f32) + y_swap(chip_sum).astype(f32)
+
+
+def share_rows(own):
+    return jnp.concatenate([own, core_swap(own)], axis=0)
+
+
+def line_scatter(terms, axis, z):
+    f32 = jnp.float32
+    bf16 = jnp.bfloat16
+    width = terms.shape[axis] // line
+
+    def block(index):
+        return lax.dynamic_slice_in_dim(terms, index * width, width, axis)
+
+    right, left = None, None
+    for step in range(1, line):
+        right_term = block(lax.rem(2 * line - step + z, line))
+        left_term = block(lax.rem(step + z, line))
+        if right is not None:
+            right_term = (right_term.astype(f32) + right.astype(f32)).astype(bf16)
+            left_term = (left_term.astype(f32) + left.astype(f32)).astype(bf16)
+        right = line_send(right_term, [(a, a + 1) for a in range(step)])
+        left = line_send(left_term, [(line - 1 - a, line - 2 - a) for a in range(step)])
+    return block(z).astype(f32) + right.astype(f32) + left.astype(f32)
+
+
+def own_columns(value, x):
+    width = value.shape[1] // (line * pair)
+    return jnp.concatenate(
+        [
+            lax.dynamic_slice_in_dim(value, (z * pair + x) * width, width, 1)
+            for z in range(line)
+        ],
+        axis=1,
+    )
+
+
+def dot_t(first, second):
+    return lax.dot_general(
+        first, second, (((0,), (0,)), ((), ())), preferred_element_type=jnp.float32
+    )
+
+
+def dot_nt(first, second):
+    return lax.dot_general(
+        first, second, (((1,), (1,)), ((), ())), preferred_element_type=jnp.float32
+    )
+
+
+def visible_scores(key, query, key_code, query_code, query_low, factor):
+    scores = dot_nt(key, query) * factor
+    codes = jnp.concatenate([key_code] * (query.shape[0] // key_code.shape[1]), axis=1)
+    return jnp.where((codes <= query_code) & (codes >= query_low), scores, low_score)
+
+
+def attend_kernel(factor, *refs):
+    live, codes, rows = refs[0], refs[1], refs[2]
+    query_refs = refs[3:7]
+    pair_refs = refs[7:15]
+    out_turned, out_log = refs[15], refs[16]
+    out_refs = refs[17:21]
+    top, total, accum = refs[21:24]
+    f32 = jnp.float32
+    bf16 = jnp.bfloat16
+    for q in range(line):
+        top[...] = jnp.full_like(top, start_max)
+        total[...] = jnp.zeros_like(total)
+        accum[...] = jnp.zeros_like(accum)
+        for k in range(2 * line):
+
+            @pl.when(live[q, k] > 0)
+            def _(q=q, k=k):
+                scores = visible_scores(
+                    pair_refs[k][0],
+                    query_refs[q][...],
+                    codes[k],
+                    rows[q : q + 1, :],
+                    rows[line + q : line + q + 1, :],
+                    factor,
+                )
+                highest = jnp.maximum(top[...], jnp.max(scores, axis=0, keepdims=True))
+                weights = jnp.exp2(scores - highest)
+                fade = jnp.exp2(top[...] - highest)
+                total[...] = total[...] * fade + jnp.sum(weights, axis=0, keepdims=True)
+                accum[...] = accum[...] * fade + dot_t(pair_refs[k][1], weights.astype(bf16))
+                top[...] = highest
+
+        turned = accum[...] / total[...]
+        out_turned[q] = turned
+        out_log[q : q + 1, :] = top[...] + jnp.log2(total[...])
+        out_refs[q][...] = turned.T.astype(bf16)
+
+
+def attend_back_kernel(factor, scale, *refs):
+    live, codes, rows = refs[0], refs[1], refs[2]
+    query_refs = refs[3:7]
+    pair_refs = refs[7:15]
+    turned, log_total = refs[15], refs[16]
+    grad_refs = refs[17:21]
+    out_query = refs[21:25]
+    out_pairs = refs[25:33]
+    key_sum, value_sum, query_sum = refs[33:36]
+    f32 = jnp.float32
+    bf16 = jnp.bfloat16
+    key_sum[...] = jnp.zeros_like(key_sum)
+    value_sum[...] = jnp.zeros_like(value_sum)
+    for q in range(line):
+        query_sum[...] = jnp.zeros_like(query_sum)
+        delta = jnp.sum(
+            grad_refs[q][...].astype(f32).T * turned[q], axis=0, keepdims=True
+        )
+        for k in range(2 * line):
+
+            @pl.when(live[q, k] > 0)
+            def _(q=q, k=k, delta=delta):
+                query, key, grad = query_refs[q][...], pair_refs[k][0], grad_refs[q][...]
+                scores = visible_scores(
+                    key,
+                    query,
+                    codes[k],
+                    rows[q : q + 1, :],
+                    rows[line + q : line + q + 1, :],
+                    factor,
+                )
+                probs = jnp.exp2(scores - log_total[q : q + 1, :])
+                grad_probs = dot_nt(pair_refs[k][1], grad)
+                grad_scores = (probs * (grad_probs - delta)).astype(bf16)
+                value_sum[k] += jnp.dot(
+                    probs.astype(bf16), grad, preferred_element_type=f32
+                )
+                key_sum[k] += jnp.dot(grad_scores, query, preferred_element_type=f32)
+                query_sum[...] += dot_t(key, grad_scores)
+
+        out_query[q][...] = (query_sum[...] * scale).T.astype(bf16)
+    for k in range(2 * line):
+        out_pairs[k][0] = (key_sum[k] * scale).astype(bf16)
+        out_pairs[k][1] = value_sum[k].astype(bf16)
+
+
+def vmem_specs(count):
+    return [pl.BlockSpec(memory_space=pltpu.VMEM)] * count
+
+
+def attend(live, codes, rows, queries, pairs):
+    count, width = queries[0].shape
+    factor = math.log2(math.e) / math.sqrt(width)
+    f32 = jnp.float32
+    return pl.pallas_call(
+        functools.partial(attend_kernel, factor),
+        out_shape=[
+            jax.ShapeDtypeStruct((line, width, count), f32),
+            jax.ShapeDtypeStruct((2 * line, count), f32),
+        ]
+        + [jax.ShapeDtypeStruct((count, width), jnp.bfloat16)] * line,
+        in_specs=[pl.BlockSpec(memory_space=pltpu.SMEM)] + vmem_specs(2 + 3 * line),
+        out_specs=vmem_specs(2 + line),
+        scratch_shapes=[
+            pltpu.VMEM((1, count), f32),
+            pltpu.VMEM((1, count), f32),
+            pltpu.VMEM((width, count), f32),
+        ],
+        compiler_params=pltpu.CompilerParams(vmem_limit_bytes=40 << 20),
+        cost_estimate=pl.CostEstimate(
+            flops=10 * 4 * count * count * width,
+            bytes_accessed=8 << 20,
+            transcendentals=10 * count * count,
+        ),
+    )(live, codes, rows, *queries, *pairs)
+
+
+def attend_back(live, codes, rows, queries, pairs, turned, log_total, grads):
+    count, width = queries[0].shape
+    scale = 1.0 / math.sqrt(width)
+    factor = math.log2(math.e) * scale
+    f32 = jnp.float32
+    return pl.pallas_call(
+        functools.partial(attend_back_kernel, factor, scale),
+        out_shape=[jax.ShapeDtypeStruct((count, width), jnp.bfloat16)] * line
+        + [jax.ShapeDtypeStruct((2, count, width), jnp.bfloat16)] * (2 * line),
+        in_specs=[pl.BlockSpec(memory_space=pltpu.SMEM)] + vmem_specs(4 + 4 * line),
+        out_specs=vmem_specs(3 * line),
+        scratch_shapes=[
+            pltpu.VMEM((2 * line, count, width), f32),
+            pltpu.VMEM((2 * line, count, width), f32),
+            pltpu.VMEM((width, count), f32),
+        ],
+        compiler_params=pltpu.CompilerParams(vmem_limit_bytes=40 << 20),
+        cost_estimate=pl.CostEstimate(
+            flops=10 * 10 * count * count * width,
+            bytes_accessed=12 << 20,
+            transcendentals=10 * count * count,
+        ),
+    )(live, codes, rows, *queries, *pairs, turned, log_total, *grads)
+
+
+def on_device_lines(
+    tokens,
+    cotangent,
+    doc_ids,
+    row_ids,
+    offsets,
+    w_query,
+    w_key,
+    w_value,
+    w_output,
+    w_gate,
+    w_up,
+    w_down,
+    gain_query,
+    gain_key,
+    gain_attn,
+    gain_mlp,
+):
+    f32 = jnp.float32
+    bf16 = jnp.bfloat16
+    row_count, model_width = tokens.shape
+    heads_here, head_width = gain_query.shape
+    local_width = heads_here * head_width
+    half_rows = row_count // 2
+    key_rows = row_count * line * pair
+    place = lax.axis_index("dp")
+    z, x = place // pair, lax.rem(place, pair)
+    core = lax.rem(lax.axis_index("mp"), 2)
+
+    def own_rows(value):
+        return lax.dynamic_slice_in_dim(value, core * half_rows, half_rows, 0)
+
+    def other_rows(value):
+        return lax.dynamic_slice_in_dim(value, (1 - core) * half_rows, half_rows, 0)
+
+    def reorder(value):
+        return jnp.concatenate([own_rows(value), other_rows(value)], axis=0)
+
+    def restore(own, other):
+        whole = jnp.zeros((row_count,) + own.shape[1:], own.dtype)
+        whole = lax.dynamic_update_slice_in_dim(whole, own, core * half_rows, 0)
+        return lax.dynamic_update_slice_in_dim(whole, other, (1 - core) * half_rows, 0)
+
+    own_tokens = own_rows(tokens)
+    tokens_in = reorder(tokens)
+    positions = reorder(offsets[0] + jnp.arange(row_count, dtype=jnp.int32))
+    labels = reorder(row_ids[0] * key_rows + doc_ids)
+
+    code = labels * key_rows + positions
+    line_codes = [code] + [line_shift(code, d) for d in range(1, line)]
+    line_codes = jnp.stack(line_codes)
+    all_codes = jnp.concatenate([line_codes, x_swap(line_codes)], axis=0)
+    query_low = (line_codes // key_rows) * key_rows
+    code_rows = jnp.concatenate([line_codes, query_low], axis=0)
+    code_columns = jnp.broadcast_to(all_codes[:, :, None], (2 * line, row_count, 128))
+    live = (
+        (jnp.min(all_codes, axis=1)[None, :] <= jnp.max(line_codes, axis=1)[:, None])
+        & (jnp.max(all_codes, axis=1)[None, :] >= jnp.min(query_low, axis=1)[:, None])
+    ).astype(jnp.int32)
+
+    freqs = rope_base ** (-jnp.arange(0, head_width // 2, dtype=f32) * 2.0 / head_width)
+    angles = positions.astype(f32)[:, None] * freqs[None, :]
+    cosines, sines = jnp.cos(angles), jnp.sin(angles)
+    cosines = jnp.concatenate([cosines, cosines], axis=1)
+    sines = jnp.concatenate([-sines, sines], axis=1)
+
+    def turn(value, sign_sines):
+        swapped = jnp.concatenate(
+            [value[:, head_width // 2 :], value[:, : head_width // 2]], axis=1
+        )
+        return value * cosines + swapped * sign_sines
+
+    other_half_tokens = x_swap(own_columns(own_tokens, 1 - x))
+    tokens_half = own_columns(tokens_in, x)
+    tokens_half_x = share_rows(other_half_tokens)
+
+    q_raw = jnp.dot(tokens_in, w_query, preferred_element_type=f32)
+    k_raw = jnp.dot(tokens_in, w_key, preferred_element_type=f32)
+    values_low = jnp.dot(tokens_in, w_value, preferred_element_type=f32).astype(bf16)
+    squares = token_sum(
+        jnp.stack([jnp.sum(q_raw * q_raw, axis=1), jnp.sum(k_raw * k_raw, axis=1)])
+    )
+    q_factor = lax.rsqrt(squares[0] / model_width + epsilon)[:, None]
+    k_factor = lax.rsqrt(squares[1] / model_width + epsilon)[:, None]
+    g_query = gain_query.reshape(1, local_width)
+    g_key = gain_key.reshape(1, local_width)
+    q_normed = q_raw * q_factor
+    k_normed = k_raw * k_factor
+
+    def head_of(value, d):
+        return lax.dynamic_slice_in_dim(
+            value, lax.rem(z + d, line) * head_width, head_width, 1
+        )
+
+    queries, pairs = [], []
+    for d in range(line):
+        query = turn(head_of(q_normed * g_query, d), sines).astype(bf16)
+        key = turn(head_of(k_normed * g_key, d), sines).astype(bf16)
+        both = jnp.stack([key, head_of(values_low, d)])
+        queries.append(query if d == 0 else line_shift(query, d))
+        pairs.append(both if d == 0 else line_shift(both, d))
+    pairs = pairs + [x_swap(both) for both in pairs]
+
+    turned, log_total, *attended_out = attend(live, code_columns, code_rows, queries, pairs)
+
+    def gather_heads(pieces):
+        home = [pieces[0]] + [line_shift(pieces[d], line - d) for d in range(1, line)]
+        twice = jnp.concatenate(home + home, axis=1)
+        return lax.dynamic_slice_in_dim(
+            twice, lax.rem(line - z, line) * head_width, local_width, 1
+        )
+
+    attended_low = gather_heads(attended_out)
+    attended_x = x_swap(attended_low)
+    attn_sum = reduce_own_rows(
+        jnp.dot(attended_low, w_output, preferred_element_type=f32).astype(bf16)
+    )
+    attn_factor = lax.rsqrt(jnp.mean(attn_sum * attn_sum, axis=1, keepdims=True) + epsilon)
+    attn_normed = attn_sum * attn_factor
+    g_attn = gain_attn.reshape(1, model_width)
+    hidden = own_tokens.astype(f32) + attn_normed * g_attn
+    own_hidden_low = hidden.astype(bf16)
+    hidden_low = share_rows(own_hidden_low)
+    hidden_half = own_columns(hidden_low, x)
+    hidden_half_x = share_rows(x_swap(own_columns(own_hidden_low, 1 - x)))
+
+    gate_val = jnp.dot(hidden_low, w_gate, preferred_element_type=f32)
+    up_val = jnp.dot(hidden_low, w_up, preferred_element_type=f32)
+    sigmoid_gate = jax.nn.sigmoid(gate_val)
+    silu_gate = gate_val * sigmoid_gate
+    act_low = (silu_gate * up_val).astype(bf16)
+    act_x = x_swap(act_low)
+    mlp_sum = reduce_own_rows(
+        jnp.dot(act_low, w_down, preferred_element_type=f32).astype(bf16)
+    )
+    mlp_factor = lax.rsqrt(jnp.mean(mlp_sum * mlp_sum, axis=1, keepdims=True) + epsilon)
+    mlp_normed = mlp_sum * mlp_factor
+    g_mlp = gain_mlp.reshape(1, model_width)
+    own_output = (hidden + mlp_normed * g_mlp).astype(bf16)
+    output = restore(own_output, core_swap(own_output))
+
+    grad_out = own_rows(cotangent).astype(f32)
+    grad_gain_mlp = jnp.sum(grad_out * mlp_normed, axis=0)
+    own_grad_mlp = norm_back(grad_out * g_mlp, mlp_normed, mlp_factor).astype(bf16)
+    grad_mlp = share_rows(own_grad_mlp)
+    grad_mlp_half = own_columns(grad_mlp, x)
+    grad_mlp_half_x = share_rows(x_swap(own_columns(own_grad_mlp, 1 - x)))
+    grad_act = dot_nt(grad_mlp, w_down)
+    slope = sigmoid_gate * (1.0 + gate_val * (1.0 - sigmoid_gate))
+    grad_gate = (grad_act * up_val * slope).astype(bf16)
+    grad_up = (grad_act * silu_gate).astype(bf16)
+    grad_gate_x = x_swap(grad_gate)
+    grad_up_x = x_swap(grad_up)
+    branch_sum = reduce_own_rows(
+        (dot_nt(grad_gate, w_gate) + dot_nt(grad_up, w_up)).astype(bf16)
+    )
+
+    terms_down = (dot_t(act_low, grad_mlp_half) + dot_t(act_x, grad_mlp_half_x)).astype(bf16)
+    terms_gate = (dot_t(hidden_half, grad_gate) + dot_t(hidden_half_x, grad_gate_x)).astype(bf16)
+    terms_up = (dot_t(hidden_half, grad_up) + dot_t(hidden_half_x, grad_up_x)).astype(bf16)
+    grad_w_down = line_scatter(terms_down, 1, z)
+    grad_w_gate = line_scatter(terms_gate, 0, z)
+    grad_w_up = line_scatter(terms_up, 0, z)
+
+    grad_hidden = grad_out + branch_sum
+    grad_gain_attn = jnp.sum(grad_hidden * attn_normed, axis=0)
+    own_grad_attn = norm_back(grad_hidden * g_attn, attn_normed, attn_factor).astype(bf16)
+    grad_attn = share_rows(own_grad_attn)
+    grad_attn_half = own_columns(grad_attn, x)
+    grad_attn_half_x = share_rows(x_swap(own_columns(own_grad_attn, 1 - x)))
+    grad_attended = dot_nt(grad_attn, w_output).astype(bf16)
+    grads = [
+        head_of(grad_attended, d) if d == 0 else line_shift(head_of(grad_attended, d), d)
+        for d in range(line)
+    ]
+    terms_out = (
+        dot_t(attended_low, grad_attn_half) + dot_t(attended_x, grad_attn_half_x)
+    ).astype(bf16)
+    grad_w_output = line_scatter(terms_out, 1, z)
+
+    back = attend_back(live, code_columns, code_rows, queries, pairs, turned, log_total, grads)
+    grad_query_pieces, grad_pairs = back[:line], back[line:]
+    grad_queries = gather_heads(grad_query_pieces).astype(f32)
+    summed_pairs = [
+        (grad_pairs[d].astype(f32) + x_swap(grad_pairs[line + d]).astype(f32)).astype(bf16)
+        for d in range(line)
+    ]
+    home = [summed_pairs[0]] + [line_shift(summed_pairs[d], line - d) for d in range(1, line)]
+
+    def place_heads(index):
+        twice = jnp.concatenate([piece[index] for piece in home + home], axis=1)
+        return lax.dynamic_slice_in_dim(
+            twice, lax.rem(line - z, line) * head_width, local_width, 1
+        )
+
+    grad_keys = place_heads(0).astype(f32)
+    grad_values_low = place_heads(1)
+
+    def turn_back(value):
+        return jnp.concatenate(
+            [
+                turn(value[:, h * head_width : (h + 1) * head_width], -sines)
+                for h in range(heads_here)
+            ],
+            axis=1,
+        )
+
+    back_q = turn_back(grad_queries)
+    back_k = turn_back(grad_keys)
+    grad_gain_query = jnp.sum(back_q * q_normed, axis=0)
+    grad_gain_key = jnp.sum(back_k * k_normed, axis=0)
+    scaled_q = back_q * g_query
+    scaled_k = back_k * g_key
+    inner = token_sum(
+        jnp.stack([jnp.sum(scaled_q * q_normed, axis=1), jnp.sum(scaled_k * k_normed, axis=1)])
+    )
+    grad_q_raw = (q_factor * (scaled_q - q_normed * inner[0][:, None] / model_width)).astype(bf16)
+    grad_k_raw = (k_factor * (scaled_k - k_normed * inner[1][:, None] / model_width)).astype(bf16)
+    grad_raw = jnp.concatenate([grad_q_raw, grad_k_raw, grad_values_low], axis=1)
+    grad_raw_x = x_swap(grad_raw)
+    input_sum = reduce_own_rows(
+        (
+            dot_nt(grad_q_raw, w_query)
+            + dot_nt(grad_k_raw, w_key)
+            + dot_nt(grad_values_low, w_value)
+        ).astype(bf16)
+    )
+    own_grad_tokens = (grad_hidden + input_sum).astype(bf16)
+    grad_tokens = restore(own_grad_tokens, core_swap(own_grad_tokens))
+    terms_raw = (dot_t(tokens_half, grad_raw) + dot_t(tokens_half_x, grad_raw_x)).astype(bf16)
+    summed_raw = line_scatter(terms_raw, 0, z)
+
+    wide = jnp.concatenate([grad_gain_attn, grad_gain_mlp])
+    wide = wide + core_swap(wide)
+    gains = jnp.concatenate([wide, grad_gain_query, grad_gain_key])
+    gains = gains + x_swap(gains)
+    for flip in (1, 2):
+        gains = gains + line_send(gains, [(a, a ^ flip) for a in range(line)])
+    piece = head_width // (line * pair)
+
+    def gain_piece(start, rows):
+        part = gains[start : start + rows * head_width].reshape(rows, head_width)
+        return lax.dynamic_slice_in_dim(part, place * piece, piece, 1)
+
+    all_heads = model_width // head_width
+    return (
+        output,
+        grad_tokens,
+        summed_raw[:, :local_width],
+        summed_raw[:, local_width : 2 * local_width],
+        summed_raw[:, 2 * local_width :],
+        grad_w_output,
+        grad_w_gate,
+        grad_w_up,
+        grad_w_down,
+        gain_piece(2 * model_width, heads_here),
+        gain_piece(2 * model_width + local_width, heads_here),
+        gain_piece(0, all_heads),
+        gain_piece(model_width, all_heads),
+    )
+
+
 def solution(mesh):
+    tuned = mesh.shape["dp"] == line * pair and mesh.shape["mp"] == 4
+    body = on_device_lines if tuned else on_device_general
     return jax.shard_map(
-        on_device,
+        body,
         mesh=mesh,
         in_specs=(
             P("dp", None),

time: 1820 us -> 797 us (0.44)
  waiting for transfers between devices: 1330 us -> 375 us
  starting transfers between devices: 2.05 us -> 143 us
  blocking collectives: 68.8 us -> 0 us
  loops' own time: 63.2 us -> 0 us
  local copies, waits for them, and re-layouts: 89.6 us -> 42.3 us
  Pallas kernels: 0 us -> 42.1 us
  matrix products: 157 us -> 119 us
  other arithmetic: 86.4 us -> 61.3 us
    reduce_scatter x9 -> x0, waiting for transfers between devices: 872 us -> none  [the longest x1 150 us: on_device(): lax.psum_scatter(grad_w_down.astype(jnp.bfloat16), 'dp', scatter_dimensio...]
    ppermute x0 -> x94, waiting for transfers between devices: none -> 375 us  [the longest x32 156 us: line_send(): lax.ppermute(value, 'dp', [(a * pair + x, b * pair + x) for a, b in moves...]
    psum x4 -> x0, waiting for transfers between devices: 222 us -> none  [the longest x1 67.5 us: on_device(): lax.psum(jnp.dot(attended_low, w_output, preferred_element_type=f32).asty...]
    unnamed x23 -> x0, waiting for transfers between devices: 170 us -> none
    ppermute x0 -> x94, starting transfers between devices: none -> 143 us  [the longest x32 80.4 us: line_send(): lax.ppermute(value, 'dp', [(a * pair + x, b * pair + x) for a, b in moves...]
    all_gather x2 -> x0, waiting for transfers between devices: 65.7 us -> none  [the longest x1 63.7 us: on_device(): lax.all_gather(keys_low.reshape(row_count, local_width), 'dp', axis=0, ti...]
    another operation x27 -> x0, loops' own time: 63.2 us -> none  [the longest x1 21 us: on_device(): lax.scan(grad_step, jnp.zeros((row_count, heads_here, head_width), f32),...]
    all_gather x2 -> x0, blocking collectives: 53.5 us -> none  [the longest x1 26.8 us: on_device(): lax.all_gather(labels, 'dp', axis=0, tiled=True)]
  transfers between devices with their start and end apart: 19 -> 94, of which waited for: 19 -> 40; matrix products, arithmetic and copies ran while one was open for 8% -> 23% of each run, Pallas kernels for 0% -> 3%
where the time goes in v1:
time: 797 us; the launch traced here: 788 us
  waiting for transfers between devices  375 us (47%)
  starting transfers between devices  143 us (18%)
  matrix products  119 us (15%)
  other arithmetic  61.3 us (8%)
  local copies, waits for them, and re-layouts  42.3 us (5%)
  Pallas kernels  42.1 us (5%)
    ppermute x32, waiting for transfers between devices, line_send(): lax.ppermute(value, 'dp', [(a * pair + x, b * pair + x) for a, b in moves...  156 us
    ppermute x21, waiting for transfers between devices, line_shift(): return lax.ppermute(value, 'dp', moves)  89.9 us
    ppermute x19, waiting for transfers between devices, x_swap(): return lax.ppermute(value, 'dp', [(i, i ^ 1) for i in range(line * pair)])  84.6 us
    ppermute x32, starting transfers between devices, line_send(): lax.ppermute(value, 'dp', [(a * pair + x, b * pair + x) for a, b in moves...  80.4 us
    dot_general x10, matrix products, dot_t(): lax.dot_general(first, second, (((0,), (0,)), ((), ())), preferred_elemen...  52.8 us
    ppermute x21, starting transfers between devices, line_shift(): return lax.ppermute(value, 'dp', moves)  39.1 us
    dot_general x7, matrix products, dot_nt(): lax.dot_general(first, second, (((1,), (1,)), ((), ())), preferred_elemen...  35.6 us
    ppermute x6, waiting for transfers between devices, y_swap(): return lax.ppermute(value, 'mp', [(i, i ^ 2) for i in range(4)])  35.4 us
  transfers between devices with their start and end apart: 94, of which 40 were waited for; matrix products, arithmetic and copies ran while one was open for 23% of the time, Pallas kernels for 3%

profile of v1, /device:TPU:0, one launch (start us, length us, event | category | flops | bytes accessed | tf_op | source)
XLA Modules:
  0.0 788.1 jit_solution(14681737674250663855)
XLA Ops:
  3.5 3.0 collective-permute-start
  18.0 4.0 convolution_convert_fusion.2
  48.0 3.2 collective-permute-start.10
  56.4 2.7 collective-permute-done.9.refs_8_
  59.7 10.7 %collective-permute-done.10.refs_9_ = bf16[2,512,128]{2,1,0:T(8,128)(2,1)S(1)} collective-permute-done((bf16[2,512,128]{2,1,0:T(8,128)(2,1)}, bf16[2,512,128]{2,1,0:T(8,128)(2,1)S(1)}, u32[]{:S(2)}, u32[]{:S(2)}) %collective-permute-start.10) | collective-permute-done | bytes 262176 | tf_op jit(solution)/shard_map/ppermute | solution.py:335
  72.5 8.0 %collective-permute-done.7.refs_5_ = bf16[512,128]{1,0:T(8,128)(2,1)} collective-permute-done((bf16[512,128]{1,0:T(8,128)(2,1)}, bf16[512,128]{1,0:T(8,128)(2,1)}, u32[]{:S(2)}, u32[]{:S(2)}) %collective-permute-start.7) | collective-permute-done | bytes 131104 | tf_op jit(solution)/shard_map/ppermute | solution.py:335
  80.7 5.5 collective-permute-done.8.refs_6_
  86.9 19.0 %shard_map.255 = (f32[4,128,512]{2,1,0:T(8,128)S(1)}, f32[8,512]{1,0:T(8,128)S(1)}, bf16[512,128]{1,0:T(8,128)(2,1)S(1)}, bf16[512,128]{1,0:T(8,128)(2,1)}, bf16...) custom-call(s32[4,8]{1,0:T(4,128)S(1)} %and_convert_fusion.refs_0_, s32[8,512,128]{2,1,0:T(8,128)S(1)} %broadcast_in_dim.2.refs_1_, ...), custom_call_target="tpu_custom_call" | custom-call | flops 1342177280 | bytes 8388608 | tf_op jit(solution)/shard_map/pallas_call | solution.py:516
  108.2 3.8 collective-permute-start.16
  112.7 3.2 collective-permute-done.16
  116.8 5.3 collective-permute-done.17
  128.8 24.4 %collective-permute-done.20 = bf16[256,2048]{1,0:T(8,128)(2,1)S(1)} collective-permute-done((bf16[256,2048]{1,0:T(8,128)(2,1)S(1)}, bf16[256,2048]{1,0:T(8,128)(2,1)S(1)}, u32[]{:S(2)}, u32[]{:S(2)}) %collective-permute-start.20) | collective-permute-done | bytes 1048608 | tf_op jit(solution)/shard_map/ppermute | solution.py:353
  157.1 6.1 fusion.12
  163.3 8.4 %multiply_convert_fusion.2 = (bf16[512,2048]{1,0:T(8,128)(2,1)}, f32[512,2048]{1,0:T(8,128)}) fusion(f32[512,2048]{1,0:T(8,128)} %fusion.12, bf16[2048,2048]{1,0:T(8,128)(2,1)S(1)} %bitcast.164, bf16[256,2048]{1,0:T(8,128)(2,1)S(1)} %collective-permute-done.21, bf16[256,2048]{1,0:T(8,128)(2,1)S(1)} %fusion.14), kind=kOutput, calls=%fused_computation.8 | convolution fusion | flops 4305453056 | bytes 20971520 | tf_op jit(solution)/shard_map/dot_general | solution.py:691
  171.7 6.8 convolution_convert_fusion
  192.3 8.4 %collective-permute-done.65 = bf16[256,1024]{1,0:T(8,128)(2,1)} collective-permute-done((bf16[256,1024]{1,0:T(8,128)(2,1)}, bf16[256,1024]{1,0:T(8,128)(2,1)}, u32[]{:S(2)}, u32[]{:S(2)}) %collective-permute-start.65) | collective-permute-done | bytes 524320 | tf_op jit(solution)/shard_map/ppermute | solution.py:345
  201.7 6.5 collective-permute-done.23
  219.0 3.9 constant_dynamic-update-slice_fusion.21
  222.9 52.0 %collective-permute-done.82 = bf16[256,1024]{1,0:T(8,128)(2,1)} collective-permute-done((bf16[256,1024]{1,0:T(8,128)(2,1)S(1)}, bf16[256,1024]{1,0:T(8,128)(2,1)}, u32[]{:S(2)}, u32[]{:S(2)}) %collective-permute-start.82) | collective-permute-done | bytes 524320 | tf_op jit(solution)/shard_map/ppermute | solution.py:345
  276.0 13.9 %multiply_convert_fusion = (bf16[512,2048]{1,0:T(8,128)(2,1)}, bf16[512,2048]{1,0:T(8,128)(2,1)}) fusion(f32[512,2048]{1,0:T(8,128)} %fusion.12, f32[512,2048]{1,0:T(8,128)} %get-tuple-element.216, bf16[2048,2048]{1,0:T(8,128)(2,1)} %param.27, bf16[256,2048]{1,0:T(8,128)(2,1)} %copy-done.57, bf16[256,2048]{1,0:T(8,128)(2,1)S(1)} %copy-done.39), kind=kOutput, calls=%fused_computation.6 | convolution fusion | flops 4312793088 | bytes 23068672 | tf_op jit(solution)/shard_map/dot_general | solution.py:413
  289.8 7.8 fusion.153
  298.0 8.7 %add_convert_fusion.5 = bf16[512,2048]{1,0:T(8,128)(2,1)S(1)} fusion(f32[512,2048]{1,0:T(8,128)S(1)} %fusion.153, bf16[512,2048]{1,0:T(8,128)(2,1)} %get-tuple-element.69, bf16[2048,2048]{1,0:T(8,128)(2,1)} %param.26), kind=kOutput, calls=%fused_computation.5 | convolution fusion | flops 4297064448 | bytes 16777216 | tf_op jit(solution)/shard_map/dot_general | solution.py:413
  306.9 7.3 fusion.37
  315.9 6.7 add_convert_fusion
  324.7 7.3 fusion.91
  337.1 8.0 %fusion.90 = f32[1024,2048]{1,0:T(8,128)} fusion(bf16[512,2048]{1,0:T(8,128)(2,1)} %get-tuple-element.69, bf16[512,256]{1,0:T(8,128)(2,1)S(1)} %copy-done.76, bf16[512,256]{1,0:T(8,128)(2,1)S(1)} %copy-done.75, bf16[512,256]{1,0:T(8,128)(2,1)S(1)} %copy-done.74, bf16[512,256]{1,0:T(8,128)(2,1)S(1)} %copy-done.73), kind=kOutput, calls=%fused_computation.238 | convolution fusion | flops 2151677952 | bytes 11534336 | tf_op jit(solution)/shard_map/dot_general | solution.py:407
  345.1 12.1 %collective-permute-done.84 = bf16[2048,256]{1,0:T(8,128)(2,1)S(1)} collective-permute-done((bf16[2048,256]{1,0:T(8,128)(2,1)S(1)}, bf16[2048,256]{1,0:T(8,128)(2,1)S(1)}, u32[]{:S(2)}, u32[]{:S(2)}) %collective-permute-start.84) | collective-permute-done | bytes 1048608 | tf_op jit(solution)/shard_map/ppermute | solution.py:339
  366.5 18.5 %collective-permute-done.85 = bf16[2048,256]{1,0:T(8,128)(2,1)S(1)} collective-permute-done((bf16[2048,256]{1,0:T(8,128)(2,1)S(1)}, bf16[2048,256]{1,0:T(8,128)(2,1)S(1)}, u32[]{:S(2)}, u32[]{:S(2)}) %collective-permute-start.85) | collective-permute-done | bytes 1048608 | tf_op jit(solution)/shard_map/ppermute | solution.py:339
  388.1 6.4 add_convert_fusion.2
  395.1 5.8 add_convert_fusion.1
  404.0 5.1 collective-permute-start.68
  410.6 6.9 collective-permute-done.57
  417.6 5.9 collective-permute-start.75
  425.0 7.6 collective-permute-done.68
  441.3 16.6 %collective-permute-done.29.refs_18_ = bf16[512,128]{1,0:T(8,128)(2,1)S(1)} collective-permute-done((bf16[512,128]{1,0:T(8,128)(2,1)S(1)}, bf16[512,128]{1,0:T(8,128)(2,1)S(1)}, u32[]{:S(2)}, u32[]{:S(2)}) %collective-permute-start.29) | collective-permute-done | bytes 131104 | tf_op jit(solution)/shard_map/ppermute | solution.py:335
  457.9 5.5 collective-permute-start.86
  465.4 23.1 %shard_map.256 = (bf16[512,128]{1,0:T(8,128)(2,1)S(1)}, bf16[512,128]{1,0:T(8,128)(2,1)S(1)}, bf16[512,128]{1,0:T(8,128)(2,1)S(1)}, bf16[512,128]{1,0:T(8,128)(2...) custom-call(s32[4,8]{1,0:T(4,128)S(1)} %and_convert_fusion.refs_0_, ...), custom_call_target="tpu_custom_call" | custom-call | flops 3355443200 | bytes 12582912 | tf_op jit(solution)/shard_map/pallas_call | solution.py:544
  495.1 5.3 collective-permute-done.33
  507.7 4.4 collective-permute-done.35
  512.8 4.9 collective-permute-done.36
  518.4 3.2 collective-permute-done.38
  521.5 2.9 collective-permute-start.60
  529.0 11.2 %collective-permute-start.39 = (bf16[2,512,128]{2,1,0:T(8,128)(2,1)S(1)}, bf16[2,512,128]{2,1,0:T(8,128)(2,1)S(1)}, u32[]{:S(2)}, u32[]{:S(2)}) collective-permute-start(bf16[2,512,128]{2,1,0:T(8,128)(2,1)S(1)} %add_convert_fusion.34), channel_id=1, source_target_pairs={{0,16},{4,20},{8,24},{12,28},{16,0},{20,4},{24,8},{28,12},{1,17},{... | collective-permute-start | bytes 786440 | tf_op jit(solution)/shard_map/ppermute | solution.py:335
  540.5 4.0 collective-permute-done.39
  545.9 24.5 %collective-permute-done.41 = bf16[2,512,128]{2,1,0:T(8,128)(2,1)S(1)} collective-permute-done((bf16[2,512,128]{2,1,0:T(8,128)(2,1)S(1)}, bf16[2,512,128]{2,1,0:T(8,128)(2,1)S(1)}, u32[]{:S(2)}, u32[]{:S(2)}) %collective-permute-start.41) | collective-permute-done | bytes 262176 | tf_op jit(solution)/shard_map/ppermute | solution.py:335
  576.0 2.7 collective-permute-done.43
  585.3 4.5 fusion.15
  591.2 3.4 collective-permute-done.93
  596.0 4.6 collective-permute-start.69
  605.3 3.5 convert_add_fusion.1
  608.8 6.2 collective-permute-start.76
  615.0 9.1 %collective-permute-done.69 = bf16[256,2048]{1,0:T(8,128)(2,1)S(1)} collective-permute-done((bf16[256,2048]{1,0:T(8,128)(2,1)S(1)}, bf16[256,2048]{1,0:T(8,128)(2,1)S(1)}, u32[]{:S(2)}, u32[]{:S(2)}) %collective-permute-start.69) | collective-permute-done | bytes 1048608 | tf_op jit(solution)/shard_map/ppermute | solution.py:339
  624.1 4.5 collective-permute-start.61
  629.5 4.8 collective-permute-done.49
  637.0 5.3 add_convert_fusion.3
  643.1 3.4 collective-permute-done.76
  646.5 4.4 collective-permute-start.50
  652.2 4.4 collective-permute-start.70
  661.1 7.9 collective-permute-done.50
  669.9 6.4 collective-permute-start.51
  679.4 48.1 %collective-permute-done.51 = bf16[256,1536]{1,0:T(8,128)(2,1)S(1)} collective-permute-done((bf16[256,1536]{1,0:T(8,128)(2,1)S(1)}, bf16[256,1536]{1,0:T(8,128)(2,1)S(1)}, u32[]{:S(2)}, u32[]{:S(2)}) %collective-permute-start.51) | collective-permute-done | bytes 786464 | tf_op jit(solution)/shard_map/ppermute | solution.py:339
  733.1 5.6 collective-permute-start.52
  740.2 11.7 %collective-permute-done.80 = bf16[256,2048]{1,0:T(8,128)(2,1)S(1)} collective-permute-done((bf16[256,2048]{1,0:T(8,128)(2,1)S(1)}, bf16[256,2048]{1,0:T(8,128)(2,1)S(1)}, u32[]{:S(2)}, u32[]{:S(2)}) %collective-permute-start.80) | collective-permute-done | bytes 1048608 | tf_op jit(solution)/shard_map/ppermute | solution.py:339
  756.1 30.1 %collective-permute-done.55 = bf16[256,1536]{1,0:T(8,128)(2,1)S(1)} collective-permute-done((bf16[256,1536]{1,0:T(8,128)(2,1)S(1)}, bf16[256,1536]{1,0:T(8,128)(2,1)S(1)}, u32[]{:S(2)}, u32[]{:S(2)}) %collective-permute-start.55) | collective-permute-done | bytes 786464 | tf_op jit(solution)/shard_map/ppermute | solution.py:339
  (533 shorter events, 193.9 us)
Async XLA Ops:
  3.5 28.8 %collective-permute-start = (s32[512]{0:T(512)}, s32[512]{0:T(512)}, u32[]{:S(2)}, u32[]{:S(2)}) collective-permute-start(s32[512]{0:T(512)} %get-tuple-element.206), channel_id=1, source_target_pairs={{0,8},{4,12},{8,16},{12,20},{16,24},{20,28},{24,0},{28,4},{1,9},{5... | collective-permute-start | bytes 6152 | tf_op jit(solution)/shard_map/ppermute | solution.py:335
  6.5 25.8 %collective-permute-start.1 = (s32[512]{0:T(512)}, s32[512]{0:T(512)}, u32[]{:S(2)}, u32[]{:S(2)}) collective-permute-start(s32[512]{0:T(512)} %get-tuple-element.206), channel_id=1, source_target_pairs={{0,16},{4,20},{8,24},{12,28},{16,0},{20,4},{24,8},{28,12},{1,17},{... | collective-permute-start | bytes 6152 | tf_op jit(solution)/shard_map/ppermute | solution.py:335
  9.1 23.2 %collective-permute-start.2 = (s32[512]{0:T(512)}, s32[512]{0:T(512)}, u32[]{:S(2)}, u32[]{:S(2)}) collective-permute-start(s32[512]{0:T(512)} %get-tuple-element.206), channel_id=1, source_target_pairs={{0,24},{4,28},{8,0},{12,4},{16,8},{20,12},{24,16},{28,20},{1,25},{... | collective-permute-start | bytes 6152 | tf_op jit(solution)/shard_map/ppermute | solution.py:335
  17.5 18.3 %collective-permute-start.4 = (f32[2,512]{1,0:T(2,128)}, f32[2,512]{1,0:T(2,128)}, u32[]{:S(2)}, u32[]{:S(2)}) collective-permute-start(f32[2,512]{1,0:T(2,128)} %pad_maximum_fusion.31), channel_id=1, source_target_pairs={{0,1},{1,0},{2,3},{3,2},{4,5},{5,4},{6,7},{7,6},{8,9},{9,8},{10,11... | collective-permute-start | bytes 12296 | tf_op jit(solution)/shard_map/ppermute | solution.py:349
  34.3 18.0 %collective-permute-start.3 = (s32[4,512]{1,0:T(4,128)}, s32[4,512]{1,0:T(4,128)}, u32[]{:S(2)}, u32[]{:S(2)}) collective-permute-start(s32[4,512]{1,0:T(4,128)} %get-tuple-element.66), channel_id=1, source_target_pairs={{0,4},{4,0},{8,12},{12,8},{16,20},{20,16},{24,28},{28,24},{1,5},{5... | collective-permute-start | bytes 24584 | tf_op jit(solution)/shard_map/ppermute | solution.py:345
  48.0 22.4 %collective-permute-start.10 = (bf16[2,512,128]{2,1,0:T(8,128)(2,1)}, bf16[2,512,128]{2,1,0:T(8,128)(2,1)S(1)}, u32[]{:S(2)}, u32[]{:S(2)}) collective-permute-start(bf16[2,512,128]{2,1,0:T(8,128)(2,1)} %pad_maximum_fusion.25), channel_id=1, source_target_pairs={{0,16},{4,20},{8,24},{12,28},{16,0},{20,4},{24,8},{28,12},{1,17},{... | collective-permute-start | bytes 786440 | tf_op jit(solution)/shard_map/ppermute | solution.py:335
  52.0 18.9 %collective-permute-start.11 = (bf16[2,512,128]{2,1,0:T(8,128)(2,1)}, bf16[2,512,128]{2,1,0:T(8,128)(2,1)S(1)}, u32[]{:S(2)}, u32[]{:S(2)}) collective-permute-start(bf16[2,512,128]{2,1,0:T(8,128)(2,1)} %pad_maximum_fusion.26), channel_id=1, source_target_pairs={{0,24},{4,28},{8,0},{12,4},{16,8},{20,12},{24,16},{28,20},{1,25},{... | collective-permute-start | bytes 786440 | tf_op jit(solution)/shard_map/ppermute | solution.py:335
  52.3 28.3 %collective-permute-start.7 = (bf16[512,128]{1,0:T(8,128)(2,1)}, bf16[512,128]{1,0:T(8,128)(2,1)}, u32[]{:S(2)}, u32[]{:S(2)}) collective-permute-start(bf16[512,128]{1,0:T(8,128)(2,1)} %get-tuple-element.122), channel_id=1, source_target_pairs={{0,16},{4,20},{8,24},{12,28},{16,0},{20,4},{24,8},{28,12},{1,17},{... | collective-permute-start | bytes 393224 | tf_op jit(solution)/shard_map/ppermute | solution.py:335
  55.9 30.3 %collective-permute-start.12 = (bf16[2,512,128]{2,1,0:T(8,128)(2,1)S(1)}, bf16[2,512,128]{2,1,0:T(8,128)(2,1)S(1)}, u32[]{:S(2)}, u32[]{:S(2)}) collective-permute-start(bf16[2,512,128]{2,1,0:T(8,128)(2,1)S(1)} %pad_maximum_fusion.23.refs_7_), channel_id=1, source_target_pairs={{0,4},{4,0},{8,12},{12,8},{16,20},{20,16},{24,28},{28,24},{1,5},{5... | collective-permute-start | bytes 786440 | tf_op jit(solution)/shard_map/ppermute | solution.py:345
  59.1 27.1 %collective-permute-start.13 = (bf16[2,512,128]{2,1,0:T(8,128)(2,1)S(1)}, bf16[2,512,128]{2,1,0:T(8,128)(2,1)S(1)}, u32[]{:S(2)}, u32[]{:S(2)}) collective-permute-start(bf16[2,512,128]{2,1,0:T(8,128)(2,1)S(1)} %collective-permute-done.9.refs_8_), channel_id=1, source_target_pairs={{0,4},{4,0},{8,12},{12,8},{16,20},{20,16},{24,28},{28,24},{1,5},{5... | collective-permute-start | bytes 786440 | tf_op jit(solution)/shard_map/ppermute | solution.py:345
  70.4 15.9 %collective-permute-start.14 = (bf16[2,512,128]{2,1,0:T(8,128)(2,1)S(1)}, bf16[2,512,128]{2,1,0:T(8,128)(2,1)S(1)}, u32[]{:S(2)}, u32[]{:S(2)}) collective-permute-start(bf16[2,512,128]{2,1,0:T(8,128)(2,1)S(1)} %collective-permute-done.10.refs_9_), channel_id=1, source_target_pairs={{0,4},{4,0},{8,12},{12,8},{16,20},{20,16},{24,28},{28,24},{1,5},{5... | collective-permute-start | bytes 786440 | tf_op jit(solution)/shard_map/ppermute | solution.py:345
  70.9 15.3 %collective-permute-start.15 = (bf16[2,512,128]{2,1,0:T(8,128)(2,1)S(1)}, bf16[2,512,128]{2,1,0:T(8,128)(2,1)S(1)}, u32[]{:S(2)}, u32[]{:S(2)}) collective-permute-start(bf16[2,512,128]{2,1,0:T(8,128)(2,1)S(1)} %collective-permute-done.11.refs_10_), channel_id=1, source_target_pairs={{0,4},{4,0},{8,12},{12,8},{16,20},{20,16},{24,28},{28,24},{1,5},{5... | collective-permute-start | bytes 786440 | tf_op jit(solution)/shard_map/ppermute | solution.py:345
  127.9 25.3 %collective-permute-start.20 = (bf16[256,2048]{1,0:T(8,128)(2,1)S(1)}, bf16[256,2048]{1,0:T(8,128)(2,1)S(1)}, u32[]{:S(2)}, u32[]{:S(2)}) collective-permute-start(bf16[256,2048]{1,0:T(8,128)(2,1)S(1)} %add_convert_fusion.24), channel_id=1, source_target_pairs={{0,2},{1,3},{2,0},{3,1},{4,6},{5,7},{6,4},{7,5},{8,10},{9,11},{10,... | collective-permute-start | bytes 3145736 | tf_op jit(solution)/shard_map/ppermute | solution.py:353
  182.7 25.5 %collective-permute-start.23 = (bf16[256,2048]{1,0:T(8,128)(2,1)}, bf16[256,2048]{1,0:T(8,128)(2,1)}, u32[]{:S(2)}, u32[]{:S(2)}) collective-permute-start(bf16[256,2048]{1,0:T(8,128)(2,1)} %add_convert_fusion.23), channel_id=1, source_target_pairs={{0,2},{1,3},{2,0},{3,1},{4,6},{5,7},{6,4},{7,5},{8,10},{9,11},{10,... | collective-permute-start | bytes 3145736 | tf_op jit(solution)/shard_map/ppermute | solution.py:353
  185.5 15.1 %collective-permute-start.65 = (bf16[256,1024]{1,0:T(8,128)(2,1)}, bf16[256,1024]{1,0:T(8,128)(2,1)}, u32[]{:S(2)}, u32[]{:S(2)}) collective-permute-start(bf16[256,1024]{1,0:T(8,128)(2,1)} %pad_maximum_fusion.19), channel_id=1, source_target_pairs={{0,4},{4,0},{8,12},{12,8},{16,20},{20,16},{24,28},{28,24},{1,5},{5... | collective-permute-start | bytes 1572872 | tf_op jit(solution)/shard_map/ppermute | solution.py:345
  187.9 408.0 %collective-permute-start.47 = (bf16[256,1024]{1,0:T(8,128)(2,1)}, bf16[256,1024]{1,0:T(8,128)(2,1)}, u32[]{:S(2)}, u32[]{:S(2)}) collective-permute-start(bf16[256,1024]{1,0:T(8,128)(2,1)} %pad_maximum_fusion.17), channel_id=1, source_target_pairs={{0,4},{4,0},{8,12},{12,8},{16,20},{20,16},{24,28},{28,24},{1,5},{5... | collective-permute-start | bytes 1572872 | tf_op jit(solution)/shard_map/ppermute | solution.py:345
  200.6 14.6 %collective-permute-start.66 = (bf16[256,1024]{1,0:T(8,128)(2,1)}, bf16[256,1024]{1,0:T(8,128)(2,1)S(1)}, u32[]{:S(2)}, u32[]{:S(2)}) collective-permute-start(bf16[256,1024]{1,0:T(8,128)(2,1)} %collective-permute-done.65), channel_id=1, source_target_pairs={{0,1},{1,0},{2,3},{3,2},{4,5},{5,4},{6,7},{7,6},{8,9},{9,8},{10,11... | collective-permute-start | bytes 1572872 | tf_op jit(solution)/shard_map/ppermute | solution.py:349
  215.2 59.8 %collective-permute-start.25 = (bf16[256,2048]{1,0:T(8,128)(2,1)S(1)}, bf16[256,2048]{1,0:T(8,128)(2,1)S(1)}, u32[]{:S(2)}, u32[]{:S(2)}) collective-permute-start(bf16[256,2048]{1,0:T(8,128)(2,1)S(1)} %fusion.5), channel_id=1, source_target_pairs={{0,1},{1,0},{2,3},{3,2},{4,5},{5,4},{6,7},{7,6},{8,9},{9,8},{10,11... | collective-permute-start | bytes 3145736 | tf_op jit(solution)/shard_map/ppermute | solution.py:349
  215.3 98.9 %collective-permute-start.81 = (bf16[512,2048]{1,0:T(8,128)(2,1)}, bf16[512,2048]{1,0:T(8,128)(2,1)}, u32[]{:S(2)}, u32[]{:S(2)}) collective-permute-start(bf16[512,2048]{1,0:T(8,128)(2,1)} %get-tuple-element.215), channel_id=1, source_target_pairs={{0,4},{4,0},{8,12},{12,8},{16,20},{20,16},{24,28},{28,24},{1,5},{5... | collective-permute-start | bytes 6291464 | tf_op jit(solution)/shard_map/ppermute | solution.py:345
  216.9 58.0 %collective-permute-start.82 = (bf16[256,1024]{1,0:T(8,128)(2,1)S(1)}, bf16[256,1024]{1,0:T(8,128)(2,1)}, u32[]{:S(2)}, u32[]{:S(2)}) collective-permute-start(bf16[256,1024]{1,0:T(8,128)(2,1)S(1)} %pad_maximum_fusion.20), channel_id=1, source_target_pairs={{0,4},{4,0},{8,12},{12,8},{16,20},{20,16},{24,28},{28,24},{1,5},{5... | collective-permute-start | bytes 1572872 | tf_op jit(solution)/shard_map/ppermute | solution.py:345
  222.9 111.9 %collective-permute-start.24 = (bf16[256,2048]{1,0:T(8,128)(2,1)}, bf16[256,2048]{1,0:T(8,128)(2,1)}, u32[]{:S(2)}, u32[]{:S(2)}) collective-permute-start(bf16[256,2048]{1,0:T(8,128)(2,1)} %get-tuple-element.62), channel_id=1, source_target_pairs={{0,1},{1,0},{2,3},{3,2},{4,5},{5,4},{6,7},{7,6},{8,9},{9,8},{10,11... | collective-permute-start | bytes 3145736 | tf_op jit(solution)/shard_map/ppermute | solution.py:349
  274.9 41.0 %collective-permute-start.83 = (bf16[256,1024]{1,0:T(8,128)(2,1)}, bf16[256,1024]{1,0:T(8,128)(2,1)}, u32[]{:S(2)}, u32[]{:S(2)}) collective-permute-start(bf16[256,1024]{1,0:T(8,128)(2,1)} %collective-permute-done.82), channel_id=1, source_target_pairs={{0,1},{1,0},{2,3},{3,2},{4,5},{5,4},{6,7},{7,6},{8,9},{9,8},{10,11... | collective-permute-start | bytes 1572872 | tf_op jit(solution)/shard_map/ppermute | solution.py:349
  297.6 89.3 %collective-permute-start.67 = (bf16[512,2048]{1,0:T(8,128)(2,1)}, bf16[512,2048]{1,0:T(8,128)(2,1)}, u32[]{:S(2)}, u32[]{:S(2)}) collective-permute-start(bf16[512,2048]{1,0:T(8,128)(2,1)} %get-tuple-element.70), channel_id=1, source_target_pairs={{0,4},{4,0},{8,12},{12,8},{16,20},{20,16},{24,28},{28,24},{1,5},{5... | collective-permute-start | bytes 6291464 | tf_op jit(solution)/shard_map/ppermute | solution.py:345
  314.2 80.3 %collective-permute-start.74 = (bf16[512,2048]{1,0:T(8,128)(2,1)}, bf16[512,2048]{1,0:T(8,128)(2,1)S(1)}, u32[]{:S(2)}, u32[]{:S(2)}) collective-permute-start(bf16[512,2048]{1,0:T(8,128)(2,1)} %get-tuple-element.69), channel_id=1, source_target_pairs={{0,4},{4,0},{8,12},{12,8},{16,20},{20,16},{24,28},{28,24},{1,5},{5... | collective-permute-start | bytes 6291464 | tf_op jit(solution)/shard_map/ppermute | solution.py:345
  315.9 16.0 %collective-permute-start.26 = (bf16[256,2048]{1,0:T(8,128)(2,1)S(1)}, bf16[256,2048]{1,0:T(8,128)(2,1)S(1)}, u32[]{:S(2)}, u32[]{:S(2)}) collective-permute-start(bf16[256,2048]{1,0:T(8,128)(2,1)S(1)} %slice.361), channel_id=1, source_target_pairs={{0,1},{1,0},{2,3},{3,2},{4,5},{5,4},{6,7},{7,6},{8,9},{9,8},{10,11... | collective-permute-start | bytes 3145736 | tf_op jit(solution)/shard_map/ppermute | solution.py:349
  332.0 25.3 %collective-permute-start.84 = (bf16[2048,256]{1,0:T(8,128)(2,1)S(1)}, bf16[2048,256]{1,0:T(8,128)(2,1)S(1)}, u32[]{:S(2)}, u32[]{:S(2)}) collective-permute-start(bf16[2048,256]{1,0:T(8,128)(2,1)S(1)} %get-tuple-element.73), channel_id=1, source_target_pairs={{0,8},{4,12},{1,9},{5,13},{2,10},{6,14},{3,11},{7,15}} | collective-permute-start | bytes 3145736 | tf_op jit(solution)/shard_map/ppermute | solution.py:339
  334.8 25.4 %collective-permute-start.27 = (bf16[256,2048]{1,0:T(8,128)(2,1)S(1)}, bf16[256,2048]{1,0:T(8,128)(2,1)S(1)}, u32[]{:S(2)}, u32[]{:S(2)}) collective-permute-start(bf16[256,2048]{1,0:T(8,128)(2,1)S(1)} %add_convert_fusion.21), channel_id=1, source_target_pairs={{0,2},{1,3},{2,0},{3,1},{4,6},{5,7},{6,4},{7,5},{8,10},{9,11},{10,... | collective-permute-start | bytes 3145736 | tf_op jit(solution)/shard_map/ppermute | solution.py:353
  360.2 24.9 %collective-permute-start.85 = (bf16[2048,256]{1,0:T(8,128)(2,1)S(1)}, bf16[2048,256]{1,0:T(8,128)(2,1)S(1)}, u32[]{:S(2)}, u32[]{:S(2)}) collective-permute-start(bf16[2048,256]{1,0:T(8,128)(2,1)S(1)} %add_convert_fusion.9), channel_id=1, source_target_pairs={{0,8},{4,12},{8,16},{12,20},{1,9},{5,13},{9,17},{13,21},{2,10},{6,... | collective-permute-start | bytes 3145736 | tf_op jit(solution)/shard_map/ppermute | solution.py:339
  366.3 70.2 %collective-permute-start.56 = (bf16[512,512]{1,0:T(8,128)(2,1)S(1)}, bf16[512,512]{1,0:T(8,128)(2,1)S(1)}, u32[]{:S(2)}, u32[]{:S(2)}) collective-permute-start(bf16[512,512]{1,0:T(8,128)(2,1)S(1)} %copy-done.60), channel_id=1, source_target_pairs={{0,4},{4,0},{8,12},{12,8},{16,20},{20,16},{24,28},{28,24},{1,5},{5... | collective-permute-start | bytes 1572872 | tf_op jit(solution)/shard_map/ppermute | solution.py:345
  385.1 19.0 %collective-permute-start.28 = (bf16[256,2048]{1,0:T(8,128)(2,1)S(1)}, bf16[256,2048]{1,0:T(8,128)(2,1)S(1)}, u32[]{:S(2)}, u32[]{:S(2)}) collective-permute-start(bf16[256,2048]{1,0:T(8,128)(2,1)S(1)} %multiply_convert_fusion.3), channel_id=1, source_target_pairs={{0,1},{1,0},{2,3},{3,2},{4,5},{5,4},{6,7},{7,6},{8,9},{9,8},{10,11... | collective-permute-start | bytes 3145736 | tf_op jit(solution)/shard_map/ppermute | solution.py:349
  387.0 36.5 %collective-permute-start.88 = (bf16[2048,256]{1,0:T(8,128)(2,1)S(1)}, bf16[2048,256]{1,0:T(8,128)(2,1)S(1)}, u32[]{:S(2)}, u32[]{:S(2)}) collective-permute-start(bf16[2048,256]{1,0:T(8,128)(2,1)S(1)} %get-tuple-element.72), channel_id=1, source_target_pairs={{24,16},{28,20},{16,8},{20,12},{25,17},{29,21},{17,9},{21,13},{26,... | collective-permute-start | bytes 3145736 | tf_op jit(solution)/shard_map/ppermute | solution.py:339
  404.0 28.6 %collective-permute-start.68 = (bf16[256,2048]{1,0:T(8,128)(2,1)S(1)}, bf16[256,2048]{1,0:T(8,128)(2,1)S(1)}, u32[]{:S(2)}, u32[]{:S(2)}) collective-permute-start(bf16[256,2048]{1,0:T(8,128)(2,1)S(1)} %get-tuple-element.81), channel_id=1, source_target_pairs={{0,8},{4,12},{1,9},{5,13},{2,10},{6,14},{3,11},{7,15}} | collective-permute-start | bytes 3145736 | tf_op jit(solution)/shard_map/ppermute | solution.py:339
  417.6 73.5 %collective-permute-start.75 = (bf16[256,2048]{1,0:T(8,128)(2,1)}, bf16[256,2048]{1,0:T(8,128)(2,1)}, u32[]{:S(2)}, u32[]{:S(2)}) collective-permute-start(bf16[256,2048]{1,0:T(8,128)(2,1)} %get-tuple-element.77), channel_id=1, source_target_pairs={{0,8},{4,12},{1,9},{5,13},{2,10},{6,14},{3,11},{7,15}} | collective-permute-start | bytes 3145736 | tf_op jit(solution)/shard_map/ppermute | solution.py:339
  432.6 25.3 %collective-permute-start.29 = (bf16[512,128]{1,0:T(8,128)(2,1)S(1)}, bf16[512,128]{1,0:T(8,128)(2,1)S(1)}, u32[]{:S(2)}, u32[]{:S(2)}) collective-permute-start(bf16[512,128]{1,0:T(8,128)(2,1)S(1)} %get-tuple-element.176), channel_id=1, source_target_pairs={{0,8},{4,12},{8,16},{12,20},{16,24},{20,28},{24,0},{28,4},{1,9},{5... | collective-permute-start | bytes 393224 | tf_op jit(solution)/shard_map/ppermute | solution.py:335
  436.4 26.9 %collective-permute-start.30 = (bf16[512,128]{1,0:T(8,128)(2,1)S(1)}, bf16[512,128]{1,0:T(8,128)(2,1)S(1)}, u32[]{:S(2)}, u32[]{:S(2)}) collective-permute-start(bf16[512,128]{1,0:T(8,128)(2,1)S(1)} %get-tuple-element.175), channel_id=1, source_target_pairs={{0,16},{4,20},{8,24},{12,28},{16,0},{20,4},{24,8},{28,12},{1,17},{... | collective-permute-start | bytes 393224 | tf_op jit(solution)/shard_map/ppermute | solution.py:335
  436.5 28.9 %collective-permute-start.31 = (bf16[512,128]{1,0:T(8,128)(2,1)S(1)}, bf16[512,128]{1,0:T(8,128)(2,1)S(1)}, u32[]{:S(2)}, u32[]{:S(2)}) collective-permute-start(bf16[512,128]{1,0:T(8,128)(2,1)S(1)} %get-tuple-element.174), channel_id=1, source_target_pairs={{0,24},{4,28},{8,0},{12,4},{16,8},{20,12},{24,16},{28,20},{1,25},{... | collective-permute-start | bytes 393224 | tf_op jit(solution)/shard_map/ppermute | solution.py:335
  457.9 146.5 %collective-permute-start.86 = (bf16[2048,256]{1,0:T(8,128)(2,1)}, bf16[2048,256]{1,0:T(8,128)(2,1)}, u32[]{:S(2)}, u32[]{:S(2)}) collective-permute-start(bf16[2048,256]{1,0:T(8,128)(2,1)} %get-tuple-element.71), channel_id=1, source_target_pairs={{0,8},{4,12},{8,16},{12,20},{16,24},{20,28},{1,9},{5,13},{9,17},{1... | collective-permute-start | bytes 3145736 | tf_op jit(solution)/shard_map/ppermute | solution.py:339
  463.4 41.8 %collective-permute-start.59 = (bf16[512,256]{1,0:T(8,128)(2,1)}, bf16[512,256]{1,0:T(8,128)(2,1)}, u32[]{:S(2)}, u32[]{:S(2)}) collective-permute-start(bf16[512,256]{1,0:T(8,128)(2,1)} %get-tuple-element.134), channel_id=1, source_target_pairs={{0,8},{4,12},{1,9},{5,13},{2,10},{6,14},{3,11},{7,15}} | collective-permute-start | bytes 786440 | tf_op jit(solution)/shard_map/ppermute | solution.py:339
  500.4 26.6 %collective-permute-start.62 = (bf16[512,256]{1,0:T(8,128)(2,1)S(1)}, bf16[512,256]{1,0:T(8,128)(2,1)S(1)}, u32[]{:S(2)}, u32[]{:S(2)}) collective-permute-start(bf16[512,256]{1,0:T(8,128)(2,1)S(1)} %copy-done.66), channel_id=1, source_target_pairs={{24,16},{28,20},{25,17},{29,21},{26,18},{30,22},{27,19},{31,23}} | collective-permute-start | bytes 786440 | tf_op jit(solution)/shard_map/ppermute | solution.py:339
  524.6 15.8 %collective-permute-start.37 = (bf16[2,512,128]{2,1,0:T(8,128)(2,1)S(1)}, bf16[2,512,128]{2,1,0:T(8,128)(2,1)S(1)}, u32[]{:S(2)}, u32[]{:S(2)}) collective-permute-start(bf16[2,512,128]{2,1,0:T(8,128)(2,1)S(1)} %add_convert_fusion.35), channel_id=1, source_target_pairs={{0,24},{4,28},{8,0},{12,4},{16,8},{20,12},{24,16},{28,20},{1,25},{... | collective-permute-start | bytes 786440 | tf_op jit(solution)/shard_map/ppermute | solution.py:335
  527.0 81.8 %collective-permute-start.71 = (bf16[256,2048]{1,0:T(8,128)(2,1)S(1)}, bf16[256,2048]{1,0:T(8,128)(2,1)S(1)}, u32[]{:S(2)}, u32[]{:S(2)}) collective-permute-start(bf16[256,2048]{1,0:T(8,128)(2,1)S(1)} %copy-done.51), channel_id=1, source_target_pairs={{24,16},{28,20},{25,17},{29,21},{26,18},{30,22},{27,19},{31,23}} | collective-permute-start | bytes 3145736 | tf_op jit(solution)/shard_map/ppermute | solution.py:339
  529.0 15.6 %collective-permute-start.39 = (bf16[2,512,128]{2,1,0:T(8,128)(2,1)S(1)}, bf16[2,512,128]{2,1,0:T(8,128)(2,1)S(1)}, u32[]{:S(2)}, u32[]{:S(2)}) collective-permute-start(bf16[2,512,128]{2,1,0:T(8,128)(2,1)S(1)} %add_convert_fusion.34), channel_id=1, source_target_pairs={{0,16},{4,20},{8,24},{12,28},{16,0},{20,4},{24,8},{28,12},{1,17},{... | collective-permute-start | bytes 786440 | tf_op jit(solution)/shard_map/ppermute | solution.py:335
  540.4 30.0 %collective-permute-start.41 = (bf16[2,512,128]{2,1,0:T(8,128)(2,1)S(1)}, bf16[2,512,128]{2,1,0:T(8,128)(2,1)S(1)}, u32[]{:S(2)}, u32[]{:S(2)}) collective-permute-start(bf16[2,512,128]{2,1,0:T(8,128)(2,1)S(1)} %add_convert_fusion.33), channel_id=1, source_target_pairs={{0,8},{4,12},{8,16},{12,20},{16,24},{20,28},{24,0},{28,4},{1,9},{5... | collective-permute-start | bytes 786440 | tf_op jit(solution)/shard_map/ppermute | solution.py:335
  544.6 60.0 %collective-permute-start.89 = (bf16[2048,256]{1,0:T(8,128)(2,1)S(1)}, bf16[2048,256]{1,0:T(8,128)(2,1)}, u32[]{:S(2)}, u32[]{:S(2)}) collective-permute-start(bf16[2048,256]{1,0:T(8,128)(2,1)S(1)} %copy-done.53), channel_id=1, source_target_pairs={{24,16},{28,20},{16,8},{20,12},{8,0},{12,4},{25,17},{29,21},{17,9}... | collective-permute-start | bytes 3145736 | tf_op jit(solution)/shard_map/ppermute | solution.py:339
  596.0 28.1 %collective-permute-start.69 = (bf16[256,2048]{1,0:T(8,128)(2,1)S(1)}, bf16[256,2048]{1,0:T(8,128)(2,1)S(1)}, u32[]{:S(2)}, u32[]{:S(2)}) collective-permute-start(bf16[256,2048]{1,0:T(8,128)(2,1)S(1)} %copy-done.52), channel_id=1, source_target_pairs={{0,8},{4,12},{8,16},{12,20},{1,9},{5,13},{9,17},{13,21},{2,10},{6,... | collective-permute-start | bytes 3145736 | tf_op jit(solution)/shard_map/ppermute | solution.py:339
  600.5 33.8 %collective-permute-start.49 = (bf16[512,1536]{1,0:T(8,128)(2,1)S(1)}, bf16[512,1536]{1,0:T(8,128)(2,1)S(1)}, u32[]{:S(2)}, u32[]{:S(2)}) collective-permute-start(bf16[512,1536]{1,0:T(8,128)(2,1)S(1)} %pad_maximum_fusion.6), channel_id=1, source_target_pairs={{0,4},{4,0},{8,12},{12,8},{16,20},{20,16},{24,28},{28,24},{1,5},{5... | collective-permute-start | bytes 4718600 | tf_op jit(solution)/shard_map/ppermute | solution.py:345
  604.4 25.0 %collective-permute-start.48 = (bf16[256,1024]{1,0:T(8,128)(2,1)}, bf16[256,1024]{1,0:T(8,128)(2,1)S(1)}, u32[]{:S(2)}, u32[]{:S(2)}) collective-permute-start(bf16[256,1024]{1,0:T(8,128)(2,1)} %collective-permute-done.47), channel_id=1, source_target_pairs={{0,1},{1,0},{2,3},{3,2},{4,5},{5,4},{6,7},{7,6},{8,9},{9,8},{10,11... | collective-permute-start | bytes 1572872 | tf_op jit(solution)/shard_map/ppermute | solution.py:349
  604.5 37.9 %collective-permute-start.78 = (bf16[256,2048]{1,0:T(8,128)(2,1)S(1)}, bf16[256,2048]{1,0:T(8,128)(2,1)S(1)}, u32[]{:S(2)}, u32[]{:S(2)}) collective-permute-start(bf16[256,2048]{1,0:T(8,128)(2,1)S(1)} %copy-done.50), channel_id=1, source_target_pairs={{24,16},{28,20},{25,17},{29,21},{26,18},{30,22},{27,19},{31,23}} | collective-permute-start | bytes 3145736 | tf_op jit(solution)/shard_map/ppermute | solution.py:339
  608.8 37.7 %collective-permute-start.76 = (bf16[256,2048]{1,0:T(8,128)(2,1)S(1)}, bf16[256,2048]{1,0:T(8,128)(2,1)S(1)}, u32[]{:S(2)}, u32[]{:S(2)}) collective-permute-start(bf16[256,2048]{1,0:T(8,128)(2,1)S(1)} %add_convert_fusion.13), channel_id=1, source_target_pairs={{0,8},{4,12},{8,16},{12,20},{1,9},{5,13},{9,17},{13,21},{2,10},{6,... | collective-permute-start | bytes 3145736 | tf_op jit(solution)/shard_map/ppermute | solution.py:339
  624.1 28.1 %collective-permute-start.61 = (bf16[512,256]{1,0:T(8,128)(2,1)S(1)}, bf16[512,256]{1,0:T(8,128)(2,1)S(1)}, u32[]{:S(2)}, u32[]{:S(2)}) collective-permute-start(bf16[512,256]{1,0:T(8,128)(2,1)S(1)} %get-tuple-element.132), channel_id=1, source_target_pairs={{0,8},{4,12},{8,16},{12,20},{16,24},{20,28},{1,9},{5,13},{9,17},{1... | collective-permute-start | bytes 786440 | tf_op jit(solution)/shard_map/ppermute | solution.py:339
  629.4 28.8 %collective-permute-start.44 = (bf16[256,2048]{1,0:T(8,128)(2,1)S(1)}, bf16[256,2048]{1,0:T(8,128)(2,1)S(1)}, u32[]{:S(2)}, u32[]{:S(2)}) collective-permute-start(bf16[256,2048]{1,0:T(8,128)(2,1)S(1)} %slice.399), channel_id=1, source_target_pairs={{0,1},{1,0},{2,3},{3,2},{4,5},{5,4},{6,7},{7,6},{8,9},{9,8},{10,11... | collective-permute-start | bytes 3145736 | tf_op jit(solution)/shard_map/ppermute | solution.py:349
  635.5 21.1 %collective-permute-start.64 = (bf16[512,256]{1,0:T(8,128)(2,1)S(1)}, bf16[512,256]{1,0:T(8,128)(2,1)S(1)}, u32[]{:S(2)}, u32[]{:S(2)}) collective-permute-start(bf16[512,256]{1,0:T(8,128)(2,1)S(1)} %add_convert_fusion.29), channel_id=1, source_target_pairs={{24,16},{28,20},{16,8},{20,12},{8,0},{12,4},{25,17},{29,21},{17,9}... | collective-permute-start | bytes 786440 | tf_op jit(solution)/shard_map/ppermute | solution.py:339
  642.4 27.5 %collective-permute-start.72 = (bf16[256,2048]{1,0:T(8,128)(2,1)S(1)}, bf16[256,2048]{1,0:T(8,128)(2,1)S(1)}, u32[]{:S(2)}, u32[]{:S(2)}) collective-permute-start(bf16[256,2048]{1,0:T(8,128)(2,1)S(1)} %get-tuple-element.80), channel_id=1, source_target_pairs={{24,16},{28,20},{16,8},{20,12},{25,17},{29,21},{17,9},{21,13},{26,... | collective-permute-start | bytes 3145736 | tf_op jit(solution)/shard_map/ppermute | solution.py:339
  646.5 22.5 %collective-permute-start.50 = (bf16[256,1536]{1,0:T(8,128)(2,1)S(1)}, bf16[256,1536]{1,0:T(8,128)(2,1)S(1)}, u32[]{:S(2)}, u32[]{:S(2)}) collective-permute-start(bf16[256,1536]{1,0:T(8,128)(2,1)S(1)} %get-tuple-element.85), channel_id=1, source_target_pairs={{0,8},{4,12},{1,9},{5,13},{2,10},{6,14},{3,11},{7,15}} | collective-permute-start | bytes 2359304 | tf_op jit(solution)/shard_map/ppermute | solution.py:339
  652.2 79.0 %collective-permute-start.70 = (bf16[256,2048]{1,0:T(8,128)(2,1)S(1)}, bf16[256,2048]{1,0:T(8,128)(2,1)S(1)}, u32[]{:S(2)}, u32[]{:S(2)}) collective-permute-start(bf16[256,2048]{1,0:T(8,128)(2,1)S(1)} %get-tuple-element.79), channel_id=1, source_target_pairs={{0,8},{4,12},{8,16},{12,20},{16,24},{20,28},{1,9},{5,13},{9,17},{1... | collective-permute-start | bytes 3145736 | tf_op jit(solution)/shard_map/ppermute | solution.py:339
  656.6 20.1 %collective-permute-start.79 = (bf16[256,2048]{1,0:T(8,128)(2,1)S(1)}, bf16[256,2048]{1,0:T(8,128)(2,1)S(1)}, u32[]{:S(2)}, u32[]{:S(2)}) collective-permute-start(bf16[256,2048]{1,0:T(8,128)(2,1)S(1)} %get-tuple-element.76), channel_id=1, source_target_pairs={{24,16},{28,20},{16,8},{20,12},{25,17},{29,21},{17,9},{21,13},{26,... | collective-permute-start | bytes 3145736 | tf_op jit(solution)/shard_map/ppermute | solution.py:339
  658.2 82.0 %collective-permute-start.77 = (bf16[256,2048]{1,0:T(8,128)(2,1)S(1)}, bf16[256,2048]{1,0:T(8,128)(2,1)S(1)}, u32[]{:S(2)}, u32[]{:S(2)}) collective-permute-start(bf16[256,2048]{1,0:T(8,128)(2,1)S(1)} %get-tuple-element.75), channel_id=1, source_target_pairs={{0,8},{4,12},{8,16},{12,20},{16,24},{20,28},{1,9},{5,13},{9,17},{1... | collective-permute-start | bytes 3145736 | tf_op jit(solution)/shard_map/ppermute | solution.py:339
  669.9 57.5 %collective-permute-start.51 = (bf16[256,1536]{1,0:T(8,128)(2,1)S(1)}, bf16[256,1536]{1,0:T(8,128)(2,1)S(1)}, u32[]{:S(2)}, u32[]{:S(2)}) collective-permute-start(bf16[256,1536]{1,0:T(8,128)(2,1)S(1)} %add_convert_fusion.28), channel_id=1, source_target_pairs={{0,8},{4,12},{8,16},{12,20},{1,9},{5,13},{9,17},{13,21},{2,10},{6,... | collective-permute-start | bytes 2359304 | tf_op jit(solution)/shard_map/ppermute | solution.py:339
  676.7 52.5 %collective-permute-start.45 = (bf16[256,2048]{1,0:T(8,128)(2,1)S(1)}, bf16[256,2048]{1,0:T(8,128)(2,1)S(1)}, u32[]{:S(2)}, u32[]{:S(2)}) collective-permute-start(bf16[256,2048]{1,0:T(8,128)(2,1)S(1)} %add_convert_fusion.20), channel_id=1, source_target_pairs={{0,2},{1,3},{2,0},{3,1},{4,6},{5,7},{6,4},{7,5},{8,10},{9,11},{10,... | collective-permute-start | bytes 3145736 | tf_op jit(solution)/shard_map/ppermute | solution.py:353
  678.1 53.1 %collective-permute-start.73 = (bf16[256,2048]{1,0:T(8,128)(2,1)S(1)}, bf16[256,2048]{1,0:T(8,128)(2,1)S(1)}, u32[]{:S(2)}, u32[]{:S(2)}) collective-permute-start(bf16[256,2048]{1,0:T(8,128)(2,1)S(1)} %add_convert_fusion.14), channel_id=1, source_target_pairs={{24,16},{28,20},{16,8},{20,12},{8,0},{12,4},{25,17},{29,21},{17,9}... | collective-permute-start | bytes 3145736 | tf_op jit(solution)/shard_map/ppermute | solution.py:339
  727.5 24.5 %collective-permute-start.80 = (bf16[256,2048]{1,0:T(8,128)(2,1)S(1)}, bf16[256,2048]{1,0:T(8,128)(2,1)S(1)}, u32[]{:S(2)}, u32[]{:S(2)}) collective-permute-start(bf16[256,2048]{1,0:T(8,128)(2,1)S(1)} %add_convert_fusion.10), channel_id=1, source_target_pairs={{24,16},{28,20},{16,8},{20,12},{8,0},{12,4},{25,17},{29,21},{17,9}... | collective-permute-start | bytes 3145736 | tf_op jit(solution)/shard_map/ppermute | solution.py:339
  731.2 22.6 %collective-permute-start.46 = (bf16[256,2048]{1,0:T(8,128)(2,1)S(1)}, bf16[256,2048]{1,0:T(8,128)(2,1)S(1)}, u32[]{:S(2)}, u32[]{:S(2)}) collective-permute-start(bf16[256,2048]{1,0:T(8,128)(2,1)S(1)} %get-tuple-element.60), channel_id=1, source_target_pairs={{0,1},{1,0},{2,3},{3,2},{4,5},{5,4},{6,7},{7,6},{8,9},{9,8},{10,11... | collective-permute-start | bytes 3145736 | tf_op jit(solution)/shard_map/ppermute | solution.py:349
  733.1 23.0 %collective-permute-start.52 = (bf16[256,1536]{1,0:T(8,128)(2,1)S(1)}, bf16[256,1536]{1,0:T(8,128)(2,1)S(1)}, u32[]{:S(2)}, u32[]{:S(2)}) collective-permute-start(bf16[256,1536]{1,0:T(8,128)(2,1)S(1)} %get-tuple-element.83), channel_id=1, source_target_pairs={{0,8},{4,12},{8,16},{12,20},{16,24},{20,28},{1,9},{5,13},{9,17},{1... | collective-permute-start | bytes 2359304 | tf_op jit(solution)/shard_map/ppermute | solution.py:339
  738.9 47.3 %collective-permute-start.55 = (bf16[256,1536]{1,0:T(8,128)(2,1)S(1)}, bf16[256,1536]{1,0:T(8,128)(2,1)S(1)}, u32[]{:S(2)}, u32[]{:S(2)}) collective-permute-start(bf16[256,1536]{1,0:T(8,128)(2,1)S(1)} %add_convert_fusion.25), channel_id=1, source_target_pairs={{24,16},{28,20},{16,8},{20,12},{8,0},{12,4},{25,17},{29,21},{17,9}... | collective-permute-start | bytes 2359304 | tf_op jit(solution)/shard_map/ppermute | solution.py:339
  (138 other events, 1635.3 us)

commit v2 on v1

--- a/solution.py
+++ b/solution.py
@@ -326,6 +326,7 @@
 pair = 2
 low_score = -1e30
 start_max = -1e20
+big_vmem = 56 << 20
 
 
 def line_shift(value, step):
@@ -335,9 +336,9 @@
     return lax.ppermute(value, "dp", moves)
 
 
-def line_send(value, moves):
+def line_flip(value, bit):
     return lax.ppermute(
-        value, "dp", [(a * pair + x, b * pair + x) for a, b in moves for x in range(pair)]
+        value, "dp", [(z * pair + x, (z ^ bit) * pair + x) for z in range(line) for x in range(pair)]
     )
 
 
@@ -353,54 +354,37 @@
     return lax.ppermute(value, "mp", [(i, i ^ 2) for i in range(4)])
 
 
+def flip_cores(value, axis):
+    quarter = value.shape[axis] // 4
+    cuts = [lax.slice_in_dim(value, i * quarter, (i + 1) * quarter, axis=axis) for i in (1, 0, 3, 2)]
+    return jnp.concatenate(cuts, axis=axis)
+
+
 def token_sum(value):
-    half = value.shape[1] // 2
-    arrived = core_swap(value)
-    value = value + jnp.concatenate([arrived[:, half:], arrived[:, :half]], axis=1)
+    value = value + flip_cores(core_swap(value), 1)
     return value + y_swap(value)
+
+
+def own_part(value):
+    quarter = value.shape[0] // 4
+    return jnp.concatenate([value[:quarter], value[2 * quarter : 3 * quarter]], axis=0)
+
+
+def other_part(value):
+    quarter = value.shape[0] // 4
+    return jnp.concatenate([value[quarter : 2 * quarter], value[3 * quarter :]], axis=0)
+
+
+def join_parts(own, other):
+    half = own.shape[0] // 2
+    return jnp.concatenate([own[:half], other[:half], own[half:], other[half:]], axis=0)
 
 
 def reduce_own_rows(partial_low):
     f32 = jnp.float32
-    half = partial_low.shape[0] // 2
-    arrived = core_swap(partial_low[half:])
-    chip_sum = (partial_low[:half].astype(f32) + arrived.astype(f32)).astype(jnp.bfloat16)
+    arrived = core_swap(other_part(partial_low))
+    chip_sum = (own_part(partial_low).astype(f32) + arrived.astype(f32)).astype(jnp.bfloat16)
     return chip_sum.astype(f32) + y_swap(chip_sum).astype(f32)
-
-
-def share_rows(own):
-    return jnp.concatenate([own, core_swap(own)], axis=0)
-
-
-def line_scatter(terms, axis, z):
-    f32 = jnp.float32
-    bf16 = jnp.bfloat16
-    width = terms.shape[axis] // line
-
-    def block(index):
-        return lax.dynamic_slice_in_dim(terms, index * width, width, axis)
-
-    right, left = None, None
-    for step in range(1, line):
-        right_term = block(lax.rem(2 * line - step + z, line))
-        left_term = block(lax.rem(step + z, line))
-        if right is not None:
-            right_term = (right_term.astype(f32) + right.astype(f32)).astype(bf16)
-            left_term = (left_term.astype(f32) + left.astype(f32)).astype(bf16)
-        right = line_send(right_term, [(a, a + 1) for a in range(step)])
-        left = line_send(left_term, [(line - 1 - a, line - 2 - a) for a in range(step)])
-    return block(z).astype(f32) + right.astype(f32) + left.astype(f32)
-
-
-def own_columns(value, x):
-    width = value.shape[1] // (line * pair)
-    return jnp.concatenate(
-        [
-            lax.dynamic_slice_in_dim(value, (z * pair + x) * width, width, 1)
-            for z in range(line)
-        ],
-        axis=1,
-    )
 
 
 def dot_t(first, second):
@@ -413,6 +397,85 @@
     return lax.dot_general(
         first, second, (((1,), (1,)), ((), ())), preferred_element_type=jnp.float32
     )
+
+
+def vmem_specs(count):
+    return [pl.BlockSpec(memory_space=pltpu.VMEM)] * count
+
+
+def project_kernel(place, own, other, wq, wk, wv, gq, gk, cosines, sines, *refs):
+    out_queries, out_pairs = refs[:line], refs[line : 2 * line]
+    out_q_raw, out_k_raw, out_squares, turned = refs[2 * line :]
+    f32 = jnp.float32
+    bf16 = jnp.bfloat16
+    width = cosines.shape[1]
+    rows = jnp.concatenate([own[...], other[...]], axis=0)
+
+    def keep(raw, gain, slot):
+        for h in range(line):
+            part = raw[:, h * width : (h + 1) * width] * gain[:, h * width : (h + 1) * width]
+            turned[slot, h] = (
+                part * cosines[...] + pltpu.roll(part, width // 2, 1) * sines[...]
+            ).astype(bf16)
+
+    q_raw = jnp.dot(rows, wq[...], preferred_element_type=f32)
+    out_q_raw[...] = q_raw
+    out_squares[0:1, :] = jnp.sum((q_raw * q_raw).T, axis=0, keepdims=True)
+    keep(q_raw, gq[...], 0)
+    k_raw = jnp.dot(rows, wk[...], preferred_element_type=f32)
+    out_k_raw[...] = k_raw
+    out_squares[1:2, :] = jnp.sum((k_raw * k_raw).T, axis=0, keepdims=True)
+    keep(k_raw, gk[...], 1)
+    v_raw = jnp.dot(rows, wv[...], preferred_element_type=f32)
+    for h in range(line):
+        turned[2, h] = v_raw[:, h * width : (h + 1) * width].astype(bf16)
+    for d in range(line):
+        head = lax.rem(place[1] + d, line)
+        out_queries[d][...] = turned[0, head]
+        out_pairs[d][0] = turned[1, head]
+        out_pairs[d][1] = turned[2, head]
+
+
+def project(place, tokens, wq, wk, wv, gq, gk, cosines, sines):
+    rows, depth = tokens.shape
+    columns = wq.shape[1]
+    width = columns // line
+    half = rows // 2
+    f32 = jnp.float32
+    bf16 = jnp.bfloat16
+    whole = lambda shape: pl.BlockSpec(shape, lambda i, p: (0, 0))
+    rows_of = lambda n: pl.BlockSpec((half, n), lambda i, p: (i, 0))
+    return pl.pallas_call(
+        project_kernel,
+        grid_spec=pltpu.PrefetchScalarGridSpec(
+            num_scalar_prefetch=1,
+            grid=(2,),
+            in_specs=[
+                pl.BlockSpec((half // 2, depth), lambda i, p: (2 * p[0] + i, 0)),
+                pl.BlockSpec((half // 2, depth), lambda i, p: (2 * (1 - p[0]) + i, 0)),
+                whole((depth, columns)),
+                whole((depth, columns)),
+                whole((depth, columns)),
+                whole((1, columns)),
+                whole((1, columns)),
+                rows_of(width),
+                rows_of(width),
+            ],
+            out_specs=[rows_of(width)] * line
+            + [pl.BlockSpec((2, half, width), lambda i, p: (0, i, 0))] * line
+            + [rows_of(columns)] * 2
+            + [pl.BlockSpec((2, half), lambda i, p: (0, i))],
+            scratch_shapes=[pltpu.VMEM((3, line, half, width), bf16)],
+        ),
+        out_shape=[jax.ShapeDtypeStruct((rows, width), bf16)] * line
+        + [jax.ShapeDtypeStruct((2, rows, width), bf16)] * line
+        + [jax.ShapeDtypeStruct((rows, columns), f32)] * 2
+        + [jax.ShapeDtypeStruct((2, rows), f32)],
+        compiler_params=pltpu.CompilerParams(vmem_limit_bytes=big_vmem),
+        cost_estimate=pl.CostEstimate(
+            flops=6 * rows * depth * columns, bytes_accessed=12 << 20, transcendentals=0
+        ),
+    )(place, tokens, tokens, wq, wk, wv, gq, gk, cosines, sines)
 
 
 def visible_scores(key, query, key_code, query_code, query_low, factor):
@@ -421,15 +484,29 @@
     return jnp.where((codes <= query_code) & (codes >= query_low), scores, low_score)
 
 
-def attend_kernel(factor, *refs):
-    live, codes, rows = refs[0], refs[1], refs[2]
-    query_refs = refs[3:7]
-    pair_refs = refs[7:15]
-    out_turned, out_log = refs[15], refs[16]
-    out_refs = refs[17:21]
-    top, total, accum = refs[21:24]
+def attend_kernel(factor, key_rows, live, notes, *refs):
+    query_refs = refs[:line]
+    pair_refs = refs[line : 3 * line]
+    out_turned, out_log, out_query, out_key, out_codes, out_rows = refs[3 * line : 3 * line + 6]
+    out_refs = refs[3 * line + 6 : 4 * line + 6]
+    top, total, accum = refs[4 * line + 6 :]
     f32 = jnp.float32
     bf16 = jnp.bfloat16
+    count, width = query_refs[0].shape
+
+    def column(row):
+        return jnp.broadcast_to(row, (width, count)).T
+
+    for k in range(2 * line):
+        out_key[k] = (pair_refs[k][0].astype(f32) * column(notes[k, 1:2, :])).astype(bf16)
+        labels = column(notes[k, 2:3, :]).astype(jnp.int32)
+        out_codes[k] = labels * key_rows + column(notes[k, 3:4, :]).astype(jnp.int32)
+    for q in range(line):
+        out_query[q] = (query_refs[q][...].astype(f32) * column(notes[q, 0:1, :])).astype(bf16)
+        base = notes[q, 2:3, :].astype(jnp.int32) * key_rows
+        out_rows[q : q + 1, :] = base + notes[q, 3:4, :].astype(jnp.int32)
+        out_rows[line + q : line + q + 1, :] = base
+
     for q in range(line):
         top[...] = jnp.full_like(top, start_max)
         total[...] = jnp.zeros_like(total)
@@ -439,11 +516,11 @@
             @pl.when(live[q, k] > 0)
             def _(q=q, k=k):
                 scores = visible_scores(
-                    pair_refs[k][0],
-                    query_refs[q][...],
-                    codes[k],
-                    rows[q : q + 1, :],
-                    rows[line + q : line + q + 1, :],
+                    out_key[k],
+                    out_query[q],
+                    out_codes[k],
+                    out_rows[q : q + 1, :],
+                    out_rows[line + q : line + q + 1, :],
                     factor,
                 )
                 highest = jnp.maximum(top[...], jnp.max(scores, axis=0, keepdims=True))
@@ -459,29 +536,25 @@
         out_refs[q][...] = turned.T.astype(bf16)
 
 
-def attend_back_kernel(factor, scale, *refs):
-    live, codes, rows = refs[0], refs[1], refs[2]
-    query_refs = refs[3:7]
-    pair_refs = refs[7:15]
-    turned, log_total = refs[15], refs[16]
-    grad_refs = refs[17:21]
-    out_query = refs[21:25]
-    out_pairs = refs[25:33]
-    key_sum, value_sum, query_sum = refs[33:36]
+def attend_back_kernel(factor, scale, live, codes, rows, queries, keys, *refs):
+    pair_refs = refs[: 2 * line]
+    turned, log_total = refs[2 * line : 2 * line + 2]
+    grad_refs = refs[2 * line + 2 : 3 * line + 2]
+    out_query = refs[3 * line + 2 : 4 * line + 2]
+    out_pairs = refs[4 * line + 2 : 6 * line + 2]
+    key_sum, value_sum, query_sum = refs[6 * line + 2 :]
     f32 = jnp.float32
     bf16 = jnp.bfloat16
     key_sum[...] = jnp.zeros_like(key_sum)
     value_sum[...] = jnp.zeros_like(value_sum)
     for q in range(line):
         query_sum[...] = jnp.zeros_like(query_sum)
-        delta = jnp.sum(
-            grad_refs[q][...].astype(f32).T * turned[q], axis=0, keepdims=True
-        )
+        delta = jnp.sum(grad_refs[q][...].astype(f32).T * turned[q], axis=0, keepdims=True)
         for k in range(2 * line):
 
             @pl.when(live[q, k] > 0)
             def _(q=q, k=k, delta=delta):
-                query, key, grad = query_refs[q][...], pair_refs[k][0], grad_refs[q][...]
+                query, key, grad = queries[q], keys[k], grad_refs[q][...]
                 scores = visible_scores(
                     key,
                     query,
@@ -505,23 +578,24 @@
         out_pairs[k][1] = value_sum[k].astype(bf16)
 
 
-def vmem_specs(count):
-    return [pl.BlockSpec(memory_space=pltpu.VMEM)] * count
-
-
-def attend(live, codes, rows, queries, pairs):
+def attend(key_rows, live, notes, queries, pairs):
     count, width = queries[0].shape
     factor = math.log2(math.e) / math.sqrt(width)
     f32 = jnp.float32
+    bf16 = jnp.bfloat16
     return pl.pallas_call(
-        functools.partial(attend_kernel, factor),
+        functools.partial(attend_kernel, factor, key_rows),
         out_shape=[
             jax.ShapeDtypeStruct((line, width, count), f32),
             jax.ShapeDtypeStruct((2 * line, count), f32),
+            jax.ShapeDtypeStruct((line, count, width), bf16),
+            jax.ShapeDtypeStruct((2 * line, count, width), bf16),
+            jax.ShapeDtypeStruct((2 * line, count, width), jnp.int32),
+            jax.ShapeDtypeStruct((2 * line, count), jnp.int32),
         ]
-        + [jax.ShapeDtypeStruct((count, width), jnp.bfloat16)] * line,
-        in_specs=[pl.BlockSpec(memory_space=pltpu.SMEM)] + vmem_specs(2 + 3 * line),
-        out_specs=vmem_specs(2 + line),
+        + [jax.ShapeDtypeStruct((count, width), bf16)] * line,
+        in_specs=[pl.BlockSpec(memory_space=pltpu.SMEM)] + vmem_specs(1 + 3 * line),
+        out_specs=vmem_specs(6 + line),
         scratch_shapes=[
             pltpu.VMEM((1, count), f32),
             pltpu.VMEM((1, count), f32),
@@ -533,11 +607,11 @@
             bytes_accessed=8 << 20,
             transcendentals=10 * count * count,
         ),
-    )(live, codes, rows, *queries, *pairs)
-
-
-def attend_back(live, codes, rows, queries, pairs, turned, log_total, grads):
-    count, width = queries[0].shape
+    )(live, notes, *queries, *pairs)
+
+
+def attend_back(live, codes, rows, queries, keys, pairs, turned, log_total, grads):
+    _, count, width = queries.shape
     scale = 1.0 / math.sqrt(width)
     factor = math.log2(math.e) * scale
     f32 = jnp.float32
@@ -545,7 +619,7 @@
         functools.partial(attend_back_kernel, factor, scale),
         out_shape=[jax.ShapeDtypeStruct((count, width), jnp.bfloat16)] * line
         + [jax.ShapeDtypeStruct((2, count, width), jnp.bfloat16)] * (2 * line),
-        in_specs=[pl.BlockSpec(memory_space=pltpu.SMEM)] + vmem_specs(4 + 4 * line),
+        in_specs=[pl.BlockSpec(memory_space=pltpu.SMEM)] + vmem_specs(6 + 3 * line),
         out_specs=vmem_specs(3 * line),
         scratch_shapes=[
             pltpu.VMEM((2 * line, count, width), f32),
@@ -558,7 +632,437 @@
             bytes_accessed=12 << 20,
             transcendentals=10 * count * count,
         ),
-    )(live, codes, rows, *queries, *pairs, turned, log_total, *grads)
+    )(live, codes, rows, queries, keys, *pairs, turned, log_total, *grads)
+
+
+def block_kernel(
+    attended,
+    w_out,
+    own_tokens,
+    own_cotangent,
+    g_attn,
+    g_mlp,
+    w_gate_in,
+    w_up_in,
+    w_down_in,
+    out_output,
+    out_hidden,
+    out_hidden_x,
+    out_act,
+    out_act_x,
+    out_mlp,
+    out_mlp_x,
+    out_gate,
+    out_gate_far,
+    out_up,
+    out_up_far,
+    out_attn,
+    out_attended,
+    out_grad_hidden,
+    out_gain,
+    w_gate,
+    w_up,
+    w_down,
+    gate_keep,
+    up_keep,
+    act_keep,
+    hidden_keep,
+    mlp_keep,
+    attn_keep,
+    grad_gate,
+    grad_up,
+    own_factor,
+    own_normed,
+    out_keep,
+    total,
+    part_send,
+    part_recv,
+    y_send,
+    y_recv,
+    send_sems,
+    recv_sems,
+    local_sems,
+):
+    f32 = jnp.float32
+    bf16 = jnp.bfloat16
+    depth = w_out.shape[1]
+    units = w_gate.shape[1]
+    tile = 512
+    count = own_tokens.shape[0] // 2
+    rows = 2 * count
+    mp = lax.axis_index("mp")
+    spot = lax.axis_index("dp")
+    core = lax.rem(mp, 2)
+    x = lax.rem(spot, 2)
+    core_peer = {"mp": mp + 1 - 2 * core}
+    y_peer = {"mp": lax.rem(mp + 2, 4)}
+    x_peer = {"dp": spot + 1 - 2 * x}
+
+    barrier = pltpu.get_barrier_semaphore()
+    for peer in (core_peer, y_peer, x_peer):
+        pl.semaphore_signal(barrier, inc=1, device_id=peer, device_id_type=pl.DeviceIdType.MESH)
+    pl.semaphore_wait(barrier, 3)
+
+    remote, started, local = [], [], []
+
+    def send(source, target, peer):
+        index = len(remote)
+        copy = pltpu.make_async_remote_copy(
+            src_ref=source,
+            dst_ref=target,
+            send_sem=send_sems.at[index],
+            recv_sem=recv_sems.at[index],
+            device_id=peer,
+            device_id_type=pl.DeviceIdType.MESH,
+        )
+        remote.append(copy)
+        copy.start()
+        return copy
+
+    def keep_out(source, target, waited=False):
+        copy = pltpu.make_async_copy(source, target, local_sems.at[len(started)])
+        started.append(copy)
+        if not waited:
+            local.append(copy)
+        copy.start()
+        return copy
+
+    loads = [keep_out(a, b, True) for a, b in ((w_gate_in, w_gate), (w_up_in, w_up), (w_down_in, w_down))]
+
+    own = lambda s: pl.ds(s * rows, count)
+    other = lambda s: pl.ds(s * rows + count, count)
+    both = lambda s: pl.ds(s * rows, rows)
+    mine = lambda s: pl.ds(s * count, count)
+    at_home = lambda s: pl.ds(pl.multiple_of(core * rows + s * count, count), count)
+    cut = lambda t: pl.ds(pl.multiple_of(t * tile, tile), tile)
+    flying = {}
+
+    def reduce_start(stage, s):
+        part_send[s] = total[count:, :].astype(bf16)
+        copy = send(part_send.at[s], part_recv.at[s], core_peer)
+        copy.wait()
+        y_send[s] = (total[:count, :] + part_recv[s].astype(f32)).astype(bf16)
+        flying[stage, s] = send(y_send.at[s], y_recv.at[stage, s], y_peer)
+
+    def reduced(stage, s):
+        flying[stage, s].wait()
+        return y_send[s].astype(f32) + y_recv[stage, s].astype(f32)
+
+    def factor_of(value):
+        return lax.rsqrt(jnp.mean(value * value, axis=1, keepdims=True) + epsilon)
+
+    def share(keep, s):
+        flying["share", s] = send(keep.at[own(s)], keep.at[other(s)], core_peer)
+
+    def project_out(s):
+        total[...] = jnp.dot(attended[both(s), :], w_out[...], preferred_element_type=f32)
+        reduce_start(0, s)
+
+    def after_attention(s):
+        value = reduced(0, s)
+        factor = factor_of(value)
+        normed = value * factor
+        own_factor[mine(s), :] = jnp.broadcast_to(factor, (count, own_factor.shape[1]))
+        own_normed[mine(s), :] = normed
+        hidden = own_tokens[mine(s), :].astype(f32) + normed * g_attn[...]
+        out_grad_hidden[mine(s), :] = hidden
+        hidden_keep[own(s), :] = hidden.astype(bf16)
+        share(hidden_keep, s)
+
+    def forward(s):
+        flying["hidden", s] = send(hidden_keep.at[own(s)], out_hidden_x.at[own(s)], x_peer)
+        flying["share", s].wait()
+        keep_out(hidden_keep.at[both(s)], out_hidden.at[both(s)])
+
+        def step(t):
+            hidden = hidden_keep[both(s), :]
+            gate = jnp.dot(hidden, w_gate[:, cut(t)], preferred_element_type=f32)
+            up = jnp.dot(hidden, w_up[:, cut(t)], preferred_element_type=f32)
+            gate_keep[both(s), cut(t)] = gate.astype(bf16)
+            up_keep[both(s), cut(t)] = up.astype(bf16)
+            act = (gate * jax.nn.sigmoid(gate) * up).astype(bf16)
+            act_keep[both(s), cut(t)] = act
+            return jnp.dot(act, w_down[cut(t), :], preferred_element_type=f32)
+
+        total[...] = step(0)
+
+        @pl.loop(1, units // tile)
+        def _(t):
+            total[...] += step(t)
+
+        reduce_start(1, s)
+        keep_out(act_keep.at[both(s)], out_act.at[both(s)])
+        half = units // 2
+        far = pl.ds(pl.multiple_of((1 - x) * half, half), half)
+        flying["act", s] = send(act_keep.at[both(s), far], out_act_x.at[both(s)], x_peer)
+
+    def turn_point(s):
+        value = reduced(1, s)
+        factor = factor_of(value)
+        normed = value * factor
+        out_keep[mine(s), :] = (out_grad_hidden[mine(s), :] + normed * g_mlp[...]).astype(bf16)
+        keep_out(out_keep.at[mine(s)], out_output.at[at_home(s)])
+        flying["output", s] = send(out_keep.at[mine(s)], out_output.at[at_home(s)], core_peer)
+        grad = own_cotangent[mine(s), :].astype(f32)
+        gain = jnp.sum(grad * normed, axis=0, keepdims=True)
+        out_gain[1:2, :] = gain if s == 0 else out_gain[1:2, :] + gain
+        mlp_keep[own(s), :] = norm_back(grad * g_mlp[...], normed, factor).astype(bf16)
+        share(mlp_keep, s)
+
+    def backward(s):
+        flying["mlp", s] = send(mlp_keep.at[own(s)], out_mlp_x.at[own(s)], x_peer)
+        flying["share", s].wait()
+        keep_out(mlp_keep.at[both(s)], out_mlp.at[both(s)])
+
+        def step(t):
+            grad_act = dot_nt(mlp_keep[both(s), :], w_down[cut(t), :])
+            gate = gate_keep[both(s), cut(t)].astype(f32)
+            up = up_keep[both(s), cut(t)].astype(f32)
+            sigmoid = jax.nn.sigmoid(gate)
+            to_gate = (grad_act * up * (sigmoid * (1.0 + gate * (1.0 - sigmoid)))).astype(bf16)
+            to_up = (grad_act * (gate * sigmoid)).astype(bf16)
+            grad_gate[:, cut(t)] = to_gate
+            grad_up[:, cut(t)] = to_up
+            return dot_nt(to_gate, w_gate[:, cut(t)]) + dot_nt(to_up, w_up[:, cut(t)])
+
+        if s > 0:
+            for copy in flying["grads"]:
+                copy.wait()
+        total[...] = step(0)
+
+        @pl.loop(1, units // tile)
+        def _(t):
+            total[...] += step(t)
+
+        reduce_start(2, s)
+        half = units // 2
+        far = pl.ds(pl.multiple_of((1 - x) * half, half), half)
+        flying["grads"] = [
+            keep_out(source, target.at[both(s)], waited=s == 0)
+            for source, target in (
+                (grad_gate, out_gate),
+                (grad_gate.at[:, far], out_gate_far),
+                (grad_up, out_up),
+                (grad_up.at[:, far], out_up_far),
+            )
+        ]
+
+    def to_attention(s):
+        value = reduced(2, s)
+        grad = own_cotangent[mine(s), :].astype(f32) + value
+        out_grad_hidden[mine(s), :] = grad
+        normed = own_normed[mine(s), :]
+        gain = jnp.sum(grad * normed, axis=0, keepdims=True)
+        out_gain[0:1, :] = gain if s == 0 else out_gain[0:1, :] + gain
+        factor = own_factor[mine(s), 0:1]
+        attn_keep[own(s), :] = norm_back(grad * g_attn[...], normed, factor).astype(bf16)
+        share(attn_keep, s)
+
+    def attended_grad(s):
+        flying["share", s].wait()
+        keep_out(attn_keep.at[both(s)], out_attn.at[both(s)])
+        out_attended[both(s), :] = dot_nt(attn_keep[both(s), :], w_out[...]).astype(bf16)
+
+    def forward_core(name, s, array):
+        flying[name, s].wait()
+        flying[name + "_core", s] = send(array.at[own(s)], array.at[other(s)], core_peer)
+
+    project_out(0)
+    project_out(1)
+    after_attention(0)
+    for load in loads:
+        load.wait()
+    forward(0)
+    after_attention(1)
+    forward(1)
+    turn_point(0)
+    backward(0)
+    turn_point(1)
+    backward(1)
+    for s in range(2):
+        forward_core("hidden", s, out_hidden_x)
+    to_attention(0)
+    attended_grad(0)
+    to_attention(1)
+    attended_grad(1)
+    for s in range(2):
+        flying["act", s].wait()
+        flying["output", s].wait()
+        forward_core("mlp", s, out_mlp_x)
+    for s in range(2):
+        flying["hidden_core", s].wait()
+        flying["mlp_core", s].wait()
+    for copy in local:
+        copy.wait()
+
+
+def block(attended, w_out, own_tokens, own_cotangent, g_attn, g_mlp, w_gate, w_up, w_down):
+    rows, columns = attended.shape
+    depth, units = w_gate.shape
+    half = rows // 2
+    quarter = rows // 4
+    f32 = jnp.float32
+    bf16 = jnp.bfloat16
+    wide = jax.ShapeDtypeStruct((rows, depth), bf16)
+    tall = jax.ShapeDtypeStruct((rows, units), bf16)
+    any_spec = pl.BlockSpec(memory_space=pl.ANY)
+    return pl.pallas_call(
+        block_kernel,
+        out_shape=[
+            wide,
+            wide,
+            wide,
+            tall,
+            jax.ShapeDtypeStruct((rows, units // 2), bf16),
+            wide,
+            wide,
+            tall,
+            jax.ShapeDtypeStruct((rows, units // 2), bf16),
+            tall,
+            jax.ShapeDtypeStruct((rows, units // 2), bf16),
+            wide,
+            jax.ShapeDtypeStruct((rows, columns), bf16),
+            jax.ShapeDtypeStruct((half, depth), f32),
+            jax.ShapeDtypeStruct((2, depth), f32),
+        ],
+        in_specs=vmem_specs(6) + [any_spec] * 3,
+        out_specs=[any_spec] * 12 + vmem_specs(3),
+        scratch_shapes=[
+            pltpu.VMEM((depth, units), bf16),
+            pltpu.VMEM((depth, units), bf16),
+            pltpu.VMEM((units, depth), bf16),
+            pltpu.VMEM((rows, units), bf16),
+            pltpu.VMEM((rows, units), bf16),
+            pltpu.VMEM((rows, units), bf16),
+            pltpu.VMEM((rows, depth), bf16),
+            pltpu.VMEM((rows, depth), bf16),
+            pltpu.VMEM((rows, depth), bf16),
+            pltpu.VMEM((half, units), bf16),
+            pltpu.VMEM((half, units), bf16),
+            pltpu.VMEM((half, 128), f32),
+            pltpu.VMEM((half, depth), f32),
+            pltpu.VMEM((half, depth), bf16),
+            pltpu.VMEM((half, depth), f32),
+            pltpu.VMEM((2, quarter, depth), bf16),
+            pltpu.VMEM((2, quarter, depth), bf16),
+            pltpu.VMEM((2, quarter, depth), bf16),
+            pltpu.VMEM((3, 2, quarter, depth), bf16),
+            pltpu.SemaphoreType.DMA((30,)),
+            pltpu.SemaphoreType.DMA((30,)),
+            pltpu.SemaphoreType.DMA((24,)),
+        ],
+        compiler_params=pltpu.CompilerParams(
+            vmem_limit_bytes=61800 << 10, collective_id=1, has_side_effects=True
+        ),
+        cost_estimate=pl.CostEstimate(
+            flops=12 * rows * depth * units,
+            bytes_accessed=60 << 20,
+            transcendentals=2 * rows * units,
+        ),
+    )(attended, w_out, own_tokens, own_cotangent, g_attn, g_mlp, w_gate, w_up, w_down)
+
+
+def weight_kernel(place, *refs):
+    first, second, first_x, second_x = refs[:4]
+    total = dot_t(first[...], second[...]) + dot_t(first_x[...], second_x[...])
+    if len(refs) == 6:
+        total = total + refs[4][...].astype(jnp.float32)
+    refs[-1][...] = total.astype(refs[-1].dtype)
+
+
+def line_block(which):
+    if which < 2:
+        return lambda p: 2 * which + 1 - p[2]
+    if which == 2:
+        return lambda p: 2 * (1 - p[3]) + p[2]
+    return lambda p: 2 * p[3] + p[2]
+
+
+def weight_term(place, first, second, cut_first, blocks, extra, kind):
+    tokens = first[0].shape[0]
+    cut_side, half_side = (first, second) if cut_first else (second, first)
+    cut_tile = cut_side[0].shape[1] // line
+    half_size = half_side[1].shape[1]
+    half_tile = min(half_size, 512)
+    while half_size % half_tile:
+        half_tile -= 128
+    half_count = half_size // half_tile
+    own_half = half_count if half_side[0].shape[1] != half_size else 0
+    count = len(blocks)
+
+    def cut_map(i, j, p):
+        index = line_block(blocks[0])(p)
+        if count == 2:
+            index = index + i * (line_block(blocks[1])(p) - line_block(blocks[0])(p))
+        return (0, index)
+
+    cut_spec = pl.BlockSpec((tokens, cut_tile), cut_map)
+    half_own = pl.BlockSpec((tokens, half_tile), lambda i, j, p: (0, j + p[4] * own_half))
+    half_far = pl.BlockSpec((tokens, half_tile), lambda i, j, p: (0, j))
+    if cut_first:
+        in_specs = [cut_spec, half_own, cut_spec, half_far]
+        tile_shape = (cut_tile, half_tile)
+        out_map = lambda i, j, p: (i, j)
+        shape = (count * cut_tile, half_size)
+        extra_map = lambda i, j, p: (extra[1](p) + i, j)
+    else:
+        in_specs = [half_own, cut_spec, half_far, cut_spec]
+        tile_shape = (half_tile, cut_tile)
+        out_map = lambda i, j, p: (j, i)
+        shape = (half_size, count * cut_tile)
+        extra_map = lambda i, j, p: (j, extra[1](p) + i)
+    args = [first[0], second[0], first[1], second[1]]
+    if extra is not None:
+        in_specs.append(pl.BlockSpec(tile_shape, extra_map))
+        args.append(extra[0])
+    return pl.pallas_call(
+        weight_kernel,
+        grid_spec=pltpu.PrefetchScalarGridSpec(
+            num_scalar_prefetch=1,
+            grid=(count, half_count),
+            in_specs=in_specs,
+            out_specs=pl.BlockSpec(tile_shape, out_map),
+        ),
+        out_shape=jax.ShapeDtypeStruct(shape, kind),
+        compiler_params=pltpu.CompilerParams(vmem_limit_bytes=big_vmem),
+        cost_estimate=pl.CostEstimate(
+            flops=4 * tokens * shape[0] * shape[1],
+            bytes_accessed=4 * tokens * (shape[0] + shape[1]) + 4 * shape[0] * shape[1],
+            transcendentals=0,
+        ),
+    )(place, *args)
+
+
+def after(value, *needed):
+    return lax.optimization_barrier((value, needed))[0]
+
+
+class Spread:
+    def __init__(self, place, x, first, second, cut_first):
+        self.place, self.x, self.operands, self.cut_first = place, x, (first, second), cut_first
+        self.sent = self.make((0, 1), None, jnp.bfloat16)
+
+    def make(self, blocks, extra, kind):
+        first, second = self.operands
+        return weight_term(self.place, first, second, self.cut_first, blocks, extra, kind)
+
+    def neighbour(self):
+        self.arrived = line_flip(self.sent, 1)
+
+    def second(self):
+        self.passed = self.make((2,), (self.arrived, lambda p: 1 - p[3]), jnp.bfloat16)
+        return self.passed
+
+    def finish(self, *needed):
+        own = self.make((3,), (self.arrived, lambda p: p[3]), jnp.float32)
+        later = after(line_flip(self.passed, 2), *needed)
+        axis = 0 if self.cut_first else 1
+        width = own.shape[axis] // pair
+        far = lambda value: lax.dynamic_slice_in_dim(value, (1 - self.x) * width, width, axis)
+        near = lambda value: lax.dynamic_slice_in_dim(value, self.x * width, width, axis)
+        to_x = (far(own) + far(later).astype(jnp.float32)).astype(jnp.bfloat16)
+        own_half = near(own) + near(later).astype(jnp.float32)
+        return own_half, x_swap(to_x).astype(jnp.float32)
 
 
 def on_device_lines(
@@ -586,9 +1090,13 @@
     local_width = heads_here * head_width
     half_rows = row_count // 2
     key_rows = row_count * line * pair
-    place = lax.axis_index("dp")
-    z, x = place // pair, lax.rem(place, pair)
+    spot = lax.axis_index("dp")
+    z, x = spot // pair, lax.rem(spot, pair)
+    z_high, z_low = z // 2, lax.rem(z, 2)
     core = lax.rem(lax.axis_index("mp"), 2)
+    place = jnp.stack([core, z, z_low, z_high, x]).astype(jnp.int32)
+
+    quarter = row_count // 4
 
     def own_rows(value):
         return lax.dynamic_slice_in_dim(value, core * half_rows, half_rows, 0)
@@ -597,177 +1105,159 @@
         return lax.dynamic_slice_in_dim(value, (1 - core) * half_rows, half_rows, 0)
 
     def reorder(value):
-        return jnp.concatenate([own_rows(value), other_rows(value)], axis=0)
+        return join_parts(own_rows(value), other_rows(value))
 
     def restore(own, other):
         whole = jnp.zeros((row_count,) + own.shape[1:], own.dtype)
         whole = lax.dynamic_update_slice_in_dim(whole, own, core * half_rows, 0)
         return lax.dynamic_update_slice_in_dim(whole, other, (1 - core) * half_rows, 0)
 
-    own_tokens = own_rows(tokens)
-    tokens_in = reorder(tokens)
+    def half_of(value, x_place):
+        width = value.shape[1] // pair
+        return lax.dynamic_slice_in_dim(value, x_place * width, width, 1)
+
+    def join_halves(near, far, axis):
+        low = jnp.where(x == 0, near, far)
+        return jnp.concatenate([low, jnp.where(x == 0, far, near)], axis=axis)
+
     positions = reorder(offsets[0] + jnp.arange(row_count, dtype=jnp.int32))
     labels = reorder(row_ids[0] * key_rows + doc_ids)
-
-    code = labels * key_rows + positions
-    line_codes = [code] + [line_shift(code, d) for d in range(1, line)]
-    line_codes = jnp.stack(line_codes)
-    all_codes = jnp.concatenate([line_codes, x_swap(line_codes)], axis=0)
-    query_low = (line_codes // key_rows) * key_rows
-    code_rows = jnp.concatenate([line_codes, query_low], axis=0)
-    code_columns = jnp.broadcast_to(all_codes[:, :, None], (2 * line, row_count, 128))
-    live = (
-        (jnp.min(all_codes, axis=1)[None, :] <= jnp.max(line_codes, axis=1)[:, None])
-        & (jnp.max(all_codes, axis=1)[None, :] >= jnp.min(query_low, axis=1)[:, None])
-    ).astype(jnp.int32)
-
     freqs = rope_base ** (-jnp.arange(0, head_width // 2, dtype=f32) * 2.0 / head_width)
     angles = positions.astype(f32)[:, None] * freqs[None, :]
     cosines, sines = jnp.cos(angles), jnp.sin(angles)
     cosines = jnp.concatenate([cosines, cosines], axis=1)
     sines = jnp.concatenate([-sines, sines], axis=1)
-
-    def turn(value, sign_sines):
-        swapped = jnp.concatenate(
-            [value[:, head_width // 2 :], value[:, : head_width // 2]], axis=1
-        )
-        return value * cosines + swapped * sign_sines
-
-    other_half_tokens = x_swap(own_columns(own_tokens, 1 - x))
-    tokens_half = own_columns(tokens_in, x)
-    tokens_half_x = share_rows(other_half_tokens)
-
-    q_raw = jnp.dot(tokens_in, w_query, preferred_element_type=f32)
-    k_raw = jnp.dot(tokens_in, w_key, preferred_element_type=f32)
-    values_low = jnp.dot(tokens_in, w_value, preferred_element_type=f32).astype(bf16)
-    squares = token_sum(
-        jnp.stack([jnp.sum(q_raw * q_raw, axis=1), jnp.sum(k_raw * k_raw, axis=1)])
-    )
-    q_factor = lax.rsqrt(squares[0] / model_width + epsilon)[:, None]
-    k_factor = lax.rsqrt(squares[1] / model_width + epsilon)[:, None]
     g_query = gain_query.reshape(1, local_width)
     g_key = gain_key.reshape(1, local_width)
-    q_normed = q_raw * q_factor
-    k_normed = k_raw * k_factor
+
+    projected = project(
+        place, tokens, w_query, w_key, w_value, g_query, g_key, cosines, sines
+    )
+    queries, pairs = projected[:line], projected[line : 2 * line]
+    q_raw, k_raw, squares = projected[2 * line :]
+    pairs = [pairs[0]] + [line_shift(pairs[d], d) for d in range(1, line)]
+    queries = [queries[0]] + [line_shift(queries[d], d) for d in range(1, line)]
+    pairs = pairs + [x_swap(both) for both in pairs]
+
+    squares = token_sum(squares)
+    factors = lax.rsqrt(squares / model_width + epsilon)
+    notes = jnp.concatenate(
+        [factors, labels.astype(f32)[None, :], positions.astype(f32)[None, :]], axis=0
+    )
+    notes = jnp.stack([notes] + [line_shift(notes, d) for d in range(1, line)])
+    notes = jnp.concatenate([notes, x_swap(notes)], axis=0)
+    codes = notes[:, 2, :].astype(jnp.int32) * key_rows + notes[:, 3, :].astype(jnp.int32)
+    lows = notes[:line, 2, :].astype(jnp.int32) * key_rows
+    live = (
+        (jnp.min(codes, axis=1)[None, :] <= jnp.max(codes[:line], axis=1)[:, None])
+        & (jnp.max(codes, axis=1)[None, :] >= jnp.min(lows, axis=1)[:, None])
+    ).astype(jnp.int32)
+
+    turned, log_total, queries_n, keys_n, code_columns, code_rows, *attended_out = attend(
+        key_rows, live, notes, queries, pairs
+    )
+
+    def gather_heads(home):
+        twice = jnp.concatenate(home + home, axis=1)
+        return lax.dynamic_slice_in_dim(
+            twice, lax.rem(line - z, line) * head_width, local_width, 1
+        )
+
+    def send_home(pieces):
+        return [pieces[0]] + [line_shift(pieces[d], line - d) for d in range(1, line)]
+
+    attended_low = gather_heads(send_home(attended_out))
+    own_tokens = own_rows(tokens)
+    tokens_in = reorder(tokens)
+    tokens_own_x = x_swap(after(own_tokens, pairs[-1]))
+    tokens_x = join_parts(tokens_own_x, core_swap(tokens_own_x))
+    attended_low = after(attended_low, tokens_x)
+    g_attn = gain_attn.reshape(1, model_width)
+    g_mlp = gain_mlp.reshape(1, model_width)
+    (
+        output,
+        hidden_low,
+        hidden_x,
+        act_low,
+        act_x,
+        grad_mlp,
+        grad_mlp_x,
+        grad_gate,
+        grad_gate_far,
+        grad_up,
+        grad_up_far,
+        grad_attn,
+        grad_attended,
+        grad_hidden,
+        wide_gains,
+    ) = block(
+        attended_low,
+        w_output,
+        own_tokens,
+        own_rows(cotangent),
+        g_attn,
+        g_mlp,
+        w_gate,
+        w_up,
+        w_down,
+    )
+    grad_gate_x = x_swap(grad_gate_far)
+    grad_up_x = x_swap(grad_up_far)
+    down = Spread(place, x, (act_low, act_x), (grad_mlp, grad_mlp_x), False)
+    down.neighbour()
+    gate = Spread(place, x, (hidden_low, hidden_x), (grad_gate, grad_gate_x), True)
+    up = Spread(place, x, (hidden_low, hidden_x), (grad_up, grad_up_x), True)
+    gate.neighbour()
+    up.neighbour()
 
     def head_of(value, d):
         return lax.dynamic_slice_in_dim(
             value, lax.rem(z + d, line) * head_width, head_width, 1
         )
 
-    queries, pairs = [], []
-    for d in range(line):
-        query = turn(head_of(q_normed * g_query, d), sines).astype(bf16)
-        key = turn(head_of(k_normed * g_key, d), sines).astype(bf16)
-        both = jnp.stack([key, head_of(values_low, d)])
-        queries.append(query if d == 0 else line_shift(query, d))
-        pairs.append(both if d == 0 else line_shift(both, d))
-    pairs = pairs + [x_swap(both) for both in pairs]
-
-    turned, log_total, *attended_out = attend(live, code_columns, code_rows, queries, pairs)
-
-    def gather_heads(pieces):
-        home = [pieces[0]] + [line_shift(pieces[d], line - d) for d in range(1, line)]
-        twice = jnp.concatenate(home + home, axis=1)
-        return lax.dynamic_slice_in_dim(
-            twice, lax.rem(line - z, line) * head_width, local_width, 1
-        )
-
-    attended_low = gather_heads(attended_out)
-    attended_x = x_swap(attended_low)
-    attn_sum = reduce_own_rows(
-        jnp.dot(attended_low, w_output, preferred_element_type=f32).astype(bf16)
-    )
-    attn_factor = lax.rsqrt(jnp.mean(attn_sum * attn_sum, axis=1, keepdims=True) + epsilon)
-    attn_normed = attn_sum * attn_factor
-    g_attn = gain_attn.reshape(1, model_width)
-    hidden = own_tokens.astype(f32) + attn_normed * g_attn
-    own_hidden_low = hidden.astype(bf16)
-    hidden_low = share_rows(own_hidden_low)
-    hidden_half = own_columns(hidden_low, x)
-    hidden_half_x = share_rows(x_swap(own_columns(own_hidden_low, 1 - x)))
-
-    gate_val = jnp.dot(hidden_low, w_gate, preferred_element_type=f32)
-    up_val = jnp.dot(hidden_low, w_up, preferred_element_type=f32)
-    sigmoid_gate = jax.nn.sigmoid(gate_val)
-    silu_gate = gate_val * sigmoid_gate
-    act_low = (silu_gate * up_val).astype(bf16)
-    act_x = x_swap(act_low)
-    mlp_sum = reduce_own_rows(
-        jnp.dot(act_low, w_down, preferred_element_type=f32).astype(bf16)
-    )
-    mlp_factor = lax.rsqrt(jnp.mean(mlp_sum * mlp_sum, axis=1, keepdims=True) + epsilon)
-    mlp_normed = mlp_sum * mlp_factor
-    g_mlp = gain_mlp.reshape(1, model_width)
-    own_output = (hidden + mlp_normed * g_mlp).astype(bf16)
-    output = restore(own_output, core_swap(own_output))
-
-    grad_out = own_rows(cotangent).astype(f32)
-    grad_gain_mlp = jnp.sum(grad_out * mlp_normed, axis=0)
-    own_grad_mlp = norm_back(grad_out * g_mlp, mlp_normed, mlp_factor).astype(bf16)
-    grad_mlp = share_rows(own_grad_mlp)
-    grad_mlp_half = own_columns(grad_mlp, x)
-    grad_mlp_half_x = share_rows(x_swap(own_columns(own_grad_mlp, 1 - x)))
-    grad_act = dot_nt(grad_mlp, w_down)
-    slope = sigmoid_gate * (1.0 + gate_val * (1.0 - sigmoid_gate))
-    grad_gate = (grad_act * up_val * slope).astype(bf16)
-    grad_up = (grad_act * silu_gate).astype(bf16)
-    grad_gate_x = x_swap(grad_gate)
-    grad_up_x = x_swap(grad_up)
-    branch_sum = reduce_own_rows(
-        (dot_nt(grad_gate, w_gate) + dot_nt(grad_up, w_up)).astype(bf16)
-    )
-
-    terms_down = (dot_t(act_low, grad_mlp_half) + dot_t(act_x, grad_mlp_half_x)).astype(bf16)
-    terms_gate = (dot_t(hidden_half, grad_gate) + dot_t(hidden_half_x, grad_gate_x)).astype(bf16)
-    terms_up = (dot_t(hidden_half, grad_up) + dot_t(hidden_half_x, grad_up_x)).astype(bf16)
-    grad_w_down = line_scatter(terms_down, 1, z)
-    grad_w_gate = line_scatter(terms_gate, 0, z)
-    grad_w_up = line_scatter(terms_up, 0, z)
-
-    grad_hidden = grad_out + branch_sum
-    grad_gain_attn = jnp.sum(grad_hidden * attn_normed, axis=0)
-    own_grad_attn = norm_back(grad_hidden * g_attn, attn_normed, attn_factor).astype(bf16)
-    grad_attn = share_rows(own_grad_attn)
-    grad_attn_half = own_columns(grad_attn, x)
-    grad_attn_half_x = share_rows(x_swap(own_columns(own_grad_attn, 1 - x)))
-    grad_attended = dot_nt(grad_attn, w_output).astype(bf16)
     grads = [
         head_of(grad_attended, d) if d == 0 else line_shift(head_of(grad_attended, d), d)
         for d in range(line)
     ]
-    terms_out = (
-        dot_t(attended_low, grad_attn_half) + dot_t(attended_x, grad_attn_half_x)
-    ).astype(bf16)
-    grad_w_output = line_scatter(terms_out, 1, z)
-
-    back = attend_back(live, code_columns, code_rows, queries, pairs, turned, log_total, grads)
+    attended_far, grad_attn_far = after(
+        (half_of(attended_low, 1 - x), own_part(grad_attn)), gate.sent, up.sent
+    )
+    attended_x = x_swap(attended_far)
+    grad_attn_own = x_swap(grad_attn_far)
+    grad_attn_x = join_parts(grad_attn_own, core_swap(grad_attn_own))
+    out = Spread(place, x, (attended_low, attended_x), (grad_attn, grad_attn_x), False)
+
+    back = attend_back(
+        live, code_columns, code_rows, queries_n, keys_n, pairs, turned, log_total, grads
+    )
     grad_query_pieces, grad_pairs = back[:line], back[line:]
-    grad_queries = gather_heads(grad_query_pieces).astype(f32)
+    far_pairs = [x_swap(grad_pairs[line + d]) for d in range(line)]
+    far_pairs = after(far_pairs, gate.sent, up.sent, down.second())
     summed_pairs = [
-        (grad_pairs[d].astype(f32) + x_swap(grad_pairs[line + d]).astype(f32)).astype(bf16)
-        for d in range(line)
+        (grad_pairs[d].astype(f32) + far_pairs[d].astype(f32)).astype(bf16) for d in range(line)
     ]
-    home = [summed_pairs[0]] + [line_shift(summed_pairs[d], line - d) for d in range(1, line)]
-
-    def place_heads(index):
-        twice = jnp.concatenate([piece[index] for piece in home + home], axis=1)
-        return lax.dynamic_slice_in_dim(
-            twice, lax.rem(line - z, line) * head_width, local_width, 1
-        )
-
-    grad_keys = place_heads(0).astype(f32)
-    grad_values_low = place_heads(1)
+    home = send_home(summed_pairs)
+    out.neighbour()
+    home = after(home, gate.second(), out.sent)
+    query_home = after(send_home(grad_query_pieces), gate.sent, up.sent)
+    grad_queries = gather_heads(query_home).astype(f32)
+    grad_keys = gather_heads([piece[0] for piece in home]).astype(f32)
+    grad_values_low = gather_heads([piece[1] for piece in home])
 
     def turn_back(value):
-        return jnp.concatenate(
-            [
-                turn(value[:, h * head_width : (h + 1) * head_width], -sines)
-                for h in range(heads_here)
-            ],
-            axis=1,
-        )
-
+        parts = []
+        for h in range(heads_here):
+            part = value[:, h * head_width : (h + 1) * head_width]
+            swapped = jnp.concatenate(
+                [part[:, head_width // 2 :], part[:, : head_width // 2]], axis=1
+            )
+            parts.append(part * cosines - swapped * sines)
+        return jnp.concatenate(parts, axis=1)
+
+    q_factor = factors[0][:, None]
+    k_factor = factors[1][:, None]
+    q_normed = q_raw * q_factor
+    k_normed = k_raw * k_factor
     back_q = turn_back(grad_queries)
     back_k = turn_back(grad_keys)
     grad_gain_query = jnp.sum(back_q * q_normed, axis=0)
@@ -779,8 +1269,9 @@
     )
     grad_q_raw = (q_factor * (scaled_q - q_normed * inner[0][:, None] / model_width)).astype(bf16)
     grad_k_raw = (k_factor * (scaled_k - k_normed * inner[1][:, None] / model_width)).astype(bf16)
-    grad_raw = jnp.concatenate([grad_q_raw, grad_k_raw, grad_values_low], axis=1)
-    grad_raw_x = x_swap(grad_raw)
+    raw_parts = (grad_q_raw, grad_k_raw, grad_values_low)
+    grad_raw = jnp.concatenate([half_of(part, x) for part in raw_parts], axis=1)
+    grad_raw_x = x_swap(jnp.concatenate([half_of(part, 1 - x) for part in raw_parts], axis=1))
     input_sum = reduce_own_rows(
         (
             dot_nt(grad_q_raw, w_query)
@@ -788,34 +1279,47 @@
             + dot_nt(grad_values_low, w_value)
         ).astype(bf16)
     )
+    grad_raw_x = after(grad_raw_x, up.second(), out.second())
+    raw = Spread(place, x, (tokens_in, tokens_x), (grad_raw, grad_raw_x), True)
+    raw.neighbour()
+    raw.second()
+    down_near, down_far = down.finish(raw.sent)
+    gate_near, gate_far = gate.finish(raw.sent)
+    up_near, up_far = up.finish(raw.sent)
+    out_near, out_far = out.finish(raw.sent)
+    raw_near, raw_far = raw.finish(raw.sent)
     own_grad_tokens = (grad_hidden + input_sum).astype(bf16)
     grad_tokens = restore(own_grad_tokens, core_swap(own_grad_tokens))
-    terms_raw = (dot_t(tokens_half, grad_raw) + dot_t(tokens_half_x, grad_raw_x)).astype(bf16)
-    summed_raw = line_scatter(terms_raw, 0, z)
-
-    wide = jnp.concatenate([grad_gain_attn, grad_gain_mlp])
+
+    wide = wide_gains.reshape(2 * model_width)
     wide = wide + core_swap(wide)
     gains = jnp.concatenate([wide, grad_gain_query, grad_gain_key])
     gains = gains + x_swap(gains)
-    for flip in (1, 2):
-        gains = gains + line_send(gains, [(a, a ^ flip) for a in range(line)])
+    for bit in (1, 2):
+        gains = gains + line_flip(gains, bit)
     piece = head_width // (line * pair)
 
     def gain_piece(start, rows):
         part = gains[start : start + rows * head_width].reshape(rows, head_width)
-        return lax.dynamic_slice_in_dim(part, place * piece, piece, 1)
+        return lax.dynamic_slice_in_dim(part, spot * piece, piece, 1)
 
     all_heads = model_width // head_width
+    part_width = local_width // pair
+
+    def raw_result(index):
+        cut = slice(index * part_width, (index + 1) * part_width)
+        return join_halves(raw_near[:, cut], raw_far[:, cut], 1)
+
     return (
         output,
         grad_tokens,
-        summed_raw[:, :local_width],
-        summed_raw[:, local_width : 2 * local_width],
-        summed_raw[:, 2 * local_width :],
-        grad_w_output,
-        grad_w_gate,
-        grad_w_up,
-        grad_w_down,
+        raw_result(0),
+        raw_result(1),
+        raw_result(2),
+        join_halves(out_near, out_far, 0),
+        join_halves(gate_near, gate_far, 1),
+        join_halves(up_near, up_far, 1),
+        join_halves(down_near, down_far, 0),
         gain_piece(2 * model_width, heads_here),
         gain_piece(2 * model_width + local_width, heads_here),
         gain_piece(0, all_heads),

time: 797 us -> 622 us (0.78)
  Pallas kernels: 42.1 us -> 217 us
  waiting for transfers between devices: 375 us -> 239 us
  matrix products: 119 us -> 3.91 us
  starting transfers between devices: 143 us -> 74.1 us
  other arithmetic: 61.3 us -> 36.5 us
    pallas_call x1 -> x18, Pallas kernels: 19 us -> 204 us  [the longest x1 98.3 us: block(): pl.pallas_call(block_kernel, out_shape=[wide, wide, wide, tall, jax.Shape...]
    dot_general x17 -> x0, matrix products: 83.8 us -> none  [the longest x10 52.8 us: dot_t(): lax.dot_general(first, second, (((0,), (0,)), ((), ())), preferred_elemen...]
    ppermute x32 -> x12, starting transfers between devices: 80.4 us -> 6.73 us  [line_flip(): lax.ppermute(value, 'dp', [(z * pair + x, (z ^ bit) * pair + x) for z in...]
    ppermute x32 -> x12, waiting for transfers between devices: 156 us -> 106 us  [line_flip(): lax.ppermute(value, 'dp', [(z * pair + x, (z ^ bit) * pair + x) for z in...]
    ppermute x6 -> x3, waiting for transfers between devices: 35.4 us -> 1.98 us  [y_swap(): return lax.ppermute(value, 'mp', [(i, i ^ 2) for i in range(4)])]
    dot_general x7 -> x3, matrix products: 35.6 us -> 3.91 us  [dot_nt(): lax.dot_general(first, second, (((1,), (1,)), ((), ())), preferred_elemen...]
    ppermute x19 -> x21, waiting for transfers between devices: 84.6 us -> 60.5 us  [x_swap(): return lax.ppermute(value, 'dp', [(i, i ^ 1) for i in range(line * pair)])]
    ppermute x21, waiting for transfers between devices: 89.9 us -> 69.2 us  [line_shift(): return lax.ppermute(value, 'dp', moves)]
  transfers between devices with their start and end apart: 94 -> 64, of which waited for: 40 -> 27; matrix products, arithmetic and copies ran while one was open for 23% -> 10% of each run, Pallas kernels for 3% -> 18%
where the time goes in v2:
time: 622 us; the launch traced here: 616 us
  waiting for transfers between devices  239 us (38%)
  Pallas kernels  217 us (35%)
  starting transfers between devices  74.1 us (12%)
  local copies, waits for them, and re-layouts  41.6 us (7%)
  other arithmetic  36.5 us (6%)
    ppermute x12, waiting for transfers between devices, line_flip(): lax.ppermute(value, 'dp', [(z * pair + x, (z ^ bit) * pair + x) for z in...  106 us
    pallas_call x1, Pallas kernels, block(): pl.pallas_call(block_kernel, out_shape=[wide, wide, wide, tall, jax.Shape...  98.3 us
    pallas_call x15, Pallas kernels, weight_term(): pl.pallas_call(weight_kernel, grid_spec=pltpu.PrefetchScalarGridSpec(num_...  78.4 us
    ppermute x21, waiting for transfers between devices, line_shift(): return lax.ppermute(value, 'dp', moves)  69.2 us
    ppermute x21, waiting for transfers between devices, x_swap(): return lax.ppermute(value, 'dp', [(i, i ^ 1) for i in range(line * pair)])  60.5 us
    ppermute x21, starting transfers between devices, line_shift(): return lax.ppermute(value, 'dp', moves)  38.9 us
    ppermute x21, starting transfers between devices, x_swap(): return lax.ppermute(value, 'dp', [(i, i ^ 1) for i in range(line * pair)])  23.4 us
    unnamed x125, local copies, waits for them, and re-layouts  22.1 us
  transfers between devices with their start and end apart: 64, of which 27 were waited for; matrix products, arithmetic and copies ran while one was open for 10% of the time, Pallas kernels for 18%

profile of v2, /device:TPU:0, one launch (start us, length us, event | category | flops | bytes accessed | tf_op | source)
XLA Modules:
  0.0 615.7 jit_solution(14821080340683505059)
XLA Ops:
  5.4 9.2 %shard_map.255 = (bf16[512,128]{1,0:T(8,128)(2,1)}, bf16[512,128]{1,0:T(8,128)(2,1)}, bf16[512,128]{1,0:T(8,128)(2,1)}, bf16[512,128]{1,0:T(8,128)(2,1)}, bf16[2...) custom-call(s32[5]{0:T(128)} %stack.47.place, ...), custom_call_target="tpu_custom_call" | custom-call | flops 3221225472 | bytes 12582912 | tf_op jit(solution)/shard_map/pallas_call | solution.py:448
  15.2 2.6 collective-permute-start.6
  17.8 2.6 collective-permute-start.7
  20.5 2.5 constant_dynamic-slice_fusion.20.own_tokens
  26.6 1.6 collective-permute-start.1
  28.3 2.0 collective-permute-done.1
  30.6 1.6 collective-permute-start.2
  32.2 2.2 collective-permute-start.4
  36.1 2.6 collective-permute-start.11
  38.7 1.6 collective-permute-start.5
  40.5 2.2 collective-permute-done.5
  42.7 5.3 collective-permute-done.11.refs_7_.refs_3_
  50.5 8.2 %collective-permute-done.10.refs_6_.refs_2_ = bf16[2,512,128]{2,1,0:T(8,128)(2,1)S(1)} collective-permute-done((bf16[2,512,128]{2,1,0:T(8,128)(2,1)S(1)}, bf16[2,512,128]{2,1,0:T(8,128)(2,1)S(1)}, u32[]{:S(2)}, u32[]{:S(2)}) %collective-permute-start.10) | collective-permute-done | bytes 262176 | tf_op jit(solution)/shard_map/ppermute | solution.py:336
  63.6 4.8 collective-permute-done.8.refs_3_
  68.4 5.1 collective-permute-done.14.refs_10_.refs_6_
  73.5 17.7 %shard_map.256 = (f32[4,128,512]{2,1,0:T(8,128)S(1)}, f32[8,512]{1,0:T(8,128)S(1)}, bf16[4,512,128]{2,1,0:T(8,128)(2,1)S(1)}, bf16[8,512,128]{2,1,0:T(8,128)(2,1...) custom-call(s32[4,8]{1,0:T(4,128)S(1)} %and_convert_fusion.live, ...), custom_call_target="tpu_custom_call" | custom-call | flops 1342177280 | bytes 8388608 | tf_op jit(solution)/shard_map/pallas_call | solution.py:586
  92.4 6.7 %collective-permute-start.17 = (bf16[512,128]{1,0:T(8,128)(2,1)S(1)}, bf16[512,128]{1,0:T(8,128)(2,1)S(1)}, u32[]{:S(2)}, u32[]{:S(2)}) collective-permute-start(bf16[512,128]{1,0:T(8,128)(2,1)S(1)} %get-tuple-element.94), channel_id=1, source_target_pairs={{0,16},{4,20},{8,24},{12,28},{16,0},{20,4},{24,8},{28,12},{1,17},{... | collective-permute-start | bytes 393224 | tf_op jit(solution)/shard_map/ppermute | solution.py:336
  100.6 5.6 collective-permute-done.17
  110.6 98.3 %shard_map.257 = (bf16[512,2048]{1,0:T(8,128)(2,1)}, bf16[512,2048]{1,0:T(8,128)(2,1)}, bf16[512,2048]{1,0:T(8,128)(2,1)}, bf16[512,2048]{1,0:T(8,128)(2,1)}, bf...) custom-call(bf16[512,512]{1,0:T(8,128)(2,1)} %constant_dynamic-slice, ...), custom_call_target="tpu_custom_call" | custom-call | flops 25769803776 | bytes 62914560 | tf_op jit(solution)/shard_map/pallas_call | solution.py:909
  217.7 7.2 %shard_map.261 = bf16[1024,1024]{1,0:T(8,128)(2,1)} custom-call(s32[5]{0:T(128)} %stack.47.place, bf16[512,2048]{1,0:T(8,128)(2,1)} %get-tuple-element.127.refs_0_, bf16[512,2048]{1,0:T(8,128)(2,1)} %get-tuple-element.128.refs_1_, bf16[512,1024]{1,0:T(8,128)(2,1)} %get-tuple-element.129.refs_2_, bf16[512,2048]{1,0:T(8,128)(2,1)} %get-tuple-element.130.refs_3_), custom_call_target="tpu_custom_call" | custom-call | flops 2147483648 | bytes 8388608 | tf_op jit(solution)/shard_map/pallas_call | solution.py:1018
  224.9 1.5 collective-permute-start.33
  227.2 1.6 copy-done.4
  229.9 13.2 %shard_map.258 = (bf16[512,128]{1,0:T(8,128)(2,1)S(1)}, bf16[512,128]{1,0:T(8,128)(2,1)S(1)}, bf16[512,128]{1,0:T(8,128)(2,1)S(1)}, bf16[512,128]{1,0:T(8,128)(2...) custom-call(s32[4,8]{1,0:T(4,128)S(1)} %and_convert_fusion.live, ...), custom_call_target="tpu_custom_call" | custom-call | flops 3355443200 | bytes 12582912 | tf_op jit(solution)/shard_map/pallas_call | solution.py:618
  243.1 12.8 %collective-permute-start.24 = (bf16[512,128]{1,0:T(8,128)(2,1)S(1)}, bf16[512,128]{1,0:T(8,128)(2,1)S(1)}, u32[]{:S(2)}, u32[]{:S(2)}) collective-permute-start(bf16[512,128]{1,0:T(8,128)(2,1)S(1)} %get-tuple-element.108), channel_id=1, source_target_pairs={{0,24},{4,28},{8,0},{12,4},{16,8},{20,12},{24,16},{28,20},{1,25},{... | collective-permute-start | bytes 393224 | tf_op jit(solution)/shard_map/ppermute | solution.py:336
  256.5 7.1 %shard_map.260 = bf16[1024,1024]{1,0:T(8,128)(2,1)} custom-call(s32[5]{0:T(128)} %stack.47.place, bf16[512,2048]{1,0:T(8,128)(2,1)} %get-tuple-element.111.refs_0_, bf16[512,2048]{1,0:T(8,128)(2,1)} %get-tuple-element.115.refs_1_, bf16[512,2048]{1,0:T(8,128)(2,1)} %get-tuple-element.113.refs_2_, bf16[512,1024]{1,0:T(8,128)(2,1)} %collective-permute-done.28.refs_3_), custom_call_target="tpu_custom_call" | custom-call | flops 2147483648 | bytes 8388608 | tf_op jit(solution)/shard_map/pallas_call | solution.py:1018
  265.1 7.1 %shard_map.259 = bf16[1024,1024]{1,0:T(8,128)(2,1)} custom-call(s32[5]{0:T(128)} %stack.47.place, bf16[512,2048]{1,0:T(8,128)(2,1)} %get-tuple-element.111.refs_0_, bf16[512,2048]{1,0:T(8,128)(2,1)} %get-tuple-element.112.refs_1_, bf16[512,2048]{1,0:T(8,128)(2,1)} %get-tuple-element.113.refs_2_, bf16[512,1024]{1,0:T(8,128)(2,1)} %collective-permute-done.27.refs_3_), custom_call_target="tpu_custom_call" | custom-call | flops 2147483648 | bytes 8388608 | tf_op jit(solution)/shard_map/pallas_call | solution.py:1018
  272.2 5.3 collective-permute-done.24
  277.5 1.6 collective-permute-start.30
  279.5 2.7 collective-permute-done.26
  285.6 4.9 shard_map.262
  292.5 27.9 %collective-permute-done.32 = bf16[2,512,128]{2,1,0:T(8,128)(2,1)} collective-permute-done((bf16[2,512,128]{2,1,0:T(8,128)(2,1)S(1)}, bf16[2,512,128]{2,1,0:T(8,128)(2,1)}, u32[]{:S(2)}, u32[]{:S(2)}) %collective-permute-start.32) | collective-permute-done | bytes 262176 | tf_op jit(solution)/shard_map/ppermute | solution.py:346
  321.3 1.7 add_convert_fusion.8
  323.8 5.1 shard_map.273
  328.8 1.7 add_convert_fusion.7
  333.3 1.6 pad_maximum_fusion.1.refs_3_
  334.8 1.6 collective-permute-start.47
  336.4 3.7 shard_map.264
  340.1 9.1 %collective-permute-done.37.refs_4_ = bf16[1024,1024]{1,0:T(8,128)(2,1)S(1)} collective-permute-done((bf16[1024,1024]{1,0:T(8,128)(2,1)}, bf16[1024,1024]{1,0:T(8,128)(2,1)S(1)}, u32[]{:S(2)}, u32[]{:S(2)}) %collective-permute-start.37) | collective-permute-done | bytes 2097184 | tf_op jit(solution)/shard_map/ppermute | solution.py:340
  350.5 4.9 shard_map.263
  355.5 34.5 %collective-permute-done.34 = bf16[2,512,128]{2,1,0:T(8,128)(2,1)} collective-permute-done((bf16[2,512,128]{2,1,0:T(8,128)(2,1)}, bf16[2,512,128]{2,1,0:T(8,128)(2,1)}, u32[]{:S(2)}, u32[]{:S(2)}) %collective-permute-start.34) | collective-permute-done | bytes 262176 | tf_op jit(solution)/shard_map/ppermute | solution.py:336
  402.0 5.0 shard_map.271
  407.1 2.0 constant_dynamic-slice_fusion.7
  409.1 36.9 %collective-permute-done.47.refs_4_ = bf16[1024,1024]{1,0:T(8,128)(2,1)S(1)} collective-permute-done((bf16[1024,1024]{1,0:T(8,128)(2,1)}, bf16[1024,1024]{1,0:T(8,128)(2,1)S(1)}, u32[]{:S(2)}, u32[]{:S(2)}) %collective-permute-start.47) | collective-permute-done | bytes 2097184 | tf_op jit(solution)/shard_map/ppermute | solution.py:340
  447.5 4.9 shard_map.265
  453.8 5.1 shard_map.272
  469.1 2.7 collective-permute-done.62
  472.7 8.8 %collective-permute-done.63 = f32[5120]{0:T(1024)S(1)} collective-permute-done((f32[5120]{0:T(1024)S(1)}, f32[5120]{0:T(1024)S(1)}, u32[]{:S(2)}, u32[]{:S(2)}) %collective-permute-start.63) | collective-permute-done | bytes 20512 | tf_op jit(solution)/shard_map/ppermute | solution.py:340
  483.7 3.3 shard_map.266
  487.0 2.9 collective-permute-start.52
  490.5 3.4 shard_map.270
  493.9 7.1 %shard_map.267 = bf16[1024,768]{1,0:T(8,128)(2,1)} custom-call(s32[5]{0:T(128)} %stack.47.place, bf16[512,2048]{1,0:T(8,128)(2,1)} %pad_maximum_fusion.2.refs_0_, bf16[512,768]{1,0:T(8,128)(2,1)} %pad_maximum_fusion.10.refs_1_, bf16[512,2048]{1,0:T(8,128)(2,1)} %pad_maximum_fusion.refs_2_, bf16[512,768]{1,0:T(8,128)(2,1)} %copy-done.16), custom_call_target="tpu_custom_call" | custom-call | flops 1610612736 | bytes 6815744 | tf_op jit(solution)/shard_map/pallas_call | solution.py:1018
  501.0 25.1 %collective-permute-done.52 = bf16[256,512]{1,0:T(8,128)(2,1)S(1)} collective-permute-done((bf16[256,512]{1,0:T(8,128)(2,1)}, bf16[256,512]{1,0:T(8,128)(2,1)S(1)}, u32[]{:S(2)}, u32[]{:S(2)}) %collective-permute-start.52) | collective-permute-done | bytes 262176 | tf_op jit(solution)/shard_map/ppermute | solution.py:340
  529.1 3.4 collective-permute-done.53
  535.7 1.6 add_convert_fusion.2
  538.3 2.0 add_convert_fusion.5
  541.4 5.9 collective-permute-done.59
  550.1 8.2 %collective-permute-done.57 = bf16[256,1024]{1,0:T(8,128)(2,1)S(1)} collective-permute-done((bf16[256,1024]{1,0:T(8,128)(2,1)S(1)}, bf16[256,1024]{1,0:T(8,128)(2,1)S(1)}, u32[]{:S(2)}, u32[]{:S(2)}) %collective-permute-start.57) | collective-permute-done | bytes 524320 | tf_op jit(solution)/shard_map/ppermute | solution.py:346
  561.3 4.7 shard_map.269
  568.3 1.7 pad_maximum_fusion.4
  570.2 1.6 convert_select_fusion.5
  571.8 4.9 shard_map.268
  576.7 21.8 %collective-permute-done.50 = bf16[512,768]{1,0:T(8,128)(2,1)} collective-permute-done((bf16[512,768]{1,0:T(8,128)(2,1)}, bf16[512,768]{1,0:T(8,128)(2,1)}, u32[]{:S(2)}, u32[]{:S(2)}) %collective-permute-start.50) | collective-permute-done | bytes 786464 | tf_op jit(solution)/shard_map/ppermute | solution.py:340
  598.5 1.7 convert_add_fusion.3
  604.0 7.4 %collective-permute-done.51 = bf16[256,768]{1,0:T(8,128)(2,1)S(1)} collective-permute-done((bf16[256,768]{1,0:T(8,128)(2,1)S(1)}, bf16[256,768]{1,0:T(8,128)(2,1)S(1)}, u32[]{:S(2)}, u32[]{:S(2)}) %collective-permute-start.51) | collective-permute-done | bytes 393248 | tf_op jit(solution)/shard_map/ppermute | solution.py:346
  (316 shorter events, 100.9 us)
Async XLA Ops:
  14.7 11.8 %collective-permute-start = (f32[2,512]{1,0:T(2,128)}, f32[2,512]{1,0:T(2,128)S(1)}, u32[]{:S(2)}, u32[]{:S(2)}) collective-permute-start(f32[2,512]{1,0:T(2,128)} %get-tuple-element.83), channel_id=1, source_target_pairs={{0,1},{1,0},{2,3},{3,2},{4,5},{5,4},{6,7},{7,6},{8,9},{9,8},{10,11... | collective-permute-start | bytes 12296 | tf_op jit(solution)/shard_map/ppermute | solution.py:350
  15.2 45.5 %collective-permute-start.6 = (bf16[512,128]{1,0:T(8,128)(2,1)}, bf16[512,128]{1,0:T(8,128)(2,1)S(1)}, u32[]{:S(2)}, u32[]{:S(2)}) collective-permute-start(bf16[512,128]{1,0:T(8,128)(2,1)} %get-tuple-element.85), channel_id=1, source_target_pairs={{0,8},{4,12},{8,16},{12,20},{16,24},{20,28},{24,0},{28,4},{1,9},{5... | collective-permute-start | bytes 393224 | tf_op jit(solution)/shard_map/ppermute | solution.py:336
  17.8 44.5 %collective-permute-start.7 = (bf16[512,128]{1,0:T(8,128)(2,1)}, bf16[512,128]{1,0:T(8,128)(2,1)S(1)}, u32[]{:S(2)}, u32[]{:S(2)}) collective-permute-start(bf16[512,128]{1,0:T(8,128)(2,1)} %get-tuple-element.86), channel_id=1, source_target_pairs={{0,16},{4,20},{8,24},{12,28},{16,0},{20,4},{24,8},{28,12},{1,17},{... | collective-permute-start | bytes 393224 | tf_op jit(solution)/shard_map/ppermute | solution.py:336
  26.6 3.7 collective-permute-start.1
  30.3 4.6 collective-permute-start.3
  30.6 5.4 collective-permute-start.2
  32.2 6.5 %collective-permute-start.4 = (f32[4,512]{1,0:T(4,128)S(1)}, f32[4,512]{1,0:T(4,128)S(1)}, u32[]{:S(2)}, u32[]{:S(2)}) collective-permute-start(f32[4,512]{1,0:T(4,128)S(1)} %get-tuple-element.243), channel_id=1, source_target_pairs={{0,24},{4,28},{8,0},{12,4},{16,8},{20,12},{24,16},{28,20},{1,25},{... | collective-permute-start | bytes 24584 | tf_op jit(solution)/shard_map/ppermute | solution.py:336
  34.9 15.0 %collective-permute-start.9 = (bf16[2,512,128]{2,1,0:T(8,128)(2,1)S(1)}, bf16[2,512,128]{2,1,0:T(8,128)(2,1)S(1)}, u32[]{:S(2)}, u32[]{:S(2)}) collective-permute-start(bf16[2,512,128]{2,1,0:T(8,128)(2,1)S(1)} %copy-done.47), channel_id=1, source_target_pairs={{0,8},{4,12},{8,16},{12,20},{16,24},{20,28},{24,0},{28,4},{1,9},{5... | collective-permute-start | bytes 786440 | tf_op jit(solution)/shard_map/ppermute | solution.py:336
  36.1 11.9 %collective-permute-start.11 = (bf16[2,512,128]{2,1,0:T(8,128)(2,1)}, bf16[2,512,128]{2,1,0:T(8,128)(2,1)S(1)}, u32[]{:S(2)}, u32[]{:S(2)}) collective-permute-start(bf16[2,512,128]{2,1,0:T(8,128)(2,1)} %get-tuple-element.91), channel_id=1, source_target_pairs={{0,24},{4,28},{8,0},{12,4},{16,8},{20,12},{24,16},{28,20},{1,25},{... | collective-permute-start | bytes 786440 | tf_op jit(solution)/shard_map/ppermute | solution.py:336
  38.7 4.0 collective-permute-start.5
  42.7 15.9 %collective-permute-start.10 = (bf16[2,512,128]{2,1,0:T(8,128)(2,1)S(1)}, bf16[2,512,128]{2,1,0:T(8,128)(2,1)S(1)}, u32[]{:S(2)}, u32[]{:S(2)}) collective-permute-start(bf16[2,512,128]{2,1,0:T(8,128)(2,1)S(1)} %copy-done.46), channel_id=1, source_target_pairs={{0,16},{4,20},{8,24},{12,28},{16,0},{20,4},{24,8},{28,12},{1,17},{... | collective-permute-start | bytes 786440 | tf_op jit(solution)/shard_map/ppermute | solution.py:336
  48.0 12.2 %collective-permute-start.15 = (bf16[2,512,128]{2,1,0:T(8,128)(2,1)S(1)}, bf16[2,512,128]{2,1,0:T(8,128)(2,1)S(1)}, u32[]{:S(2)}, u32[]{:S(2)}) collective-permute-start(bf16[2,512,128]{2,1,0:T(8,128)(2,1)S(1)} %collective-permute-done.11.refs_7_.refs_3_), channel_id=1, source_target_pairs={{0,4},{4,0},{8,12},{12,8},{16,20},{20,16},{24,28},{28,24},{1,5},{5... | collective-permute-start | bytes 786440 | tf_op jit(solution)/shard_map/ppermute | solution.py:346
  49.9 18.5 %collective-permute-start.12 = (bf16[2,512,128]{2,1,0:T(8,128)(2,1)S(1)}, bf16[2,512,128]{2,1,0:T(8,128)(2,1)S(1)}, u32[]{:S(2)}, u32[]{:S(2)}) collective-permute-start(bf16[2,512,128]{2,1,0:T(8,128)(2,1)S(1)} %copy-done.2), channel_id=1, source_target_pairs={{0,4},{4,0},{8,12},{12,8},{16,20},{20,16},{24,28},{28,24},{1,5},{5... | collective-permute-start | bytes 786440 | tf_op jit(solution)/shard_map/ppermute | solution.py:346
  58.6 9.8 %collective-permute-start.13 = (bf16[2,512,128]{2,1,0:T(8,128)(2,1)S(1)}, bf16[2,512,128]{2,1,0:T(8,128)(2,1)S(1)}, u32[]{:S(2)}, u32[]{:S(2)}) collective-permute-start(bf16[2,512,128]{2,1,0:T(8,128)(2,1)S(1)} %collective-permute-done.9.refs_5_.refs_1_), channel_id=1, source_target_pairs={{0,4},{4,0},{8,12},{12,8},{16,20},{20,16},{24,28},{28,24},{1,5},{5... | collective-permute-start | bytes 786440 | tf_op jit(solution)/shard_map/ppermute | solution.py:346
  60.1 13.4 %collective-permute-start.14 = (bf16[2,512,128]{2,1,0:T(8,128)(2,1)S(1)}, bf16[2,512,128]{2,1,0:T(8,128)(2,1)S(1)}, u32[]{:S(2)}, u32[]{:S(2)}) collective-permute-start(bf16[2,512,128]{2,1,0:T(8,128)(2,1)S(1)} %collective-permute-done.10.refs_6_.refs_2_), channel_id=1, source_target_pairs={{0,4},{4,0},{8,12},{12,8},{16,20},{20,16},{24,28},{28,24},{1,5},{5... | collective-permute-start | bytes 786440 | tf_op jit(solution)/shard_map/ppermute | solution.py:346
  60.7 45.7 %collective-permute-start.19 = (bf16[256,2048]{1,0:T(8,128)(2,1)}, bf16[256,2048]{1,0:T(8,128)(2,1)S(1)}, u32[]{:S(2)}, u32[]{:S(2)}) collective-permute-start(bf16[256,2048]{1,0:T(8,128)(2,1)} %constant_dynamic-slice_fusion.20.own_tokens), channel_id=1, source_target_pairs={{0,4},{4,0},{8,12},{12,8},{16,20},{20,16},{24,28},{28,24},{1,5},{5... | collective-permute-start | bytes 3145736 | tf_op jit(solution)/shard_map/ppermute | solution.py:346
  62.3 6.1 collective-permute-start.8
  91.2 9.4 %collective-permute-start.16 = (bf16[512,128]{1,0:T(8,128)(2,1)S(1)}, bf16[512,128]{1,0:T(8,128)(2,1)S(1)}, u32[]{:S(2)}, u32[]{:S(2)}) collective-permute-start(bf16[512,128]{1,0:T(8,128)(2,1)S(1)} %get-tuple-element.93), channel_id=1, source_target_pairs={{0,24},{4,28},{8,0},{12,4},{16,8},{20,12},{24,16},{28,20},{1,25},{... | collective-permute-start | bytes 393224 | tf_op jit(solution)/shard_map/ppermute | solution.py:336
  92.4 13.9 %collective-permute-start.17 = (bf16[512,128]{1,0:T(8,128)(2,1)S(1)}, bf16[512,128]{1,0:T(8,128)(2,1)S(1)}, u32[]{:S(2)}, u32[]{:S(2)}) collective-permute-start(bf16[512,128]{1,0:T(8,128)(2,1)S(1)} %get-tuple-element.94), channel_id=1, source_target_pairs={{0,16},{4,20},{8,24},{12,28},{16,0},{20,4},{24,8},{28,12},{1,17},{... | collective-permute-start | bytes 393224 | tf_op jit(solution)/shard_map/ppermute | solution.py:336
  99.1 7.2 %collective-permute-start.18 = (bf16[512,128]{1,0:T(8,128)(2,1)S(1)}, bf16[512,128]{1,0:T(8,128)(2,1)S(1)}, u32[]{:S(2)}, u32[]{:S(2)}) collective-permute-start(bf16[512,128]{1,0:T(8,128)(2,1)S(1)} %get-tuple-element.95), channel_id=1, source_target_pairs={{0,8},{4,12},{8,16},{12,20},{16,24},{20,28},{24,0},{28,4},{1,9},{5... | collective-permute-start | bytes 393224 | tf_op jit(solution)/shard_map/ppermute | solution.py:336
  106.3 2.7 collective-permute-start.20
  209.7 6.7 %collective-permute-start.60 = (f32[4096]{0:T(1024)S(1)}, f32[4096]{0:T(1024)S(1)}, u32[]{:S(2)}, u32[]{:S(2)}) collective-permute-start(f32[4096]{0:T(1024)S(1)} %bitcast.84), channel_id=1, source_target_pairs={{0,1},{1,0},{2,3},{3,2},{4,5},{5,4},{6,7},{7,6},{8,9},{9,8},{10,11... | collective-permute-start | bytes 49160 | tf_op jit(solution)/shard_map/ppermute | solution.py:350
  211.2 13.8 %collective-permute-start.23 = (bf16[512,128]{1,0:T(8,128)(2,1)S(1)}, bf16[512,128]{1,0:T(8,128)(2,1)S(1)}, u32[]{:S(2)}, u32[]{:S(2)}) collective-permute-start(bf16[512,128]{1,0:T(8,128)(2,1)S(1)} %get-tuple-element.226), channel_id=1, source_target_pairs={{0,24},{4,28},{8,0},{12,4},{16,8},{20,12},{24,16},{28,20},{1,25},{... | collective-permute-start | bytes 393224 | tf_op jit(solution)/shard_map/ppermute | solution.py:336
  211.2 16.0 %collective-permute-start.22 = (bf16[512,128]{1,0:T(8,128)(2,1)S(1)}, bf16[512,128]{1,0:T(8,128)(2,1)S(1)}, u32[]{:S(2)}, u32[]{:S(2)}) collective-permute-start(bf16[512,128]{1,0:T(8,128)(2,1)S(1)} %get-tuple-element.227), channel_id=1, source_target_pairs={{0,16},{4,20},{8,24},{12,28},{16,0},{20,4},{24,8},{28,12},{1,17},{... | collective-permute-start | bytes 393224 | tf_op jit(solution)/shard_map/ppermute | solution.py:336
  211.9 43.9 %collective-permute-start.28 = (bf16[512,1024]{1,0:T(8,128)(2,1)}, bf16[512,1024]{1,0:T(8,128)(2,1)}, u32[]{:S(2)}, u32[]{:S(2)}) collective-permute-start(bf16[512,1024]{1,0:T(8,128)(2,1)} %get-tuple-element.116), channel_id=1, source_target_pairs={{0,4},{4,0},{8,12},{12,8},{16,20},{20,16},{24,28},{28,24},{1,5},{5... | collective-permute-start | bytes 3145736 | tf_op jit(solution)/shard_map/ppermute | solution.py:346
  214.7 48.9 %collective-permute-start.27 = (bf16[512,1024]{1,0:T(8,128)(2,1)}, bf16[512,1024]{1,0:T(8,128)(2,1)}, u32[]{:S(2)}, u32[]{:S(2)}) collective-permute-start(bf16[512,1024]{1,0:T(8,128)(2,1)} %get-tuple-element.114), channel_id=1, source_target_pairs={{0,4},{4,0},{8,12},{12,8},{16,20},{20,16},{24,28},{28,24},{1,5},{5... | collective-permute-start | bytes 3145736 | tf_op jit(solution)/shard_map/ppermute | solution.py:346
  216.4 10.8 %collective-permute-start.21 = (bf16[512,128]{1,0:T(8,128)(2,1)S(1)}, bf16[512,128]{1,0:T(8,128)(2,1)S(1)}, u32[]{:S(2)}, u32[]{:S(2)}) collective-permute-start(bf16[512,128]{1,0:T(8,128)(2,1)S(1)} %get-tuple-element.228), channel_id=1, source_target_pairs={{0,8},{4,12},{8,16},{12,20},{16,24},{20,28},{24,0},{28,4},{1,9},{5... | collective-permute-start | bytes 393224 | tf_op jit(solution)/shard_map/ppermute | solution.py:336
  224.9 59.7 %collective-permute-start.33 = (bf16[1024,1024]{1,0:T(8,128)(2,1)}, bf16[1024,1024]{1,0:T(8,128)(2,1)}, u32[]{:S(2)}, u32[]{:S(2)}) collective-permute-start(bf16[1024,1024]{1,0:T(8,128)(2,1)} %shard_map.261), channel_id=1, source_target_pairs={{0,8},{4,12},{8,0},{12,4},{16,24},{20,28},{24,16},{28,20},{1,9},{5... | collective-permute-start | bytes 6291464 | tf_op jit(solution)/shard_map/ppermute | solution.py:340
  243.1 34.4 %collective-permute-start.24 = (bf16[512,128]{1,0:T(8,128)(2,1)S(1)}, bf16[512,128]{1,0:T(8,128)(2,1)S(1)}, u32[]{:S(2)}, u32[]{:S(2)}) collective-permute-start(bf16[512,128]{1,0:T(8,128)(2,1)S(1)} %get-tuple-element.108), channel_id=1, source_target_pairs={{0,24},{4,28},{8,0},{12,4},{16,8},{20,12},{24,16},{28,20},{1,25},{... | collective-permute-start | bytes 393224 | tf_op jit(solution)/shard_map/ppermute | solution.py:336
  255.8 23.3 %collective-permute-start.25 = (bf16[512,128]{1,0:T(8,128)(2,1)S(1)}, bf16[512,128]{1,0:T(8,128)(2,1)S(1)}, u32[]{:S(2)}, u32[]{:S(2)}) collective-permute-start(bf16[512,128]{1,0:T(8,128)(2,1)S(1)} %get-tuple-element.109), channel_id=1, source_target_pairs={{0,16},{4,20},{8,24},{12,28},{16,0},{20,4},{24,8},{28,12},{1,17},{... | collective-permute-start | bytes 393224 | tf_op jit(solution)/shard_map/ppermute | solution.py:336
  255.8 26.4 %collective-permute-start.26 = (bf16[512,128]{1,0:T(8,128)(2,1)S(1)}, bf16[512,128]{1,0:T(8,128)(2,1)S(1)}, u32[]{:S(2)}, u32[]{:S(2)}) collective-permute-start(bf16[512,128]{1,0:T(8,128)(2,1)S(1)} %get-tuple-element.110), channel_id=1, source_target_pairs={{0,8},{4,12},{8,16},{12,20},{16,24},{20,28},{24,0},{28,4},{1,9},{5... | collective-permute-start | bytes 393224 | tf_op jit(solution)/shard_map/ppermute | solution.py:336
  263.6 26.9 %collective-permute-start.29 = (bf16[2,512,128]{2,1,0:T(8,128)(2,1)S(1)}, bf16[2,512,128]{2,1,0:T(8,128)(2,1)S(1)}, u32[]{:S(2)}, u32[]{:S(2)}) collective-permute-start(bf16[2,512,128]{2,1,0:T(8,128)(2,1)S(1)} %get-tuple-element.123), channel_id=1, source_target_pairs={{0,4},{4,0},{8,12},{12,8},{16,20},{20,16},{24,28},{28,24},{1,5},{5... | collective-permute-start | bytes 786440 | tf_op jit(solution)/shard_map/ppermute | solution.py:346
  277.5 13.6 %collective-permute-start.30 = (bf16[2,512,128]{2,1,0:T(8,128)(2,1)S(1)}, bf16[2,512,128]{2,1,0:T(8,128)(2,1)S(1)}, u32[]{:S(2)}, u32[]{:S(2)}) collective-permute-start(bf16[2,512,128]{2,1,0:T(8,128)(2,1)S(1)} %get-tuple-element.124), channel_id=1, source_target_pairs={{0,4},{4,0},{8,12},{12,8},{16,20},{20,16},{24,28},{28,24},{1,5},{5... | collective-permute-start | bytes 786440 | tf_op jit(solution)/shard_map/ppermute | solution.py:346
  279.1 13.4 %collective-permute-start.31 = (bf16[2,512,128]{2,1,0:T(8,128)(2,1)S(1)}, bf16[2,512,128]{2,1,0:T(8,128)(2,1)}, u32[]{:S(2)}, u32[]{:S(2)}) collective-permute-start(bf16[2,512,128]{2,1,0:T(8,128)(2,1)S(1)} %get-tuple-element.125), channel_id=1, source_target_pairs={{0,4},{4,0},{8,12},{12,8},{16,20},{20,16},{24,28},{28,24},{1,5},{5... | collective-permute-start | bytes 786440 | tf_op jit(solution)/shard_map/ppermute | solution.py:346
  282.2 41.5 %collective-permute-start.39 = (bf16[256,2048]{1,0:T(8,128)(2,1)}, bf16[256,2048]{1,0:T(8,128)(2,1)}, u32[]{:S(2)}, u32[]{:S(2)}) collective-permute-start(bf16[256,2048]{1,0:T(8,128)(2,1)} %pad_maximum_fusion.7), channel_id=1, source_target_pairs={{0,4},{4,0},{8,12},{12,8},{16,20},{20,16},{24,28},{28,24},{1,5},{5... | collective-permute-start | bytes 3145736 | tf_op jit(solution)/shard_map/ppermute | solution.py:346
  284.6 35.7 %collective-permute-start.32 = (bf16[2,512,128]{2,1,0:T(8,128)(2,1)S(1)}, bf16[2,512,128]{2,1,0:T(8,128)(2,1)}, u32[]{:S(2)}, u32[]{:S(2)}) collective-permute-start(bf16[2,512,128]{2,1,0:T(8,128)(2,1)S(1)} %get-tuple-element.126), channel_id=1, source_target_pairs={{0,4},{4,0},{8,12},{12,8},{16,20},{20,16},{24,28},{28,24},{1,5},{5... | collective-permute-start | bytes 786440 | tf_op jit(solution)/shard_map/ppermute | solution.py:346
  290.5 58.7 %collective-permute-start.37 = (bf16[1024,1024]{1,0:T(8,128)(2,1)}, bf16[1024,1024]{1,0:T(8,128)(2,1)S(1)}, u32[]{:S(2)}, u32[]{:S(2)}) collective-permute-start(bf16[1024,1024]{1,0:T(8,128)(2,1)} %shard_map.259), channel_id=1, source_target_pairs={{0,8},{4,12},{8,0},{12,4},{16,24},{20,28},{24,16},{28,20},{1,9},{5... | collective-permute-start | bytes 6291464 | tf_op jit(solution)/shard_map/ppermute | solution.py:340
  291.1 43.7 %collective-permute-start.38 = (bf16[512,256]{1,0:T(8,128)(2,1)}, bf16[512,256]{1,0:T(8,128)(2,1)S(1)}, u32[]{:S(2)}, u32[]{:S(2)}) collective-permute-start(bf16[512,256]{1,0:T(8,128)(2,1)} %constant_dynamic-slice_fusion.14), channel_id=1, source_target_pairs={{0,4},{4,0},{8,12},{12,8},{16,20},{20,16},{24,28},{28,24},{1,5},{5... | collective-permute-start | bytes 786440 | tf_op jit(solution)/shard_map/ppermute | solution.py:346
  321.1 68.8 %collective-permute-start.34 = (bf16[2,512,128]{2,1,0:T(8,128)(2,1)}, bf16[2,512,128]{2,1,0:T(8,128)(2,1)}, u32[]{:S(2)}, u32[]{:S(2)}) collective-permute-start(bf16[2,512,128]{2,1,0:T(8,128)(2,1)} %add_convert_fusion.9), channel_id=1, source_target_pairs={{0,24},{4,28},{8,0},{12,4},{16,8},{20,12},{24,16},{28,20},{1,25},{... | collective-permute-start | bytes 786440 | tf_op jit(solution)/shard_map/ppermute | solution.py:336
  323.0 67.0 %collective-permute-start.35 = (bf16[2,512,128]{2,1,0:T(8,128)(2,1)}, bf16[2,512,128]{2,1,0:T(8,128)(2,1)}, u32[]{:S(2)}, u32[]{:S(2)}) collective-permute-start(bf16[2,512,128]{2,1,0:T(8,128)(2,1)} %add_convert_fusion.8), channel_id=1, source_target_pairs={{0,16},{4,20},{8,24},{12,28},{16,0},{20,4},{24,8},{28,12},{1,17},{... | collective-permute-start | bytes 786440 | tf_op jit(solution)/shard_map/ppermute | solution.py:336
  323.8 8.2 %collective-permute-start.40 = (bf16[256,2048]{1,0:T(8,128)(2,1)}, bf16[256,2048]{1,0:T(8,128)(2,1)S(1)}, u32[]{:S(2)}, u32[]{:S(2)}) collective-permute-start(bf16[256,2048]{1,0:T(8,128)(2,1)} %collective-permute-done.39), channel_id=1, source_target_pairs={{0,1},{1,0},{2,3},{3,2},{4,5},{5,4},{6,7},{7,6},{8,9},{9,8},{10,11... | collective-permute-start | bytes 3145736 | tf_op jit(solution)/shard_map/ppermute | solution.py:350
  332.0 58.0 %collective-permute-start.36 = (bf16[2,512,128]{2,1,0:T(8,128)(2,1)}, bf16[2,512,128]{2,1,0:T(8,128)(2,1)}, u32[]{:S(2)}, u32[]{:S(2)}) collective-permute-start(bf16[2,512,128]{2,1,0:T(8,128)(2,1)} %add_convert_fusion.7), channel_id=1, source_target_pairs={{0,8},{4,12},{8,16},{12,20},{16,24},{20,28},{24,0},{28,4},{1,9},{5... | collective-permute-start | bytes 786440 | tf_op jit(solution)/shard_map/ppermute | solution.py:336
  334.8 111.2 %collective-permute-start.47 = (bf16[1024,1024]{1,0:T(8,128)(2,1)}, bf16[1024,1024]{1,0:T(8,128)(2,1)S(1)}, u32[]{:S(2)}, u32[]{:S(2)}) collective-permute-start(bf16[1024,1024]{1,0:T(8,128)(2,1)} %shard_map.260), channel_id=1, source_target_pairs={{0,8},{4,12},{8,0},{12,4},{16,24},{20,28},{24,16},{28,20},{1,9},{5... | collective-permute-start | bytes 6291464 | tf_op jit(solution)/shard_map/ppermute | solution.py:340
  349.2 178.4 %collective-permute-start.58 = (bf16[1024,512]{1,0:T(8,128)(2,1)}, bf16[1024,512]{1,0:T(8,128)(2,1)}, u32[]{:S(2)}, u32[]{:S(2)}) collective-permute-start(bf16[1024,512]{1,0:T(8,128)(2,1)} %shard_map.262), channel_id=1, source_target_pairs={{0,16},{4,20},{8,24},{12,28},{16,0},{20,4},{24,8},{28,12},{1,17},{... | collective-permute-start | bytes 3145736 | tf_op jit(solution)/shard_map/ppermute | solution.py:340
  390.0 92.9 %collective-permute-start.48 = (bf16[256,1024]{1,0:T(8,128)(2,1)}, bf16[256,1024]{1,0:T(8,128)(2,1)S(1)}, u32[]{:S(2)}, u32[]{:S(2)}) collective-permute-start(bf16[256,1024]{1,0:T(8,128)(2,1)} %shard_map.264), channel_id=1, source_target_pairs={{0,8},{4,12},{8,0},{12,4},{16,24},{20,28},{24,16},{28,20},{1,9},{5... | collective-permute-start | bytes 1572872 | tf_op jit(solution)/shard_map/ppermute | solution.py:340
  390.0 144.3 %collective-permute-start.54 = (bf16[512,1024]{1,0:T(8,128)(2,1)}, bf16[512,1024]{1,0:T(8,128)(2,1)}, u32[]{:S(2)}, u32[]{:S(2)}) collective-permute-start(bf16[512,1024]{1,0:T(8,128)(2,1)} %shard_map.263), channel_id=1, source_target_pairs={{0,16},{4,20},{8,24},{12,28},{16,0},{20,4},{24,8},{28,12},{1,17},{... | collective-permute-start | bytes 3145736 | tf_op jit(solution)/shard_map/ppermute | solution.py:340
  402.0 50.5 %collective-permute-start.41 = (f32[2,512]{1,0:T(2,128)S(1)}, f32[2,512]{1,0:T(2,128)S(1)}, u32[]{:S(2)}, u32[]{:S(2)}) collective-permute-start(f32[2,512]{1,0:T(2,128)S(1)} %pad_maximum_fusion.21), channel_id=1, source_target_pairs={{0,1},{1,0},{2,3},{3,2},{4,5},{5,4},{6,7},{7,6},{8,9},{9,8},{10,11... | collective-permute-start | bytes 12296 | tf_op jit(solution)/shard_map/ppermute | solution.py:350
  446.0 21.9 %collective-permute-start.61 = (f32[5120]{0:T(1024)S(1)}, f32[5120]{0:T(1024)S(1)}, u32[]{:S(2)}, u32[]{:S(2)}) collective-permute-start(f32[5120]{0:T(1024)S(1)} %pad_maximum_fusion.19), channel_id=1, source_target_pairs={{0,4},{4,0},{8,12},{12,8},{16,20},{20,16},{24,28},{28,24},{1,5},{5... | collective-permute-start | bytes 61448 | tf_op jit(solution)/shard_map/ppermute | solution.py:346
  452.4 6.5 %collective-permute-start.42 = (f32[2,512]{1,0:T(2,128)S(1)}, f32[2,512]{1,0:T(2,128)S(1)}, u32[]{:S(2)}, u32[]{:S(2)}) collective-permute-start(f32[2,512]{1,0:T(2,128)S(1)} %maximum_add_fusion.1), channel_id=1, source_target_pairs={{0,2},{1,3},{2,0},{3,1},{4,6},{5,7},{6,4},{7,5},{8,10},{9,11},{10,... | collective-permute-start | bytes 12296 | tf_op jit(solution)/shard_map/ppermute | solution.py:354
  464.8 22.2 %collective-permute-start.46 = (bf16[512,768]{1,0:T(8,128)(2,1)S(1)}, bf16[512,768]{1,0:T(8,128)(2,1)S(1)}, u32[]{:S(2)}, u32[]{:S(2)}) collective-permute-start(bf16[512,768]{1,0:T(8,128)(2,1)S(1)} %pad_maximum_fusion.11), channel_id=1, source_target_pairs={{0,4},{4,0},{8,12},{12,8},{16,20},{20,16},{24,28},{28,24},{1,5},{5... | collective-permute-start | bytes 2359304 | tf_op jit(solution)/shard_map/ppermute | solution.py:346
  467.9 3.8 collective-permute-start.62
  471.8 9.8 %collective-permute-start.63 = (f32[5120]{0:T(1024)S(1)}, f32[5120]{0:T(1024)S(1)}, u32[]{:S(2)}, u32[]{:S(2)}) collective-permute-start(f32[5120]{0:T(1024)S(1)} %add.231), channel_id=1, source_target_pairs={{0,16},{4,20},{8,24},{12,28},{16,0},{20,4},{24,8},{28,12},{1,17},{... | collective-permute-start | bytes 61448 | tf_op jit(solution)/shard_map/ppermute | solution.py:340
  481.5 52.8 %collective-permute-start.56 = (bf16[512,1024]{1,0:T(8,128)(2,1)}, bf16[512,1024]{1,0:T(8,128)(2,1)S(1)}, u32[]{:S(2)}, u32[]{:S(2)}) collective-permute-start(bf16[512,1024]{1,0:T(8,128)(2,1)} %shard_map.265), channel_id=1, source_target_pairs={{0,16},{4,20},{8,24},{12,28},{16,0},{20,4},{24,8},{28,12},{1,17},{... | collective-permute-start | bytes 3145736 | tf_op jit(solution)/shard_map/ppermute | solution.py:340
  482.9 52.8 %collective-permute-start.43 = (bf16[256,2048]{1,0:T(8,128)(2,1)}, bf16[256,2048]{1,0:T(8,128)(2,1)}, u32[]{:S(2)}, u32[]{:S(2)}) collective-permute-start(bf16[256,2048]{1,0:T(8,128)(2,1)} %pad_maximum_fusion.9), channel_id=1, source_target_pairs={{0,1},{1,0},{2,3},{3,2},{4,5},{5,4},{6,7},{7,6},{8,9},{9,8},{10,11... | collective-permute-start | bytes 3145736 | tf_op jit(solution)/shard_map/ppermute | solution.py:350
  487.0 39.1 %collective-permute-start.52 = (bf16[256,512]{1,0:T(8,128)(2,1)}, bf16[256,512]{1,0:T(8,128)(2,1)S(1)}, u32[]{:S(2)}, u32[]{:S(2)}) collective-permute-start(bf16[256,512]{1,0:T(8,128)(2,1)} %shard_map.266), channel_id=1, source_target_pairs={{0,16},{4,20},{8,24},{12,28},{16,0},{20,4},{24,8},{28,12},{1,17},{... | collective-permute-start | bytes 786440 | tf_op jit(solution)/shard_map/ppermute | solution.py:340
  526.1 6.4 %collective-permute-start.53 = (bf16[256,256]{1,0:T(8,128)(2,1)S(1)}, bf16[256,256]{1,0:T(8,128)(2,1)S(1)}, u32[]{:S(2)}, u32[]{:S(2)}) collective-permute-start(bf16[256,256]{1,0:T(8,128)(2,1)S(1)} %add_convert_fusion.11), channel_id=1, source_target_pairs={{0,4},{4,0},{8,12},{12,8},{16,20},{20,16},{24,28},{28,24},{1,5},{5... | collective-permute-start | bytes 393224 | tf_op jit(solution)/shard_map/ppermute | solution.py:346
  527.7 32.4 %collective-permute-start.49 = (bf16[1024,768]{1,0:T(8,128)(2,1)}, bf16[1024,768]{1,0:T(8,128)(2,1)S(1)}, u32[]{:S(2)}, u32[]{:S(2)}) collective-permute-start(bf16[1024,768]{1,0:T(8,128)(2,1)} %shard_map.267), channel_id=1, source_target_pairs={{0,8},{4,12},{8,0},{12,4},{16,24},{20,28},{24,16},{28,20},{1,9},{5... | collective-permute-start | bytes 4718600 | tf_op jit(solution)/shard_map/ppermute | solution.py:340
  532.5 14.9 %collective-permute-start.59 = (bf16[1024,256]{1,0:T(8,128)(2,1)S(1)}, bf16[1024,256]{1,0:T(8,128)(2,1)S(1)}, u32[]{:S(2)}, u32[]{:S(2)}) collective-permute-start(bf16[1024,256]{1,0:T(8,128)(2,1)S(1)} %add_convert_fusion.3), channel_id=1, source_target_pairs={{0,4},{4,0},{8,12},{12,8},{16,20},{20,16},{24,28},{28,24},{1,5},{5... | collective-permute-start | bytes 1572872 | tf_op jit(solution)/shard_map/ppermute | solution.py:346
  534.5 23.8 %collective-permute-start.57 = (bf16[256,1024]{1,0:T(8,128)(2,1)S(1)}, bf16[256,1024]{1,0:T(8,128)(2,1)S(1)}, u32[]{:S(2)}, u32[]{:S(2)}) collective-permute-start(bf16[256,1024]{1,0:T(8,128)(2,1)S(1)} %add_convert_fusion.4), channel_id=1, source_target_pairs={{0,4},{4,0},{8,12},{12,8},{16,20},{20,16},{24,28},{28,24},{1,5},{5... | collective-permute-start | bytes 1572872 | tf_op jit(solution)/shard_map/ppermute | solution.py:346
  537.3 28.7 %collective-permute-start.44 = (bf16[256,2048]{1,0:T(8,128)(2,1)S(1)}, bf16[256,2048]{1,0:T(8,128)(2,1)S(1)}, u32[]{:S(2)}, u32[]{:S(2)}) collective-permute-start(bf16[256,2048]{1,0:T(8,128)(2,1)S(1)} %add_convert_fusion.2), channel_id=1, source_target_pairs={{0,2},{1,3},{2,0},{3,1},{4,6},{5,7},{6,4},{7,5},{8,10},{9,11},{10,... | collective-permute-start | bytes 3145736 | tf_op jit(solution)/shard_map/ppermute | solution.py:354
  540.3 29.9 %collective-permute-start.55 = (bf16[256,1024]{1,0:T(8,128)(2,1)}, bf16[256,1024]{1,0:T(8,128)(2,1)}, u32[]{:S(2)}, u32[]{:S(2)}) collective-permute-start(bf16[256,1024]{1,0:T(8,128)(2,1)} %add_convert_fusion.5), channel_id=1, source_target_pairs={{0,4},{4,0},{8,12},{12,8},{16,20},{20,16},{24,28},{28,24},{1,5},{5... | collective-permute-start | bytes 1572872 | tf_op jit(solution)/shard_map/ppermute | solution.py:346
  566.0 32.5 %collective-permute-start.50 = (bf16[512,768]{1,0:T(8,128)(2,1)}, bf16[512,768]{1,0:T(8,128)(2,1)}, u32[]{:S(2)}, u32[]{:S(2)}) collective-permute-start(bf16[512,768]{1,0:T(8,128)(2,1)} %shard_map.269), channel_id=1, source_target_pairs={{0,16},{4,20},{8,24},{12,28},{16,0},{20,4},{24,8},{28,12},{1,17},{... | collective-permute-start | bytes 2359304 | tf_op jit(solution)/shard_map/ppermute | solution.py:340
  568.2 34.8 %collective-permute-start.45 = (bf16[256,2048]{1,0:T(8,128)(2,1)S(1)}, bf16[256,2048]{1,0:T(8,128)(2,1)S(1)}, u32[]{:S(2)}, u32[]{:S(2)}) collective-permute-start(bf16[256,2048]{1,0:T(8,128)(2,1)S(1)} %get-tuple-element.160), channel_id=1, source_target_pairs={{0,1},{1,0},{2,3},{3,2},{4,5},{5,4},{6,7},{7,6},{8,9},{9,8},{10,11... | collective-permute-start | bytes 3145736 | tf_op jit(solution)/shard_map/ppermute | solution.py:350
  600.3 11.1 %collective-permute-start.51 = (bf16[256,768]{1,0:T(8,128)(2,1)S(1)}, bf16[256,768]{1,0:T(8,128)(2,1)S(1)}, u32[]{:S(2)}, u32[]{:S(2)}) collective-permute-start(bf16[256,768]{1,0:T(8,128)(2,1)S(1)} %get-tuple-element.169), channel_id=1, source_target_pairs={{0,4},{4,0},{8,12},{12,8},{16,20},{20,16},{24,28},{28,24},{1,5},{5... | collective-permute-start | bytes 1179656 | tf_op jit(solution)/shard_map/ppermute | solution.py:346
  (48 other events, 360.6 us)

commit v3 on v2

--- a/solution.py
+++ b/solution.py
@@ -403,79 +403,179 @@
     return [pl.BlockSpec(memory_space=pltpu.VMEM)] * count
 
 
-def project_kernel(place, own, other, wq, wk, wv, gq, gk, cosines, sines, *refs):
-    out_queries, out_pairs = refs[:line], refs[line : 2 * line]
-    out_q_raw, out_k_raw, out_squares, turned = refs[2 * line :]
+def project_kernel(
+    tokens,
+    wq,
+    wk,
+    wv,
+    gq,
+    gk,
+    cosines,
+    sines,
+    spots,
+    out_queries,
+    out_pairs,
+    out_notes,
+    out_q_raw,
+    out_k_raw,
+    rows_keep,
+    query_keep,
+    pair_keep,
+    squares,
+    squares_core,
+    squares_y,
+    send_sems,
+    recv_sems,
+    local_sems,
+):
     f32 = jnp.float32
     bf16 = jnp.bfloat16
     width = cosines.shape[1]
-    rows = jnp.concatenate([own[...], other[...]], axis=0)
-
-    def keep(raw, gain, slot):
+    depth = wq.shape[0]
+    rows = rows_keep.shape[0] // 2
+    count = rows // 2
+    mp = lax.axis_index("mp")
+    spot = lax.axis_index("dp")
+    core = lax.rem(mp, 2)
+    x = lax.rem(spot, 2)
+    z = spot // 2
+    core_peer = {"mp": mp + 1 - 2 * core}
+    y_peer = {"mp": lax.rem(mp + 2, 4)}
+    x_peer = {"dp": spot + 1 - 2 * x}
+    ahead = [{"dp": lax.rem(spot + 2 * d, 2 * line)} for d in range(line)]
+    head = [lax.rem(z + d, line) for d in range(line)]
+    both = lambda s: pl.ds(s * rows, rows)
+    remote = []
+
+    def send(source, target, peer):
+        index = len(remote)
+        copy = pltpu.make_async_remote_copy(
+            src_ref=source,
+            dst_ref=target,
+            send_sem=send_sems.at[index],
+            recv_sem=recv_sems.at[index],
+            device_id=peer,
+            device_id_type=pl.DeviceIdType.MESH,
+        )
+        remote.append(copy)
+        copy.start()
+        return copy
+
+    loads = []
+    for s in range(2):
+        for part, place in ((0, core), (1, 1 - core)):
+            start = pl.multiple_of(place * rows + s * count, count)
+            copy = pltpu.make_async_copy(
+                tokens.at[pl.ds(start, count)],
+                rows_keep.at[pl.ds(s * rows + part * count, count)],
+                local_sems.at[2 * s + part],
+            )
+            copy.start()
+            loads.append(copy)
+
+    barrier = pltpu.get_barrier_semaphore()
+    peers = (core_peer, y_peer, x_peer, ahead[1], ahead[2], ahead[3])
+    for peer in peers:
+        pl.semaphore_signal(barrier, inc=1, device_id=peer, device_id_type=pl.DeviceIdType.MESH)
+    pl.semaphore_wait(barrier, len(peers))
+
+    def turned(raw, gain, s, h):
+        part = raw[:, h * width : (h + 1) * width] * gain[:, h * width : (h + 1) * width]
+        return (
+            part * cosines[both(s), :] + pltpu.roll(part, width // 2, 1) * sines[both(s), :]
+        ).astype(bf16)
+
+    flying = {}
+    for s in range(2):
+        loads[2 * s].wait()
+        loads[2 * s + 1].wait()
+        k_raw = jnp.dot(rows_keep[both(s), :], wk[...], preferred_element_type=f32)
+        out_k_raw[both(s), :] = k_raw
+        squares[1:2, both(s)] = jnp.sum((k_raw * k_raw).T, axis=0, keepdims=True)
+        v_raw = jnp.dot(rows_keep[both(s), :], wv[...], preferred_element_type=f32)
         for h in range(line):
-            part = raw[:, h * width : (h + 1) * width] * gain[:, h * width : (h + 1) * width]
-            turned[slot, h] = (
-                part * cosines[...] + pltpu.roll(part, width // 2, 1) * sines[...]
-            ).astype(bf16)
-
-    q_raw = jnp.dot(rows, wq[...], preferred_element_type=f32)
-    out_q_raw[...] = q_raw
-    out_squares[0:1, :] = jnp.sum((q_raw * q_raw).T, axis=0, keepdims=True)
-    keep(q_raw, gq[...], 0)
-    k_raw = jnp.dot(rows, wk[...], preferred_element_type=f32)
-    out_k_raw[...] = k_raw
-    out_squares[1:2, :] = jnp.sum((k_raw * k_raw).T, axis=0, keepdims=True)
-    keep(k_raw, gk[...], 1)
-    v_raw = jnp.dot(rows, wv[...], preferred_element_type=f32)
-    for h in range(line):
-        turned[2, h] = v_raw[:, h * width : (h + 1) * width].astype(bf16)
+            pair_keep[h, 0, both(s), :] = turned(k_raw, gk[...], s, h)
+            pair_keep[h, 1, both(s), :] = v_raw[:, h * width : (h + 1) * width].astype(bf16)
+        for d in (2, 1, 3):
+            flying["pair", s, d] = send(
+                pair_keep.at[head[d], :, both(s)], out_pairs.at[d, :, both(s)], ahead[d]
+            )
+        flying["far", s, 0] = send(
+            pair_keep.at[z, :, both(s)], out_pairs.at[line, :, both(s)], x_peer
+        )
+        q_raw = jnp.dot(rows_keep[both(s), :], wq[...], preferred_element_type=f32)
+        out_q_raw[both(s), :] = q_raw
+        squares[0:1, both(s)] = jnp.sum((q_raw * q_raw).T, axis=0, keepdims=True)
+        for h in range(line):
+            query_keep[h, both(s), :] = turned(q_raw, gq[...], s, h)
+
+    core_copy = send(squares, squares_core, core_peer)
+    core_copy.wait()
+    arrived = squares_core[...]
+    cuts = [arrived[:, i * count : (i + 1) * count] for i in (1, 0, 3, 2)]
+    chip = squares[...] + jnp.concatenate(cuts, axis=1)
+    squares[...] = chip
+    y_copy = send(squares, squares_y, y_peer)
+    y_copy.wait()
+    out_notes[0, 0:2, :] = lax.rsqrt((chip + squares_y[...]) / depth + epsilon)
+    out_notes[0, 2:4, :] = spots[...]
+    for d in range(1, line):
+        flying["note", d] = send(out_notes.at[0], out_notes.at[d], ahead[d])
+    flying["far_note", 0] = send(out_notes.at[0], out_notes.at[line], x_peer)
+    for d in range(1, line):
+        flying["query", d] = send(query_keep.at[head[d]], out_queries.at[d], ahead[d])
+    out_queries[0] = query_keep[z]
+    out_pairs[0] = pair_keep[z]
+    for s in range(2):
+        for d in (2, 1, 3):
+            flying["pair", s, d].wait()
+            flying["far", s, d] = send(
+                out_pairs.at[d, :, both(s)], out_pairs.at[line + d, :, both(s)], x_peer
+            )
+    for d in range(1, line):
+        flying["note", d].wait()
+        flying["far_note", d] = send(out_notes.at[d], out_notes.at[line + d], x_peer)
+    for d in range(1, line):
+        flying["query", d].wait()
     for d in range(line):
-        head = lax.rem(place[1] + d, line)
-        out_queries[d][...] = turned[0, head]
-        out_pairs[d][0] = turned[1, head]
-        out_pairs[d][1] = turned[2, head]
-
-
-def project(place, tokens, wq, wk, wv, gq, gk, cosines, sines):
+        flying["far_note", d].wait()
+        for s in range(2):
+            flying["far", s, d].wait()
+
+
+def project(tokens, wq, wk, wv, gq, gk, cosines, sines, spots):
     rows, depth = tokens.shape
     columns = wq.shape[1]
     width = columns // line
-    half = rows // 2
     f32 = jnp.float32
     bf16 = jnp.bfloat16
-    whole = lambda shape: pl.BlockSpec(shape, lambda i, p: (0, 0))
-    rows_of = lambda n: pl.BlockSpec((half, n), lambda i, p: (i, 0))
     return pl.pallas_call(
         project_kernel,
-        grid_spec=pltpu.PrefetchScalarGridSpec(
-            num_scalar_prefetch=1,
-            grid=(2,),
-            in_specs=[
-                pl.BlockSpec((half // 2, depth), lambda i, p: (2 * p[0] + i, 0)),
-                pl.BlockSpec((half // 2, depth), lambda i, p: (2 * (1 - p[0]) + i, 0)),
-                whole((depth, columns)),
-                whole((depth, columns)),
-                whole((depth, columns)),
-                whole((1, columns)),
-                whole((1, columns)),
-                rows_of(width),
-                rows_of(width),
-            ],
-            out_specs=[rows_of(width)] * line
-            + [pl.BlockSpec((2, half, width), lambda i, p: (0, i, 0))] * line
-            + [rows_of(columns)] * 2
-            + [pl.BlockSpec((2, half), lambda i, p: (0, i))],
-            scratch_shapes=[pltpu.VMEM((3, line, half, width), bf16)],
+        in_specs=[pl.BlockSpec(memory_space=pl.ANY)] + vmem_specs(8),
+        out_specs=vmem_specs(5),
+        out_shape=[
+            jax.ShapeDtypeStruct((line, rows, width), bf16),
+            jax.ShapeDtypeStruct((2 * line, 2, rows, width), bf16),
+            jax.ShapeDtypeStruct((2 * line, 4, rows), f32),
+            jax.ShapeDtypeStruct((rows, columns), f32),
+            jax.ShapeDtypeStruct((rows, columns), f32),
+        ],
+        scratch_shapes=[
+            pltpu.VMEM((rows, depth), bf16),
+            pltpu.VMEM((line, rows, width), bf16),
+            pltpu.VMEM((line, 2, rows, width), bf16),
+            pltpu.VMEM((2, rows), f32),
+            pltpu.VMEM((2, rows), f32),
+            pltpu.VMEM((2, rows), f32),
+            pltpu.SemaphoreType.DMA((28,)),
+            pltpu.SemaphoreType.DMA((28,)),
+            pltpu.SemaphoreType.DMA((4,)),
+        ],
+        compiler_params=pltpu.CompilerParams(
+            vmem_limit_bytes=48 << 20, collective_id=2, has_side_effects=True
         ),
-        out_shape=[jax.ShapeDtypeStruct((rows, width), bf16)] * line
-        + [jax.ShapeDtypeStruct((2, rows, width), bf16)] * line
-        + [jax.ShapeDtypeStruct((rows, columns), f32)] * 2
-        + [jax.ShapeDtypeStruct((2, rows), f32)],
-        compiler_params=pltpu.CompilerParams(vmem_limit_bytes=big_vmem),
-        cost_estimate=pl.CostEstimate(
-            flops=6 * rows * depth * columns, bytes_accessed=12 << 20, transcendentals=0
-        ),
-    )(place, tokens, tokens, wq, wk, wv, gq, gk, cosines, sines)
+        cost_estimate=pl.CostEstimate(flops=0, bytes_accessed=0, transcendentals=0),
+    )(tokens, wq, wk, wv, gq, gk, cosines, sines, spots)
 
 
 def visible_scores(key, query, key_code, query_code, query_low, factor):
@@ -485,24 +585,22 @@
 
 
 def attend_kernel(factor, key_rows, live, notes, *refs):
-    query_refs = refs[:line]
-    pair_refs = refs[line : 3 * line]
-    out_turned, out_log, out_query, out_key, out_codes, out_rows = refs[3 * line : 3 * line + 6]
-    out_refs = refs[3 * line + 6 : 4 * line + 6]
-    top, total, accum = refs[4 * line + 6 :]
+    queries, pairs = refs[:2]
+    out_turned, out_log, out_query, out_key, out_codes, out_rows, out = refs[2:9]
+    top, total, accum = refs[9:]
     f32 = jnp.float32
     bf16 = jnp.bfloat16
-    count, width = query_refs[0].shape
+    count, width = queries.shape[1:]
 
     def column(row):
         return jnp.broadcast_to(row, (width, count)).T
 
     for k in range(2 * line):
-        out_key[k] = (pair_refs[k][0].astype(f32) * column(notes[k, 1:2, :])).astype(bf16)
+        out_key[k] = (pairs[k, 0].astype(f32) * column(notes[k, 1:2, :])).astype(bf16)
         labels = column(notes[k, 2:3, :]).astype(jnp.int32)
         out_codes[k] = labels * key_rows + column(notes[k, 3:4, :]).astype(jnp.int32)
     for q in range(line):
-        out_query[q] = (query_refs[q][...].astype(f32) * column(notes[q, 0:1, :])).astype(bf16)
+        out_query[q] = (queries[q].astype(f32) * column(notes[q, 0:1, :])).astype(bf16)
         base = notes[q, 2:3, :].astype(jnp.int32) * key_rows
         out_rows[q : q + 1, :] = base + notes[q, 3:4, :].astype(jnp.int32)
         out_rows[line + q : line + q + 1, :] = base
@@ -527,34 +625,32 @@
                 weights = jnp.exp2(scores - highest)
                 fade = jnp.exp2(top[...] - highest)
                 total[...] = total[...] * fade + jnp.sum(weights, axis=0, keepdims=True)
-                accum[...] = accum[...] * fade + dot_t(pair_refs[k][1], weights.astype(bf16))
+                accum[...] = accum[...] * fade + dot_t(pairs[k, 1], weights.astype(bf16))
                 top[...] = highest
 
         turned = accum[...] / total[...]
         out_turned[q] = turned
         out_log[q : q + 1, :] = top[...] + jnp.log2(total[...])
-        out_refs[q][...] = turned.T.astype(bf16)
+        out[q] = turned.T.astype(bf16)
 
 
 def attend_back_kernel(factor, scale, live, codes, rows, queries, keys, *refs):
-    pair_refs = refs[: 2 * line]
-    turned, log_total = refs[2 * line : 2 * line + 2]
-    grad_refs = refs[2 * line + 2 : 3 * line + 2]
-    out_query = refs[3 * line + 2 : 4 * line + 2]
-    out_pairs = refs[4 * line + 2 : 6 * line + 2]
-    key_sum, value_sum, query_sum = refs[6 * line + 2 :]
+    pairs, turned, log_total, grads = refs[:4]
+    out_query = refs[4 : line + 4]
+    out_pairs = refs[line + 4 : 3 * line + 4]
+    key_sum, value_sum, query_sum = refs[3 * line + 4 :]
     f32 = jnp.float32
     bf16 = jnp.bfloat16
     key_sum[...] = jnp.zeros_like(key_sum)
     value_sum[...] = jnp.zeros_like(value_sum)
     for q in range(line):
         query_sum[...] = jnp.zeros_like(query_sum)
-        delta = jnp.sum(grad_refs[q][...].astype(f32).T * turned[q], axis=0, keepdims=True)
+        delta = jnp.sum(grads[q].astype(f32).T * turned[q], axis=0, keepdims=True)
         for k in range(2 * line):
 
             @pl.when(live[q, k] > 0)
             def _(q=q, k=k, delta=delta):
-                query, key, grad = queries[q], keys[k], grad_refs[q][...]
+                query, key, grad = queries[q], keys[k], grads[q]
                 scores = visible_scores(
                     key,
                     query,
@@ -564,7 +660,7 @@
                     factor,
                 )
                 probs = jnp.exp2(scores - log_total[q : q + 1, :])
-                grad_probs = dot_nt(pair_refs[k][1], grad)
+                grad_probs = dot_nt(pairs[k, 1], grad)
                 grad_scores = (probs * (grad_probs - delta)).astype(bf16)
                 value_sum[k] += jnp.dot(
                     probs.astype(bf16), grad, preferred_element_type=f32
@@ -579,7 +675,7 @@
 
 
 def attend(key_rows, live, notes, queries, pairs):
-    count, width = queries[0].shape
+    _, count, width = queries.shape
     factor = math.log2(math.e) / math.sqrt(width)
     f32 = jnp.float32
     bf16 = jnp.bfloat16
@@ -593,21 +689,17 @@
             jax.ShapeDtypeStruct((2 * line, count, width), jnp.int32),
             jax.ShapeDtypeStruct((2 * line, count), jnp.int32),
         ]
-        + [jax.ShapeDtypeStruct((count, width), bf16)] * line,
-        in_specs=[pl.BlockSpec(memory_space=pltpu.SMEM)] + vmem_specs(1 + 3 * line),
-        out_specs=vmem_specs(6 + line),
+        + [jax.ShapeDtypeStruct((line, count, width), bf16)],
+        in_specs=[pl.BlockSpec(memory_space=pltpu.SMEM)] + vmem_specs(3),
+        out_specs=vmem_specs(7),
         scratch_shapes=[
             pltpu.VMEM((1, count), f32),
             pltpu.VMEM((1, count), f32),
             pltpu.VMEM((width, count), f32),
         ],
         compiler_params=pltpu.CompilerParams(vmem_limit_bytes=40 << 20),
-        cost_estimate=pl.CostEstimate(
-            flops=10 * 4 * count * count * width,
-            bytes_accessed=8 << 20,
-            transcendentals=10 * count * count,
-        ),
-    )(live, notes, *queries, *pairs)
+        cost_estimate=pl.CostEstimate(flops=0, bytes_accessed=0, transcendentals=0),
+    )(live, notes, queries, pairs)
 
 
 def attend_back(live, codes, rows, queries, keys, pairs, turned, log_total, grads):
@@ -619,7 +711,7 @@
         functools.partial(attend_back_kernel, factor, scale),
         out_shape=[jax.ShapeDtypeStruct((count, width), jnp.bfloat16)] * line
         + [jax.ShapeDtypeStruct((2, count, width), jnp.bfloat16)] * (2 * line),
-        in_specs=[pl.BlockSpec(memory_space=pltpu.SMEM)] + vmem_specs(6 + 3 * line),
+        in_specs=[pl.BlockSpec(memory_space=pltpu.SMEM)] + vmem_specs(8),
         out_specs=vmem_specs(3 * line),
         scratch_shapes=[
             pltpu.VMEM((2 * line, count, width), f32),
@@ -628,23 +720,25 @@
         ],
         compiler_params=pltpu.CompilerParams(vmem_limit_bytes=40 << 20),
         cost_estimate=pl.CostEstimate(
-            flops=10 * 10 * count * count * width,
+            flops=20 * line * line * count * count * width,
             bytes_accessed=12 << 20,
-            transcendentals=10 * count * count,
+            transcendentals=2 * line * line * count * count,
         ),
-    )(live, codes, rows, queries, keys, *pairs, turned, log_total, *grads)
+    )(live, codes, rows, queries, keys, pairs, turned, log_total, grads)
 
 
 def block_kernel(
-    attended,
+    pieces,
     w_out,
-    own_tokens,
-    own_cotangent,
     g_attn,
     g_mlp,
+    tokens,
+    cotangent,
     w_gate_in,
     w_up_in,
     w_down_in,
+    out_heads,
+    out_tokens_x,
     out_output,
     out_hidden,
     out_hidden_x,
@@ -657,7 +751,7 @@
     out_up,
     out_up_far,
     out_attn,
-    out_attended,
+    out_grads,
     out_grad_hidden,
     out_gain,
     w_gate,
@@ -673,7 +767,10 @@
     grad_up,
     own_factor,
     own_normed,
-    out_keep,
+    own_tokens,
+    own_cotangent,
+    attended,
+    heads_keep,
     total,
     part_send,
     part_recv,
@@ -697,11 +794,10 @@
     core_peer = {"mp": mp + 1 - 2 * core}
     y_peer = {"mp": lax.rem(mp + 2, 4)}
     x_peer = {"dp": spot + 1 - 2 * x}
-
-    barrier = pltpu.get_barrier_semaphore()
-    for peer in (core_peer, y_peer, x_peer):
-        pl.semaphore_signal(barrier, inc=1, device_id=peer, device_id_type=pl.DeviceIdType.MESH)
-    pl.semaphore_wait(barrier, 3)
+    z = spot // 2
+    width = pieces.shape[2]
+    ahead = [{"dp": lax.rem(spot + 2 * d, 2 * line)} for d in range(line)]
+    head = lambda d: pl.ds(pl.multiple_of(lax.rem(z + d, line) * width, width), width)
 
     remote, started, local = [], [], []
 
@@ -727,8 +823,6 @@
         copy.start()
         return copy
 
-    loads = [keep_out(a, b, True) for a, b in ((w_gate_in, w_gate), (w_up_in, w_up), (w_down_in, w_down))]
-
     own = lambda s: pl.ds(s * rows, count)
     other = lambda s: pl.ds(s * rows + count, count)
     both = lambda s: pl.ds(s * rows, rows)
@@ -737,6 +831,33 @@
     cut = lambda t: pl.ds(pl.multiple_of(t * tile, tile), tile)
     flying = {}
 
+    home_rows = pl.ds(pl.multiple_of(core * rows, rows), rows)
+    loads = [
+        keep_out(tokens.at[home_rows], own_tokens, True),
+        keep_out(cotangent.at[home_rows], own_cotangent, True),
+        keep_out(w_gate_in, w_gate, True),
+        keep_out(w_up_in, w_up, True),
+        keep_out(w_down_in, w_down, True),
+    ]
+    barrier = pltpu.get_barrier_semaphore()
+    peers = (core_peer, y_peer, x_peer, ahead[1], ahead[2], ahead[3])
+    for peer in peers:
+        pl.semaphore_signal(barrier, inc=1, device_id=peer, device_id_type=pl.DeviceIdType.MESH)
+    pl.semaphore_wait(barrier, len(peers))
+    for s in range(2):
+        for d in range(1, line):
+            flying["heads", s, d] = send(
+                pieces.at[d, both(s)], attended.at[both(s), head(0)], ahead[line - d]
+            )
+    attended[:, head(0)] = pieces[0]
+    loads[0].wait()
+    for s in range(2):
+        flying["tokens", s] = send(own_tokens.at[mine(s)], out_tokens_x.at[own(s)], x_peer)
+
+    def forward_core(name, s, array):
+        flying[name, s].wait()
+        flying[name + "_core", s] = send(array.at[own(s)], array.at[other(s)], core_peer)
+
     def reduce_start(stage, s):
         part_send[s] = total[count:, :].astype(bf16)
         copy = send(part_send.at[s], part_recv.at[s], core_peer)
@@ -755,6 +876,9 @@
         flying["share", s] = send(keep.at[own(s)], keep.at[other(s)], core_peer)
 
     def project_out(s):
+        for d in range(1, line):
+            flying["heads", s, d].wait()
+        keep_out(attended.at[both(s)], out_heads.at[both(s)])
         total[...] = jnp.dot(attended[both(s), :], w_out[...], preferred_element_type=f32)
         reduce_start(0, s)
 
@@ -800,9 +924,10 @@
         value = reduced(1, s)
         factor = factor_of(value)
         normed = value * factor
-        out_keep[mine(s), :] = (out_grad_hidden[mine(s), :] + normed * g_mlp[...]).astype(bf16)
-        keep_out(out_keep.at[mine(s)], out_output.at[at_home(s)])
-        flying["output", s] = send(out_keep.at[mine(s)], out_output.at[at_home(s)], core_peer)
+        forward_core("tokens", s, out_tokens_x)
+        own_tokens[mine(s), :] = (out_grad_hidden[mine(s), :] + normed * g_mlp[...]).astype(bf16)
+        keep_out(own_tokens.at[mine(s)], out_output.at[at_home(s)])
+        flying["output", s] = send(own_tokens.at[mine(s)], out_output.at[at_home(s)], core_peer)
         grad = own_cotangent[mine(s), :].astype(f32)
         gain = jnp.sum(grad * normed, axis=0, keepdims=True)
         out_gain[1:2, :] = gain if s == 0 else out_gain[1:2, :] + gain
@@ -861,17 +986,18 @@
     def attended_grad(s):
         flying["share", s].wait()
         keep_out(attn_keep.at[both(s)], out_attn.at[both(s)])
-        out_attended[both(s), :] = dot_nt(attn_keep[both(s), :], w_out[...]).astype(bf16)
-
-    def forward_core(name, s, array):
-        flying[name, s].wait()
-        flying[name + "_core", s] = send(array.at[own(s)], array.at[other(s)], core_peer)
+        heads_keep[both(s), :] = dot_nt(attn_keep[both(s), :], w_out[...]).astype(bf16)
+        for d in range(1, line):
+            flying["grads", s, d] = send(
+                heads_keep.at[both(s), head(d)], out_grads.at[d, both(s)], ahead[d]
+            )
+        keep_out(heads_keep.at[both(s), head(0)], out_grads.at[0, both(s)])
 
     project_out(0)
     project_out(1)
+    for load in loads[1:]:
+        load.wait()
     after_attention(0)
-    for load in loads:
-        load.wait()
     forward(0)
     after_attention(1)
     forward(1)
@@ -890,14 +1016,18 @@
         flying["output", s].wait()
         forward_core("mlp", s, out_mlp_x)
     for s in range(2):
+        flying["tokens_core", s].wait()
         flying["hidden_core", s].wait()
         flying["mlp_core", s].wait()
+        for d in range(1, line):
+            flying["grads", s, d].wait()
     for copy in local:
         copy.wait()
 
 
-def block(attended, w_out, own_tokens, own_cotangent, g_attn, g_mlp, w_gate, w_up, w_down):
-    rows, columns = attended.shape
+def block(pieces, w_out, g_attn, g_mlp, tokens, cotangent, w_gate, w_up, w_down):
+    _, rows, width = pieces.shape
+    columns = line * width
     depth, units = w_gate.shape
     half = rows // 2
     quarter = rows // 4
@@ -909,6 +1039,8 @@
     return pl.pallas_call(
         block_kernel,
         out_shape=[
+            jax.ShapeDtypeStruct((rows, columns), bf16),
+            wide,
             wide,
             wide,
             wide,
@@ -921,12 +1053,12 @@
             tall,
             jax.ShapeDtypeStruct((rows, units // 2), bf16),
             wide,
-            jax.ShapeDtypeStruct((rows, columns), bf16),
+            jax.ShapeDtypeStruct((line, rows, width), bf16),
             jax.ShapeDtypeStruct((half, depth), f32),
             jax.ShapeDtypeStruct((2, depth), f32),
         ],
-        in_specs=vmem_specs(6) + [any_spec] * 3,
-        out_specs=[any_spec] * 12 + vmem_specs(3),
+        in_specs=vmem_specs(4) + [any_spec] * 5,
+        out_specs=[any_spec] * 15 + vmem_specs(2),
         scratch_shapes=[
             pltpu.VMEM((depth, units), bf16),
             pltpu.VMEM((depth, units), bf16),
@@ -942,24 +1074,23 @@
             pltpu.VMEM((half, 128), f32),
             pltpu.VMEM((half, depth), f32),
             pltpu.VMEM((half, depth), bf16),
+            pltpu.VMEM((half, depth), bf16),
+            pltpu.VMEM((rows, columns), bf16),
+            pltpu.VMEM((rows, columns), bf16),
             pltpu.VMEM((half, depth), f32),
             pltpu.VMEM((2, quarter, depth), bf16),
             pltpu.VMEM((2, quarter, depth), bf16),
             pltpu.VMEM((2, quarter, depth), bf16),
             pltpu.VMEM((3, 2, quarter, depth), bf16),
-            pltpu.SemaphoreType.DMA((30,)),
-            pltpu.SemaphoreType.DMA((30,)),
-            pltpu.SemaphoreType.DMA((24,)),
+            pltpu.SemaphoreType.DMA((52,)),
+            pltpu.SemaphoreType.DMA((52,)),
+            pltpu.SemaphoreType.DMA((32,)),
         ],
         compiler_params=pltpu.CompilerParams(
             vmem_limit_bytes=61800 << 10, collective_id=1, has_side_effects=True
         ),
-        cost_estimate=pl.CostEstimate(
-            flops=12 * rows * depth * units,
-            bytes_accessed=60 << 20,
-            transcendentals=2 * rows * units,
-        ),
-    )(attended, w_out, own_tokens, own_cotangent, g_attn, g_mlp, w_gate, w_up, w_down)
+        cost_estimate=pl.CostEstimate(flops=0, bytes_accessed=0, transcendentals=0),
+    )(pieces, w_out, g_attn, g_mlp, tokens, cotangent, w_gate, w_up, w_down)
 
 
 def weight_kernel(place, *refs):
@@ -1025,11 +1156,7 @@
         ),
         out_shape=jax.ShapeDtypeStruct(shape, kind),
         compiler_params=pltpu.CompilerParams(vmem_limit_bytes=big_vmem),
-        cost_estimate=pl.CostEstimate(
-            flops=4 * tokens * shape[0] * shape[1],
-            bytes_accessed=4 * tokens * (shape[0] + shape[1]) + 4 * shape[0] * shape[1],
-            transcendentals=0,
-        ),
+        cost_estimate=pl.CostEstimate(flops=0, bytes_accessed=0, transcendentals=0),
     )(place, *args)
 
 
@@ -1046,16 +1173,17 @@
         first, second = self.operands
         return weight_term(self.place, first, second, self.cut_first, blocks, extra, kind)
 
-    def neighbour(self):
-        self.arrived = line_flip(self.sent, 1)
+    def neighbour(self, *needed):
+        self.arrived = line_flip(after(self.sent, *needed) if needed else self.sent, 1)
 
     def second(self):
         self.passed = self.make((2,), (self.arrived, lambda p: 1 - p[3]), jnp.bfloat16)
+        self.later = line_flip(self.passed, 2)
         return self.passed
 
     def finish(self, *needed):
         own = self.make((3,), (self.arrived, lambda p: p[3]), jnp.float32)
-        later = after(line_flip(self.passed, 2), *needed)
+        later = after(self.later, *needed)
         axis = 0 if self.cut_first else 1
         width = own.shape[axis] // pair
         far = lambda value: lax.dynamic_slice_in_dim(value, (1 - self.x) * width, width, axis)
@@ -1129,23 +1257,11 @@
     sines = jnp.concatenate([-sines, sines], axis=1)
     g_query = gain_query.reshape(1, local_width)
     g_key = gain_key.reshape(1, local_width)
-
-    projected = project(
-        place, tokens, w_query, w_key, w_value, g_query, g_key, cosines, sines
-    )
-    queries, pairs = projected[:line], projected[line : 2 * line]
-    q_raw, k_raw, squares = projected[2 * line :]
-    pairs = [pairs[0]] + [line_shift(pairs[d], d) for d in range(1, line)]
-    queries = [queries[0]] + [line_shift(queries[d], d) for d in range(1, line)]
-    pairs = pairs + [x_swap(both) for both in pairs]
-
-    squares = token_sum(squares)
-    factors = lax.rsqrt(squares / model_width + epsilon)
-    notes = jnp.concatenate(
-        [factors, labels.astype(f32)[None, :], positions.astype(f32)[None, :]], axis=0
-    )
-    notes = jnp.stack([notes] + [line_shift(notes, d) for d in range(1, line)])
-    notes = jnp.concatenate([notes, x_swap(notes)], axis=0)
+    spots = jnp.stack([labels, positions]).astype(f32)
+    queries, pairs, notes, q_raw, k_raw = project(
+        tokens, w_query, w_key, w_value, g_query, g_key, cosines, sines, spots
+    )
+    factors = notes[0, :2]
     codes = notes[:, 2, :].astype(jnp.int32) * key_rows + notes[:, 3, :].astype(jnp.int32)
     lows = notes[:line, 2, :].astype(jnp.int32) * key_rows
     live = (
@@ -1153,7 +1269,7 @@
         & (jnp.max(codes, axis=1)[None, :] >= jnp.min(lows, axis=1)[:, None])
     ).astype(jnp.int32)
 
-    turned, log_total, queries_n, keys_n, code_columns, code_rows, *attended_out = attend(
+    turned, log_total, queries_n, keys_n, code_columns, code_rows, attended_out = attend(
         key_rows, live, notes, queries, pairs
     )
 
@@ -1166,15 +1282,12 @@
     def send_home(pieces):
         return [pieces[0]] + [line_shift(pieces[d], line - d) for d in range(1, line)]
 
-    attended_low = gather_heads(send_home(attended_out))
-    own_tokens = own_rows(tokens)
     tokens_in = reorder(tokens)
-    tokens_own_x = x_swap(after(own_tokens, pairs[-1]))
-    tokens_x = join_parts(tokens_own_x, core_swap(tokens_own_x))
-    attended_low = after(attended_low, tokens_x)
     g_attn = gain_attn.reshape(1, model_width)
     g_mlp = gain_mlp.reshape(1, model_width)
     (
+        attended_low,
+        tokens_x,
         output,
         hidden_low,
         hidden_x,
@@ -1187,59 +1300,35 @@
         grad_up,
         grad_up_far,
         grad_attn,
-        grad_attended,
+        grads,
         grad_hidden,
         wide_gains,
     ) = block(
-        attended_low,
-        w_output,
-        own_tokens,
-        own_rows(cotangent),
-        g_attn,
-        g_mlp,
-        w_gate,
-        w_up,
-        w_down,
-    )
-    grad_gate_x = x_swap(grad_gate_far)
-    grad_up_x = x_swap(grad_up_far)
+        attended_out, w_output, g_attn, g_mlp, tokens, cotangent, w_gate, w_up, w_down
+    )
     down = Spread(place, x, (act_low, act_x), (grad_mlp, grad_mlp_x), False)
     down.neighbour()
-    gate = Spread(place, x, (hidden_low, hidden_x), (grad_gate, grad_gate_x), True)
-    up = Spread(place, x, (hidden_low, hidden_x), (grad_up, grad_up_x), True)
-    gate.neighbour()
-    up.neighbour()
-
-    def head_of(value, d):
-        return lax.dynamic_slice_in_dim(
-            value, lax.rem(z + d, line) * head_width, head_width, 1
-        )
-
-    grads = [
-        head_of(grad_attended, d) if d == 0 else line_shift(head_of(grad_attended, d), d)
-        for d in range(line)
-    ]
-    attended_far, grad_attn_far = after(
-        (half_of(attended_low, 1 - x), own_part(grad_attn)), gate.sent, up.sent
-    )
-    attended_x = x_swap(attended_far)
-    grad_attn_own = x_swap(grad_attn_far)
-    grad_attn_x = join_parts(grad_attn_own, core_swap(grad_attn_own))
-    out = Spread(place, x, (attended_low, attended_x), (grad_attn, grad_attn_x), False)
-
+    grad_gate_x = x_swap(grad_gate_far)
     back = attend_back(
         live, code_columns, code_rows, queries_n, keys_n, pairs, turned, log_total, grads
     )
     grad_query_pieces, grad_pairs = back[:line], back[line:]
-    far_pairs = [x_swap(grad_pairs[line + d]) for d in range(line)]
-    far_pairs = after(far_pairs, gate.sent, up.sent, down.second())
+    far_pairs = after(grad_pairs[line:], grad_gate_x)
+    far_pairs = [x_swap(part) for part in far_pairs]
+    query_home = send_home(grad_query_pieces)
     summed_pairs = [
         (grad_pairs[d].astype(f32) + far_pairs[d].astype(f32)).astype(bf16) for d in range(line)
     ]
     home = send_home(summed_pairs)
-    out.neighbour()
-    home = after(home, gate.second(), out.sent)
-    query_home = after(send_home(grad_query_pieces), gate.sent, up.sent)
+    grad_gate_x = after(grad_gate_x, summed_pairs)
+    gate = Spread(place, x, (hidden_low, hidden_x), (grad_gate, grad_gate_x), True)
+    gate.neighbour(down.arrived)
+    grad_up_x = x_swap(after(grad_up_far, gate.sent))
+    up = Spread(place, x, (hidden_low, hidden_x), (grad_up, grad_up_x), True)
+    up.neighbour(gate.arrived)
+    down.arrived = after(down.arrived, summed_pairs)
+    down.second()
+    home, query_home = after((home, query_home), gate.sent, down.passed)
     grad_queries = gather_heads(query_home).astype(f32)
     grad_keys = gather_heads([piece[0] for piece in home]).astype(f32)
     grad_values_low = gather_heads([piece[1] for piece in home])
@@ -1267,6 +1356,7 @@
     inner = token_sum(
         jnp.stack([jnp.sum(scaled_q * q_normed, axis=1), jnp.sum(scaled_k * k_normed, axis=1)])
     )
+    inner = after(inner, down.later)
     grad_q_raw = (q_factor * (scaled_q - q_normed * inner[0][:, None] / model_width)).astype(bf16)
     grad_k_raw = (k_factor * (scaled_k - k_normed * inner[1][:, None] / model_width)).astype(bf16)
     raw_parts = (grad_q_raw, grad_k_raw, grad_values_low)
@@ -1279,15 +1369,29 @@
             + dot_nt(grad_values_low, w_value)
         ).astype(bf16)
     )
-    grad_raw_x = after(grad_raw_x, up.second(), out.second())
+    grad_raw_x = after(grad_raw_x, gate.second(), up.sent)
     raw = Spread(place, x, (tokens_in, tokens_x), (grad_raw, grad_raw_x), True)
-    raw.neighbour()
+    raw.neighbour(up.arrived)
+    attended_far, grad_attn_far = after(
+        (half_of(attended_low, 1 - x), own_part(grad_attn)), up.sent
+    )
+    attended_x = x_swap(attended_far)
+    grad_attn_own = x_swap(grad_attn_far)
+    grad_attn_x = join_parts(grad_attn_own, core_swap(grad_attn_own))
+    grad_attn_x = after(grad_attn_x, raw.sent, gate.later)
+    out = Spread(place, x, (attended_low, attended_x), (grad_attn, grad_attn_x), False)
+    out.neighbour(up.arrived)
+    up.arrived = after(up.arrived, out.sent)
+    up.second()
+    raw.arrived = after(raw.arrived, up.passed)
     raw.second()
-    down_near, down_far = down.finish(raw.sent)
-    gate_near, gate_far = gate.finish(raw.sent)
-    up_near, up_far = up.finish(raw.sent)
-    out_near, out_far = out.finish(raw.sent)
-    raw_near, raw_far = raw.finish(raw.sent)
+    out.arrived = after(out.arrived, raw.passed, up.later)
+    out.second()
+    down_near, down_far = down.finish(up.passed)
+    gate_near, gate_far = gate.finish(raw.passed)
+    up_near, up_far = up.finish(raw.passed, out.passed)
+    out_near, out_far = out.finish(raw.passed, out.passed)
+    raw_near, raw_far = raw.finish(raw.passed, out.passed)
     own_grad_tokens = (grad_hidden + input_sum).astype(bf16)
     grad_tokens = restore(own_grad_tokens, core_swap(own_grad_tokens))
 
@@ -1295,8 +1399,9 @@
     wide = wide + core_swap(wide)
     gains = jnp.concatenate([wide, grad_gain_query, grad_gain_key])
     gains = gains + x_swap(gains)
-    for bit in (1, 2):
-        gains = gains + line_flip(gains, bit)
+    gains = after(gains, raw.sent)
+    for part in [line_shift(gains, d) for d in range(1, line)]:
+        gains = gains + after(part, raw.passed, out.passed)
     piece = head_width // (line * pair)
 
     def gain_piece(start, rows):

time: 622 us -> 580 us (0.932)
  waiting for transfers between devices: 239 us -> 155 us
  Pallas kernels: 217 us -> 269 us
  starting transfers between devices: 74.1 us -> 64.8 us
    ppermute x21 -> x9, waiting for transfers between devices: 69.2 us -> 11.6 us  [line_shift(): return lax.ppermute(value, 'dp', moves)]
    pallas_call x2, Pallas kernels: 108 us -> 154 us  [the longest x1 107 us: block(): pl.pallas_call(block_kernel, out_shape=[jax.ShapeDtypeStruct((rows, colum...]
    ppermute x12 -> x10, starting transfers between devices: 6.73 us -> 37.4 us  [line_flip(): lax.ppermute(value, 'dp', [(z * pair + x, (z ^ bit) * pair + x) for z in...]
    ppermute x21 -> x9, starting transfers between devices: 38.9 us -> 13 us  [line_shift(): return lax.ppermute(value, 'dp', moves)]
    ppermute x21 -> x15, waiting for transfers between devices: 60.5 us -> 43.7 us  [x_swap(): return lax.ppermute(value, 'dp', [(i, i ^ 1) for i in range(line * pair)])]
    ppermute x21 -> x15, starting transfers between devices: 23.4 us -> 13.1 us  [x_swap(): return lax.ppermute(value, 'dp', [(i, i ^ 1) for i in range(line * pair)])]
    ppermute x12 -> x10, waiting for transfers between devices: 106 us -> 98.1 us  [line_flip(): lax.ppermute(value, 'dp', [(z * pair + x, (z ^ bit) * pair + x) for z in...]
  transfers between devices with their start and end apart: 64 -> 41, of which waited for: 27 -> 16; matrix products, arithmetic and copies ran while one was open for 10% -> 10% of each run, Pallas kernels for 18% -> 17%
where the time goes in v3:
time: 580 us; the launch traced here: 573 us
  Pallas kernels  269 us (46%)
  waiting for transfers between devices  155 us (27%)
  starting transfers between devices  64.8 us (11%)
  local copies, waits for them, and re-layouts  40.2 us (7%)
  other arithmetic  37.9 us (7%)
    pallas_call x1, Pallas kernels, block(): pl.pallas_call(block_kernel, out_shape=[jax.ShapeDtypeStruct((rows, colum...  107 us
    ppermute x10, waiting for transfers between devices, line_flip(): lax.ppermute(value, 'dp', [(z * pair + x, (z ^ bit) * pair + x) for z in...  98.1 us
    pallas_call x15, Pallas kernels, weight_term(): pl.pallas_call(weight_kernel, grid_spec=pltpu.PrefetchScalarGridSpec(num_...  79.4 us
    pallas_call x1, Pallas kernels, project(): pl.pallas_call(project_kernel, in_specs=[pl.BlockSpec(memory_space=pl.ANY...  46.2 us
    ppermute x15, waiting for transfers between devices, x_swap(): return lax.ppermute(value, 'dp', [(i, i ^ 1) for i in range(line * pair)])  43.7 us
    ppermute x10, starting transfers between devices, line_flip(): lax.ppermute(value, 'dp', [(z * pair + x, (z ^ bit) * pair + x) for z in...  37.4 us
    unnamed x125, local copies, waits for them, and re-layouts  21.1 us
    pallas_call x1, Pallas kernels, attend(): pl.pallas_call(functools.partial(attend_kernel, factor, key_rows), out_sh...  18.6 us
  transfers between devices with their start and end apart: 41, of which 16 were waited for; matrix products, arithmetic and copies ran while one was open for 10% of the time, Pallas kernels for 17%

profile of v3, /device:TPU:0, one launch (start us, length us, event | category | flops | bytes accessed | tf_op | source)
XLA Modules:
  0.0 573.5 jit_solution(14255188398208680030)
XLA Ops:
  4.2 46.2 %shard_map.255 = (bf16[4,512,128]{2,1,0:T(8,128)(2,1)S(1)}, bf16[8,2,512,128]{3,2,1,0:T(8,128)(2,1)S(1)}, f32[8,4,512]{2,1,0:T(4,128)S(1)}, f32[512,512]{1,0:T(8,128)S(1)}, f32[512,512]{1,0:T(8,128)S(1)}) custom-call(bf16[512,2048]{1,0:T(8,128)(2,1)} %tokens.3, bf16[2048,512]{1,0:T(8,128)(2,1)} %wq.1, bf16[2048,512]{1,0:T(8,128)(2,1)} %wk.1, ...), custom_call_target="tpu_custom_call" | custom-call | tf_op jit(solution)/shard_map/pallas_call | solution.py:552
  51.2 18.6 %shard_map.256 = (f32[4,128,512]{2,1,0:T(8,128)S(1)}, f32[8,512]{1,0:T(8,128)S(1)}, bf16[4,512,128]{2,1,0:T(8,128)(2,1)S(1)}, bf16[8,512,128]{2,1,0:T(8,128)(2,1...) custom-call(s32[4,8]{1,0:T(4,128)S(1)} %and_convert_fusion.live, ...), custom_call_target="tpu_custom_call" | custom-call | tf_op jit(solution)/shard_map/pallas_call | solution.py:682
  75.2 107.5 %shard_map.257 = (bf16[512,512]{1,0:T(8,128)(2,1)}, bf16[512,2048]{1,0:T(8,128)(2,1)}, bf16[512,2048]{1,0:T(8,128)(2,1)}, bf16[512,2048]{1,0:T(8,128)(2,1)}, bf1...) custom-call(bf16[4,512,128]{2,1,0:T(8,128)(2,1)} %copy-done.2, ...), custom_call_target="tpu_custom_call" | custom-call | tf_op jit(solution)/shard_map/pallas_call | solution.py:1039
  182.6 1.7 collective-permute-start
  185.1 7.6 %shard_map.260 = bf16[1024,1024]{1,0:T(8,128)(2,1)} custom-call(s32[5]{0:T(128)} %stack.44.place, bf16[512,2048]{1,0:T(8,128)(2,1)} %get-tuple-element.124.refs_0_, bf16[512,2048]{1,0:T(8,128)(2,1)} %get-tuple-element.125.refs_1_, bf16[512,1024]{1,0:T(8,128)(2,1)} %get-tuple-element.126.refs_2_, bf16[512,2048]{1,0:T(8,128)(2,1)} %get-tuple-element.127.refs_3_), custom_call_target="tpu_custom_call" | custom-call | tf_op jit(solution)/shard_map/pallas_call | solution.py:1149
  196.3 17.4 %shard_map.258 = (bf16[512,128]{1,0:T(8,128)(2,1)S(1)}, bf16[512,128]{1,0:T(8,128)(2,1)S(1)}, bf16[512,128]{1,0:T(8,128)(2,1)S(1)}, bf16[512,128]{1,0:T(8,128)(2...) custom-call(s32[4,8]{1,0:T(4,128)S(1)} %and_convert_fusion.live, ...), custom_call_target="tpu_custom_call" | custom-call | flops 10737418240 | bytes 12582912 | tf_op jit(solution)/shard_map/pallas_call | solution.py:710
  213.8 2.0 collective-permute-start.4
  215.8 2.2 collective-permute-start.8
  218.4 4.6 collective-permute-done.2
  223.8 4.8 collective-permute-done.4
  228.6 2.3 collective-permute-start.3
  231.7 6.7 %collective-permute-done.6 = bf16[2,512,128]{2,1,0:T(8,128)(2,1)S(1)} collective-permute-done((bf16[2,512,128]{2,1,0:T(8,128)(2,1)S(1)}, bf16[2,512,128]{2,1,0:T(8,128)(2,1)S(1)}, u32[]{:S(2)}, u32[]{:S(2)}) %collective-permute-start.6) | collective-permute-done | bytes 262176 | tf_op jit(solution)/shard_map/ppermute | solution.py:346
  238.4 1.5 collective-permute-start.5
  240.7 9.2 %collective-permute-done.8 = bf16[512,128]{1,0:T(8,128)(2,1)S(1)} collective-permute-done((bf16[512,128]{1,0:T(8,128)(2,1)S(1)}, bf16[512,128]{1,0:T(8,128)(2,1)S(1)}, u32[]{:S(2)}, u32[]{:S(2)}) %collective-permute-start.8) | collective-permute-done | bytes 131104 | tf_op jit(solution)/shard_map/ppermute | solution.py:336
  250.0 4.5 collective-permute-start.10
  255.5 7.1 %shard_map.259 = bf16[1024,1024]{1,0:T(8,128)(2,1)} custom-call(s32[5]{0:T(128)} %stack.44.place, bf16[512,2048]{1,0:T(8,128)(2,1)} %get-tuple-element.120.refs_0_, bf16[512,2048]{1,0:T(8,128)(2,1)} %get-tuple-element.121.refs_1_, bf16[512,2048]{1,0:T(8,128)(2,1)} %get-tuple-element.122.refs_2_, bf16[512,1024]{1,0:T(8,128)(2,1)} %collective-permute-done.refs_3_), custom_call_target="tpu_custom_call" | custom-call | tf_op jit(solution)/shard_map/pallas_call | solution.py:1149
  262.6 5.0 shard_map.261
  267.6 2.4 collective-permute-done.9
  282.5 27.3 %collective-permute-start.19 = (bf16[1024,1024]{1,0:T(8,128)(2,1)}, bf16[1024,1024]{1,0:T(8,128)(2,1)}, u32[]{:S(2)}, u32[]{:S(2)}) collective-permute-start(bf16[1024,1024]{1,0:T(8,128)(2,1)} %shard_map.259), channel_id=1, source_target_pairs={{0,8},{4,12},{8,0},{12,4},{16,24},{20,28},{24,16},{28,20},{1,9},{5... | collective-permute-start | bytes 6291464 | tf_op jit(solution)/shard_map/ppermute | solution.py:340
  309.8 8.2 %collective-permute-done.14 = bf16[1024,512]{1,0:T(8,128)(2,1)S(1)} collective-permute-done((bf16[1024,512]{1,0:T(8,128)(2,1)}, bf16[1024,512]{1,0:T(8,128)(2,1)S(1)}, u32[]{:S(2)}, u32[]{:S(2)}) %collective-permute-start.14) | collective-permute-done | bytes 1048608 | tf_op jit(solution)/shard_map/ppermute | solution.py:340
  323.2 1.3 add_convert_fusion
  328.8 1.8 constant_dynamic-slice_fusion.6
  330.6 2.3 pad_maximum_fusion.8
  335.6 7.2 %shard_map.263 = bf16[1024,1024]{1,0:T(8,128)(2,1)} custom-call(s32[5]{0:T(128)} %stack.44.place, bf16[512,2048]{1,0:T(8,128)(2,1)} %get-tuple-element.120.refs_0_, bf16[512,2048]{1,0:T(8,128)(2,1)} %get-tuple-element.142.refs_1_, bf16[512,2048]{1,0:T(8,128)(2,1)} %get-tuple-element.122.refs_2_, bf16[512,1024]{1,0:T(8,128)(2,1)} %collective-permute-done.20.refs_3_), custom_call_target="tpu_custom_call" | custom-call | tf_op jit(solution)/shard_map/pallas_call | solution.py:1149
  343.3 19.7 %collective-permute-done.19.refs_4_ = bf16[1024,1024]{1,0:T(8,128)(2,1)} collective-permute-done((bf16[1024,1024]{1,0:T(8,128)(2,1)}, bf16[1024,1024]{1,0:T(8,128)(2,1)}, u32[]{:S(2)}, u32[]{:S(2)}) %collective-permute-start.19) | collective-permute-done | bytes 2097184 | tf_op jit(solution)/shard_map/ppermute | solution.py:340
  363.0 1.7 add_convert_fusion.2
  367.4 1.6 pad_maximum_fusion.refs_0_
  368.9 5.2 shard_map.273
  374.1 1.7 collective-permute-start.23
  376.8 2.3 fusion.16
  379.0 5.1 shard_map.262
  384.2 3.4 collective-permute-done.18.refs_3_
  387.6 3.9 collective-permute-start.26
  391.6 6.8 %shard_map.264 = bf16[1024,768]{1,0:T(8,128)(2,1)} custom-call(s32[5]{0:T(128)} %stack.44.place, bf16[512,2048]{1,0:T(8,128)(2,1)} %pad_maximum_fusion.refs_0_, bf16[512,768]{1,0:T(8,128)(2,1)} %pad_maximum_fusion.9.refs_1_, bf16[512,2048]{1,0:T(8,128)(2,1)} %get-tuple-element.140.refs_2_, bf16[512,768]{1,0:T(8,128)(2,1)} %copy-done.22), custom_call_target="tpu_custom_call" | custom-call | tf_op jit(solution)/shard_map/pallas_call | solution.py:1149
  400.3 2.8 constant_dynamic-update-slice_fusion.9
  403.1 30.2 %collective-permute-done.21.refs_4_ = bf16[1024,1024]{1,0:T(8,128)(2,1)S(1)} collective-permute-done((bf16[1024,1024]{1,0:T(8,128)(2,1)}, bf16[1024,1024]{1,0:T(8,128)(2,1)S(1)}, u32[]{:S(2)}, u32[]{:S(2)}) %collective-permute-start.21) | collective-permute-done | bytes 2097184 | tf_op jit(solution)/shard_map/ppermute | solution.py:340
  433.3 2.1 fusion.17
  435.4 1.6 pad_maximum_fusion.1.refs_3_
  437.7 3.7 shard_map.265
  441.4 5.1 shard_map.266
  447.9 1.7 collective-permute-start.37
  450.9 10.4 %collective-permute-done.37 = f32[5120]{0:T(1024)S(1)} collective-permute-done((f32[5120]{0:T(1024)S(1)}, f32[5120]{0:T(1024)S(1)}, u32[]{:S(2)}, u32[]{:S(2)}) %collective-permute-start.37) | collective-permute-done | bytes 20512 | tf_op jit(solution)/shard_map/ppermute | solution.py:346
  461.3 1.6 collective-permute-start.40
  462.8 5.0 shard_map.271
  467.9 5.2 shard_map.272
  474.0 1.3 constant_dynamic-update-slice_fusion.8
  477.3 10.5 %collective-permute-done.22.refs_4_ = bf16[1024,768]{1,0:T(8,128)(2,1)} collective-permute-done((bf16[1024,768]{1,0:T(8,128)(2,1)}, bf16[1024,768]{1,0:T(8,128)(2,1)}, u32[]{:S(2)}, u32[]{:S(2)}) %collective-permute-start.22) | collective-permute-done | bytes 1572896 | tf_op jit(solution)/shard_map/ppermute | solution.py:340
  487.9 1.5 pad_maximum_fusion.4
  489.3 4.7 shard_map.268
  494.0 10.1 %collective-permute-done.28.refs_4_ = bf16[256,1024]{1,0:T(8,128)(2,1)S(1)} collective-permute-done((bf16[256,1024]{1,0:T(8,128)(2,1)}, bf16[256,1024]{1,0:T(8,128)(2,1)S(1)}, u32[]{:S(2)}, u32[]{:S(2)}) %collective-permute-start.28) | collective-permute-done | bytes 524320 | tf_op jit(solution)/shard_map/ppermute | solution.py:340
  504.8 3.3 shard_map.269
  508.4 2.7 collective-permute-start.27
  513.4 3.5 shard_map.270
  518.7 19.3 %collective-permute-done.31 = bf16[256,512]{1,0:T(8,128)(2,1)S(1)} collective-permute-done((bf16[256,512]{1,0:T(8,128)(2,1)}, bf16[256,512]{1,0:T(8,128)(2,1)S(1)}, u32[]{:S(2)}, u32[]{:S(2)}) %collective-permute-start.31) | collective-permute-done | bytes 262176 | tf_op jit(solution)/shard_map/ppermute | solution.py:340
  540.0 4.8 shard_map.267
  544.8 1.4 collective-permute-start.34
  547.8 1.3 convert_select_fusion.5
  549.1 8.7 %collective-permute-done.34 = bf16[256,1024]{1,0:T(8,128)(2,1)S(1)} collective-permute-done((bf16[256,1024]{1,0:T(8,128)(2,1)S(1)}, bf16[256,1024]{1,0:T(8,128)(2,1)S(1)}, u32[]{:S(2)}, u32[]{:S(2)}) %collective-permute-start.34) | collective-permute-done | bytes 524320 | tf_op jit(solution)/shard_map/ppermute | solution.py:346
  557.8 1.3 convert_select_fusion.3
  559.4 1.8 collective-permute-start.30
  561.2 1.5 pad_maximum_fusion.2
  562.6 1.5 pad_maximum_fusion.3
  564.1 5.0 collective-permute-done.30
  571.9 1.3 copy.56
  (255 shorter events, 64.6 us)
Async XLA Ops:
  3.8 46.5 %copy-start.23 = (f32[512,64]{1,0:T(8,128)}, f32[512,64]{1,0:T(8,128)S(1)}, u32[]{:S(2)}) copy-start(f32[512,64]{1,0:T(8,128)S(1)} %get-tuple-element.258) | copy-start | bytes 393220
  182.6 31.1 %collective-permute-start = (bf16[512,1024]{1,0:T(8,128)(2,1)}, bf16[512,1024]{1,0:T(8,128)(2,1)}, u32[]{:S(2)}, u32[]{:S(2)}) collective-permute-start(bf16[512,1024]{1,0:T(8,128)(2,1)} %get-tuple-element.108), channel_id=1, source_target_pairs={{0,4},{4,0},{8,12},{12,8},{16,20},{20,16},{24,28},{28,24},{1,5},{5... | collective-permute-start | bytes 3145736 | tf_op jit(solution)/shard_map/ppermute | solution.py:346
  185.0 8.8 %copy-start.1 = (bf16[8,2,512,128]{3,2,1,0:T(8,128)(2,1)S(1)}, bf16[8,2,512,128]{3,2,1,0:T(8,128)(2,1)}, u32[]{:S(2)}) copy-start(bf16[8,2,512,128]{3,2,1,0:T(8,128)(2,1)} %copy-done) | copy-start | bytes 6291460
  185.1 8.8 %copy-start.6 = (s32[8,512,128]{2,1,0:T(8,128)S(1)}, s32[8,512,128]{2,1,0:T(8,128)}, u32[]{:S(2)}) copy-start(s32[8,512,128]{2,1,0:T(8,128)} %copy-done.5) | copy-start | bytes 6291460
  185.1 8.8 %copy-start.11 = (bf16[4,512,128]{2,1,0:T(8,128)(2,1)S(1)}, bf16[4,512,128]{2,1,0:T(8,128)(2,1)}, u32[]{:S(2)}) copy-start(bf16[4,512,128]{2,1,0:T(8,128)(2,1)} %get-tuple-element.102.refs_3_) | copy-start | bytes 1572868
  192.7 57.3 %collective-permute-start.11 = (bf16[1024,1024]{1,0:T(8,128)(2,1)}, bf16[1024,1024]{1,0:T(8,128)(2,1)}, u32[]{:S(2)}, u32[]{:S(2)}) collective-permute-start(bf16[1024,1024]{1,0:T(8,128)(2,1)} %shard_map.260), channel_id=1, source_target_pairs={{0,8},{4,12},{8,0},{12,4},{16,24},{20,28},{24,16},{28,20},{1,9},{5... | collective-permute-start | bytes 6291464 | tf_op jit(solution)/shard_map/ppermute | solution.py:340
  213.8 26.9 %copy-start.12 = (bf16[512,128]{1,0:T(8,128)(2,1)}, bf16[512,128]{1,0:T(8,128)(2,1)S(1)}, u32[]{:S(2)}) copy-start(bf16[512,128]{1,0:T(8,128)(2,1)S(1)} %get-tuple-element.118) | copy-start | bytes 393220
  213.8 9.2 %collective-permute-start.2 = (bf16[2,512,128]{2,1,0:T(8,128)(2,1)S(1)}, bf16[2,512,128]{2,1,0:T(8,128)(2,1)S(1)}, u32[]{:S(2)}, u32[]{:S(2)}) collective-permute-start(bf16[2,512,128]{2,1,0:T(8,128)(2,1)S(1)} %get-tuple-element.111), channel_id=1, source_target_pairs={{0,4},{4,0},{8,12},{12,8},{16,20},{20,16},{24,28},{28,24},{1,5},{5... | collective-permute-start | bytes 786440 | tf_op jit(solution)/shard_map/ppermute | solution.py:346
  213.8 14.8 %collective-permute-start.4 = (bf16[2,512,128]{2,1,0:T(8,128)(2,1)S(1)}, bf16[2,512,128]{2,1,0:T(8,128)(2,1)S(1)}, u32[]{:S(2)}, u32[]{:S(2)}) collective-permute-start(bf16[2,512,128]{2,1,0:T(8,128)(2,1)S(1)} %get-tuple-element.113), channel_id=1, source_target_pairs={{0,4},{4,0},{8,12},{12,8},{16,20},{20,16},{24,28},{28,24},{1,5},{5... | collective-permute-start | bytes 786440 | tf_op jit(solution)/shard_map/ppermute | solution.py:346
  215.8 34.1 %collective-permute-start.8 = (bf16[512,128]{1,0:T(8,128)(2,1)S(1)}, bf16[512,128]{1,0:T(8,128)(2,1)S(1)}, u32[]{:S(2)}, u32[]{:S(2)}) collective-permute-start(bf16[512,128]{1,0:T(8,128)(2,1)S(1)} %get-tuple-element.117), channel_id=1, source_target_pairs={{0,24},{4,28},{8,0},{12,4},{16,8},{20,12},{24,16},{28,20},{1,25},{... | collective-permute-start | bytes 393224 | tf_op jit(solution)/shard_map/ppermute | solution.py:336
  218.0 31.8 %collective-permute-start.1 = (bf16[2,512,128]{2,1,0:T(8,128)(2,1)}, bf16[2,512,128]{2,1,0:T(8,128)(2,1)}, u32[]{:S(2)}, u32[]{:S(2)}) collective-permute-start(bf16[2,512,128]{2,1,0:T(8,128)(2,1)} %get-tuple-element.109), channel_id=1, source_target_pairs={{0,4},{4,0},{8,12},{12,8},{16,20},{20,16},{24,28},{28,24},{1,5},{5... | collective-permute-start | bytes 786440 | tf_op jit(solution)/shard_map/ppermute | solution.py:346
  223.0 15.4 %collective-permute-start.6 = (bf16[2,512,128]{2,1,0:T(8,128)(2,1)S(1)}, bf16[2,512,128]{2,1,0:T(8,128)(2,1)S(1)}, u32[]{:S(2)}, u32[]{:S(2)}) collective-permute-start(bf16[2,512,128]{2,1,0:T(8,128)(2,1)S(1)} %get-tuple-element.115), channel_id=1, source_target_pairs={{0,4},{4,0},{8,12},{12,8},{16,20},{20,16},{24,28},{28,24},{1,5},{5... | collective-permute-start | bytes 786440 | tf_op jit(solution)/shard_map/ppermute | solution.py:346
  228.6 41.4 %collective-permute-start.3 = (bf16[2,512,128]{2,1,0:T(8,128)(2,1)}, bf16[2,512,128]{2,1,0:T(8,128)(2,1)S(1)}, u32[]{:S(2)}, u32[]{:S(2)}) collective-permute-start(bf16[2,512,128]{2,1,0:T(8,128)(2,1)} %add_convert_fusion.9), channel_id=1, source_target_pairs={{0,24},{4,28},{8,0},{12,4},{16,8},{20,12},{24,16},{28,20},{1,25},{... | collective-permute-start | bytes 786440 | tf_op jit(solution)/shard_map/ppermute | solution.py:336
  238.4 31.6 %collective-permute-start.5 = (bf16[2,512,128]{2,1,0:T(8,128)(2,1)}, bf16[2,512,128]{2,1,0:T(8,128)(2,1)}, u32[]{:S(2)}, u32[]{:S(2)}) collective-permute-start(bf16[2,512,128]{2,1,0:T(8,128)(2,1)} %add_convert_fusion.8), channel_id=1, source_target_pairs={{0,16},{4,20},{8,24},{12,28},{16,0},{20,4},{24,8},{28,12},{1,17},{... | collective-permute-start | bytes 786440 | tf_op jit(solution)/shard_map/ppermute | solution.py:336
  249.9 4.6 copy-start.49
  249.9 20.2 %collective-permute-start.7 = (bf16[2,512,128]{2,1,0:T(8,128)(2,1)}, bf16[2,512,128]{2,1,0:T(8,128)(2,1)}, u32[]{:S(2)}, u32[]{:S(2)}) collective-permute-start(bf16[2,512,128]{2,1,0:T(8,128)(2,1)} %add_convert_fusion.7), channel_id=1, source_target_pairs={{0,8},{4,12},{8,16},{12,20},{16,24},{20,28},{24,0},{28,4},{1,9},{5... | collective-permute-start | bytes 786440 | tf_op jit(solution)/shard_map/ppermute | solution.py:336
  249.9 20.1 %collective-permute-start.9 = (bf16[512,128]{1,0:T(8,128)(2,1)}, bf16[512,128]{1,0:T(8,128)(2,1)S(1)}, u32[]{:S(2)}, u32[]{:S(2)}) collective-permute-start(bf16[512,128]{1,0:T(8,128)(2,1)} %copy-done.12), channel_id=1, source_target_pairs={{0,16},{4,20},{8,24},{12,28},{16,0},{20,4},{24,8},{28,12},{1,17},{... | collective-permute-start | bytes 393224 | tf_op jit(solution)/shard_map/ppermute | solution.py:336
  250.0 20.0 %collective-permute-start.10 = (bf16[512,128]{1,0:T(8,128)(2,1)S(1)}, bf16[512,128]{1,0:T(8,128)(2,1)S(1)}, u32[]{:S(2)}, u32[]{:S(2)}) collective-permute-start(bf16[512,128]{1,0:T(8,128)(2,1)S(1)} %get-tuple-element.119), channel_id=1, source_target_pairs={{0,8},{4,12},{8,16},{12,20},{16,24},{20,28},{24,0},{28,4},{1,9},{5... | collective-permute-start | bytes 393224 | tf_op jit(solution)/shard_map/ppermute | solution.py:336
  262.6 7.4 %copy-start.50 = (bf16[512,128]{1,0:T(8,128)(2,1)S(1)}, bf16[512,128]{1,0:T(8,128)(2,1)}, u32[]{:S(2)}) copy-start(bf16[512,128]{1,0:T(8,128)(2,1)} %copy-done.49) | copy-start | bytes 393220
  270.0 48.1 %collective-permute-start.14 = (bf16[1024,512]{1,0:T(8,128)(2,1)}, bf16[1024,512]{1,0:T(8,128)(2,1)S(1)}, u32[]{:S(2)}, u32[]{:S(2)}) collective-permute-start(bf16[1024,512]{1,0:T(8,128)(2,1)} %shard_map.261), channel_id=1, source_target_pairs={{0,16},{4,20},{8,24},{12,28},{16,0},{20,4},{24,8},{28,12},{1,17},{... | collective-permute-start | bytes 3145736 | tf_op jit(solution)/shard_map/ppermute | solution.py:340
  274.7 48.2 %copy-start.41 = (bf16[512,1024]{1,0:T(8,128)(2,1)}, bf16[512,1024]{1,0:T(8,128)(2,1)S(1)}, u32[]{:S(2)}) copy-start(bf16[512,1024]{1,0:T(8,128)(2,1)S(1)} %get-tuple-element.236) | copy-start | bytes 3145732
  280.2 1.2 collective-permute-start.12
  281.5 28.3 %collective-permute-start.13 = (f32[2,512]{1,0:T(2,128)S(1)}, f32[2,512]{1,0:T(2,128)S(1)}, u32[]{:S(2)}, u32[]{:S(2)}) collective-permute-start(f32[2,512]{1,0:T(2,128)S(1)} %maximum_add_fusion), channel_id=1, source_target_pairs={{0,2},{1,3},{2,0},{3,1},{4,6},{5,7},{6,4},{7,5},{8,10},{9,11},{10,... | collective-permute-start | bytes 12296 | tf_op jit(solution)/shard_map/ppermute | solution.py:354
  282.1 86.9 %collective-permute-start.36 = (f32[4096]{0:T(1024)S(1)}, f32[4096]{0:T(1024)S(1)}, u32[]{:S(2)}, u32[]{:S(2)}) collective-permute-start(f32[4096]{0:T(1024)S(1)} %bitcast.67), channel_id=1, source_target_pairs={{0,1},{1,0},{2,3},{3,2},{4,5},{5,4},{6,7},{7,6},{8,9},{9,8},{10,11... | collective-permute-start | bytes 49160 | tf_op jit(solution)/shard_map/ppermute | solution.py:350
  282.1 53.6 %collective-permute-start.20 = (bf16[512,1024]{1,0:T(8,128)(2,1)}, bf16[512,1024]{1,0:T(8,128)(2,1)}, u32[]{:S(2)}, u32[]{:S(2)}) collective-permute-start(bf16[512,1024]{1,0:T(8,128)(2,1)} %get-tuple-element.144), channel_id=1, source_target_pairs={{0,4},{4,0},{8,12},{12,8},{16,20},{20,16},{24,28},{28,24},{1,5},{5... | collective-permute-start | bytes 3145736 | tf_op jit(solution)/shard_map/ppermute | solution.py:346
  282.5 80.5 %collective-permute-start.19 = (bf16[1024,1024]{1,0:T(8,128)(2,1)}, bf16[1024,1024]{1,0:T(8,128)(2,1)}, u32[]{:S(2)}, u32[]{:S(2)}) collective-permute-start(bf16[1024,1024]{1,0:T(8,128)(2,1)} %shard_map.259), channel_id=1, source_target_pairs={{0,8},{4,12},{8,0},{12,4},{16,24},{20,28},{24,16},{28,20},{1,9},{5... | collective-permute-start | bytes 6291464 | tf_op jit(solution)/shard_map/ppermute | solution.py:340
  326.8 36.2 %collective-permute-start.15 = (bf16[256,2048]{1,0:T(8,128)(2,1)}, bf16[256,2048]{1,0:T(8,128)(2,1)}, u32[]{:S(2)}, u32[]{:S(2)}) collective-permute-start(bf16[256,2048]{1,0:T(8,128)(2,1)} %pad_maximum_fusion.7), channel_id=1, source_target_pairs={{0,1},{1,0},{2,3},{3,2},{4,5},{5,4},{6,7},{7,6},{8,9},{9,8},{10,11... | collective-permute-start | bytes 3145736 | tf_op jit(solution)/shard_map/ppermute | solution.py:350
  335.6 27.4 %copy-start.34 = (bf16[128,2048]{1,0:T(8,128)(2,1)S(1)}, bf16[128,2048]{1,0:T(8,128)(2,1)}, u32[]{:S(2)}) copy-start(bf16[128,2048]{1,0:T(8,128)(2,1)} %get-tuple-element.190) | copy-start | bytes 1572868
  335.6 27.4 %copy-start.35 = (bf16[128,2048]{1,0:T(8,128)(2,1)S(1)}, bf16[128,2048]{1,0:T(8,128)(2,1)}, u32[]{:S(2)}) copy-start(bf16[128,2048]{1,0:T(8,128)(2,1)} %get-tuple-element.193) | copy-start | bytes 1572868
  342.9 33.9 %collective-permute-start.24 = (bf16[256,2048]{1,0:T(8,128)(2,1)}, bf16[256,2048]{1,0:T(8,128)(2,1)}, u32[]{:S(2)}, u32[]{:S(2)}) collective-permute-start(bf16[256,2048]{1,0:T(8,128)(2,1)} %pad_maximum_fusion.8), channel_id=1, source_target_pairs={{0,4},{4,0},{8,12},{12,8},{16,20},{20,16},{24,28},{28,24},{1,5},{5... | collective-permute-start | bytes 3145736 | tf_op jit(solution)/shard_map/ppermute | solution.py:346
  363.0 70.3 %collective-permute-start.21 = (bf16[1024,1024]{1,0:T(8,128)(2,1)}, bf16[1024,1024]{1,0:T(8,128)(2,1)S(1)}, u32[]{:S(2)}, u32[]{:S(2)}) collective-permute-start(bf16[1024,1024]{1,0:T(8,128)(2,1)} %shard_map.263), channel_id=1, source_target_pairs={{0,8},{4,12},{8,0},{12,4},{16,24},{20,28},{24,16},{28,20},{1,9},{5... | collective-permute-start | bytes 6291464 | tf_op jit(solution)/shard_map/ppermute | solution.py:340
  364.7 33.6 %collective-permute-start.16 = (bf16[256,2048]{1,0:T(8,128)(2,1)S(1)}, bf16[256,2048]{1,0:T(8,128)(2,1)S(1)}, u32[]{:S(2)}, u32[]{:S(2)}) collective-permute-start(bf16[256,2048]{1,0:T(8,128)(2,1)S(1)} %add_convert_fusion.2), channel_id=1, source_target_pairs={{0,2},{1,3},{2,0},{3,1},{4,6},{5,7},{6,4},{7,5},{8,10},{9,11},{10,... | collective-permute-start | bytes 3145736 | tf_op jit(solution)/shard_map/ppermute | solution.py:354
  367.0 20.6 %collective-permute-start.18 = (bf16[512,768]{1,0:T(8,128)(2,1)}, bf16[512,768]{1,0:T(8,128)(2,1)S(1)}, u32[]{:S(2)}, u32[]{:S(2)}) collective-permute-start(bf16[512,768]{1,0:T(8,128)(2,1)} %pad_maximum_fusion.10), channel_id=1, source_target_pairs={{0,4},{4,0},{8,12},{12,8},{16,20},{20,16},{24,28},{28,24},{1,5},{5... | collective-permute-start | bytes 2359304 | tf_op jit(solution)/shard_map/ppermute | solution.py:346
  368.9 5.2 copy-start.51
  368.9 6.9 %copy-start.47 = (bf16[512,256]{1,0:T(8,128)(2,1)S(1)}, bf16[512,256]{1,0:T(8,128)(2,1)}, u32[]{:S(2)}) copy-start(bf16[512,256]{1,0:T(8,128)(2,1)} %get-tuple-element.233) | copy-start | bytes 786436
  374.1 62.8 %collective-permute-start.23 = (bf16[512,256]{1,0:T(8,128)(2,1)S(1)}, bf16[512,256]{1,0:T(8,128)(2,1)S(1)}, u32[]{:S(2)}, u32[]{:S(2)}) collective-permute-start(bf16[512,256]{1,0:T(8,128)(2,1)S(1)} %copy-done.51), channel_id=1, source_target_pairs={{0,4},{4,0},{8,12},{12,8},{16,20},{20,16},{24,28},{28,24},{1,5},{5... | collective-permute-start | bytes 786440 | tf_op jit(solution)/shard_map/ppermute | solution.py:346
  376.8 56.5 %collective-permute-start.25 = (bf16[256,2048]{1,0:T(8,128)(2,1)}, bf16[256,2048]{1,0:T(8,128)(2,1)}, u32[]{:S(2)}, u32[]{:S(2)}) collective-permute-start(bf16[256,2048]{1,0:T(8,128)(2,1)} %collective-permute-done.24), channel_id=1, source_target_pairs={{0,1},{1,0},{2,3},{3,2},{4,5},{5,4},{6,7},{7,6},{8,9},{9,8},{10,11... | collective-permute-start | bytes 3145736 | tf_op jit(solution)/shard_map/ppermute | solution.py:350
  387.6 49.3 %collective-permute-start.26 = (bf16[512,1024]{1,0:T(8,128)(2,1)}, bf16[512,1024]{1,0:T(8,128)(2,1)}, u32[]{:S(2)}, u32[]{:S(2)}) collective-permute-start(bf16[512,1024]{1,0:T(8,128)(2,1)} %shard_map.262), channel_id=1, source_target_pairs={{0,16},{4,20},{8,24},{12,28},{16,0},{20,4},{24,8},{28,12},{1,17},{... | collective-permute-start | bytes 3145736 | tf_op jit(solution)/shard_map/ppermute | solution.py:340
  403.0 33.9 %copy-start.30 = (bf16[512,2048]{1,0:T(8,128)(2,1)}, bf16[512,2048]{1,0:T(8,128)(2,1)S(1)}, u32[]{:S(2)}) copy-start(bf16[512,2048]{1,0:T(8,128)(2,1)S(1)} %get-tuple-element.173) | copy-start | bytes 6291460
  403.0 32.3 %copy-start.36 = (bf16[128,2048]{1,0:T(8,128)(2,1)S(1)}, bf16[128,2048]{1,0:T(8,128)(2,1)}, u32[]{:S(2)}) copy-start(bf16[128,2048]{1,0:T(8,128)(2,1)} %get-tuple-element.206) | copy-start | bytes 1572868
  403.0 32.3 %copy-start.37 = (bf16[128,2048]{1,0:T(8,128)(2,1)S(1)}, bf16[128,2048]{1,0:T(8,128)(2,1)}, u32[]{:S(2)}) copy-start(bf16[128,2048]{1,0:T(8,128)(2,1)} %get-tuple-element.207) | copy-start | bytes 1572868
  403.1 70.1 %collective-permute-start.17 = (bf16[256,2048]{1,0:T(8,128)(2,1)}, bf16[256,2048]{1,0:T(8,128)(2,1)}, u32[]{:S(2)}, u32[]{:S(2)}) collective-permute-start(bf16[256,2048]{1,0:T(8,128)(2,1)} %get-tuple-element.174), channel_id=1, source_target_pairs={{0,1},{1,0},{2,3},{3,2},{4,5},{5,4},{6,7},{7,6},{8,9},{9,8},{10,11... | collective-permute-start | bytes 3145736 | tf_op jit(solution)/shard_map/ppermute | solution.py:350
  433.3 54.6 %collective-permute-start.22 = (bf16[1024,768]{1,0:T(8,128)(2,1)}, bf16[1024,768]{1,0:T(8,128)(2,1)}, u32[]{:S(2)}, u32[]{:S(2)}) collective-permute-start(bf16[1024,768]{1,0:T(8,128)(2,1)} %shard_map.264), channel_id=1, source_target_pairs={{0,8},{4,12},{8,0},{12,4},{16,24},{20,28},{24,16},{28,20},{1,9},{5... | collective-permute-start | bytes 4718600 | tf_op jit(solution)/shard_map/ppermute | solution.py:340
  441.4 5.2 copy-start.18
  441.4 5.2 copy-start.44
  447.6 27.8 %collective-permute-start.35 = (bf16[1024,256]{1,0:T(8,128)(2,1)}, bf16[1024,256]{1,0:T(8,128)(2,1)}, u32[]{:S(2)}, u32[]{:S(2)}) collective-permute-start(bf16[1024,256]{1,0:T(8,128)(2,1)} %add_convert_fusion.3), channel_id=1, source_target_pairs={{0,4},{4,0},{8,12},{12,8},{16,20},{20,16},{24,28},{28,24},{1,5},{5... | collective-permute-start | bytes 1572872 | tf_op jit(solution)/shard_map/ppermute | solution.py:346
  447.9 13.4 %collective-permute-start.37 = (f32[5120]{0:T(1024)S(1)}, f32[5120]{0:T(1024)S(1)}, u32[]{:S(2)}, u32[]{:S(2)}) collective-permute-start(f32[5120]{0:T(1024)S(1)} %pad_maximum_fusion.17), channel_id=1, source_target_pairs={{0,4},{4,0},{8,12},{12,8},{16,20},{20,16},{24,28},{28,24},{1,5},{5... | collective-permute-start | bytes 61448 | tf_op jit(solution)/shard_map/ppermute | solution.py:346
  449.6 54.4 %collective-permute-start.29 = (bf16[512,1024]{1,0:T(8,128)(2,1)}, bf16[512,1024]{1,0:T(8,128)(2,1)}, u32[]{:S(2)}, u32[]{:S(2)}) collective-permute-start(bf16[512,1024]{1,0:T(8,128)(2,1)} %shard_map.266), channel_id=1, source_target_pairs={{0,16},{4,20},{8,24},{12,28},{16,0},{20,4},{24,8},{28,12},{1,17},{... | collective-permute-start | bytes 3145736 | tf_op jit(solution)/shard_map/ppermute | solution.py:340
  461.3 46.8 %collective-permute-start.40 = (f32[5120]{0:T(1024)S(1)}, f32[5120]{0:T(1024)S(1)}, u32[]{:S(2)}, u32[]{:S(2)}) collective-permute-start(f32[5120]{0:T(1024)S(1)} %fusion.12), channel_id=1, source_target_pairs={{0,24},{4,28},{8,0},{12,4},{16,8},{20,12},{24,16},{28,20},{1,25},{... | collective-permute-start | bytes 61448 | tf_op jit(solution)/shard_map/ppermute | solution.py:336
  467.9 6.1 %copy-start.31 = (bf16[512,2048]{1,0:T(8,128)(2,1)S(1)}, bf16[512,2048]{1,0:T(8,128)(2,1)}, u32[]{:S(2)}) copy-start(bf16[512,2048]{1,0:T(8,128)(2,1)} %copy-done.30) | copy-start | bytes 6291460
  473.1 35.0 %collective-permute-start.39 = (f32[5120]{0:T(1024)S(1)}, f32[5120]{0:T(1024)S(1)}, u32[]{:S(2)}, u32[]{:S(2)}) collective-permute-start(f32[5120]{0:T(1024)S(1)} %fusion.12), channel_id=1, source_target_pairs={{0,16},{4,20},{8,24},{12,28},{16,0},{20,4},{24,8},{28,12},{1,17},{... | collective-permute-start | bytes 61448 | tf_op jit(solution)/shard_map/ppermute | solution.py:336
  475.4 28.7 %collective-permute-start.28 = (bf16[256,1024]{1,0:T(8,128)(2,1)}, bf16[256,1024]{1,0:T(8,128)(2,1)S(1)}, u32[]{:S(2)}, u32[]{:S(2)}) collective-permute-start(bf16[256,1024]{1,0:T(8,128)(2,1)} %shard_map.265), channel_id=1, source_target_pairs={{0,8},{4,12},{8,0},{12,4},{16,24},{20,28},{24,16},{28,20},{1,9},{5... | collective-permute-start | bytes 1572872 | tf_op jit(solution)/shard_map/ppermute | solution.py:340
  487.9 20.3 %collective-permute-start.38 = (f32[5120]{0:T(1024)S(1)}, f32[5120]{0:T(1024)S(1)}, u32[]{:S(2)}, u32[]{:S(2)}) collective-permute-start(f32[5120]{0:T(1024)S(1)} %fusion.12), channel_id=1, source_target_pairs={{0,8},{4,12},{8,16},{12,20},{16,24},{20,28},{24,0},{28,4},{1,9},{5... | collective-permute-start | bytes 61448 | tf_op jit(solution)/shard_map/ppermute | solution.py:336
  494.0 14.4 %copy-start.48 = (bf16[512,768]{1,0:T(8,128)(2,1)S(1)}, bf16[512,768]{1,0:T(8,128)(2,1)}, u32[]{:S(2)}) copy-start(bf16[512,768]{1,0:T(8,128)(2,1)} %shard_map.268) | copy-start | bytes 2359300
  494.0 17.2 %copy-start.20 = (f32[512,1024]{1,0:T(8,128)S(1)}, f32[512,1024]{1,0:T(8,128)}, u32[]{:S(2)}) copy-start(f32[512,1024]{1,0:T(8,128)} %shard_map.271) | copy-start | bytes 6291460
  508.2 29.9 %collective-permute-start.31 = (bf16[256,512]{1,0:T(8,128)(2,1)}, bf16[256,512]{1,0:T(8,128)(2,1)S(1)}, u32[]{:S(2)}, u32[]{:S(2)}) collective-permute-start(bf16[256,512]{1,0:T(8,128)(2,1)} %shard_map.269), channel_id=1, source_target_pairs={{0,16},{4,20},{8,24},{12,28},{16,0},{20,4},{24,8},{28,12},{1,17},{... | collective-permute-start | bytes 786440 | tf_op jit(solution)/shard_map/ppermute | solution.py:340
  508.4 50.7 %collective-permute-start.27 = (bf16[512,768]{1,0:T(8,128)(2,1)S(1)}, bf16[512,768]{1,0:T(8,128)(2,1)S(1)}, u32[]{:S(2)}, u32[]{:S(2)}) collective-permute-start(bf16[512,768]{1,0:T(8,128)(2,1)S(1)} %copy-done.48), channel_id=1, source_target_pairs={{0,16},{4,20},{8,24},{12,28},{16,0},{20,4},{24,8},{28,12},{1,17},{... | collective-permute-start | bytes 2359304 | tf_op jit(solution)/shard_map/ppermute | solution.py:340
  513.0 4.5 copy-start.19
  513.0 34.8 %collective-permute-start.33 = (bf16[256,1024]{1,0:T(8,128)(2,1)S(1)}, bf16[256,1024]{1,0:T(8,128)(2,1)S(1)}, u32[]{:S(2)}, u32[]{:S(2)}) collective-permute-start(bf16[256,1024]{1,0:T(8,128)(2,1)S(1)} %add_convert_fusion.5), channel_id=1, source_target_pairs={{0,4},{4,0},{8,12},{12,8},{16,20},{20,16},{24,28},{28,24},{1,5},{5... | collective-permute-start | bytes 1572872 | tf_op jit(solution)/shard_map/ppermute | solution.py:346
  516.8 21.2 %copy-start.29 = (f32[256,512]{1,0:T(8,128)S(1)}, f32[256,512]{1,0:T(8,128)}, u32[]{:S(2)}) copy-start(f32[256,512]{1,0:T(8,128)} %shard_map.270) | copy-start | bytes 1572868
  538.7 8.1 %collective-permute-start.32 = (bf16[256,256]{1,0:T(8,128)(2,1)}, bf16[256,256]{1,0:T(8,128)(2,1)S(1)}, u32[]{:S(2)}, u32[]{:S(2)}) collective-permute-start(bf16[256,256]{1,0:T(8,128)(2,1)} %add_convert_fusion.11), channel_id=1, source_target_pairs={{0,4},{4,0},{8,12},{12,8},{16,20},{20,16},{24,28},{28,24},{1,5},{5... | collective-permute-start | bytes 393224 | tf_op jit(solution)/shard_map/ppermute | solution.py:346
  544.8 13.0 %collective-permute-start.34 = (bf16[256,1024]{1,0:T(8,128)(2,1)S(1)}, bf16[256,1024]{1,0:T(8,128)(2,1)S(1)}, u32[]{:S(2)}, u32[]{:S(2)}) collective-permute-start(bf16[256,1024]{1,0:T(8,128)(2,1)S(1)} %add_convert_fusion.4), channel_id=1, source_target_pairs={{0,4},{4,0},{8,12},{12,8},{16,20},{20,16},{24,28},{28,24},{1,5},{5... | collective-permute-start | bytes 1572872 | tf_op jit(solution)/shard_map/ppermute | solution.py:346
  549.1 10.1 %copy-start.25 = (f32[512,768]{1,0:T(8,128)S(1)}, f32[512,768]{1,0:T(8,128)}, u32[]{:S(2)}) copy-start(f32[512,768]{1,0:T(8,128)} %shard_map.267) | copy-start | bytes 4718596
  559.4 9.7 %collective-permute-start.30 = (bf16[256,768]{1,0:T(8,128)(2,1)S(1)}, bf16[256,768]{1,0:T(8,128)(2,1)S(1)}, u32[]{:S(2)}, u32[]{:S(2)}) collective-permute-start(bf16[256,768]{1,0:T(8,128)(2,1)S(1)} %get-tuple-element.183), channel_id=1, source_target_pairs={{0,4},{4,0},{8,12},{12,8},{16,20},{20,16},{24,28},{28,24},{1,5},{5... | collective-permute-start | bytes 1179656 | tf_op jit(solution)/shard_map/ppermute | solution.py:346
  (30 other events, 60.1 us)

commit v4 on v3

--- a/solution.py
+++ b/solution.py
@@ -636,9 +636,7 @@
 
 def attend_back_kernel(factor, scale, live, codes, rows, queries, keys, *refs):
     pairs, turned, log_total, grads = refs[:4]
-    out_query = refs[4 : line + 4]
-    out_pairs = refs[line + 4 : 3 * line + 4]
-    key_sum, value_sum, query_sum = refs[3 * line + 4 :]
+    out_query, out_near, out_far, key_sum, value_sum, query_sum = refs[4:]
     f32 = jnp.float32
     bf16 = jnp.bfloat16
     key_sum[...] = jnp.zeros_like(key_sum)
@@ -668,10 +666,11 @@
                 key_sum[k] += jnp.dot(grad_scores, query, preferred_element_type=f32)
                 query_sum[...] += dot_t(key, grad_scores)
 
-        out_query[q][...] = (query_sum[...] * scale).T.astype(bf16)
-    for k in range(2 * line):
-        out_pairs[k][0] = (key_sum[k] * scale).astype(bf16)
-        out_pairs[k][1] = value_sum[k].astype(bf16)
+        out_query[q] = (query_sum[...] * scale).T.astype(bf16)
+    for k in range(line):
+        for out, base in ((out_near, 0), (out_far, line)):
+            out[k, 0] = (key_sum[base + k] * scale).astype(bf16)
+            out[k, 1] = value_sum[base + k].astype(bf16)
 
 
 def attend(key_rows, live, notes, queries, pairs):
@@ -709,10 +708,10 @@
     f32 = jnp.float32
     return pl.pallas_call(
         functools.partial(attend_back_kernel, factor, scale),
-        out_shape=[jax.ShapeDtypeStruct((count, width), jnp.bfloat16)] * line
-        + [jax.ShapeDtypeStruct((2, count, width), jnp.bfloat16)] * (2 * line),
+        out_shape=[jax.ShapeDtypeStruct((line, count, width), jnp.bfloat16)]
+        + [jax.ShapeDtypeStruct((line, 2, count, width), jnp.bfloat16)] * 2,
         in_specs=[pl.BlockSpec(memory_space=pltpu.SMEM)] + vmem_specs(8),
-        out_specs=vmem_specs(3 * line),
+        out_specs=vmem_specs(3),
         scratch_shapes=[
             pltpu.VMEM((2 * line, count, width), f32),
             pltpu.VMEM((2 * line, count, width), f32),
@@ -738,14 +737,13 @@
     w_up_in,
     w_down_in,
     out_heads,
-    out_tokens_x,
     out_output,
     out_hidden,
-    out_hidden_x,
+    out_hidden_z,
     out_act,
-    out_act_x,
+    out_act_z,
     out_mlp,
-    out_mlp_x,
+    out_mlp_z,
     out_gate,
     out_gate_far,
     out_up,
@@ -790,11 +788,11 @@
     mp = lax.axis_index("mp")
     spot = lax.axis_index("dp")
     core = lax.rem(mp, 2)
-    x = lax.rem(spot, 2)
     core_peer = {"mp": mp + 1 - 2 * core}
     y_peer = {"mp": lax.rem(mp + 2, 4)}
-    x_peer = {"dp": spot + 1 - 2 * x}
     z = spot // 2
+    z_low = lax.rem(z, 2)
+    z_peer = {"dp": spot + 2 - 4 * z_low}
     width = pieces.shape[2]
     ahead = [{"dp": lax.rem(spot + 2 * d, 2 * line)} for d in range(line)]
     head = lambda d: pl.ds(pl.multiple_of(lax.rem(z + d, line) * width, width), width)
@@ -840,7 +838,7 @@
         keep_out(w_down_in, w_down, True),
     ]
     barrier = pltpu.get_barrier_semaphore()
-    peers = (core_peer, y_peer, x_peer, ahead[1], ahead[2], ahead[3])
+    peers = (core_peer, y_peer, ahead[1], ahead[2], ahead[3])
     for peer in peers:
         pl.semaphore_signal(barrier, inc=1, device_id=peer, device_id_type=pl.DeviceIdType.MESH)
     pl.semaphore_wait(barrier, len(peers))
@@ -850,9 +848,6 @@
                 pieces.at[d, both(s)], attended.at[both(s), head(0)], ahead[line - d]
             )
     attended[:, head(0)] = pieces[0]
-    loads[0].wait()
-    for s in range(2):
-        flying["tokens", s] = send(own_tokens.at[mine(s)], out_tokens_x.at[own(s)], x_peer)
 
     def forward_core(name, s, array):
         flying[name, s].wait()
@@ -894,7 +889,7 @@
         share(hidden_keep, s)
 
     def forward(s):
-        flying["hidden", s] = send(hidden_keep.at[own(s)], out_hidden_x.at[own(s)], x_peer)
+        flying["hidden", s] = send(hidden_keep.at[own(s)], out_hidden_z.at[own(s)], z_peer)
         flying["share", s].wait()
         keep_out(hidden_keep.at[both(s)], out_hidden.at[both(s)])
 
@@ -917,14 +912,13 @@
         reduce_start(1, s)
         keep_out(act_keep.at[both(s)], out_act.at[both(s)])
         half = units // 2
-        far = pl.ds(pl.multiple_of((1 - x) * half, half), half)
-        flying["act", s] = send(act_keep.at[both(s), far], out_act_x.at[both(s)], x_peer)
+        far = pl.ds(pl.multiple_of((1 - z_low) * half, half), half)
+        flying["act", s] = send(act_keep.at[both(s), far], out_act_z.at[both(s)], z_peer)
 
     def turn_point(s):
         value = reduced(1, s)
         factor = factor_of(value)
         normed = value * factor
-        forward_core("tokens", s, out_tokens_x)
         own_tokens[mine(s), :] = (out_grad_hidden[mine(s), :] + normed * g_mlp[...]).astype(bf16)
         keep_out(own_tokens.at[mine(s)], out_output.at[at_home(s)])
         flying["output", s] = send(own_tokens.at[mine(s)], out_output.at[at_home(s)], core_peer)
@@ -935,7 +929,7 @@
         share(mlp_keep, s)
 
     def backward(s):
-        flying["mlp", s] = send(mlp_keep.at[own(s)], out_mlp_x.at[own(s)], x_peer)
+        flying["mlp", s] = send(mlp_keep.at[own(s)], out_mlp_z.at[own(s)], z_peer)
         flying["share", s].wait()
         keep_out(mlp_keep.at[both(s)], out_mlp.at[both(s)])
 
@@ -961,7 +955,7 @@
 
         reduce_start(2, s)
         half = units // 2
-        far = pl.ds(pl.multiple_of((1 - x) * half, half), half)
+        far = pl.ds(pl.multiple_of((1 - z_low) * half, half), half)
         flying["grads"] = [
             keep_out(source, target.at[both(s)], waited=s == 0)
             for source, target in (
@@ -995,7 +989,7 @@
 
     project_out(0)
     project_out(1)
-    for load in loads[1:]:
+    for load in loads:
         load.wait()
     after_attention(0)
     forward(0)
@@ -1006,7 +1000,7 @@
     turn_point(1)
     backward(1)
     for s in range(2):
-        forward_core("hidden", s, out_hidden_x)
+        forward_core("hidden", s, out_hidden_z)
     to_attention(0)
     attended_grad(0)
     to_attention(1)
@@ -1014,9 +1008,8 @@
     for s in range(2):
         flying["act", s].wait()
         flying["output", s].wait()
-        forward_core("mlp", s, out_mlp_x)
+        forward_core("mlp", s, out_mlp_z)
     for s in range(2):
-        flying["tokens_core", s].wait()
         flying["hidden_core", s].wait()
         flying["mlp_core", s].wait()
         for d in range(1, line):
@@ -1043,7 +1036,6 @@
             wide,
             wide,
             wide,
-            wide,
             tall,
             jax.ShapeDtypeStruct((rows, units // 2), bf16),
             wide,
@@ -1058,7 +1050,7 @@
             jax.ShapeDtypeStruct((2, depth), f32),
         ],
         in_specs=vmem_specs(4) + [any_spec] * 5,
-        out_specs=[any_spec] * 15 + vmem_specs(2),
+        out_specs=[any_spec] * 14 + vmem_specs(2),
         scratch_shapes=[
             pltpu.VMEM((depth, units), bf16),
             pltpu.VMEM((depth, units), bf16),
@@ -1082,8 +1074,8 @@
             pltpu.VMEM((2, quarter, depth), bf16),
             pltpu.VMEM((2, quarter, depth), bf16),
             pltpu.VMEM((3, 2, quarter, depth), bf16),
-            pltpu.SemaphoreType.DMA((52,)),
-            pltpu.SemaphoreType.DMA((52,)),
+            pltpu.SemaphoreType.DMA((48,)),
+            pltpu.SemaphoreType.DMA((48,)),
             pltpu.SemaphoreType.DMA((32,)),
         ],
         compiler_params=pltpu.CompilerParams(
@@ -1093,104 +1085,717 @@
     )(pieces, w_out, g_attn, g_mlp, tokens, cotangent, w_gate, w_up, w_down)
 
 
-def weight_kernel(place, *refs):
-    first, second, first_x, second_x = refs[:4]
-    total = dot_t(first[...], second[...]) + dot_t(first_x[...], second_x[...])
-    if len(refs) == 6:
-        total = total + refs[4][...].astype(jnp.float32)
-    refs[-1][...] = total.astype(refs[-1].dtype)
-
-
-def line_block(which):
-    if which < 2:
-        return lambda p: 2 * which + 1 - p[2]
-    if which == 2:
-        return lambda p: 2 * (1 - p[3]) + p[2]
-    return lambda p: 2 * p[3] + p[2]
-
-
-def weight_term(place, first, second, cut_first, blocks, extra, kind):
-    tokens = first[0].shape[0]
-    cut_side, half_side = (first, second) if cut_first else (second, first)
-    cut_tile = cut_side[0].shape[1] // line
-    half_size = half_side[1].shape[1]
-    half_tile = min(half_size, 512)
-    while half_size % half_tile:
-        half_tile -= 128
-    half_count = half_size // half_tile
-    own_half = half_count if half_side[0].shape[1] != half_size else 0
-    count = len(blocks)
-
-    def cut_map(i, j, p):
-        index = line_block(blocks[0])(p)
-        if count == 2:
-            index = index + i * (line_block(blocks[1])(p) - line_block(blocks[0])(p))
-        return (0, index)
-
-    cut_spec = pl.BlockSpec((tokens, cut_tile), cut_map)
-    half_own = pl.BlockSpec((tokens, half_tile), lambda i, j, p: (0, j + p[4] * own_half))
-    half_far = pl.BlockSpec((tokens, half_tile), lambda i, j, p: (0, j))
-    if cut_first:
-        in_specs = [cut_spec, half_own, cut_spec, half_far]
-        tile_shape = (cut_tile, half_tile)
-        out_map = lambda i, j, p: (i, j)
-        shape = (count * cut_tile, half_size)
-        extra_map = lambda i, j, p: (extra[1](p) + i, j)
-    else:
-        in_specs = [half_own, cut_spec, half_far, cut_spec]
-        tile_shape = (half_tile, cut_tile)
-        out_map = lambda i, j, p: (j, i)
-        shape = (half_size, count * cut_tile)
-        extra_map = lambda i, j, p: (j, extra[1](p) + i)
-    args = [first[0], second[0], first[1], second[1]]
-    if extra is not None:
-        in_specs.append(pl.BlockSpec(tile_shape, extra_map))
-        args.append(extra[0])
+class Courier:
+    def __init__(self, send_sems, recv_sems, local_sems):
+        self.send_sems, self.recv_sems, self.local_sems = send_sems, recv_sems, local_sems
+        self.remote, self.local = 0, 0
+
+    def send(self, source, target, peer):
+        copy = pltpu.make_async_remote_copy(
+            src_ref=source,
+            dst_ref=target,
+            send_sem=self.send_sems.at[self.remote],
+            recv_sem=self.recv_sems.at[self.remote],
+            device_id=peer,
+            device_id_type=pl.DeviceIdType.MESH,
+        )
+        self.remote += 1
+        copy.start()
+        return copy
+
+    def move(self, source, target):
+        copy = pltpu.make_async_copy(source, target, self.local_sems.at[self.local])
+        self.local += 1
+        copy.start()
+        return copy
+
+
+def greet(peers):
+    barrier = pltpu.get_barrier_semaphore()
+    for peer in peers:
+        pl.semaphore_signal(barrier, inc=1, device_id=peer, device_id_type=pl.DeviceIdType.MESH)
+    pl.semaphore_wait(barrier, len(peers))
+
+
+class Spot:
+    def __init__(self):
+        mp = lax.axis_index("mp")
+        spot = lax.axis_index("dp")
+        self.core = lax.rem(mp, 2)
+        self.x = lax.rem(spot, 2)
+        self.z = spot // 2
+        self.z_low = lax.rem(self.z, 2)
+        self.z_high = self.z // 2
+        self.core_peer = {"mp": mp + 1 - 2 * self.core}
+        self.y_peer = {"mp": lax.rem(mp + 2, 4)}
+        self.x_peer = {"dp": spot + 1 - 2 * self.x}
+        self.z_peer = {"dp": spot + 2 - 4 * self.z_low}
+        self.far_peer = {"dp": lax.rem(spot + 4, 8)}
+        self.ahead = [{"dp": lax.rem(spot + 2 * d, 2 * line)} for d in range(line)]
+        self.all = (self.core_peer, self.y_peer, self.x_peer) + tuple(self.ahead[1:])
+
+
+class Job:
+    def __init__(self, first, first_z, second, second_z, cut_first):
+        self.operands, self.cut_first = (first, first_z, second, second_z), cut_first
+        self.tile = (first if cut_first else second).shape[1] // (line * pair)
+
+    def at(self, ref, index):
+        block = pl.ds(pl.multiple_of(index * self.tile, self.tile), self.tile)
+        return ref.at[block, :] if self.cut_first else ref.at[:, block]
+
+    def span(self, ref, index):
+        block = pl.ds(pl.multiple_of(index * 2 * self.tile, 2 * self.tile), 2 * self.tile)
+        return ref.at[block, :] if self.cut_first else ref.at[:, block]
+
+    def term(self, index):
+        first, first_z, second, second_z = self.operands
+        block = pl.ds(pl.multiple_of(index * self.tile, self.tile), self.tile)
+        if self.cut_first:
+            return dot_t(first[:, block], second[...]) + dot_t(first_z[:, block], second_z[...])
+        return dot_t(first[...], second[:, block]) + dot_t(first_z[...], second_z[:, block])
+
+    def send_terms(self, spot, target):
+        @pl.loop(0, line)
+        def _(i):
+            self.at(target, i)[...] = self.term(i * pair + 1 - spot.x).astype(jnp.bfloat16)
+
+    def second_terms(self, spot, arrived, target):
+        @pl.loop(0, 2)
+        def _(i):
+            total = self.term((2 * (1 - spot.z_high) + i) * pair + spot.x)
+            total = total + self.at(arrived, i)[...].astype(jnp.float32)
+            self.at(target, i)[...] = total.astype(jnp.bfloat16)
+
+    def own_term(self, spot, side, arrived):
+        total = self.term((2 * spot.z_high + side) * pair + spot.x)
+        return total + self.at(arrived, side)[...].astype(jnp.float32)
+
+
+def middle_kernel(
+    grad_queries,
+    near,
+    far,
+    q_raw,
+    k_raw,
+    factors,
+    cosines,
+    sines,
+    gq,
+    gk,
+    act,
+    act_z,
+    mlp,
+    mlp_z,
+    hidden,
+    hidden_z,
+    gate,
+    gate_far,
+    up_far,
+    out_own_down,
+    out_r2_down,
+    out_r1_gate,
+    out_gate_z,
+    out_up_z,
+    out_raw_z,
+    r1_down,
+    out_raw,
+    out_raw_own,
+    out_gain,
+    act_v,
+    act_zv,
+    mlp_v,
+    mlp_zv,
+    hidden_v,
+    hidden_zv,
+    gate_v,
+    gate_zv,
+    send_down,
+    send_gate,
+    r1_v,
+    r1_own,
+    s2_v,
+    own_v,
+    far_in,
+    sums,
+    query_home,
+    pair_home,
+    scaled,
+    raw_far,
+    inner,
+    inner_core,
+    inner_y,
+    send_sems,
+    recv_sems,
+    local_sems,
+):
+    f32 = jnp.float32
+    bf16 = jnp.bfloat16
+    spot = Spot()
+    mail = Courier(send_sems, recv_sems, local_sems)
+    count, width = cosines.shape
+    columns = line * width
+    depth = mlp_v.shape[1]
+    half = act_v.shape[1]
+    own_half = pl.ds(pl.multiple_of(spot.z_low * half, half), half)
+    loads = [
+        mail.move(act.at[:, own_half], act_v),
+        mail.move(act_z, act_zv),
+        mail.move(mlp, mlp_v),
+        mail.move(mlp_z, mlp_zv),
+        mail.move(hidden, hidden_v),
+        mail.move(hidden_z, hidden_zv),
+        mail.move(gate.at[:, own_half], gate_v),
+    ]
+    greet(spot.all)
+    far_copy = mail.send(far, far_in, spot.x_peer)
+    my_head = pl.ds(pl.multiple_of(spot.z * width, width), width)
+    query_copies = [
+        mail.send(grad_queries.at[d], query_home.at[:, my_head], spot.ahead[line - d])
+        for d in range(1, line)
+    ]
+    gate_copy = mail.send(gate_far, gate_zv, spot.z_peer)
+    query_home[:, my_head] = grad_queries[0]
+    for load in loads:
+        load.wait()
+    down = Job(act_v, act_zv, mlp_v, mlp_zv, False)
+    down.send_terms(spot, send_down)
+    down_copy = mail.send(send_down, r1_down, spot.x_peer)
+
+    far_copy.wait()
+    sums[...] = (near[...].astype(f32) + far_in[...].astype(f32)).astype(bf16)
+    pair_copies = [
+        mail.send(sums.at[d], pair_home.at[:, :, my_head], spot.ahead[line - d])
+        for d in range(1, line)
+    ]
+    pair_home[:, :, my_head] = sums[0]
+    gate_copy.wait()
+    up_copy = mail.send(up_far, out_up_z, spot.z_peer)
+    keep_gate = mail.move(gate_zv, out_gate_z)
+    gates = Job(hidden_v, hidden_zv, gate_v, gate_zv, True)
+    gates.send_terms(spot, send_gate)
+    gate_terms = mail.send(send_gate, out_r1_gate, spot.x_peer)
+
+    for copy in query_copies + pair_copies:
+        copy.wait()
+
+    def column(row):
+        return jnp.broadcast_to(row, (width, count)).T
+
+    sources = ((query_home, None, q_raw, gq), (pair_home, 0, k_raw, gk))
+    factor_columns = [column(factors[which : which + 1, :]) for which in range(2)]
+    for which, (home, slot, raw, gain) in enumerate(sources):
+        inner_sum = jnp.zeros((count, width), f32)
+        for h in range(line):
+            cut = slice(h * width, (h + 1) * width)
+            part = (home[:, cut] if slot is None else home[slot, :, cut]).astype(f32)
+            back = part * cosines[...] - pltpu.roll(part, width // 2, 1) * sines[...]
+            normed = raw[:, cut] * factor_columns[which]
+            out_gain[which : which + 1, cut] = jnp.sum(back * normed, axis=0, keepdims=True)
+            value = back * gain[:, cut]
+            scaled[which, :, cut] = value
+            inner_sum = inner_sum + value * normed
+        inner[which : which + 1, :] = jnp.sum(inner_sum.T, axis=0, keepdims=True)
+    core_copy = mail.send(inner, inner_core, spot.core_peer)
+    core_copy.wait()
+    arrived = inner_core[...]
+    quarter = count // 4
+    cuts = [arrived[:, i * quarter : (i + 1) * quarter] for i in (1, 0, 3, 2)]
+    chip = inner[...] + jnp.concatenate(cuts, axis=1)
+    inner[...] = chip
+    y_copy = mail.send(inner, inner_y, spot.y_peer)
+    y_copy.wait()
+    inner_all = (chip + inner_y[...]) / depth
+    for which, (home, slot, raw, gain) in enumerate(sources):
+        inner_column = column(inner_all[which : which + 1, :])
+        for h in range(line):
+            cut = slice(h * width, (h + 1) * width)
+            normed = raw[:, cut] * factor_columns[which]
+            value = factor_columns[which] * (scaled[which, :, cut] - normed * inner_column)
+            base = which * columns + h * width
+            out_raw[:, base : base + width] = value.astype(bf16)
+    out_raw[:, 2 * columns :] = pair_home[1]
+    part_width = columns // 2
+    for which in range(3):
+        cut = slice(which * part_width, (which + 1) * part_width)
+        base = which * columns
+
+        def side(index):
+            start = pl.multiple_of(base + index * part_width, part_width)
+            return out_raw[:, pl.ds(start, part_width)]
+
+        out_raw_own[:, cut] = side(spot.z_low)
+        raw_far[:, cut] = side(1 - spot.z_low)
+    raw_copy = mail.send(raw_far, out_raw_z, spot.z_peer)
+
+    down_copy.wait()
+    loads = [
+        mail.move(down.span(r1_down, 1 - spot.z_high), r1_v),
+        mail.move(down.span(r1_down, spot.z_high), r1_own),
+    ]
+    loads[0].wait()
+    down.second_terms(spot, r1_v, s2_v)
+    second_copy = mail.send(s2_v, out_r2_down, spot.far_peer)
+    loads[1].wait()
+
+    @pl.loop(0, 2)
+    def _(i):
+        down.at(own_v, i)[...] = down.own_term(spot, i, r1_own)
+
+    keep_own = mail.move(own_v, out_own_down)
+    for copy in (up_copy, gate_terms, raw_copy, second_copy, keep_gate, keep_own):
+        copy.wait()
+
+
+def middle(small, large):
+    f32 = jnp.float32
+    bf16 = jnp.bfloat16
+    grad_queries, near, far, q_raw = small[:4]
+    act, act_z, grad_mlp = large[:3]
+    _, count, width = grad_queries.shape
+    columns = line * width
+    depth = grad_mlp.shape[1]
+    units = act.shape[1]
+    half = units // 2
+    cut = depth // 2
+    any_spec = pl.BlockSpec(memory_space=pl.ANY)
+    shape = jax.ShapeDtypeStruct
     return pl.pallas_call(
-        weight_kernel,
-        grid_spec=pltpu.PrefetchScalarGridSpec(
-            num_scalar_prefetch=1,
-            grid=(count, half_count),
-            in_specs=in_specs,
-            out_specs=pl.BlockSpec(tile_shape, out_map),
+        middle_kernel,
+        in_specs=vmem_specs(10) + [any_spec] * 9,
+        out_specs=[any_spec] * 7 + vmem_specs(3),
+        out_shape=[
+            shape((half, cut // 2), f32),
+            shape((half, cut // 2), bf16),
+            shape((cut, half), bf16),
+            shape((count, half), bf16),
+            shape((count, half), bf16),
+            shape((count, 3 * columns // 2), bf16),
+            shape((half, cut), bf16),
+            shape((count, 3 * columns), bf16),
+            shape((count, 3 * columns // 2), bf16),
+            shape((2, columns), f32),
+        ],
+        scratch_shapes=[
+            pltpu.VMEM((count, half), bf16),
+            pltpu.VMEM((count, half), bf16),
+            pltpu.VMEM((count, depth), bf16),
+            pltpu.VMEM((count, depth), bf16),
+            pltpu.VMEM((count, depth), bf16),
+            pltpu.VMEM((count, depth), bf16),
+            pltpu.VMEM((count, half), bf16),
+            pltpu.VMEM((count, half), bf16),
+            pltpu.VMEM((half, cut), bf16),
+            pltpu.VMEM((cut, half), bf16),
+            pltpu.VMEM((half, cut // 2), bf16),
+            pltpu.VMEM((half, cut // 2), bf16),
+            pltpu.VMEM((half, cut // 2), bf16),
+            pltpu.VMEM((half, cut // 2), f32),
+            pltpu.VMEM(near.shape, bf16),
+            pltpu.VMEM(near.shape, bf16),
+            pltpu.VMEM((count, columns), bf16),
+            pltpu.VMEM((2, count, columns), bf16),
+            pltpu.VMEM((2, count, columns), f32),
+            pltpu.VMEM((count, 3 * columns // 2), bf16),
+            pltpu.VMEM((2, count), f32),
+            pltpu.VMEM((2, count), f32),
+            pltpu.VMEM((2, count), f32),
+            pltpu.SemaphoreType.DMA((16,)),
+            pltpu.SemaphoreType.DMA((16,)),
+            pltpu.SemaphoreType.DMA((16,)),
+        ],
+        compiler_params=pltpu.CompilerParams(
+            vmem_limit_bytes=big_vmem, collective_id=3, has_side_effects=True
         ),
-        out_shape=jax.ShapeDtypeStruct(shape, kind),
-        compiler_params=pltpu.CompilerParams(vmem_limit_bytes=big_vmem),
-        cost_estimate=pl.CostEstimate(flops=0, bytes_accessed=0, transcendentals=0),
-    )(place, *args)
-
-
-def after(value, *needed):
-    return lax.optimization_barrier((value, needed))[0]
-
-
-class Spread:
-    def __init__(self, place, x, first, second, cut_first):
-        self.place, self.x, self.operands, self.cut_first = place, x, (first, second), cut_first
-        self.sent = self.make((0, 1), None, jnp.bfloat16)
-
-    def make(self, blocks, extra, kind):
-        first, second = self.operands
-        return weight_term(self.place, first, second, self.cut_first, blocks, extra, kind)
-
-    def neighbour(self, *needed):
-        self.arrived = line_flip(after(self.sent, *needed) if needed else self.sent, 1)
-
-    def second(self):
-        self.passed = self.make((2,), (self.arrived, lambda p: 1 - p[3]), jnp.bfloat16)
-        self.later = line_flip(self.passed, 2)
-        return self.passed
-
-    def finish(self, *needed):
-        own = self.make((3,), (self.arrived, lambda p: p[3]), jnp.float32)
-        later = after(self.later, *needed)
-        axis = 0 if self.cut_first else 1
-        width = own.shape[axis] // pair
-        far = lambda value: lax.dynamic_slice_in_dim(value, (1 - self.x) * width, width, axis)
-        near = lambda value: lax.dynamic_slice_in_dim(value, self.x * width, width, axis)
-        to_x = (far(own) + far(later).astype(jnp.float32)).astype(jnp.bfloat16)
-        own_half = near(own) + near(later).astype(jnp.float32)
-        return own_half, x_swap(to_x).astype(jnp.float32)
+    )(*small, *large)
+
+
+def last_kernel(
+    raw,
+    raw_own,
+    raw_z,
+    wide,
+    narrow,
+    attended,
+    hidden,
+    hidden_z,
+    gate,
+    gate_z,
+    up,
+    up_z,
+    attn,
+    tokens,
+    own_down,
+    r2_down,
+    r1_gate,
+    w_query,
+    w_key,
+    w_value,
+    grad_hidden,
+    *refs,
+):
+    outs, refs = refs[:14], refs[14:]
+    near_down, near_gate, near_up, near_raw, near_out = outs[:5]
+    far_down, far_gate, far_up, far_raw, far_out = outs[5:10]
+    out_tokens, r1_up, r1_raw, r1_out = outs[10:]
+    out_wide, out_narrow = refs[:2]
+    (
+        hidden_v,
+        hidden_zv,
+        gate_v,
+        gate_zv,
+        up_v,
+        up_zv,
+        tokens_v,
+        tokens_zv,
+        attn_v,
+        attn_zv,
+        heads_v,
+        heads_far,
+        heads_zv,
+        send_up,
+        send_raw,
+        send_out,
+        r1_wide,
+        r1_raw_v,
+        r1_out_v,
+        s2_gate,
+        s2_up,
+        s2_raw,
+        s2_out,
+        r2_gate,
+        r2_up,
+        r2_raw,
+        r2_out,
+        own_down_v,
+        r2_down_v,
+        fin_down,
+        fin_gate,
+        fin_up,
+        fin_raw,
+        fin_out,
+        keep_down,
+        keep_gate,
+        keep_up,
+        keep_raw,
+        keep_out,
+        weight_v,
+        total,
+        part_send,
+        part_recv,
+        y_send,
+        y_recv,
+        hidden_own,
+        token_keep,
+        wide_core,
+        wide_x,
+        narrow_x,
+        wide_z,
+        narrow_z,
+        send_sems,
+        recv_sems,
+        local_sems,
+    ) = refs[2:]
+    f32 = jnp.float32
+    bf16 = jnp.bfloat16
+    spot = Spot()
+    mail = Courier(send_sems, recv_sems, local_sems)
+    rows_all = tokens_v.shape[0]
+    rows = rows_all // 2
+    count = rows // 2
+    half = gate_v.shape[1]
+    own_half = pl.ds(pl.multiple_of(spot.z_low * half, half), half)
+    heads_half = heads_v.shape[1]
+    side_heads = lambda side: pl.ds(pl.multiple_of(side * heads_half, heads_half), heads_half)
+    own = lambda s: pl.ds(s * rows, count)
+    other = lambda s: pl.ds(s * rows + count, count)
+    both = lambda s: pl.ds(s * rows, rows)
+    mine = lambda s: pl.ds(s * count, count)
+
+    first_loads = [
+        mail.move(hidden, hidden_v),
+        mail.move(hidden_z, hidden_zv),
+        mail.move(up.at[:, own_half], up_v),
+        mail.move(up_z, up_zv),
+    ]
+    token_loads, attn_loads = [], []
+    for s in range(2):
+        for part, place in ((0, spot.core), (1, 1 - spot.core)):
+            start = pl.multiple_of(place * rows + s * count, count)
+            target = tokens_v.at[pl.ds(s * rows + part * count, count)]
+            token_loads.append(mail.move(tokens.at[pl.ds(start, count)], target))
+    attn_load = mail.move(attn, attn_v)
+    later_loads = [
+        mail.move(gate.at[:, own_half], gate_v),
+        mail.move(gate_z, gate_zv),
+    ]
+    greet(spot.all)
+    wide_copy = mail.send(wide, wide_core, spot.core_peer)
+    for load in first_loads:
+        load.wait()
+    ups = Job(hidden_v, hidden_zv, up_v, up_zv, True)
+    gates = Job(hidden_v, hidden_zv, gate_v, gate_zv, True)
+    raws = Job(tokens_v, tokens_zv, raw_own, raw_z, True)
+    outs_job = Job(heads_v, heads_zv, attn_v, attn_zv, False)
+    for load in token_loads:
+        load.wait()
+    token_copies = [
+        mail.send(tokens_v.at[own(s)], tokens_zv.at[own(s)], spot.z_peer) for s in range(2)
+    ]
+    heads_far[...] = attended[:, side_heads(1 - spot.z_low)]
+    heads_v[...] = attended[:, side_heads(spot.z_low)]
+    heads_copy = mail.send(heads_far, heads_zv, spot.z_peer)
+    ups.send_terms(spot, send_up)
+    wide_copy.wait()
+    out_wide[...] = wide[...] + wide_core[...]
+    out_narrow[...] = narrow[...]
+    wide_x_copy = mail.send(out_wide, wide_x, spot.x_peer)
+    narrow_x_copy = mail.send(out_narrow, narrow_x, spot.x_peer)
+    up_copy = mail.send(send_up, r1_up, spot.x_peer)
+
+    r1_load = mail.move(gates.span(r1_gate, 1 - spot.z_high), r1_wide.at[0])
+    r1_gate_own = mail.move(gates.span(r1_gate, spot.z_high), r1_wide.at[1])
+    for load in later_loads:
+        load.wait()
+    r1_load.wait()
+    gates.second_terms(spot, r1_wide.at[0], s2_gate)
+    gate_copy = mail.send(s2_gate, r2_gate, spot.far_peer)
+    attn_load.wait()
+    attn_copies = [
+        mail.send(attn_v.at[own(s)], attn_zv.at[own(s)], spot.z_peer) for s in range(2)
+    ]
+
+    input_weights = (w_query, w_key, w_value)
+    columns = w_query.shape[1]
+    flying = {}
+    for which, source in enumerate(input_weights):
+        load = mail.move(source, weight_v)
+        load.wait()
+        for s in range(2):
+            term = dot_nt(raw[both(s), which * columns : (which + 1) * columns], weight_v[...])
+            total[both(s), :] = term if which == 0 else total[both(s), :] + term
+    for s in range(2):
+        part_send[s] = total[other(s), :].astype(bf16)
+        flying["core", s] = mail.send(part_send.at[s], part_recv.at[s], spot.core_peer)
+    hidden_load = mail.move(grad_hidden, hidden_own)
+    for s in range(2):
+        flying["core", s].wait()
+        y_send[s] = (total[own(s), :] + part_recv[s].astype(f32)).astype(bf16)
+        flying["y", s] = mail.send(y_send.at[s], y_recv.at[s], spot.y_peer)
+
+    near_copies, far_copies = [], []
+
+    def finish(job, value_of, fin, far, keep, target):
+        fin[...] = value_of(1 - spot.z_low).astype(bf16)
+        far_copies.append(mail.send(fin, far, spot.z_peer))
+        keep[...] = value_of(spot.z_low)
+        near_copies.append(mail.move(keep, target))
+
+    down_loads = [mail.move(own_down, own_down_v), mail.move(r2_down, r2_down_v)]
+    for load in down_loads:
+        load.wait()
+    down = Job(heads_v, heads_zv, attn_v, attn_zv, False)
+    finish(
+        down,
+        lambda side: down.at(own_down_v, side)[...] + down.at(r2_down_v, side)[...].astype(f32),
+        fin_down,
+        far_down,
+        keep_down,
+        near_down,
+    )
+
+    for s in range(2):
+        token_copies[s].wait()
+    token_core = [
+        mail.send(tokens_zv.at[own(s)], tokens_zv.at[other(s)], spot.core_peer) for s in range(2)
+    ]
+    for copy in token_core:
+        copy.wait()
+    raws.send_terms(spot, send_raw)
+    wide_x_copy.wait()
+    narrow_x_copy.wait()
+    out_wide[...] = out_wide[...] + wide_x[...]
+    out_narrow[...] = out_narrow[...] + narrow_x[...]
+    raw_copy = mail.send(send_raw, r1_raw, spot.x_peer)
+    for s in range(2):
+        attn_copies[s].wait()
+    attn_core = [
+        mail.send(attn_zv.at[own(s)], attn_zv.at[other(s)], spot.core_peer) for s in range(2)
+    ]
+    for copy in attn_core:
+        copy.wait()
+    heads_copy.wait()
+    outs_job.send_terms(spot, send_out)
+    out_copy = mail.send(send_out, r1_out, spot.x_peer)
+
+    hidden_load.wait()
+    for s in range(2):
+        flying["y", s].wait()
+        value = y_send[s].astype(f32) + y_recv[s].astype(f32)
+        token_keep[mine(s), :] = (hidden_own[mine(s), :] + value).astype(bf16)
+        home = pl.ds(pl.multiple_of(spot.core * rows + s * count, count), count)
+        flying["keep", s] = mail.move(token_keep.at[mine(s)], out_tokens.at[home])
+        flying["tokens", s] = mail.send(
+            token_keep.at[mine(s)], out_tokens.at[home], spot.core_peer
+        )
+    gain_copies = []
+    for d in range(1, line):
+        gain_copies.append(mail.send(out_wide, wide_z.at[d - 1], spot.ahead[d]))
+        gain_copies.append(mail.send(out_narrow, narrow_z.at[d - 1], spot.ahead[d]))
+
+    up_copy.wait()
+    r1_up_second = mail.move(ups.span(r1_up, 1 - spot.z_high), r1_wide.at[2])
+    r1_up_own = mail.move(ups.span(r1_up, spot.z_high), r1_wide.at[3])
+    r1_up_second.wait()
+    ups.second_terms(spot, r1_wide.at[2], s2_up)
+    second_up = mail.send(s2_up, r2_up, spot.far_peer)
+
+    def final_of(job, r1_own, r2):
+        return lambda side: job.own_term(spot, side, r1_own) + job.at(r2, side)[...].astype(f32)
+
+    r1_gate_own.wait()
+    gate_copy.wait()
+    finish(gates, final_of(gates, r1_wide.at[1], r2_gate), fin_gate, far_gate, keep_gate, near_gate)
+
+    raw_copy.wait()
+    raw_loads = [
+        mail.move(raws.span(r1_raw, 1 - spot.z_high), r1_raw_v.at[0]),
+        mail.move(raws.span(r1_raw, spot.z_high), r1_raw_v.at[1]),
+    ]
+    for load in raw_loads:
+        load.wait()
+    raws.second_terms(spot, r1_raw_v.at[0], s2_raw)
+    second_raw = mail.send(s2_raw, r2_raw, spot.far_peer)
+    out_copy.wait()
+    out_loads = [
+        mail.move(outs_job.span(r1_out, 1 - spot.z_high), r1_out_v.at[0]),
+        mail.move(outs_job.span(r1_out, spot.z_high), r1_out_v.at[1]),
+    ]
+    for load in out_loads:
+        load.wait()
+    outs_job.second_terms(spot, r1_out_v.at[0], s2_out)
+    second_out = mail.send(s2_out, r2_out, spot.far_peer)
+    r1_up_own.wait()
+    second_up.wait()
+    finish(ups, final_of(ups, r1_wide.at[3], r2_up), fin_up, far_up, keep_up, near_up)
+    second_raw.wait()
+    finish(raws, final_of(raws, r1_raw_v.at[1], r2_raw), fin_raw, far_raw, keep_raw, near_raw)
+    second_out.wait()
+    finish(
+        outs_job, final_of(outs_job, r1_out_v.at[1], r2_out), fin_out, far_out, keep_out, near_out
+    )
+    for copy in gain_copies:
+        copy.wait()
+    for d in range(1, line):
+        out_wide[...] = out_wide[...] + wide_z[d - 1]
+        out_narrow[...] = out_narrow[...] + narrow_z[d - 1]
+    for s in range(2):
+        flying["keep", s].wait()
+        flying["tokens", s].wait()
+    for copy in near_copies + far_copies:
+        copy.wait()
+
+
+def last(small, large):
+    f32 = jnp.float32
+    bf16 = jnp.bfloat16
+    raw, raw_own, raw_z, wide, narrow, attended = small
+    hidden, gate = large[0], large[2]
+    count, depth = hidden.shape
+    units = gate.shape[1]
+    half = units // 2
+    block = depth // (line * pair)
+    columns = attended.shape[1]
+    heads_half = columns // 2
+    raw_half = raw_own.shape[1]
+    rows = count // 2
+    any_spec = pl.BlockSpec(memory_space=pl.ANY)
+    shape = jax.ShapeDtypeStruct
+    vmem = lambda *size: pltpu.VMEM(size, bf16)
+    wide_vmem = lambda *size: pltpu.VMEM(size, f32)
+    return pl.pallas_call(
+        last_kernel,
+        in_specs=vmem_specs(6) + [any_spec] * len(large),
+        out_specs=[any_spec] * 14 + vmem_specs(2),
+        out_shape=[
+            shape((half, block), f32),
+            shape((block, half), f32),
+            shape((block, half), f32),
+            shape((block, raw_half), f32),
+            shape((heads_half, block), f32),
+            shape((half, block), bf16),
+            shape((block, half), bf16),
+            shape((block, half), bf16),
+            shape((block, raw_half), bf16),
+            shape((heads_half, block), bf16),
+            shape((count, depth), bf16),
+            shape((line * block, half), bf16),
+            shape((line * block, raw_half), bf16),
+            shape((heads_half, line * block), bf16),
+            shape(wide.shape, f32),
+            shape(narrow.shape, f32),
+        ],
+        scratch_shapes=[
+            vmem(count, depth),
+            vmem(count, depth),
+            vmem(count, half),
+            vmem(count, half),
+            vmem(count, half),
+            vmem(count, half),
+            vmem(count, depth),
+            vmem(count, depth),
+            vmem(count, depth),
+            vmem(count, depth),
+            vmem(count, heads_half),
+            vmem(count, heads_half),
+            vmem(count, heads_half),
+            vmem(line * block, half),
+            vmem(line * block, raw_half),
+            vmem(heads_half, line * block),
+            vmem(4, 2 * block, half),
+            vmem(2, 2 * block, raw_half),
+            vmem(2, heads_half, 2 * block),
+            vmem(2 * block, half),
+            vmem(2 * block, half),
+            vmem(2 * block, raw_half),
+            vmem(heads_half, 2 * block),
+            vmem(2 * block, half),
+            vmem(2 * block, half),
+            vmem(2 * block, raw_half),
+            vmem(heads_half, 2 * block),
+            wide_vmem(half, 2 * block),
+            vmem(half, 2 * block),
+            vmem(half, block),
+            vmem(block, half),
+            vmem(block, half),
+            vmem(block, raw_half),
+            vmem(heads_half, block),
+            wide_vmem(half, block),
+            wide_vmem(block, half),
+            wide_vmem(block, half),
+            wide_vmem(block, raw_half),
+            wide_vmem(heads_half, block),
+            vmem(depth, columns),
+            wide_vmem(count, depth),
+            vmem(2, rows // 2, depth),
+            vmem(2, rows // 2, depth),
+            vmem(2, rows // 2, depth),
+            vmem(2, rows // 2, depth),
+            wide_vmem(rows, depth),
+            vmem(rows, depth),
+            wide_vmem(*wide.shape),
+            wide_vmem(*wide.shape),
+            wide_vmem(*narrow.shape),
+            wide_vmem(line - 1, *wide.shape),
+            wide_vmem(line - 1, *narrow.shape),
+            pltpu.SemaphoreType.DMA((48,)),
+            pltpu.SemaphoreType.DMA((48,)),
+            pltpu.SemaphoreType.DMA((40,)),
+        ],
+        compiler_params=pltpu.CompilerParams(
+            vmem_limit_bytes=61800 << 10, collective_id=4, has_side_effects=True
+        ),
+    )(*small, *large)
 
 
 def on_device_lines(
@@ -1240,13 +1845,13 @@
         whole = lax.dynamic_update_slice_in_dim(whole, own, core * half_rows, 0)
         return lax.dynamic_update_slice_in_dim(whole, other, (1 - core) * half_rows, 0)
 
-    def half_of(value, x_place):
-        width = value.shape[1] // pair
-        return lax.dynamic_slice_in_dim(value, x_place * width, width, 1)
+    def half_of(value, side):
+        width = value.shape[1] // 2
+        return lax.dynamic_slice_in_dim(value, side * width, width, 1)
 
     def join_halves(near, far, axis):
-        low = jnp.where(x == 0, near, far)
-        return jnp.concatenate([low, jnp.where(x == 0, far, near)], axis=axis)
+        low = jnp.where(z_low == 0, near, far)
+        return jnp.concatenate([low, jnp.where(z_low == 0, far, near)], axis=axis)
 
     positions = reorder(offsets[0] + jnp.arange(row_count, dtype=jnp.int32))
     labels = reorder(row_ids[0] * key_rows + doc_ids)
@@ -1287,14 +1892,13 @@
     g_mlp = gain_mlp.reshape(1, model_width)
     (
         attended_low,
-        tokens_x,
         output,
         hidden_low,
-        hidden_x,
+        hidden_z,
         act_low,
-        act_x,
+        act_z,
         grad_mlp,
-        grad_mlp_x,
+        grad_mlp_z,
         grad_gate,
         grad_gate_far,
         grad_up,
@@ -1306,102 +1910,59 @@
     ) = block(
         attended_out, w_output, g_attn, g_mlp, tokens, cotangent, w_gate, w_up, w_down
     )
-    down = Spread(place, x, (act_low, act_x), (grad_mlp, grad_mlp_x), False)
-    down.neighbour()
-    grad_gate_x = x_swap(grad_gate_far)
     back = attend_back(
         live, code_columns, code_rows, queries_n, keys_n, pairs, turned, log_total, grads
     )
-    grad_query_pieces, grad_pairs = back[:line], back[line:]
-    far_pairs = after(grad_pairs[line:], grad_gate_x)
-    far_pairs = [x_swap(part) for part in far_pairs]
-    query_home = send_home(grad_query_pieces)
-    summed_pairs = [
-        (grad_pairs[d].astype(f32) + far_pairs[d].astype(f32)).astype(bf16) for d in range(line)
-    ]
-    home = send_home(summed_pairs)
-    grad_gate_x = after(grad_gate_x, summed_pairs)
-    gate = Spread(place, x, (hidden_low, hidden_x), (grad_gate, grad_gate_x), True)
-    gate.neighbour(down.arrived)
-    grad_up_x = x_swap(after(grad_up_far, gate.sent))
-    up = Spread(place, x, (hidden_low, hidden_x), (grad_up, grad_up_x), True)
-    up.neighbour(gate.arrived)
-    down.arrived = after(down.arrived, summed_pairs)
-    down.second()
-    home, query_home = after((home, query_home), gate.sent, down.passed)
-    grad_queries = gather_heads(query_home).astype(f32)
-    grad_keys = gather_heads([piece[0] for piece in home]).astype(f32)
-    grad_values_low = gather_heads([piece[1] for piece in home])
-
-    def turn_back(value):
-        parts = []
-        for h in range(heads_here):
-            part = value[:, h * head_width : (h + 1) * head_width]
-            swapped = jnp.concatenate(
-                [part[:, head_width // 2 :], part[:, : head_width // 2]], axis=1
-            )
-            parts.append(part * cosines - swapped * sines)
-        return jnp.concatenate(parts, axis=1)
-
-    q_factor = factors[0][:, None]
-    k_factor = factors[1][:, None]
-    q_normed = q_raw * q_factor
-    k_normed = k_raw * k_factor
-    back_q = turn_back(grad_queries)
-    back_k = turn_back(grad_keys)
-    grad_gain_query = jnp.sum(back_q * q_normed, axis=0)
-    grad_gain_key = jnp.sum(back_k * k_normed, axis=0)
-    scaled_q = back_q * g_query
-    scaled_k = back_k * g_key
-    inner = token_sum(
-        jnp.stack([jnp.sum(scaled_q * q_normed, axis=1), jnp.sum(scaled_k * k_normed, axis=1)])
-    )
-    inner = after(inner, down.later)
-    grad_q_raw = (q_factor * (scaled_q - q_normed * inner[0][:, None] / model_width)).astype(bf16)
-    grad_k_raw = (k_factor * (scaled_k - k_normed * inner[1][:, None] / model_width)).astype(bf16)
-    raw_parts = (grad_q_raw, grad_k_raw, grad_values_low)
-    grad_raw = jnp.concatenate([half_of(part, x) for part in raw_parts], axis=1)
-    grad_raw_x = x_swap(jnp.concatenate([half_of(part, 1 - x) for part in raw_parts], axis=1))
-    input_sum = reduce_own_rows(
+    (
+        own_down,
+        r2_down,
+        r1_gate,
+        grad_gate_z,
+        grad_up_z,
+        raw_z,
+        _,
+        raw,
+        raw_own,
+        narrow_gains,
+    ) = middle(
+        (*back, q_raw, k_raw, factors, cosines, sines, g_query, g_key),
         (
-            dot_nt(grad_q_raw, w_query)
-            + dot_nt(grad_k_raw, w_key)
-            + dot_nt(grad_values_low, w_value)
-        ).astype(bf16)
-    )
-    grad_raw_x = after(grad_raw_x, gate.second(), up.sent)
-    raw = Spread(place, x, (tokens_in, tokens_x), (grad_raw, grad_raw_x), True)
-    raw.neighbour(up.arrived)
-    attended_far, grad_attn_far = after(
-        (half_of(attended_low, 1 - x), own_part(grad_attn)), up.sent
-    )
-    attended_x = x_swap(attended_far)
-    grad_attn_own = x_swap(grad_attn_far)
-    grad_attn_x = join_parts(grad_attn_own, core_swap(grad_attn_own))
-    grad_attn_x = after(grad_attn_x, raw.sent, gate.later)
-    out = Spread(place, x, (attended_low, attended_x), (grad_attn, grad_attn_x), False)
-    out.neighbour(up.arrived)
-    up.arrived = after(up.arrived, out.sent)
-    up.second()
-    raw.arrived = after(raw.arrived, up.passed)
-    raw.second()
-    out.arrived = after(out.arrived, raw.passed, up.later)
-    out.second()
-    down_near, down_far = down.finish(up.passed)
-    gate_near, gate_far = gate.finish(raw.passed)
-    up_near, up_far = up.finish(raw.passed, out.passed)
-    out_near, out_far = out.finish(raw.passed, out.passed)
-    raw_near, raw_far = raw.finish(raw.passed, out.passed)
-    own_grad_tokens = (grad_hidden + input_sum).astype(bf16)
-    grad_tokens = restore(own_grad_tokens, core_swap(own_grad_tokens))
-
-    wide = wide_gains.reshape(2 * model_width)
-    wide = wide + core_swap(wide)
-    gains = jnp.concatenate([wide, grad_gain_query, grad_gain_key])
-    gains = gains + x_swap(gains)
-    gains = after(gains, raw.sent)
-    for part in [line_shift(gains, d) for d in range(1, line)]:
-        gains = gains + after(part, raw.passed, out.passed)
+            act_low,
+            act_z,
+            grad_mlp,
+            grad_mlp_z,
+            hidden_low,
+            hidden_z,
+            grad_gate,
+            grad_gate_far,
+            grad_up_far,
+        ),
+    )
+    results = last(
+        (raw, raw_own, raw_z, wide_gains, narrow_gains, attended_low),
+        (
+            hidden_low,
+            hidden_z,
+            grad_gate,
+            grad_gate_z,
+            grad_up,
+            grad_up_z,
+            grad_attn,
+            tokens,
+            own_down,
+            r2_down,
+            r1_gate,
+            w_query,
+            w_key,
+            w_value,
+            grad_hidden,
+        ),
+    )
+    down_near, gate_near, up_near, raw_near, out_near = results[:5]
+    down_far, gate_far, up_far, raw_far, out_far = [part.astype(f32) for part in results[5:10]]
+    grad_tokens = results[10]
+    wide, narrow = results[14:]
+    gains = jnp.concatenate([wide.reshape(2 * model_width), narrow.reshape(2 * local_width)])
     piece = head_width // (line * pair)
 
     def gain_piece(start, rows):

time: 580 us -> 569 us (0.981)
  Pallas kernels: 269 us -> 521 us
  waiting for transfers between devices: 155 us -> 0 us
  starting transfers between devices: 64.8 us -> 0 us
  other arithmetic: 37.9 us -> 13 us
  local copies, waits for them, and re-layouts: 40.2 us -> 22.1 us
    pallas_call x15 -> x2, Pallas kernels: 79.4 us -> 331 us  [the longest x1 206 us: last(): pl.pallas_call(last_kernel, in_specs=vmem_specs(6) + [any_spec] * len(lar...]
    ppermute x41 -> x0, waiting for transfers between devices: 155 us -> none  [the longest x10 98.1 us: line_flip(): lax.ppermute(value, 'dp', [(z * pair + x, (z ^ bit) * pair + x) for z in...]
    ppermute x41 -> x0, starting transfers between devices: 64.8 us -> none  [the longest x10 37.4 us: line_flip(): lax.ppermute(value, 'dp', [(z * pair + x, (z ^ bit) * pair + x) for z in...]
    convert_element_type x14 -> x1, other arithmetic: 9.93 us -> 0.05 us  [on_device_lines(): part.astype(f32)]
    concatenate x12 -> x7, other arithmetic: 13.1 us -> 7.81 us  [join_halves(): return jnp.concatenate([low, jnp.where(z_low == 0, far, near)], axis=axis)]
    unnamed x125 -> x60, local copies, waits for them, and re-layouts: 21.1 us -> 18.8 us
  transfers between devices with their start and end apart: 41 -> 0, of which waited for: 16 -> 0; matrix products, arithmetic and copies ran while one was open for 10% -> 0% of each run, Pallas kernels for 17% -> 0%
where the time goes in v4:
time: 569 us; the launch traced here: 559 us
  Pallas kernels  521 us (92%)
  local copies, waits for them, and re-layouts  22.1 us (4%)
  other arithmetic  13 us (2%)
    pallas_call x1, Pallas kernels, last(): pl.pallas_call(last_kernel, in_specs=vmem_specs(6) + [any_spec] * len(lar...  206 us
    pallas_call x1, Pallas kernels, middle(): pl.pallas_call(middle_kernel, in_specs=vmem_specs(10) + [any_spec] * 9, o...  126 us
    pallas_call x1, Pallas kernels, block(): pl.pallas_call(block_kernel, out_shape=[jax.ShapeDtypeStruct((rows, colum...  110 us
    pallas_call x1, Pallas kernels, project(): pl.pallas_call(project_kernel, in_specs=[pl.BlockSpec(memory_space=pl.ANY...  46.3 us
    pallas_call x1, Pallas kernels, attend_back(): pl.pallas_call(functools.partial(attend_back_kernel, factor, scale), out_...  18.8 us
    unnamed x60, local copies, waits for them, and re-layouts  18.8 us
    pallas_call x1, Pallas kernels, attend(): pl.pallas_call(functools.partial(attend_kernel, factor, key_rows), out_sh...  14.5 us

profile of v4, /device:TPU:0, one launch (start us, length us, event | category | flops | bytes accessed | tf_op | source)
XLA Modules:
  0.0 559.0 jit_solution(1691080084538156219)
XLA Ops:
  0.6 0.0 copy-start.8
  0.7 0.0 copy-start.9
  1.3 0.7 broadcast_add_fusion
  2.7 0.1 fusion.5
  2.8 1.0 fusion
  3.8 0.1 pad_maximum_fusion.8.sines
  3.9 0.0 copy-start
  4.0 0.1 pad_maximum_fusion.7.cosines
  4.1 0.0 copy-start.1
  4.2 0.0 copy-done.8
  4.2 46.3 %shard_map.255 = (bf16[4,512,128]{2,1,0:T(8,128)(2,1)S(1)}, bf16[8,2,512,128]{3,2,1,0:T(8,128)(2,1)S(1)}, f32[8,4,512]{2,1,0:T(4,128)S(1)}, f32[512,512]{1,0:T(8,128)S(1)}, f32[512,512]{1,0:T(8,128)S(1)}) custom-call(bf16[512,2048]{1,0:T(8,128)(2,1)} %tokens.5, bf16[2048,512]{1,0:T(8,128)(2,1)} %w_query.1, bf16[2048,512]{1,0:T(8,128)(2,1)} %w_key.1, ...), custom_call_target="tpu_custom_call" | custom-call | tf_op jit(solution)/shard_map/pallas_call | solution.py:552
  50.4 0.0 copy-done
  50.5 0.0 copy-done.1
  50.5 0.0 copy-start.2
  50.5 1.0 copy-done.2
  51.4 1.0 copy-done.3
  52.4 0.4 fusion.2
  52.8 0.2 slice_reduce_fusion
  53.0 0.2 multiply_reduce_fusion
  53.2 0.1 and_convert_fusion.live
  53.2 14.5 %shard_map.256 = (f32[4,128,512]{2,1,0:T(8,128)S(1)}, f32[8,512]{1,0:T(8,128)S(1)}, bf16[4,512,128]{2,1,0:T(8,128)(2,1)S(1)}, bf16[8,512,128]{2,1,0:T(8,128)(2,1...) custom-call(s32[4,8]{1,0:T(4,128)S(1)} %and_convert_fusion.live, ...), custom_call_target="tpu_custom_call" | custom-call | tf_op jit(solution)/shard_map/pallas_call | solution.py:681
  67.8 0.0 copy-start.6
  67.8 0.8 copy-done.6
  68.6 1.3 copy-done.10
  69.9 1.0 copy-done.12
  70.9 0.8 copy-done.14
  71.7 110.5 %shard_map.257 = (bf16[512,512]{1,0:T(8,128)(2,1)}, bf16[512,2048]{1,0:T(8,128)(2,1)}, bf16[512,2048]{1,0:T(8,128)(2,1)}, bf16[512,2048]{1,0:T(8,128)(2,1)}, bf1...) custom-call(bf16[4,512,128]{2,1,0:T(8,128)(2,1)} %copy-done.6, ...), custom_call_target="tpu_custom_call" | custom-call | tf_op jit(solution)/shard_map/pallas_call | solution.py:1032
  182.2 0.0 copy-start.11
  182.2 1.6 copy-done.11
  183.8 1.2 copy-done.13
  185.0 1.0 copy-done.15
  186.0 1.0 copy-done.16
  187.1 18.8 %shard_map.258 = (bf16[4,512,128]{2,1,0:T(8,128)(2,1)S(1)}, bf16[4,2,512,128]{3,2,1,0:T(8,128)(2,1)S(1)}, bf16[4,2,512,128]{3,2,1,0:T(8,128)(2,1)S(1)}) custom-call(s32[4,8]{1,0:T(4,128)S(1)} %and_convert_fusion.live, s32[8,512,128]{2,1,0:T(8,128)S(1)} %copy-done.11, s32[8,512]{1,0:T(8,128)S(1)} %get-tuple-element.72.rows, ...), custom_call_target="tpu_custom_call" | custom-call | flops 10737418240 | bytes 12582912 | tf_op jit(solution)/shard_map/pallas_call | solution.py:709
  205.8 0.0 copy-start.4
  205.9 1.0 copy-done.4
  206.8 1.0 copy-done.5
  207.8 0.8 copy-done.7
  208.6 0.6 slice_bitcast_fusion.factors
  209.2 125.6 %shard_map.259 = (f32[1024,512]{1,0:T(8,128)}, bf16[1024,512]{1,0:T(8,128)(2,1)}, bf16[1024,1024]{1,0:T(8,128)(2,1)}, bf16[512,1024]{1,0:T(8,128)(2,1)}, bf16[51...) custom-call(bf16[4,512,128]{2,1,0:T(8,128)(2,1)} %copy-done.7, ...), custom_call_target="tpu_custom_call" | custom-call | tf_op jit(solution)/shard_map/pallas_call | solution.py:1363
  334.8 205.7 %shard_map.260 = (f32[1024,256]{1,0:T(8,128)}, f32[256,1024]{1,0:T(8,128)}, f32[256,1024]{1,0:T(8,128)}, f32[256,768]{1,0:T(8,128)}, f32[256,256]{1,0:T(8,128)},...) custom-call(bf16[512,1536]{1,0:T(8,128)(2,1)} %get-tuple-element.92., ...), custom_call_target="tpu_custom_call" | custom-call | tf_op jit(solution)/shard_map/pallas_call | solution.py:1716
  540.5 1.5 convert_select_fusion.1
  542.0 1.5 pad_maximum_fusion.2
  543.5 0.1 copy-done.20
  543.6 0.5 copy-done.23
  544.1 0.3 convert_select_fusion.3
  544.5 1.5 pad_maximum_fusion.1
  545.9 0.1 copy-done.19
  546.0 0.5 copy-done.22
  546.5 0.3 convert_select_fusion.5
  546.9 1.5 pad_maximum_fusion
  548.4 0.8 pad_maximum_fusion.6
  549.2 0.1 convert_element_type.46
  549.3 0.4 copy-done.21
  549.7 0.1 slice_select_fusion.1
  549.9 0.9 pad_maximum_fusion.5
  550.7 0.9 pad_maximum_fusion.4
  551.6 0.9 pad_maximum_fusion.3
  552.5 0.7 constant_dynamic-slice_fusion
  553.2 0.7 constant_dynamic-slice_fusion.1
  553.8 0.7 constant_dynamic-slice_fusion.2
  554.5 0.6 constant_dynamic-slice_fusion.3
  555.1 1.3 copy.33
  556.5 1.0 copy-done.18
  557.5 1.3 copy.34
  (40 shorter events, 0.2 us)
Async XLA Ops:
  0.6 3.5 copy-start.8
  0.7 3.5 copy-start.9
  3.9 46.5 %copy-start = (f32[512,128]{1,0:T(8,128)}, f32[512,128]{1,0:T(8,128)S(1)}, u32[]{:S(2)}) copy-start(f32[512,128]{1,0:T(8,128)S(1)} %pad_maximum_fusion.8.sines) | copy-start | bytes 786436
  4.1 46.4 %copy-start.1 = (f32[512,128]{1,0:T(8,128)}, f32[512,128]{1,0:T(8,128)S(1)}, u32[]{:S(2)}) copy-start(f32[512,128]{1,0:T(8,128)S(1)} %pad_maximum_fusion.7.cosines) | copy-start | bytes 786436
  50.5 1.0 copy-start.2
  51.4 1.0 copy-start.3
  67.8 0.8 copy-start.6
  68.6 1.3 copy-start.10
  69.9 1.0 copy-start.12
  70.9 0.8 copy-start.14
  182.2 1.6 copy-start.11
  183.7 1.2 copy-start.13
  185.0 1.0 copy-start.15
  186.0 1.0 copy-start.16
  205.8 1.0 copy-start.4
  206.8 1.0 copy-start.5
  207.8 0.8 copy-start.7
  542.0 1.6 copy-start.20
  542.0 2.1 copy-start.23
  544.4 1.6 copy-start.19
  544.5 2.1 copy-start.22
  546.9 1.5 copy-start.25
  546.9 1.5 copy-start.26
  546.9 2.4 copy-start.24
  548.4 1.3 copy-start.21
  549.8 2.6 copy-start.27
  549.8 4.0 copy-start.28
  549.9 5.3 copy-start.17
  555.1 2.3 copy-start.18

commit v5 on v4

--- a/solution.py
+++ b/solution.py
@@ -737,15 +737,17 @@
     w_up_in,
     w_down_in,
     out_heads,
+    out_tokens_x,
     out_output,
     out_hidden,
     out_hidden_z,
     out_act,
-    out_act_z,
+    out_act_x,
     out_mlp,
-    out_mlp_z,
+    out_mlp_x,
     out_gate,
     out_gate_far,
+    out_gate_z,
     out_up,
     out_up_far,
     out_attn,
@@ -793,6 +795,8 @@
     z = spot // 2
     z_low = lax.rem(z, 2)
     z_peer = {"dp": spot + 2 - 4 * z_low}
+    x = lax.rem(spot, 2)
+    x_peer = {"dp": spot + 1 - 2 * x}
     width = pieces.shape[2]
     ahead = [{"dp": lax.rem(spot + 2 * d, 2 * line)} for d in range(line)]
     head = lambda d: pl.ds(pl.multiple_of(lax.rem(z + d, line) * width, width), width)
@@ -838,7 +842,7 @@
         keep_out(w_down_in, w_down, True),
     ]
     barrier = pltpu.get_barrier_semaphore()
-    peers = (core_peer, y_peer, ahead[1], ahead[2], ahead[3])
+    peers = (core_peer, y_peer, x_peer, ahead[1], ahead[2], ahead[3])
     for peer in peers:
         pl.semaphore_signal(barrier, inc=1, device_id=peer, device_id_type=pl.DeviceIdType.MESH)
     pl.semaphore_wait(barrier, len(peers))
@@ -848,6 +852,10 @@
                 pieces.at[d, both(s)], attended.at[both(s), head(0)], ahead[line - d]
             )
     attended[:, head(0)] = pieces[0]
+
+    loads[0].wait()
+    for s in range(2):
+        flying["tokens", s] = send(own_tokens.at[mine(s)], out_tokens_x.at[own(s)], x_peer)
 
     def forward_core(name, s, array):
         flying[name, s].wait()
@@ -912,13 +920,14 @@
         reduce_start(1, s)
         keep_out(act_keep.at[both(s)], out_act.at[both(s)])
         half = units // 2
-        far = pl.ds(pl.multiple_of((1 - z_low) * half, half), half)
-        flying["act", s] = send(act_keep.at[both(s), far], out_act_z.at[both(s)], z_peer)
+        far = pl.ds(pl.multiple_of((1 - x) * half, half), half)
+        flying["act", s] = send(act_keep.at[both(s), far], out_act_x.at[both(s)], x_peer)
 
     def turn_point(s):
         value = reduced(1, s)
         factor = factor_of(value)
         normed = value * factor
+        forward_core("tokens", s, out_tokens_x)
         own_tokens[mine(s), :] = (out_grad_hidden[mine(s), :] + normed * g_mlp[...]).astype(bf16)
         keep_out(own_tokens.at[mine(s)], out_output.at[at_home(s)])
         flying["output", s] = send(own_tokens.at[mine(s)], out_output.at[at_home(s)], core_peer)
@@ -929,7 +938,7 @@
         share(mlp_keep, s)
 
     def backward(s):
-        flying["mlp", s] = send(mlp_keep.at[own(s)], out_mlp_z.at[own(s)], z_peer)
+        flying["mlp", s] = send(mlp_keep.at[own(s)], out_mlp_x.at[own(s)], x_peer)
         flying["share", s].wait()
         keep_out(mlp_keep.at[both(s)], out_mlp.at[both(s)])
 
@@ -945,8 +954,7 @@
             return dot_nt(to_gate, w_gate[:, cut(t)]) + dot_nt(to_up, w_up[:, cut(t)])
 
         if s > 0:
-            for copy in flying["grads"]:
-                copy.wait()
+            gate_to_z(0)
         total[...] = step(0)
 
         @pl.loop(1, units // tile)
@@ -957,7 +965,7 @@
         half = units // 2
         far = pl.ds(pl.multiple_of((1 - z_low) * half, half), half)
         flying["grads"] = [
-            keep_out(source, target.at[both(s)], waited=s == 0)
+            keep_out(source, target.at[both(s)], waited=True)
             for source, target in (
                 (grad_gate, out_gate),
                 (grad_gate.at[:, far], out_gate_far),
@@ -965,6 +973,11 @@
                 (grad_up.at[:, far], out_up_far),
             )
         ]
+
+    def gate_to_z(s):
+        for copy in flying["grads"]:
+            copy.wait()
+        flying["gate_z", s] = send(out_gate_far.at[both(s)], out_gate_z.at[both(s)], z_peer)
 
     def to_attention(s):
         value = reduced(2, s)
@@ -989,7 +1002,7 @@
 
     project_out(0)
     project_out(1)
-    for load in loads:
+    for load in loads[1:]:
         load.wait()
     after_attention(0)
     forward(0)
@@ -999,6 +1012,7 @@
     backward(0)
     turn_point(1)
     backward(1)
+    gate_to_z(1)
     for s in range(2):
         forward_core("hidden", s, out_hidden_z)
     to_attention(0)
@@ -1008,8 +1022,10 @@
     for s in range(2):
         flying["act", s].wait()
         flying["output", s].wait()
-        forward_core("mlp", s, out_mlp_z)
+        forward_core("mlp", s, out_mlp_x)
     for s in range(2):
+        flying["tokens_core", s].wait()
+        flying["gate_z", s].wait()
         flying["hidden_core", s].wait()
         flying["mlp_core", s].wait()
         for d in range(1, line):
@@ -1036,11 +1052,13 @@
             wide,
             wide,
             wide,
+            wide,
             tall,
             jax.ShapeDtypeStruct((rows, units // 2), bf16),
             wide,
             wide,
             tall,
+            jax.ShapeDtypeStruct((rows, units // 2), bf16),
             jax.ShapeDtypeStruct((rows, units // 2), bf16),
             tall,
             jax.ShapeDtypeStruct((rows, units // 2), bf16),
@@ -1050,7 +1068,7 @@
             jax.ShapeDtypeStruct((2, depth), f32),
         ],
         in_specs=vmem_specs(4) + [any_spec] * 5,
-        out_specs=[any_spec] * 14 + vmem_specs(2),
+        out_specs=[any_spec] * 16 + vmem_specs(2),
         scratch_shapes=[
             pltpu.VMEM((depth, units), bf16),
             pltpu.VMEM((depth, units), bf16),
@@ -1074,8 +1092,8 @@
             pltpu.VMEM((2, quarter, depth), bf16),
             pltpu.VMEM((2, quarter, depth), bf16),
             pltpu.VMEM((3, 2, quarter, depth), bf16),
-            pltpu.SemaphoreType.DMA((48,)),
-            pltpu.SemaphoreType.DMA((48,)),
+            pltpu.SemaphoreType.DMA((56,)),
+            pltpu.SemaphoreType.DMA((56,)),
             pltpu.SemaphoreType.DMA((32,)),
         ],
         compiler_params=pltpu.CompilerParams(
@@ -1136,9 +1154,13 @@
 
 
 class Job:
-    def __init__(self, first, first_z, second, second_z, cut_first):
-        self.operands, self.cut_first = (first, first_z, second, second_z), cut_first
+    def __init__(self, spot, over_x, first, first_far, second, second_far, cut_first):
+        self.operands, self.cut_first = (first, first_far, second, second_far), cut_first
         self.tile = (first if cut_first else second).shape[1] // (line * pair)
+        self.spot, self.over_x = spot, over_x
+        self.side = spot.x if over_x else spot.z_low
+        self.partner = spot.x_peer if over_x else spot.z_peer
+        self.first_peer = spot.z_peer if over_x else spot.x_peer
 
     def at(self, ref, index):
         block = pl.ds(pl.multiple_of(index * self.tile, self.tile), self.tile)
@@ -1149,26 +1171,35 @@
         return ref.at[block, :] if self.cut_first else ref.at[:, block]
 
     def term(self, index):
-        first, first_z, second, second_z = self.operands
+        first, first_far, second, second_far = self.operands
         block = pl.ds(pl.multiple_of(index * self.tile, self.tile), self.tile)
         if self.cut_first:
-            return dot_t(first[:, block], second[...]) + dot_t(first_z[:, block], second_z[...])
-        return dot_t(first[...], second[:, block]) + dot_t(first_z[...], second_z[:, block])
-
-    def send_terms(self, spot, target):
+            return dot_t(first[:, block], second[...]) + dot_t(first_far[:, block], second_far[...])
+        return dot_t(first[...], second[:, block]) + dot_t(first_far[...], second_far[:, block])
+
+    def block_of(self, high, index):
+        if self.over_x:
+            return (2 * high + self.spot.z_low) * pair + index
+        return (2 * high + index) * pair + self.spot.x
+
+    def send_terms(self, target):
         @pl.loop(0, line)
         def _(i):
-            self.at(target, i)[...] = self.term(i * pair + 1 - spot.x).astype(jnp.bfloat16)
-
-    def second_terms(self, spot, arrived, target):
+            if self.over_x:
+                index = (i // 2) * 4 + (1 - self.spot.z_low) * 2 + lax.rem(i, 2)
+            else:
+                index = i * pair + 1 - self.spot.x
+            self.at(target, i)[...] = self.term(index).astype(jnp.bfloat16)
+
+    def second_terms(self, arrived, target):
         @pl.loop(0, 2)
         def _(i):
-            total = self.term((2 * (1 - spot.z_high) + i) * pair + spot.x)
+            total = self.term(self.block_of(1 - self.spot.z_high, i))
             total = total + self.at(arrived, i)[...].astype(jnp.float32)
             self.at(target, i)[...] = total.astype(jnp.bfloat16)
 
-    def own_term(self, spot, side, arrived):
-        total = self.term((2 * spot.z_high + side) * pair + spot.x)
+    def own_term(self, side, arrived):
+        total = self.term(self.block_of(self.spot.z_high, side))
         return total + self.at(arrived, side)[...].astype(jnp.float32)
 
 
@@ -1184,20 +1215,21 @@
     gq,
     gk,
     act,
-    act_z,
+    act_x,
     mlp,
-    mlp_z,
+    mlp_x,
     hidden,
     hidden_z,
     gate,
-    gate_far,
+    gate_z,
+    up,
     up_far,
     out_own_down,
     out_r2_down,
     out_r1_gate,
-    out_gate_z,
+    out_r1_up,
     out_up_z,
-    out_raw_z,
+    out_raw_x,
     r1_down,
     out_raw,
     out_raw_own,
@@ -1210,8 +1242,11 @@
     hidden_zv,
     gate_v,
     gate_zv,
+    up_v,
+    up_zv,
     send_down,
     send_gate,
+    send_up,
     r1_v,
     r1_own,
     s2_v,
@@ -1238,14 +1273,17 @@
     depth = mlp_v.shape[1]
     half = act_v.shape[1]
     own_half = pl.ds(pl.multiple_of(spot.z_low * half, half), half)
+    x_half = pl.ds(pl.multiple_of(spot.x * half, half), half)
     loads = [
-        mail.move(act.at[:, own_half], act_v),
-        mail.move(act_z, act_zv),
+        mail.move(act.at[:, x_half], act_v),
+        mail.move(act_x, act_zv),
         mail.move(mlp, mlp_v),
-        mail.move(mlp_z, mlp_zv),
+        mail.move(mlp_x, mlp_zv),
         mail.move(hidden, hidden_v),
         mail.move(hidden_z, hidden_zv),
         mail.move(gate.at[:, own_half], gate_v),
+        mail.move(gate_z, gate_zv),
+        mail.move(up.at[:, own_half], up_v),
     ]
     greet(spot.all)
     far_copy = mail.send(far, far_in, spot.x_peer)
@@ -1254,27 +1292,30 @@
         mail.send(grad_queries.at[d], query_home.at[:, my_head], spot.ahead[line - d])
         for d in range(1, line)
     ]
-    gate_copy = mail.send(gate_far, gate_zv, spot.z_peer)
+    up_copy = mail.send(up_far, up_zv, spot.z_peer)
     query_home[:, my_head] = grad_queries[0]
-    for load in loads:
+    for load in loads[:4]:
         load.wait()
-    down = Job(act_v, act_zv, mlp_v, mlp_zv, False)
-    down.send_terms(spot, send_down)
-    down_copy = mail.send(send_down, r1_down, spot.x_peer)
-
+    down = Job(spot, True, act_v, act_zv, mlp_v, mlp_zv, False)
+    down.send_terms(send_down)
+    down_copy = mail.send(send_down, r1_down, down.first_peer)
+    for load in loads[4:]:
+        load.wait()
+    gates = Job(spot, False, hidden_v, hidden_zv, gate_v, gate_zv, True)
+    gates.send_terms(send_gate)
     far_copy.wait()
+    gate_terms = mail.send(send_gate, out_r1_gate, gates.first_peer)
     sums[...] = (near[...].astype(f32) + far_in[...].astype(f32)).astype(bf16)
     pair_copies = [
         mail.send(sums.at[d], pair_home.at[:, :, my_head], spot.ahead[line - d])
         for d in range(1, line)
     ]
     pair_home[:, :, my_head] = sums[0]
-    gate_copy.wait()
-    up_copy = mail.send(up_far, out_up_z, spot.z_peer)
-    keep_gate = mail.move(gate_zv, out_gate_z)
-    gates = Job(hidden_v, hidden_zv, gate_v, gate_zv, True)
-    gates.send_terms(spot, send_gate)
-    gate_terms = mail.send(send_gate, out_r1_gate, spot.x_peer)
+    up_copy.wait()
+    keep_up = mail.move(up_zv, out_up_z)
+    ups = Job(spot, False, hidden_v, hidden_zv, up_v, up_zv, True)
+    ups.send_terms(send_up)
+    up_terms = mail.send(send_up, out_r1_up, ups.first_peer)
 
     for copy in query_copies + pair_copies:
         copy.wait()
@@ -1324,9 +1365,9 @@
             start = pl.multiple_of(base + index * part_width, part_width)
             return out_raw[:, pl.ds(start, part_width)]
 
-        out_raw_own[:, cut] = side(spot.z_low)
-        raw_far[:, cut] = side(1 - spot.z_low)
-    raw_copy = mail.send(raw_far, out_raw_z, spot.z_peer)
+        out_raw_own[:, cut] = side(spot.x)
+        raw_far[:, cut] = side(1 - spot.x)
+    raw_copy = mail.send(raw_far, out_raw_x, spot.x_peer)
 
     down_copy.wait()
     loads = [
@@ -1334,16 +1375,16 @@
         mail.move(down.span(r1_down, spot.z_high), r1_own),
     ]
     loads[0].wait()
-    down.second_terms(spot, r1_v, s2_v)
+    down.second_terms(r1_v, s2_v)
     second_copy = mail.send(s2_v, out_r2_down, spot.far_peer)
     loads[1].wait()
 
     @pl.loop(0, 2)
     def _(i):
-        down.at(own_v, i)[...] = down.own_term(spot, i, r1_own)
+        down.at(own_v, i)[...] = down.own_term(i, r1_own)
 
     keep_own = mail.move(own_v, out_own_down)
-    for copy in (up_copy, gate_terms, raw_copy, second_copy, keep_gate, keep_own):
+    for copy in (gate_terms, up_terms, raw_copy, second_copy, keep_up, keep_own):
         copy.wait()
 
 
@@ -1351,7 +1392,7 @@
     f32 = jnp.float32
     bf16 = jnp.bfloat16
     grad_queries, near, far, q_raw = small[:4]
-    act, act_z, grad_mlp = large[:3]
+    act, act_x, grad_mlp = large[:3]
     _, count, width = grad_queries.shape
     columns = line * width
     depth = grad_mlp.shape[1]
@@ -1362,13 +1403,13 @@
     shape = jax.ShapeDtypeStruct
     return pl.pallas_call(
         middle_kernel,
-        in_specs=vmem_specs(10) + [any_spec] * 9,
+        in_specs=vmem_specs(10) + [any_spec] * 10,
         out_specs=[any_spec] * 7 + vmem_specs(3),
         out_shape=[
             shape((half, cut // 2), f32),
             shape((half, cut // 2), bf16),
             shape((cut, half), bf16),
-            shape((count, half), bf16),
+            shape((cut, half), bf16),
             shape((count, half), bf16),
             shape((count, 3 * columns // 2), bf16),
             shape((half, cut), bf16),
@@ -1385,7 +1426,10 @@
             pltpu.VMEM((count, depth), bf16),
             pltpu.VMEM((count, half), bf16),
             pltpu.VMEM((count, half), bf16),
+            pltpu.VMEM((count, half), bf16),
+            pltpu.VMEM((count, half), bf16),
             pltpu.VMEM((half, cut), bf16),
+            pltpu.VMEM((cut, half), bf16),
             pltpu.VMEM((cut, half), bf16),
             pltpu.VMEM((half, cut // 2), bf16),
             pltpu.VMEM((half, cut // 2), bf16),
@@ -1405,7 +1449,7 @@
             pltpu.SemaphoreType.DMA((16,)),
         ],
         compiler_params=pltpu.CompilerParams(
-            vmem_limit_bytes=big_vmem, collective_id=3, has_side_effects=True
+            vmem_limit_bytes=60 << 20, collective_id=3, has_side_effects=True
         ),
     )(*small, *large)
 
@@ -1413,7 +1457,7 @@
 def last_kernel(
     raw,
     raw_own,
-    raw_z,
+    raw_x,
     wide,
     narrow,
     attended,
@@ -1425,19 +1469,21 @@
     up_z,
     attn,
     tokens,
+    tokens_x,
     own_down,
     r2_down,
     r1_gate,
+    r1_up,
     w_query,
     w_key,
     w_value,
     grad_hidden,
     *refs,
 ):
-    outs, refs = refs[:14], refs[14:]
+    outs, refs = refs[:13], refs[13:]
     near_down, near_gate, near_up, near_raw, near_out = outs[:5]
     far_down, far_gate, far_up, far_raw, far_out = outs[5:10]
-    out_tokens, r1_up, r1_raw, r1_out = outs[10:]
+    out_tokens, r1_raw, r1_out = outs[10:]
     out_wide, out_narrow = refs[:2]
     (
         hidden_v,
@@ -1447,13 +1493,12 @@
         up_v,
         up_zv,
         tokens_v,
-        tokens_zv,
+        tokens_xv,
         attn_v,
-        attn_zv,
+        attn_xv,
         heads_v,
         heads_far,
-        heads_zv,
-        send_up,
+        heads_xv,
         send_raw,
         send_out,
         r1_wide,
@@ -1512,58 +1557,52 @@
     both = lambda s: pl.ds(s * rows, rows)
     mine = lambda s: pl.ds(s * count, count)
 
-    first_loads = [
-        mail.move(hidden, hidden_v),
-        mail.move(hidden_z, hidden_zv),
-        mail.move(up.at[:, own_half], up_v),
-        mail.move(up_z, up_zv),
-    ]
-    token_loads, attn_loads = [], []
+    token_loads = [mail.move(tokens_x, tokens_xv)]
     for s in range(2):
         for part, place in ((0, spot.core), (1, 1 - spot.core)):
             start = pl.multiple_of(place * rows + s * count, count)
             target = tokens_v.at[pl.ds(s * rows + part * count, count)]
             token_loads.append(mail.move(tokens.at[pl.ds(start, count)], target))
     attn_load = mail.move(attn, attn_v)
-    later_loads = [
-        mail.move(gate.at[:, own_half], gate_v),
-        mail.move(gate_z, gate_zv),
-    ]
+    r1_loads = []
+    first_loads = [mail.move(hidden, hidden_v), mail.move(hidden_z, hidden_zv)]
+    gate_loads = [mail.move(gate.at[:, own_half], gate_v), mail.move(gate_z, gate_zv)]
+    up_loads = [mail.move(up.at[:, own_half], up_v), mail.move(up_z, up_zv)]
+    ups = Job(spot, False, hidden_v, hidden_zv, up_v, up_zv, True)
+    gates = Job(spot, False, hidden_v, hidden_zv, gate_v, gate_zv, True)
+    raws = Job(spot, True, tokens_v, tokens_xv, raw_own, raw_x, True)
+    outs_job = Job(spot, True, heads_v, heads_xv, attn_v, attn_xv, False)
+    gate_second = mail.move(gates.span(r1_gate, 1 - spot.z_high), r1_wide.at[0])
+    gate_own = mail.move(gates.span(r1_gate, spot.z_high), r1_wide.at[1])
+    up_second = mail.move(ups.span(r1_up, 1 - spot.z_high), r1_wide.at[2])
+    up_own = mail.move(ups.span(r1_up, spot.z_high), r1_wide.at[3])
     greet(spot.all)
     wide_copy = mail.send(wide, wide_core, spot.core_peer)
-    for load in first_loads:
-        load.wait()
-    ups = Job(hidden_v, hidden_zv, up_v, up_zv, True)
-    gates = Job(hidden_v, hidden_zv, gate_v, gate_zv, True)
-    raws = Job(tokens_v, tokens_zv, raw_own, raw_z, True)
-    outs_job = Job(heads_v, heads_zv, attn_v, attn_zv, False)
+    attn_load.wait()
+    attn_copies = [
+        mail.send(attn_v.at[own(s)], attn_xv.at[own(s)], spot.x_peer) for s in range(2)
+    ]
+    heads_far[...] = attended[:, side_heads(1 - spot.x)]
+    heads_v[...] = attended[:, side_heads(spot.x)]
+    heads_copy = mail.send(heads_far, heads_xv, spot.x_peer)
     for load in token_loads:
         load.wait()
-    token_copies = [
-        mail.send(tokens_v.at[own(s)], tokens_zv.at[own(s)], spot.z_peer) for s in range(2)
-    ]
-    heads_far[...] = attended[:, side_heads(1 - spot.z_low)]
-    heads_v[...] = attended[:, side_heads(spot.z_low)]
-    heads_copy = mail.send(heads_far, heads_zv, spot.z_peer)
-    ups.send_terms(spot, send_up)
+    raws.send_terms(send_raw)
+    raw_copy = mail.send(send_raw, r1_raw, raws.first_peer)
     wide_copy.wait()
     out_wide[...] = wide[...] + wide_core[...]
     out_narrow[...] = narrow[...]
     wide_x_copy = mail.send(out_wide, wide_x, spot.x_peer)
     narrow_x_copy = mail.send(out_narrow, narrow_x, spot.x_peer)
-    up_copy = mail.send(send_up, r1_up, spot.x_peer)
-
-    r1_load = mail.move(gates.span(r1_gate, 1 - spot.z_high), r1_wide.at[0])
-    r1_gate_own = mail.move(gates.span(r1_gate, spot.z_high), r1_wide.at[1])
-    for load in later_loads:
+
+    for load in (*first_loads, *gate_loads, gate_second):
         load.wait()
-    r1_load.wait()
-    gates.second_terms(spot, r1_wide.at[0], s2_gate)
+    gates.second_terms(r1_wide.at[0], s2_gate)
     gate_copy = mail.send(s2_gate, r2_gate, spot.far_peer)
-    attn_load.wait()
-    attn_copies = [
-        mail.send(attn_v.at[own(s)], attn_zv.at[own(s)], spot.z_peer) for s in range(2)
-    ]
+    for load in (*up_loads, up_second):
+        load.wait()
+    ups.second_terms(r1_wide.at[2], s2_up)
+    second_up = mail.send(s2_up, r2_up, spot.far_peer)
 
     input_weights = (w_query, w_key, w_value)
     columns = w_query.shape[1]
@@ -1586,15 +1625,15 @@
     near_copies, far_copies = [], []
 
     def finish(job, value_of, fin, far, keep, target):
-        fin[...] = value_of(1 - spot.z_low).astype(bf16)
-        far_copies.append(mail.send(fin, far, spot.z_peer))
-        keep[...] = value_of(spot.z_low)
+        fin[...] = value_of(1 - job.side).astype(bf16)
+        far_copies.append(mail.send(fin, far, job.partner))
+        keep[...] = value_of(job.side)
         near_copies.append(mail.move(keep, target))
 
     down_loads = [mail.move(own_down, own_down_v), mail.move(r2_down, r2_down_v)]
     for load in down_loads:
         load.wait()
-    down = Job(heads_v, heads_zv, attn_v, attn_zv, False)
+    down = outs_job
     finish(
         down,
         lambda side: down.at(own_down_v, side)[...] + down.at(r2_down_v, side)[...].astype(f32),
@@ -1604,29 +1643,20 @@
         near_down,
     )
 
-    for s in range(2):
-        token_copies[s].wait()
-    token_core = [
-        mail.send(tokens_zv.at[own(s)], tokens_zv.at[other(s)], spot.core_peer) for s in range(2)
-    ]
-    for copy in token_core:
-        copy.wait()
-    raws.send_terms(spot, send_raw)
     wide_x_copy.wait()
     narrow_x_copy.wait()
     out_wide[...] = out_wide[...] + wide_x[...]
     out_narrow[...] = out_narrow[...] + narrow_x[...]
-    raw_copy = mail.send(send_raw, r1_raw, spot.x_peer)
     for s in range(2):
         attn_copies[s].wait()
     attn_core = [
-        mail.send(attn_zv.at[own(s)], attn_zv.at[other(s)], spot.core_peer) for s in range(2)
+        mail.send(attn_xv.at[own(s)], attn_xv.at[other(s)], spot.core_peer) for s in range(2)
     ]
     for copy in attn_core:
         copy.wait()
     heads_copy.wait()
-    outs_job.send_terms(spot, send_out)
-    out_copy = mail.send(send_out, r1_out, spot.x_peer)
+    outs_job.send_terms(send_out)
+    out_copy = mail.send(send_out, r1_out, outs_job.first_peer)
 
     hidden_load.wait()
     for s in range(2):
@@ -1643,19 +1673,8 @@
         gain_copies.append(mail.send(out_wide, wide_z.at[d - 1], spot.ahead[d]))
         gain_copies.append(mail.send(out_narrow, narrow_z.at[d - 1], spot.ahead[d]))
 
-    up_copy.wait()
-    r1_up_second = mail.move(ups.span(r1_up, 1 - spot.z_high), r1_wide.at[2])
-    r1_up_own = mail.move(ups.span(r1_up, spot.z_high), r1_wide.at[3])
-    r1_up_second.wait()
-    ups.second_terms(spot, r1_wide.at[2], s2_up)
-    second_up = mail.send(s2_up, r2_up, spot.far_peer)
-
     def final_of(job, r1_own, r2):
-        return lambda side: job.own_term(spot, side, r1_own) + job.at(r2, side)[...].astype(f32)
-
-    r1_gate_own.wait()
-    gate_copy.wait()
-    finish(gates, final_of(gates, r1_wide.at[1], r2_gate), fin_gate, far_gate, keep_gate, near_gate)
+        return lambda side: job.own_term(side, r1_own) + job.at(r2, side)[...].astype(f32)
 
     raw_copy.wait()
     raw_loads = [
@@ -1664,7 +1683,7 @@
     ]
     for load in raw_loads:
         load.wait()
-    raws.second_terms(spot, r1_raw_v.at[0], s2_raw)
+    raws.second_terms(r1_raw_v.at[0], s2_raw)
     second_raw = mail.send(s2_raw, r2_raw, spot.far_peer)
     out_copy.wait()
     out_loads = [
@@ -1673,9 +1692,13 @@
     ]
     for load in out_loads:
         load.wait()
-    outs_job.second_terms(spot, r1_out_v.at[0], s2_out)
+    outs_job.second_terms(r1_out_v.at[0], s2_out)
     second_out = mail.send(s2_out, r2_out, spot.far_peer)
-    r1_up_own.wait()
+    gate_own.wait()
+    gate_copy.wait()
+    finish(gates, final_of(gates, r1_wide.at[1], r2_gate), fin_gate, far_gate, keep_gate, near_gate)
+
+    up_own.wait()
     second_up.wait()
     finish(ups, final_of(ups, r1_wide.at[3], r2_up), fin_up, far_up, keep_up, near_up)
     second_raw.wait()
@@ -1699,7 +1722,7 @@
 def last(small, large):
     f32 = jnp.float32
     bf16 = jnp.bfloat16
-    raw, raw_own, raw_z, wide, narrow, attended = small
+    raw, raw_own, raw_x, wide, narrow, attended = small
     hidden, gate = large[0], large[2]
     count, depth = hidden.shape
     units = gate.shape[1]
@@ -1716,7 +1739,7 @@
     return pl.pallas_call(
         last_kernel,
         in_specs=vmem_specs(6) + [any_spec] * len(large),
-        out_specs=[any_spec] * 14 + vmem_specs(2),
+        out_specs=[any_spec] * 13 + vmem_specs(2),
         out_shape=[
             shape((half, block), f32),
             shape((block, half), f32),
@@ -1729,7 +1752,6 @@
             shape((block, raw_half), bf16),
             shape((heads_half, block), bf16),
             shape((count, depth), bf16),
-            shape((line * block, half), bf16),
             shape((line * block, raw_half), bf16),
             shape((heads_half, line * block), bf16),
             shape(wide.shape, f32),
@@ -1749,7 +1771,6 @@
             vmem(count, heads_half),
             vmem(count, heads_half),
             vmem(count, heads_half),
-            vmem(line * block, half),
             vmem(line * block, raw_half),
             vmem(heads_half, line * block),
             vmem(4, 2 * block, half),
@@ -1849,9 +1870,9 @@
         width = value.shape[1] // 2
         return lax.dynamic_slice_in_dim(value, side * width, width, 1)
 
-    def join_halves(near, far, axis):
-        low = jnp.where(z_low == 0, near, far)
-        return jnp.concatenate([low, jnp.where(z_low == 0, far, near)], axis=axis)
+    def join_halves(near, far, axis, side):
+        low = jnp.where(side == 0, near, far)
+        return jnp.concatenate([low, jnp.where(side == 0, far, near)], axis=axis)
 
     positions = reorder(offsets[0] + jnp.arange(row_count, dtype=jnp.int32))
     labels = reorder(row_ids[0] * key_rows + doc_ids)
@@ -1892,15 +1913,17 @@
     g_mlp = gain_mlp.reshape(1, model_width)
     (
         attended_low,
+        tokens_x,
         output,
         hidden_low,
         hidden_z,
         act_low,
-        act_z,
+        act_x,
         grad_mlp,
-        grad_mlp_z,
+        grad_mlp_x,
         grad_gate,
-        grad_gate_far,
+        _,
+        grad_gate_z,
         grad_up,
         grad_up_far,
         grad_attn,
@@ -1917,9 +1940,9 @@
         own_down,
         r2_down,
         r1_gate,
-        grad_gate_z,
+        r1_up,
         grad_up_z,
-        raw_z,
+        raw_x,
         _,
         raw,
         raw_own,
@@ -1928,18 +1951,19 @@
         (*back, q_raw, k_raw, factors, cosines, sines, g_query, g_key),
         (
             act_low,
-            act_z,
+            act_x,
             grad_mlp,
-            grad_mlp_z,
+            grad_mlp_x,
             hidden_low,
             hidden_z,
             grad_gate,
-            grad_gate_far,
+            grad_gate_z,
+            grad_up,
             grad_up_far,
         ),
     )
     results = last(
-        (raw, raw_own, raw_z, wide_gains, narrow_gains, attended_low),
+        (raw, raw_own, raw_x, wide_gains, narrow_gains, attended_low),
         (
             hidden_low,
             hidden_z,
@@ -1949,9 +1973,11 @@
             grad_up_z,
             grad_attn,
             tokens,
+            tokens_x,
             own_down,
             r2_down,
             r1_gate,
+            r1_up,
             w_query,
             w_key,
             w_value,
@@ -1961,7 +1987,7 @@
     down_near, gate_near, up_near, raw_near, out_near = results[:5]
     down_far, gate_far, up_far, raw_far, out_far = [part.astype(f32) for part in results[5:10]]
     grad_tokens = results[10]
-    wide, narrow = results[14:]
+    wide, narrow = results[13:]
     gains = jnp.concatenate([wide.reshape(2 * model_width), narrow.reshape(2 * local_width)])
     piece = head_width // (line * pair)
 
@@ -1974,7 +2000,7 @@
 
     def raw_result(index):
         cut = slice(index * part_width, (index + 1) * part_width)
-        return join_halves(raw_near[:, cut], raw_far[:, cut], 1)
+        return join_halves(raw_near[:, cut], raw_far[:, cut], 1, x)
 
     return (
         output,
@@ -1982,10 +2008,10 @@
         raw_result(0),
         raw_result(1),
         raw_result(2),
-        join_halves(out_near, out_far, 0),
-        join_halves(gate_near, gate_far, 1),
-        join_halves(up_near, up_far, 1),
-        join_halves(down_near, down_far, 0),
+        join_halves(out_near, out_far, 0, x),
+        join_halves(gate_near, gate_far, 1, z_low),
+        join_halves(up_near, up_far, 1, z_low),
+        join_halves(down_near, down_far, 0, x),
         gain_piece(2 * model_width, heads_here),
         gain_piece(2 * model_width + local_width, heads_here),
         gain_piece(0, all_heads),

time: 569 us -> 543 us (0.954)
  Pallas kernels: 521 us -> 499 us
    pallas_call x1, Pallas kernels: 206 us -> 162 us  [last(): pl.pallas_call(last_kernel, in_specs=vmem_specs(6) + [any_spec] * len(lar...]
    pallas_call x1, Pallas kernels: 126 us -> 157 us  [middle(): pl.pallas_call(middle_kernel, in_specs=vmem_specs(10) + [any_spec] * 10,...]
    pallas_call x1, Pallas kernels: 18.8 us -> 12.6 us  [attend_back(): pl.pallas_call(functools.partial(attend_back_kernel, factor, scale), out_...]
where the time goes in v5:
time: 543 us; the launch traced here: 536 us
  Pallas kernels  499 us (92%)
  local copies, waits for them, and re-layouts  22.1 us (4%)
  other arithmetic  12.9 us (2%)
    pallas_call x1, Pallas kernels, last(): pl.pallas_call(last_kernel, in_specs=vmem_specs(6) + [any_spec] * len(lar...  162 us
    pallas_call x1, Pallas kernels, middle(): pl.pallas_call(middle_kernel, in_specs=vmem_specs(10) + [any_spec] * 10,...  157 us
    pallas_call x1, Pallas kernels, block(): pl.pallas_call(block_kernel, out_shape=[jax.ShapeDtypeStruct((rows, colum...  107 us
    pallas_call x1, Pallas kernels, project(): pl.pallas_call(project_kernel, in_specs=[pl.BlockSpec(memory_space=pl.ANY...  46.3 us
    unnamed x60, local copies, waits for them, and re-layouts  18.8 us
    pallas_call x1, Pallas kernels, attend(): pl.pallas_call(functools.partial(attend_kernel, factor, key_rows), out_sh...  14.6 us
    pallas_call x1, Pallas kernels, attend_back(): pl.pallas_call(functools.partial(attend_back_kernel, factor, scale), out_...  12.6 us

profile of v5, /device:TPU:0, one launch (start us, length us, event | category | flops | bytes accessed | tf_op | source)
XLA Modules:
  0.0 536.3 jit_solution(10582365577808415690)
XLA Ops:
  0.6 0.0 copy-start.8
  0.7 0.0 copy-start.9
  1.3 0.7 broadcast_add_fusion
  2.7 0.1 fusion.5
  2.8 1.0 fusion
  3.8 0.1 pad_maximum_fusion.8.sines
  3.9 0.0 copy-start
  4.0 0.1 pad_maximum_fusion.7.cosines
  4.1 0.0 copy-start.1
  4.2 0.0 copy-done.8
  4.2 0.0 copy-done.9
  4.2 46.3 %shard_map.255 = (bf16[4,512,128]{2,1,0:T(8,128)(2,1)S(1)}, bf16[8,2,512,128]{3,2,1,0:T(8,128)(2,1)S(1)}, f32[8,4,512]{2,1,0:T(4,128)S(1)}, f32[512,512]{1,0:T(8,128)S(1)}, f32[512,512]{1,0:T(8,128)S(1)}) custom-call(bf16[512,2048]{1,0:T(8,128)(2,1)} %tokens.5, bf16[2048,512]{1,0:T(8,128)(2,1)} %w_query.1, bf16[2048,512]{1,0:T(8,128)(2,1)} %w_key.1, ...), custom_call_target="tpu_custom_call" | custom-call | tf_op jit(solution)/shard_map/pallas_call | solution.py:552
  50.5 0.0 copy-start.2
  50.5 1.0 copy-done.2
  51.4 1.0 copy-done.3
  52.4 0.4 fusion.2
  52.8 0.2 slice_reduce_fusion
  53.0 0.2 multiply_reduce_fusion
  53.2 0.1 and_convert_fusion.live
  53.2 14.6 %shard_map.256 = (f32[4,128,512]{2,1,0:T(8,128)S(1)}, f32[8,512]{1,0:T(8,128)S(1)}, bf16[4,512,128]{2,1,0:T(8,128)(2,1)S(1)}, bf16[8,512,128]{2,1,0:T(8,128)(2,1...) custom-call(s32[4,8]{1,0:T(4,128)S(1)} %and_convert_fusion.live, ...), custom_call_target="tpu_custom_call" | custom-call | tf_op jit(solution)/shard_map/pallas_call | solution.py:681
  67.8 0.0 copy-start.6
  67.8 0.8 copy-done.6
  68.6 1.3 copy-done.10
  69.9 1.0 copy-done.12
  70.9 0.8 copy-done.14
  71.7 106.8 %shard_map.257 = (bf16[512,512]{1,0:T(8,128)(2,1)}, bf16[512,2048]{1,0:T(8,128)(2,1)}, bf16[512,2048]{1,0:T(8,128)(2,1)}, bf16[512,2048]{1,0:T(8,128)(2,1)}, bf1...) custom-call(bf16[4,512,128]{2,1,0:T(8,128)(2,1)} %copy-done.6, ...), custom_call_target="tpu_custom_call" | custom-call | tf_op jit(solution)/shard_map/pallas_call | solution.py:1048
  178.5 0.0 copy-start.11
  178.5 1.6 copy-done.11
  180.1 1.2 copy-done.13
  181.4 1.0 copy-done.15
  182.4 1.0 copy-done.16
  183.4 12.6 %shard_map.258 = (bf16[4,512,128]{2,1,0:T(8,128)(2,1)S(1)}, bf16[4,2,512,128]{3,2,1,0:T(8,128)(2,1)S(1)}, bf16[4,2,512,128]{3,2,1,0:T(8,128)(2,1)S(1)}) custom-call(s32[4,8]{1,0:T(4,128)S(1)} %and_convert_fusion.live, s32[8,512,128]{2,1,0:T(8,128)S(1)} %copy-done.11, s32[8,512]{1,0:T(8,128)S(1)} %get-tuple-element.73.rows, ...), custom_call_target="tpu_custom_call" | custom-call | flops 10737418240 | bytes 12582912 | tf_op jit(solution)/shard_map/pallas_call | solution.py:709
  196.1 0.0 copy-start.4
  196.1 1.0 copy-done.4
  197.1 1.0 copy-done.5
  198.0 0.8 copy-done.7
  198.8 0.6 slice_bitcast_fusion.factors
  199.4 156.7 %shard_map.259 = (f32[1024,512]{1,0:T(8,128)}, bf16[1024,512]{1,0:T(8,128)(2,1)}, bf16[1024,1024]{1,0:T(8,128)(2,1)}, bf16[1024,1024]{1,0:T(8,128)(2,1)}, bf16[5...) custom-call(bf16[4,512,128]{2,1,0:T(8,128)(2,1)} %copy-done.7, ...), custom_call_target="tpu_custom_call" | custom-call | tf_op jit(solution)/shard_map/pallas_call | solution.py:1404
  356.2 161.7 %shard_map.260 = (f32[1024,256]{1,0:T(8,128)}, f32[256,1024]{1,0:T(8,128)}, f32[256,1024]{1,0:T(8,128)}, f32[256,768]{1,0:T(8,128)}, f32[256,256]{1,0:T(8,128)},...) custom-call(bf16[512,1536]{1,0:T(8,128)(2,1)} %get-tuple-element.94., ...), custom_call_target="tpu_custom_call" | custom-call | tf_op jit(solution)/shard_map/pallas_call | solution.py:1739
  517.9 1.5 convert_select_fusion.1
  519.4 1.5 pad_maximum_fusion.2
  520.9 0.1 copy-done.20
  521.0 0.5 copy-done.23
  521.5 0.3 convert_select_fusion.3
  521.8 1.5 pad_maximum_fusion.1
  523.3 0.1 copy-done.19
  523.4 0.5 copy-done.22
  523.9 0.3 convert_select_fusion.5
  524.2 1.5 pad_maximum_fusion
  525.7 0.0 copy-done.26
  525.8 0.8 pad_maximum_fusion.6
  526.6 0.1 convert_element_type.46
  526.7 0.4 copy-done.21
  527.0 0.1 slice_select_fusion.1
  527.2 0.9 pad_maximum_fusion.5
  528.1 0.9 pad_maximum_fusion.4
  528.9 0.9 pad_maximum_fusion.3
  529.8 0.7 constant_dynamic-slice_fusion
  530.5 0.7 constant_dynamic-slice_fusion.1
  531.2 0.7 constant_dynamic-slice_fusion.2
  531.8 0.6 constant_dynamic-slice_fusion.3
  532.5 1.3 copy.33
  533.8 1.0 copy-done.18
  534.8 1.3 copy.34
  (40 shorter events, 0.2 us)
Async XLA Ops:
  0.6 3.5 copy-start.8
  0.7 3.5 copy-start.9
  3.9 46.5 %copy-start = (f32[512,128]{1,0:T(8,128)}, f32[512,128]{1,0:T(8,128)S(1)}, u32[]{:S(2)}) copy-start(f32[512,128]{1,0:T(8,128)S(1)} %pad_maximum_fusion.8.sines) | copy-start | bytes 786436
  4.1 46.4 %copy-start.1 = (f32[512,128]{1,0:T(8,128)}, f32[512,128]{1,0:T(8,128)S(1)}, u32[]{:S(2)}) copy-start(f32[512,128]{1,0:T(8,128)S(1)} %pad_maximum_fusion.7.cosines) | copy-start | bytes 786436
  50.5 1.0 copy-start.2
  51.4 1.0 copy-start.3
  67.8 0.8 copy-start.6
  68.6 1.3 copy-start.10
  69.9 1.0 copy-start.12
  70.9 0.8 copy-start.14
  178.5 1.6 copy-start.11
  180.1 1.2 copy-start.13
  181.3 1.0 copy-start.15
  182.4 1.0 copy-start.16
  196.1 1.0 copy-start.4
  197.1 1.0 copy-start.5
  198.0 0.8 copy-start.7
  519.4 1.6 copy-start.20
  519.4 2.1 copy-start.23
  521.8 1.6 copy-start.19
  521.8 2.1 copy-start.22
  524.2 1.5 copy-start.25
  524.2 1.5 copy-start.26
  524.2 2.4 copy-start.24
  525.7 1.3 copy-start.21
  527.2 2.6 copy-start.27
  527.2 4.0 copy-start.28
  527.2 5.3 copy-start.17
  532.5 2.3 copy-start.18

commit v6 on v5

--- a/solution.py
+++ b/solution.py
@@ -1191,12 +1191,15 @@
                 index = i * pair + 1 - self.spot.x
             self.at(target, i)[...] = self.term(index).astype(jnp.bfloat16)
 
+    def second_term(self, arrived, target, i):
+        total = self.term(self.block_of(1 - self.spot.z_high, i))
+        total = total + self.at(arrived, i)[...].astype(jnp.float32)
+        self.at(target, i)[...] = total.astype(jnp.bfloat16)
+
     def second_terms(self, arrived, target):
         @pl.loop(0, 2)
         def _(i):
-            total = self.term(self.block_of(1 - self.spot.z_high, i))
-            total = total + self.at(arrived, i)[...].astype(jnp.float32)
-            self.at(target, i)[...] = total.astype(jnp.bfloat16)
+            self.second_term(arrived, target, i)
 
     def own_term(self, side, arrived):
         total = self.term(self.block_of(self.spot.z_high, side))
@@ -1204,8 +1207,8 @@
 
 
 def middle_kernel(
-    grad_queries,
-    near,
+    grad_queries_in,
+    near_in,
     far,
     q_raw,
     k_raw,
@@ -1223,12 +1226,12 @@
     gate,
     gate_z,
     up,
-    up_far,
+    up_z,
     out_own_down,
     out_r2_down,
     out_r1_gate,
     out_r1_up,
-    out_up_z,
+    out_r2_gate,
     out_raw_x,
     r1_down,
     out_raw,
@@ -1251,6 +1254,10 @@
     r1_own,
     s2_v,
     own_v,
+    r1_gate_v,
+    s2_gate,
+    grad_queries,
+    near,
     far_in,
     sums,
     query_home,
@@ -1284,15 +1291,18 @@
         mail.move(gate.at[:, own_half], gate_v),
         mail.move(gate_z, gate_zv),
         mail.move(up.at[:, own_half], up_v),
+        mail.move(up_z, up_zv),
     ]
+    small_loads = [mail.move(grad_queries_in, grad_queries), mail.move(near_in, near)]
     greet(spot.all)
     far_copy = mail.send(far, far_in, spot.x_peer)
     my_head = pl.ds(pl.multiple_of(spot.z * width, width), width)
+    for load in small_loads:
+        load.wait()
     query_copies = [
         mail.send(grad_queries.at[d], query_home.at[:, my_head], spot.ahead[line - d])
         for d in range(1, line)
     ]
-    up_copy = mail.send(up_far, up_zv, spot.z_peer)
     query_home[:, my_head] = grad_queries[0]
     for load in loads[:4]:
         load.wait()
@@ -1311,12 +1321,23 @@
         for d in range(1, line)
     ]
     pair_home[:, :, my_head] = sums[0]
-    up_copy.wait()
-    keep_up = mail.move(up_zv, out_up_z)
     ups = Job(spot, False, hidden_v, hidden_zv, up_v, up_zv, True)
     ups.send_terms(send_up)
     up_terms = mail.send(send_up, out_r1_up, ups.first_peer)
 
+    down_copy.wait()
+    loads = [
+        mail.move(down.span(r1_down, 1 - spot.z_high), r1_v),
+        mail.move(down.span(r1_down, spot.z_high), r1_own),
+    ]
+    loads[0].wait()
+    down.second_terms(r1_v, s2_v)
+    second_copy = mail.send(s2_v, out_r2_down, spot.far_peer)
+    gate_terms.wait()
+    gate_load = mail.move(gates.span(out_r1_gate, 1 - spot.z_high), r1_gate_v)
+    gate_load.wait()
+    gates.second_term(r1_gate_v, s2_gate, 0)
+    gate_second = mail.send(gates.at(s2_gate, 0), out_r2_gate, spot.far_peer)
     for copy in query_copies + pair_copies:
         copy.wait()
 
@@ -1369,14 +1390,6 @@
         raw_far[:, cut] = side(1 - spot.x)
     raw_copy = mail.send(raw_far, out_raw_x, spot.x_peer)
 
-    down_copy.wait()
-    loads = [
-        mail.move(down.span(r1_down, 1 - spot.z_high), r1_v),
-        mail.move(down.span(r1_down, spot.z_high), r1_own),
-    ]
-    loads[0].wait()
-    down.second_terms(r1_v, s2_v)
-    second_copy = mail.send(s2_v, out_r2_down, spot.far_peer)
     loads[1].wait()
 
     @pl.loop(0, 2)
@@ -1384,7 +1397,7 @@
         down.at(own_v, i)[...] = down.own_term(i, r1_own)
 
     keep_own = mail.move(own_v, out_own_down)
-    for copy in (gate_terms, up_terms, raw_copy, second_copy, keep_up, keep_own):
+    for copy in (gate_second, up_terms, raw_copy, second_copy, keep_own):
         copy.wait()
 
 
@@ -1403,14 +1416,14 @@
     shape = jax.ShapeDtypeStruct
     return pl.pallas_call(
         middle_kernel,
-        in_specs=vmem_specs(10) + [any_spec] * 10,
+        in_specs=[pl.BlockSpec(memory_space=pltpu.HBM)] * 3 + vmem_specs(7) + [any_spec] * 10,
         out_specs=[any_spec] * 7 + vmem_specs(3),
         out_shape=[
             shape((half, cut // 2), f32),
             shape((half, cut // 2), bf16),
             shape((cut, half), bf16),
             shape((cut, half), bf16),
-            shape((count, half), bf16),
+            shape((cut // 4, half), bf16),
             shape((count, 3 * columns // 2), bf16),
             shape((half, cut), bf16),
             shape((count, 3 * columns), bf16),
@@ -1435,6 +1448,10 @@
             pltpu.VMEM((half, cut // 2), bf16),
             pltpu.VMEM((half, cut // 2), bf16),
             pltpu.VMEM((half, cut // 2), f32),
+            pltpu.VMEM((cut // 2, half), bf16),
+            pltpu.VMEM((cut // 2, half), bf16),
+            pltpu.VMEM(grad_queries.shape, bf16),
+            pltpu.VMEM(near.shape, bf16),
             pltpu.VMEM(near.shape, bf16),
             pltpu.VMEM(near.shape, bf16),
             pltpu.VMEM((count, columns), bf16),
@@ -1474,6 +1491,7 @@
     r2_down,
     r1_gate,
     r1_up,
+    r2_gate_in,
     w_query,
     w_key,
     w_value,
@@ -1572,6 +1590,7 @@
     gates = Job(spot, False, hidden_v, hidden_zv, gate_v, gate_zv, True)
     raws = Job(spot, True, tokens_v, tokens_xv, raw_own, raw_x, True)
     outs_job = Job(spot, True, heads_v, heads_xv, attn_v, attn_xv, False)
+    gate_arrived = mail.move(r2_gate_in, gates.at(r2_gate, 0))
     gate_second = mail.move(gates.span(r1_gate, 1 - spot.z_high), r1_wide.at[0])
     gate_own = mail.move(gates.span(r1_gate, spot.z_high), r1_wide.at[1])
     up_second = mail.move(ups.span(r1_up, 1 - spot.z_high), r1_wide.at[2])
@@ -1597,8 +1616,8 @@
 
     for load in (*first_loads, *gate_loads, gate_second):
         load.wait()
-    gates.second_terms(r1_wide.at[0], s2_gate)
-    gate_copy = mail.send(s2_gate, r2_gate, spot.far_peer)
+    gates.second_term(r1_wide.at[0], s2_gate, 1)
+    gate_copy = mail.send(gates.at(s2_gate, 1), gates.at(r2_gate, 1), spot.far_peer)
     for load in (*up_loads, up_second):
         load.wait()
     ups.second_terms(r1_wide.at[2], s2_up)
@@ -1658,6 +1677,14 @@
     outs_job.send_terms(send_out)
     out_copy = mail.send(send_out, r1_out, outs_job.first_peer)
 
+    def final_of(job, r1_own, r2):
+        return lambda side: job.own_term(side, r1_own) + job.at(r2, side)[...].astype(f32)
+
+    for load in (gate_own, gate_arrived):
+        load.wait()
+    gate_copy.wait()
+    finish(gates, final_of(gates, r1_wide.at[1], r2_gate), fin_gate, far_gate, keep_gate, near_gate)
+
     hidden_load.wait()
     for s in range(2):
         flying["y", s].wait()
@@ -1672,9 +1699,6 @@
     for d in range(1, line):
         gain_copies.append(mail.send(out_wide, wide_z.at[d - 1], spot.ahead[d]))
         gain_copies.append(mail.send(out_narrow, narrow_z.at[d - 1], spot.ahead[d]))
-
-    def final_of(job, r1_own, r2):
-        return lambda side: job.own_term(side, r1_own) + job.at(r2, side)[...].astype(f32)
 
     raw_copy.wait()
     raw_loads = [
@@ -1694,10 +1718,6 @@
         load.wait()
     outs_job.second_terms(r1_out_v.at[0], s2_out)
     second_out = mail.send(s2_out, r2_out, spot.far_peer)
-    gate_own.wait()
-    gate_copy.wait()
-    finish(gates, final_of(gates, r1_wide.at[1], r2_gate), fin_gate, far_gate, keep_gate, near_gate)
-
     up_own.wait()
     second_up.wait()
     finish(ups, final_of(ups, r1_wide.at[3], r2_up), fin_up, far_up, keep_up, near_up)
@@ -1819,6 +1839,76 @@
     )(*small, *large)
 
 
+def join_kernel(*refs):
+    sources, out_output, out_tokens = refs[:12], refs[12], refs[13]
+    outs, parts, sems = refs[14:21], refs[21:33], refs[33]
+    nears, fars = parts[:5], parts[5:10]
+    loads = [
+        pltpu.make_async_copy(source, part, sems.at[i])
+        for i, (source, part) in enumerate(zip(sources, parts))
+    ]
+    for load in loads[10:] + loads[:10]:
+        load.start()
+    copies = []
+    for i, target in ((10, out_output), (11, out_tokens)):
+        loads[i].wait()
+        copies.append(pltpu.make_async_copy(parts[i], target, sems.at[i + 2]))
+        copies[-1].start()
+    for load in loads[:10]:
+        load.wait()
+    spot = lax.axis_index("dp")
+    x = lax.rem(spot, 2)
+    z_low = lax.rem(spot // 2, 2)
+
+    def place(out, near, far, side, axis):
+        size = near.shape[axis]
+        for value, index in ((near, side), (far.astype(jnp.float32), 1 - side)):
+            cut = pl.ds(pl.multiple_of(index * size, size), size)
+            if axis == 0:
+                out[cut, :] = value
+            else:
+                out[:, cut] = value
+
+    place(outs[6], nears[0][...], fars[0][...], x, 0)
+    place(outs[4], nears[1][...], fars[1][...], z_low, 1)
+    place(outs[5], nears[2][...], fars[2][...], z_low, 1)
+    width = nears[3].shape[1] // 3
+    for which in range(3):
+        cut = slice(which * width, (which + 1) * width)
+        place(outs[which], nears[3][:, cut], fars[3][:, cut], x, 1)
+    place(outs[3], nears[4][...], fars[4][...], x, 0)
+    for copy in copies:
+        copy.wait()
+
+
+def join(nears, fars, output, tokens):
+    f32 = jnp.float32
+    shape = jax.ShapeDtypeStruct
+    any_spec = pl.BlockSpec(memory_space=pl.ANY)
+    far_spec = pl.BlockSpec(memory_space=pltpu.HBM)
+    down, gate, up, raw, out = [part.shape for part in nears]
+    third = shape((raw[0], 2 * raw[1] // 3), f32)
+    return pl.pallas_call(
+        join_kernel,
+        in_specs=[far_spec] * 12,
+        out_specs=[any_spec] * 2 + vmem_specs(7),
+        out_shape=[
+            shape(output.shape, output.dtype),
+            shape(tokens.shape, tokens.dtype),
+            third,
+            third,
+            third,
+            shape((2 * out[0], out[1]), f32),
+            shape((gate[0], 2 * gate[1]), f32),
+            shape((up[0], 2 * up[1]), f32),
+            shape((2 * down[0], down[1]), f32),
+        ],
+        scratch_shapes=[pltpu.VMEM(part.shape, part.dtype) for part in (*nears, *fars, output, tokens)]
+        + [pltpu.SemaphoreType.DMA((14,))],
+        compiler_params=pltpu.CompilerParams(vmem_limit_bytes=60 << 20),
+    )(*nears, *fars, output, tokens)
+
+
 def on_device_lines(
     tokens,
     cotangent,
@@ -1870,10 +1960,6 @@
         width = value.shape[1] // 2
         return lax.dynamic_slice_in_dim(value, side * width, width, 1)
 
-    def join_halves(near, far, axis, side):
-        low = jnp.where(side == 0, near, far)
-        return jnp.concatenate([low, jnp.where(side == 0, far, near)], axis=axis)
-
     positions = reorder(offsets[0] + jnp.arange(row_count, dtype=jnp.int32))
     labels = reorder(row_ids[0] * key_rows + doc_ids)
     freqs = rope_base ** (-jnp.arange(0, head_width // 2, dtype=f32) * 2.0 / head_width)
@@ -1933,6 +2019,7 @@
     ) = block(
         attended_out, w_output, g_attn, g_mlp, tokens, cotangent, w_gate, w_up, w_down
     )
+    grad_up_z = line_flip(grad_up_far, 1)
     back = attend_back(
         live, code_columns, code_rows, queries_n, keys_n, pairs, turned, log_total, grads
     )
@@ -1941,7 +2028,7 @@
         r2_down,
         r1_gate,
         r1_up,
-        grad_up_z,
+        r2_gate,
         raw_x,
         _,
         raw,
@@ -1959,7 +2046,7 @@
             grad_gate,
             grad_gate_z,
             grad_up,
-            grad_up_far,
+            grad_up_z,
         ),
     )
     results = last(
@@ -1978,15 +2065,14 @@
             r2_down,
             r1_gate,
             r1_up,
+            r2_gate,
             w_query,
             w_key,
             w_value,
             grad_hidden,
         ),
     )
-    down_near, gate_near, up_near, raw_near, out_near = results[:5]
-    down_far, gate_far, up_far, raw_far, out_far = [part.astype(f32) for part in results[5:10]]
-    grad_tokens = results[10]
+    joined = join(results[:5], results[5:10], output, results[10])
     wide, narrow = results[13:]
     gains = jnp.concatenate([wide.reshape(2 * model_width), narrow.reshape(2 * local_width)])
     piece = head_width // (line * pair)
@@ -1996,22 +2082,8 @@
         return lax.dynamic_slice_in_dim(part, spot * piece, piece, 1)
 
     all_heads = model_width // head_width
-    part_width = local_width // pair
-
-    def raw_result(index):
-        cut = slice(index * part_width, (index + 1) * part_width)
-        return join_halves(raw_near[:, cut], raw_far[:, cut], 1, x)
-
     return (
-        output,
-        grad_tokens,
-        raw_result(0),
-        raw_result(1),
-        raw_result(2),
-        join_halves(out_near, out_far, 0, x),
-        join_halves(gate_near, gate_far, 1, z_low),
-        join_halves(up_near, up_far, 1, z_low),
-        join_halves(down_near, down_far, 0, x),
+        *joined,
         gain_piece(2 * model_width, heads_here),
         gain_piece(2 * model_width + local_width, heads_here),
         gain_piece(0, all_heads),

time: 543 us -> 518 us (0.954)
  Pallas kernels: 499 us -> 483 us
  other arithmetic: 12.9 us -> 2.82 us
    pallas_call x1, Pallas kernels: 162 us -> 135 us  [last(): pl.pallas_call(last_kernel, in_specs=vmem_specs(6) + [any_spec] * len(lar...]
    concatenate x7 -> x0, other arithmetic: 7.81 us -> none  [join_halves(): return jnp.concatenate([low, jnp.where(side == 0, far, near)], axis=axis)]
    pallas_call x1, Pallas kernels: 12.6 us -> 19.8 us  [attend_back(): pl.pallas_call(functools.partial(attend_back_kernel, factor, scale), out_...]
    unnamed x60 -> x34, local copies, waits for them, and re-layouts: 18.8 us -> 13.8 us
    pallas_call x1 -> x2, Pallas kernels: 157 us -> 159 us  [the longest x1 150 us: middle(): pl.pallas_call(middle_kernel, in_specs=[pl.BlockSpec(memory_space=pltpu.H...]
  transfers between devices with their start and end apart: 0 -> 1, of which waited for: 0 -> 0; matrix products, arithmetic and copies ran while one was open for 0% -> 0% of each run, Pallas kernels for 0% -> 4%
where the time goes in v6:
time: 518 us; the launch traced here: 509 us
  Pallas kernels  483 us (93%)
  local copies, waits for them, and re-layouts  18.7 us (4%)
    pallas_call x1, Pallas kernels, middle(): pl.pallas_call(middle_kernel, in_specs=[pl.BlockSpec(memory_space=pltpu.H...  150 us
    pallas_call x1, Pallas kernels, last(): pl.pallas_call(last_kernel, in_specs=vmem_specs(6) + [any_spec] * len(lar...  135 us
    pallas_call x1, Pallas kernels, block(): pl.pallas_call(block_kernel, out_shape=[jax.ShapeDtypeStruct((rows, colum...  106 us
    pallas_call x1, Pallas kernels, project(): pl.pallas_call(project_kernel, in_specs=[pl.BlockSpec(memory_space=pl.ANY...  46.2 us
    pallas_call x1, Pallas kernels, attend_back(): pl.pallas_call(functools.partial(attend_back_kernel, factor, scale), out_...  19.8 us
    pallas_call x1, Pallas kernels, attend(): pl.pallas_call(functools.partial(attend_kernel, factor, key_rows), out_sh...  16 us
    unnamed x34, local copies, waits for them, and re-layouts  13.8 us
  transfers between devices with their start and end apart: 1, of which 0 were waited for; matrix products, arithmetic and copies ran while one was open for 0% of the time, Pallas kernels for 4%

profile of v6, /device:TPU:0, one launch (start us, length us, event | category | flops | bytes accessed | tf_op | source)
XLA Modules:
  0.0 508.8 jit_solution(7568832794600593789)
XLA Ops:
  0.6 0.0 copy-start.9
  0.7 0.0 copy-start.8
  2.0 0.7 broadcast_add_fusion
  2.7 0.1 fusion.5
  2.8 1.0 fusion
  3.8 0.1 pad_maximum_fusion.cosines
  4.0 0.0 copy-start.1
  4.0 0.1 pad_maximum_fusion.1.sines
  4.2 0.0 copy-start
  4.2 0.0 copy-done.9
  4.2 0.0 copy-done.8
  4.2 46.2 %shard_map.255 = (bf16[4,512,128]{2,1,0:T(8,128)(2,1)S(1)}, bf16[8,2,512,128]{3,2,1,0:T(8,128)(2,1)S(1)}, f32[8,4,512]{2,1,0:T(4,128)S(1)}, f32[512,512]{1,0:T(8,128)S(1)}, f32[512,512]{1,0:T(8,128)S(1)}) custom-call(bf16[512,2048]{1,0:T(8,128)(2,1)} %tokens.5, bf16[2048,512]{1,0:T(8,128)(2,1)} %w_query.1, bf16[2048,512]{1,0:T(8,128)(2,1)} %w_key.1, ...), custom_call_target="tpu_custom_call" | custom-call | tf_op jit(solution)/shard_map/pallas_call | solution.py:552
  50.4 0.0 copy-done.1
  50.4 0.0 copy-done
  50.4 0.0 copy-start.2
  50.4 1.0 copy-done.2
  51.4 0.0 copy-start.3
  51.4 1.0 copy-done.3
  52.4 0.2 multiply_reduce_fusion
  52.5 0.4 fusion.2
  52.9 0.2 slice_reduce_fusion
  53.1 0.1 and_convert_fusion.live
  53.2 16.0 %shard_map.256 = (f32[4,128,512]{2,1,0:T(8,128)S(1)}, f32[8,512]{1,0:T(8,128)S(1)}, bf16[4,512,128]{2,1,0:T(8,128)(2,1)S(1)}, bf16[8,512,128]{2,1,0:T(8,128)(2,1...) custom-call(s32[4,8]{1,0:T(4,128)S(1)} %and_convert_fusion.live, ...), custom_call_target="tpu_custom_call" | custom-call | tf_op jit(solution)/shard_map/pallas_call | solution.py:681
  69.2 0.0 copy-start.6
  69.2 0.8 copy-done.6
  70.0 0.0 copy-start.10
  70.0 1.3 copy-done.10
  71.3 0.0 copy-start.12
  71.4 1.0 copy-done.12
  72.3 0.0 copy-start.14
  72.3 1.0 copy-done.14
  73.3 106.2 %shard_map.257 = (bf16[512,512]{1,0:T(8,128)(2,1)}, bf16[512,2048]{1,0:T(8,128)(2,1)}, bf16[512,2048]{1,0:T(8,128)(2,1)}, bf16[512,2048]{1,0:T(8,128)(2,1)}, bf1...) custom-call(bf16[4,512,128]{2,1,0:T(8,128)(2,1)} %copy-done.6, ...), custom_call_target="tpu_custom_call" | custom-call | tf_op jit(solution)/shard_map/pallas_call | solution.py:1048
  179.5 2.2 collective-permute-start
  181.7 0.6 slice_bitcast_fusion.factors
  182.3 0.0 copy-start.11
  182.3 1.6 copy-done.11
  183.9 0.0 copy-start.13
  183.9 1.2 copy-done.13
  185.1 0.0 copy-start.15
  185.1 1.2 copy-done.15
  186.3 0.0 copy-start.16
  186.3 1.0 copy-done.16
  187.4 19.8 %shard_map.258 = (bf16[4,512,128]{2,1,0:T(8,128)(2,1)S(1)}, bf16[4,2,512,128]{3,2,1,0:T(8,128)(2,1)S(1)}, bf16[4,2,512,128]{3,2,1,0:T(8,128)(2,1)S(1)}) custom-call(s32[4,8]{1,0:T(4,128)S(1)} %and_convert_fusion.live, s32[8,512,128]{2,1,0:T(8,128)S(1)} %copy-done.11, s32[8,512]{1,0:T(8,128)S(1)} %get-tuple-element.80.rows, ...), custom_call_target="tpu_custom_call" | custom-call | flops 10737418240 | bytes 12582912 | tf_op jit(solution)/shard_map/pallas_call | solution.py:709
  207.2 0.0 copy-start.4
  207.2 1.0 copy-done.4
  208.1 0.0 copy-start.5
  208.1 1.0 copy-done.5
  209.1 0.0 copy-start.7
  209.1 0.8 copy-done.7
  209.9 0.0 collective-permute-done.up_z
  209.9 149.7 %shard_map.259 = (f32[1024,512]{1,0:T(8,128)}, bf16[1024,512]{1,0:T(8,128)(2,1)}, bf16[1024,1024]{1,0:T(8,128)(2,1)}, bf16[1024,1024]{1,0:T(8,128)(2,1)}, bf16[2...) custom-call(bf16[4,512,128]{2,1,0:T(8,128)(2,1)} %copy-done.7, ...), custom_call_target="tpu_custom_call" | custom-call | tf_op jit(solution)/shard_map/pallas_call | solution.py:1417
  359.6 135.2 %shard_map.260 = (f32[1024,256]{1,0:T(8,128)}, f32[256,1024]{1,0:T(8,128)}, f32[256,1024]{1,0:T(8,128)}, f32[256,768]{1,0:T(8,128)}, f32[256,256]{1,0:T(8,128)},...) custom-call(bf16[512,1536]{1,0:T(8,128)(2,1)} %get-tuple-element.102, ...), custom_call_target="tpu_custom_call" | custom-call | tf_op jit(solution)/shard_map/pallas_call | solution.py:1759
  494.9 0.8 fusion.4
  495.6 0.7 constant_dynamic-slice_fusion.2
  496.3 0.6 constant_dynamic-slice_fusion.3
  496.9 0.8 fusion.3
  497.7 0.7 constant_dynamic-slice_fusion
  498.4 0.7 constant_dynamic-slice_fusion.1
  499.1 9.4 %shard_map.261 = (bf16[512,2048]{1,0:T(8,128)(2,1)}, bf16[512,2048]{1,0:T(8,128)(2,1)}, f32[256,512]{1,0:T(8,128)}, f32[256,512]{1,0:T(8,128)}, f32[256,512]{1,0...) custom-call(f32[1024,256]{1,0:T(8,128)} %get-tuple-element.116.refs_0_, ...), custom_call_target="tpu_custom_call" | custom-call | tf_op jit(solution)/shard_map/pallas_call | solution.py:1891
  (9 shorter events, 0.1 us)
Async XLA Ops:
  0.6 3.5 copy-start.9
  0.7 3.5 copy-start.8
  4.0 46.4 %copy-start.1 = (f32[512,128]{1,0:T(8,128)}, f32[512,128]{1,0:T(8,128)S(1)}, u32[]{:S(2)}) copy-start(f32[512,128]{1,0:T(8,128)S(1)} %pad_maximum_fusion.cosines) | copy-start | bytes 786436
  4.2 46.3 %copy-start = (f32[512,128]{1,0:T(8,128)}, f32[512,128]{1,0:T(8,128)S(1)}, u32[]{:S(2)}) copy-start(f32[512,128]{1,0:T(8,128)S(1)} %pad_maximum_fusion.1.sines) | copy-start | bytes 786436
  50.4 1.0 copy-start.2
  51.4 1.0 copy-start.3
  69.2 0.8 copy-start.6
  70.0 1.3 copy-start.10
  71.3 1.0 copy-start.12
  72.3 1.0 copy-start.14
  179.5 30.4 %collective-permute-start = (bf16[512,1024]{1,0:T(8,128)(2,1)}, bf16[512,1024]{1,0:T(8,128)(2,1)}, u32[]{:S(2)}, u32[]{:S(2)}) collective-permute-start(bf16[512,1024]{1,0:T(8,128)(2,1)} %get-tuple-element.101), channel_id=1, source_target_pairs={{0,8},{4,12},{8,0},{12,4},{16,24},{20,28},{24,16},{28,20},{1,9},{5... | collective-permute-start | bytes 3145736 | tf_op jit(solution)/shard_map/ppermute | solution.py:340
  182.3 1.6 copy-start.11
  183.9 1.2 copy-start.13
  185.1 1.2 copy-start.15
  186.3 1.0 copy-start.16
  207.2 1.0 copy-start.4
  208.1 1.0 copy-start.5
  209.1 0.8 copy-start.7

commit v7 on v6

--- a/solution.py
+++ b/solution.py
@@ -609,10 +609,10 @@
         top[...] = jnp.full_like(top, start_max)
         total[...] = jnp.zeros_like(total)
         accum[...] = jnp.zeros_like(accum)
-        for k in range(2 * line):
-
+        @pl.loop(0, 2 * line)
+        def _(k, q=q):
             @pl.when(live[q, k] > 0)
-            def _(q=q, k=k):
+            def _():
                 scores = visible_scores(
                     out_key[k],
                     out_query[q],
@@ -644,10 +644,10 @@
     for q in range(line):
         query_sum[...] = jnp.zeros_like(query_sum)
         delta = jnp.sum(grads[q].astype(f32).T * turned[q], axis=0, keepdims=True)
-        for k in range(2 * line):
-
+        @pl.loop(0, 2 * line)
+        def _(k, q=q, delta=delta):
             @pl.when(live[q, k] > 0)
-            def _(q=q, k=k, delta=delta):
+            def _():
                 query, key, grad = queries[q], keys[k], grads[q]
                 scores = visible_scores(
                     key,
@@ -1182,14 +1182,24 @@
             return (2 * high + self.spot.z_low) * pair + index
         return (2 * high + index) * pair + self.spot.x
 
-    def send_terms(self, target):
-        @pl.loop(0, line)
+    def make_half(self, target, high):
+        @pl.loop(0, 2)
         def _(i):
             if self.over_x:
-                index = (i // 2) * 4 + (1 - self.spot.z_low) * 2 + lax.rem(i, 2)
+                index = (2 * high + 1 - self.spot.z_low) * pair + i
             else:
-                index = i * pair + 1 - self.spot.x
-            self.at(target, i)[...] = self.term(index).astype(jnp.bfloat16)
+                index = (2 * high + i) * pair + 1 - self.spot.x
+            self.at(target, 2 * high + i)[...] = self.term(index).astype(jnp.bfloat16)
+
+    def send_half(self, mail, target, remote, high):
+        return mail.send(self.span(target, high), self.span(remote, high), self.first_peer)
+
+    def start_first(self, mail, target, remote):
+        copies = []
+        for high in (1 - self.spot.z_high, self.spot.z_high):
+            self.make_half(target, high)
+            copies.append(self.send_half(mail, target, remote, high))
+        return copies
 
     def second_term(self, arrived, target, i):
         total = self.term(self.block_of(1 - self.spot.z_high, i))
@@ -1307,14 +1317,15 @@
     for load in loads[:4]:
         load.wait()
     down = Job(spot, True, act_v, act_zv, mlp_v, mlp_zv, False)
-    down.send_terms(send_down)
-    down_copy = mail.send(send_down, r1_down, down.first_peer)
+    down_first = down.start_first(mail, send_down, r1_down)
     for load in loads[4:]:
         load.wait()
     gates = Job(spot, False, hidden_v, hidden_zv, gate_v, gate_zv, True)
-    gates.send_terms(send_gate)
+    both = (1 - spot.z_high, spot.z_high)
+    for high in both:
+        gates.make_half(send_gate, high)
     far_copy.wait()
-    gate_terms = mail.send(send_gate, out_r1_gate, gates.first_peer)
+    gate_first = [gates.send_half(mail, send_gate, out_r1_gate, high) for high in both]
     sums[...] = (near[...].astype(f32) + far_in[...].astype(f32)).astype(bf16)
     pair_copies = [
         mail.send(sums.at[d], pair_home.at[:, :, my_head], spot.ahead[line - d])
@@ -1322,22 +1333,18 @@
     ]
     pair_home[:, :, my_head] = sums[0]
     ups = Job(spot, False, hidden_v, hidden_zv, up_v, up_zv, True)
-    ups.send_terms(send_up)
-    up_terms = mail.send(send_up, out_r1_up, ups.first_peer)
-
-    down_copy.wait()
-    loads = [
-        mail.move(down.span(r1_down, 1 - spot.z_high), r1_v),
-        mail.move(down.span(r1_down, spot.z_high), r1_own),
-    ]
-    loads[0].wait()
+    up_first = ups.start_first(mail, send_up, out_r1_up)
+
+    down_first[0].wait()
+    down_load = mail.move(down.span(r1_down, 1 - spot.z_high), r1_v)
+    down_load.wait()
     down.second_terms(r1_v, s2_v)
     second_copy = mail.send(s2_v, out_r2_down, spot.far_peer)
-    gate_terms.wait()
+    gate_first[0].wait()
     gate_load = mail.move(gates.span(out_r1_gate, 1 - spot.z_high), r1_gate_v)
     gate_load.wait()
-    gates.second_term(r1_gate_v, s2_gate, 0)
-    gate_second = mail.send(gates.at(s2_gate, 0), out_r2_gate, spot.far_peer)
+    gates.second_terms(r1_gate_v, s2_gate)
+    gate_second = mail.send(s2_gate, out_r2_gate, spot.far_peer)
     for copy in query_copies + pair_copies:
         copy.wait()
 
@@ -1390,14 +1397,16 @@
         raw_far[:, cut] = side(1 - spot.x)
     raw_copy = mail.send(raw_far, out_raw_x, spot.x_peer)
 
-    loads[1].wait()
+    down_first[1].wait()
+    own_load = mail.move(down.span(r1_down, spot.z_high), r1_own)
+    own_load.wait()
 
     @pl.loop(0, 2)
     def _(i):
         down.at(own_v, i)[...] = down.own_term(i, r1_own)
 
     keep_own = mail.move(own_v, out_own_down)
-    for copy in (gate_second, up_terms, raw_copy, second_copy, keep_own):
+    for copy in (gate_second, gate_first[1], *up_first, raw_copy, second_copy, keep_own):
         copy.wait()
 
 
@@ -1423,7 +1432,7 @@
             shape((half, cut // 2), bf16),
             shape((cut, half), bf16),
             shape((cut, half), bf16),
-            shape((cut // 4, half), bf16),
+            shape((cut // 2, half), bf16),
             shape((count, 3 * columns // 2), bf16),
             shape((half, cut), bf16),
             shape((count, 3 * columns), bf16),
@@ -1461,9 +1470,9 @@
             pltpu.VMEM((2, count), f32),
             pltpu.VMEM((2, count), f32),
             pltpu.VMEM((2, count), f32),
-            pltpu.SemaphoreType.DMA((16,)),
-            pltpu.SemaphoreType.DMA((16,)),
-            pltpu.SemaphoreType.DMA((16,)),
+            pltpu.SemaphoreType.DMA((28,)),
+            pltpu.SemaphoreType.DMA((28,)),
+            pltpu.SemaphoreType.DMA((28,)),
         ],
         compiler_params=pltpu.CompilerParams(
             vmem_limit_bytes=60 << 20, collective_id=3, has_side_effects=True
@@ -1522,7 +1531,6 @@
         r1_wide,
         r1_raw_v,
         r1_out_v,
-        s2_gate,
         s2_up,
         s2_raw,
         s2_out,
@@ -1590,8 +1598,7 @@
     gates = Job(spot, False, hidden_v, hidden_zv, gate_v, gate_zv, True)
     raws = Job(spot, True, tokens_v, tokens_xv, raw_own, raw_x, True)
     outs_job = Job(spot, True, heads_v, heads_xv, attn_v, attn_xv, False)
-    gate_arrived = mail.move(r2_gate_in, gates.at(r2_gate, 0))
-    gate_second = mail.move(gates.span(r1_gate, 1 - spot.z_high), r1_wide.at[0])
+    gate_second = mail.move(r2_gate_in, r2_gate)
     gate_own = mail.move(gates.span(r1_gate, spot.z_high), r1_wide.at[1])
     up_second = mail.move(ups.span(r1_up, 1 - spot.z_high), r1_wide.at[2])
     up_own = mail.move(ups.span(r1_up, spot.z_high), r1_wide.at[3])
@@ -1606,23 +1613,33 @@
     heads_copy = mail.send(heads_far, heads_xv, spot.x_peer)
     for load in token_loads:
         load.wait()
-    raws.send_terms(send_raw)
-    raw_copy = mail.send(send_raw, r1_raw, raws.first_peer)
+    raw_first = raws.start_first(mail, send_raw, r1_raw)
     wide_copy.wait()
     out_wide[...] = wide[...] + wide_core[...]
     out_narrow[...] = narrow[...]
     wide_x_copy = mail.send(out_wide, wide_x, spot.x_peer)
     narrow_x_copy = mail.send(out_narrow, narrow_x, spot.x_peer)
 
-    for load in (*first_loads, *gate_loads, gate_second):
-        load.wait()
-    gates.second_term(r1_wide.at[0], s2_gate, 1)
-    gate_copy = mail.send(gates.at(s2_gate, 1), gates.at(r2_gate, 1), spot.far_peer)
-    for load in (*up_loads, up_second):
+    for load in (*first_loads, *up_loads, up_second):
         load.wait()
     ups.second_terms(r1_wide.at[2], s2_up)
     second_up = mail.send(s2_up, r2_up, spot.far_peer)
 
+    for s in range(2):
+        attn_copies[s].wait()
+    attn_core = [
+        mail.send(attn_xv.at[own(s)], attn_xv.at[other(s)], spot.core_peer) for s in range(2)
+    ]
+    for copy in attn_core:
+        copy.wait()
+    heads_copy.wait()
+    out_first = outs_job.start_first(mail, send_out, r1_out)
+
+    raw_first[0].wait()
+    raw_load = mail.move(raws.span(r1_raw, 1 - spot.z_high), r1_raw_v.at[0])
+    raw_load.wait()
+    raws.second_terms(r1_raw_v.at[0], s2_raw)
+    second_raw = mail.send(s2_raw, r2_raw, spot.far_peer)
     input_weights = (w_query, w_key, w_value)
     columns = w_query.shape[1]
     flying = {}
@@ -1641,6 +1658,10 @@
         y_send[s] = (total[own(s), :] + part_recv[s].astype(f32)).astype(bf16)
         flying["y", s] = mail.send(y_send.at[s], y_recv.at[s], spot.y_peer)
 
+    wide_x_copy.wait()
+    narrow_x_copy.wait()
+    out_wide[...] = out_wide[...] + wide_x[...]
+    out_narrow[...] = out_narrow[...] + narrow_x[...]
     near_copies, far_copies = [], []
 
     def finish(job, value_of, fin, far, keep, target):
@@ -1662,27 +1683,24 @@
         near_down,
     )
 
-    wide_x_copy.wait()
-    narrow_x_copy.wait()
-    out_wide[...] = out_wide[...] + wide_x[...]
-    out_narrow[...] = out_narrow[...] + narrow_x[...]
-    for s in range(2):
-        attn_copies[s].wait()
-    attn_core = [
-        mail.send(attn_xv.at[own(s)], attn_xv.at[other(s)], spot.core_peer) for s in range(2)
+    out_first[0].wait()
+    out_load = mail.move(outs_job.span(r1_out, 1 - spot.z_high), r1_out_v.at[0])
+    out_load.wait()
+    outs_job.second_terms(r1_out_v.at[0], s2_out)
+    second_out = mail.send(s2_out, r2_out, spot.far_peer)
+    raw_first[1].wait()
+    out_first[1].wait()
+    own_loads = [
+        mail.move(raws.span(r1_raw, spot.z_high), r1_raw_v.at[1]),
+        mail.move(outs_job.span(r1_out, spot.z_high), r1_out_v.at[1]),
     ]
-    for copy in attn_core:
-        copy.wait()
-    heads_copy.wait()
-    outs_job.send_terms(send_out)
-    out_copy = mail.send(send_out, r1_out, outs_job.first_peer)
-
+    for load in own_loads:
+        load.wait()
     def final_of(job, r1_own, r2):
         return lambda side: job.own_term(side, r1_own) + job.at(r2, side)[...].astype(f32)
 
-    for load in (gate_own, gate_arrived):
+    for load in (*gate_loads, gate_own, gate_second):
         load.wait()
-    gate_copy.wait()
     finish(gates, final_of(gates, r1_wide.at[1], r2_gate), fin_gate, far_gate, keep_gate, near_gate)
 
     hidden_load.wait()
@@ -1700,24 +1718,6 @@
         gain_copies.append(mail.send(out_wide, wide_z.at[d - 1], spot.ahead[d]))
         gain_copies.append(mail.send(out_narrow, narrow_z.at[d - 1], spot.ahead[d]))
 
-    raw_copy.wait()
-    raw_loads = [
-        mail.move(raws.span(r1_raw, 1 - spot.z_high), r1_raw_v.at[0]),
-        mail.move(raws.span(r1_raw, spot.z_high), r1_raw_v.at[1]),
-    ]
-    for load in raw_loads:
-        load.wait()
-    raws.second_terms(r1_raw_v.at[0], s2_raw)
-    second_raw = mail.send(s2_raw, r2_raw, spot.far_peer)
-    out_copy.wait()
-    out_loads = [
-        mail.move(outs_job.span(r1_out, 1 - spot.z_high), r1_out_v.at[0]),
-        mail.move(outs_job.span(r1_out, spot.z_high), r1_out_v.at[1]),
-    ]
-    for load in out_loads:
-        load.wait()
-    outs_job.second_terms(r1_out_v.at[0], s2_out)
-    second_out = mail.send(s2_out, r2_out, spot.far_peer)
     up_own.wait()
     second_up.wait()
     finish(ups, final_of(ups, r1_wide.at[3], r2_up), fin_up, far_up, keep_up, near_up)
@@ -1797,7 +1797,6 @@
             vmem(2, 2 * block, raw_half),
             vmem(2, heads_half, 2 * block),
             vmem(2 * block, half),
-            vmem(2 * block, half),
             vmem(2 * block, raw_half),
             vmem(heads_half, 2 * block),
             vmem(2 * block, half),

time: 518 us -> 495 us (0.956)
  Pallas kernels: 483 us -> 456 us
  waiting for transfers between devices: 0.01 us -> 5.54 us
    pallas_call x1, Pallas kernels: 135 us -> 121 us  [last(): pl.pallas_call(last_kernel, in_specs=vmem_specs(6) + [any_spec] * len(lar...]
    pallas_call x1, Pallas kernels: 19.8 us -> 9.63 us  [attend_back(): pl.pallas_call(functools.partial(attend_back_kernel, factor, scale), out_...]
    pallas_call x1, Pallas kernels: 16 us -> 9.7 us  [attend(): pl.pallas_call(functools.partial(attend_kernel, factor, key_rows), out_sh...]
    ppermute x1, waiting for transfers between devices: 0.01 us -> 5.54 us  [line_flip(): lax.ppermute(value, 'dp', [(z * pair + x, (z ^ bit) * pair + x) for z in...]
  transfers between devices with their start and end apart: 1 -> 1, of which waited for: 0 -> 1; matrix products, arithmetic and copies ran while one was open for 0% -> 0% of each run, Pallas kernels for 4% -> 2%
where the time goes in v7:
time: 495 us; the launch traced here: 488 us
  Pallas kernels  456 us (92%)
  local copies, waits for them, and re-layouts  18.7 us (4%)
  waiting for transfers between devices  5.54 us (1%)
    pallas_call x1, Pallas kernels, middle(): pl.pallas_call(middle_kernel, in_specs=[pl.BlockSpec(memory_space=pltpu.H...  153 us
    pallas_call x1, Pallas kernels, last(): pl.pallas_call(last_kernel, in_specs=vmem_specs(6) + [any_spec] * len(lar...  121 us
    pallas_call x1, Pallas kernels, block(): pl.pallas_call(block_kernel, out_shape=[jax.ShapeDtypeStruct((rows, colum...  107 us
    pallas_call x1, Pallas kernels, project(): pl.pallas_call(project_kernel, in_specs=[pl.BlockSpec(memory_space=pl.ANY...  46.2 us
    unnamed x34, local copies, waits for them, and re-layouts  13.8 us
  transfers between devices with their start and end apart: 1, of which 1 were waited for; matrix products, arithmetic and copies ran while one was open for 0% of the time, Pallas kernels for 2%

profile of v7, /device:TPU:0, one launch (start us, length us, event | category | flops | bytes accessed | tf_op | source)
XLA Modules:
  0.0 487.8 jit_solution(7866432325633363898)
XLA Ops:
  0.6 0.0 copy-start.9
  0.7 0.0 copy-start.8
  2.0 0.7 broadcast_add_fusion
  2.7 0.1 fusion.5
  2.8 1.0 fusion
  3.8 0.1 pad_maximum_fusion.cosines
  4.0 0.0 copy-start.1
  4.0 0.1 pad_maximum_fusion.1.sines
  4.2 0.0 copy-start
  4.2 0.0 copy-done.9
  4.2 0.0 copy-done.8
  4.2 46.2 %shard_map.255 = (bf16[4,512,128]{2,1,0:T(8,128)(2,1)S(1)}, bf16[8,2,512,128]{3,2,1,0:T(8,128)(2,1)S(1)}, f32[8,4,512]{2,1,0:T(4,128)S(1)}, f32[512,512]{1,0:T(8,128)S(1)}, f32[512,512]{1,0:T(8,128)S(1)}) custom-call(bf16[512,2048]{1,0:T(8,128)(2,1)} %tokens.5, bf16[2048,512]{1,0:T(8,128)(2,1)} %w_query.1, bf16[2048,512]{1,0:T(8,128)(2,1)} %w_key.1, ...), custom_call_target="tpu_custom_call" | custom-call | tf_op jit(solution)/shard_map/pallas_call | solution.py:552
  50.4 0.0 copy-done.1
  50.4 0.0 copy-done
  50.4 0.0 copy-start.2
  50.4 1.0 copy-done.2
  51.4 0.0 copy-start.3
  51.4 1.0 copy-done.3
  52.4 0.2 multiply_reduce_fusion
  52.5 0.4 fusion.2
  52.9 0.2 slice_reduce_fusion
  53.1 0.1 and_convert_fusion.live
  53.2 9.7 %shard_map.256 = (f32[4,128,512]{2,1,0:T(8,128)S(1)}, f32[8,512]{1,0:T(8,128)S(1)}, bf16[4,512,128]{2,1,0:T(8,128)(2,1)S(1)}, bf16[8,512,128]{2,1,0:T(8,128)(2,1...) custom-call(s32[4,8]{1,0:T(4,128)S(1)} %and_convert_fusion.live, ...), custom_call_target="tpu_custom_call" | custom-call | tf_op jit(solution)/shard_map/pallas_call | solution.py:681
  62.9 0.0 copy-start.6
  62.9 0.8 copy-done.6
  63.7 0.0 copy-start.10
  63.7 1.3 copy-done.10
  65.0 0.0 copy-start.12
  65.0 1.0 copy-done.12
  66.0 0.0 copy-start.14
  66.0 1.0 copy-done.14
  67.0 106.6 %shard_map.257 = (bf16[512,512]{1,0:T(8,128)(2,1)}, bf16[512,2048]{1,0:T(8,128)(2,1)}, bf16[512,2048]{1,0:T(8,128)(2,1)}, bf16[512,2048]{1,0:T(8,128)(2,1)}, bf1...) custom-call(bf16[4,512,128]{2,1,0:T(8,128)(2,1)} %copy-done.6, ...), custom_call_target="tpu_custom_call" | custom-call | tf_op jit(solution)/shard_map/pallas_call | solution.py:1048
  173.6 2.6 collective-permute-start
  176.2 0.6 slice_bitcast_fusion.factors
  176.8 0.0 copy-start.11
  176.8 1.6 copy-done.11
  178.4 0.0 copy-start.13
  178.4 1.2 copy-done.13
  179.6 0.0 copy-start.15
  179.6 1.2 copy-done.15
  180.8 0.0 copy-start.16
  180.8 1.0 copy-done.16
  181.8 9.6 %shard_map.258 = (bf16[4,512,128]{2,1,0:T(8,128)(2,1)S(1)}, bf16[4,2,512,128]{3,2,1,0:T(8,128)(2,1)S(1)}, bf16[4,2,512,128]{3,2,1,0:T(8,128)(2,1)S(1)}) custom-call(s32[4,8]{1,0:T(4,128)S(1)} %and_convert_fusion.live, s32[8,512,128]{2,1,0:T(8,128)S(1)} %copy-done.11, s32[8,512]{1,0:T(8,128)S(1)} %get-tuple-element.80.rows, ...), custom_call_target="tpu_custom_call" | custom-call | flops 10737418240 | bytes 12582912 | tf_op jit(solution)/shard_map/pallas_call | solution.py:709
  191.5 0.0 copy-start.4
  191.5 1.0 copy-done.4
  192.5 0.0 copy-start.5
  192.5 1.0 copy-done.5
  193.4 0.0 copy-start.7
  193.4 0.8 copy-done.7
  194.2 5.5 %collective-permute-done.up_z = bf16[512,1024]{1,0:T(8,128)(2,1)} collective-permute-done((bf16[512,1024]{1,0:T(8,128)(2,1)}, bf16[512,1024]{1,0:T(8,128)(2,1)}, u32[]{:S(2)}, u32[]{:S(2)}) %collective-permute-start) | collective-permute-done | bytes 1048608 | tf_op jit(solution)/shard_map/ppermute | solution.py:340
  199.8 153.3 %shard_map.259 = (f32[1024,512]{1,0:T(8,128)}, bf16[1024,512]{1,0:T(8,128)(2,1)}, bf16[1024,1024]{1,0:T(8,128)(2,1)}, bf16[1024,1024]{1,0:T(8,128)(2,1)}, bf16[5...) custom-call(bf16[4,512,128]{2,1,0:T(8,128)(2,1)} %copy-done.7, ...), custom_call_target="tpu_custom_call" | custom-call | tf_op jit(solution)/shard_map/pallas_call | solution.py:1426
  353.0 120.9 %shard_map.260 = (f32[1024,256]{1,0:T(8,128)}, f32[256,1024]{1,0:T(8,128)}, f32[256,1024]{1,0:T(8,128)}, f32[256,768]{1,0:T(8,128)}, f32[256,256]{1,0:T(8,128)},...) custom-call(bf16[512,1536]{1,0:T(8,128)(2,1)} %get-tuple-element.102, ...), custom_call_target="tpu_custom_call" | custom-call | tf_op jit(solution)/shard_map/pallas_call | solution.py:1759
  473.9 0.8 fusion.4
  474.7 0.7 constant_dynamic-slice_fusion.2
  475.3 0.6 constant_dynamic-slice_fusion.3
  476.0 0.8 fusion.3
  476.8 0.7 constant_dynamic-slice_fusion
  477.5 0.7 constant_dynamic-slice_fusion.1
  478.1 9.4 %shard_map.261 = (bf16[512,2048]{1,0:T(8,128)(2,1)}, bf16[512,2048]{1,0:T(8,128)(2,1)}, f32[256,512]{1,0:T(8,128)}, f32[256,512]{1,0:T(8,128)}, f32[256,512]{1,0...) custom-call(f32[1024,256]{1,0:T(8,128)} %get-tuple-element.116.refs_0_, ...), custom_call_target="tpu_custom_call" | custom-call | tf_op jit(solution)/shard_map/pallas_call | solution.py:1890
  (9 shorter events, 0.1 us)
Async XLA Ops:
  0.6 3.5 copy-start.9
  0.7 3.5 copy-start.8
  4.0 46.4 %copy-start.1 = (f32[512,128]{1,0:T(8,128)}, f32[512,128]{1,0:T(8,128)S(1)}, u32[]{:S(2)}) copy-start(f32[512,128]{1,0:T(8,128)S(1)} %pad_maximum_fusion.cosines) | copy-start | bytes 786436
  4.2 46.3 %copy-start = (f32[512,128]{1,0:T(8,128)}, f32[512,128]{1,0:T(8,128)S(1)}, u32[]{:S(2)}) copy-start(f32[512,128]{1,0:T(8,128)S(1)} %pad_maximum_fusion.1.sines) | copy-start | bytes 786436
  50.4 1.0 copy-start.2
  51.4 1.0 copy-start.3
  62.9 0.8 copy-start.6
  63.7 1.3 copy-start.10
  65.0 1.0 copy-start.12
  66.0 1.0 copy-start.14
  173.6 26.2 %collective-permute-start = (bf16[512,1024]{1,0:T(8,128)(2,1)}, bf16[512,1024]{1,0:T(8,128)(2,1)}, u32[]{:S(2)}, u32[]{:S(2)}) collective-permute-start(bf16[512,1024]{1,0:T(8,128)(2,1)} %get-tuple-element.101), channel_id=1, source_target_pairs={{0,8},{4,12},{8,0},{12,4},{16,24},{20,28},{24,16},{28,20},{1,9},{5... | collective-permute-start | bytes 3145736 | tf_op jit(solution)/shard_map/ppermute | solution.py:340
  176.8 1.6 copy-start.11
  178.4 1.2 copy-start.13
  179.6 1.2 copy-start.15
  180.8 1.0 copy-start.16
  191.5 1.0 copy-start.4
  192.5 1.0 copy-start.5
  193.4 0.8 copy-start.7

commit v8 on v7

--- a/solution.py
+++ b/solution.py
@@ -584,10 +584,23 @@
     return jnp.where((codes <= query_code) & (codes >= query_low), scores, low_score)
 
 
+def fill_keys(key_rows, notes, pairs, keys, codes):
+    count, width = keys.shape[1:]
+
+    def column(row):
+        return jnp.broadcast_to(row, (width, count)).T
+
+    for k in range(2 * line):
+        factor = column(notes[k, 1:2, :])
+        keys[k] = (pairs[k, 0].astype(jnp.float32) * factor).astype(jnp.bfloat16)
+        labels = column(notes[k, 2:3, :]).astype(jnp.int32)
+        codes[k] = labels * key_rows + column(notes[k, 3:4, :]).astype(jnp.int32)
+
+
 def attend_kernel(factor, key_rows, live, notes, *refs):
     queries, pairs = refs[:2]
-    out_turned, out_log, out_query, out_key, out_codes, out_rows, out = refs[2:9]
-    top, total, accum = refs[9:]
+    out_turned, out_log, out_query, out_rows, out = refs[2:7]
+    top, total, accum, out_key, out_codes = refs[7:]
     f32 = jnp.float32
     bf16 = jnp.bfloat16
     count, width = queries.shape[1:]
@@ -595,10 +608,7 @@
     def column(row):
         return jnp.broadcast_to(row, (width, count)).T
 
-    for k in range(2 * line):
-        out_key[k] = (pairs[k, 0].astype(f32) * column(notes[k, 1:2, :])).astype(bf16)
-        labels = column(notes[k, 2:3, :]).astype(jnp.int32)
-        out_codes[k] = labels * key_rows + column(notes[k, 3:4, :]).astype(jnp.int32)
+    fill_keys(key_rows, notes, pairs, out_key, out_codes)
     for q in range(line):
         out_query[q] = (queries[q].astype(f32) * column(notes[q, 0:1, :])).astype(bf16)
         base = notes[q, 2:3, :].astype(jnp.int32) * key_rows
@@ -634,9 +644,10 @@
         out[q] = turned.T.astype(bf16)
 
 
-def attend_back_kernel(factor, scale, live, codes, rows, queries, keys, *refs):
+def attend_back_kernel(factor, scale, key_rows, live, notes, rows, queries, *refs):
     pairs, turned, log_total, grads = refs[:4]
-    out_query, out_near, out_far, key_sum, value_sum, query_sum = refs[4:]
+    out_query, out_near, out_far, key_sum, value_sum, query_sum, keys, codes = refs[4:]
+    fill_keys(key_rows, notes, pairs, keys, codes)
     f32 = jnp.float32
     bf16 = jnp.bfloat16
     key_sum[...] = jnp.zeros_like(key_sum)
@@ -684,38 +695,40 @@
             jax.ShapeDtypeStruct((line, width, count), f32),
             jax.ShapeDtypeStruct((2 * line, count), f32),
             jax.ShapeDtypeStruct((line, count, width), bf16),
-            jax.ShapeDtypeStruct((2 * line, count, width), bf16),
-            jax.ShapeDtypeStruct((2 * line, count, width), jnp.int32),
             jax.ShapeDtypeStruct((2 * line, count), jnp.int32),
         ]
         + [jax.ShapeDtypeStruct((line, count, width), bf16)],
         in_specs=[pl.BlockSpec(memory_space=pltpu.SMEM)] + vmem_specs(3),
-        out_specs=vmem_specs(7),
+        out_specs=vmem_specs(5),
         scratch_shapes=[
             pltpu.VMEM((1, count), f32),
             pltpu.VMEM((1, count), f32),
             pltpu.VMEM((width, count), f32),
+            pltpu.VMEM((2 * line, count, width), bf16),
+            pltpu.VMEM((2 * line, count, width), jnp.int32),
         ],
         compiler_params=pltpu.CompilerParams(vmem_limit_bytes=40 << 20),
         cost_estimate=pl.CostEstimate(flops=0, bytes_accessed=0, transcendentals=0),
     )(live, notes, queries, pairs)
 
 
-def attend_back(live, codes, rows, queries, keys, pairs, turned, log_total, grads):
+def attend_back(key_rows, live, notes, rows, queries, pairs, turned, log_total, grads):
     _, count, width = queries.shape
     scale = 1.0 / math.sqrt(width)
     factor = math.log2(math.e) * scale
     f32 = jnp.float32
     return pl.pallas_call(
-        functools.partial(attend_back_kernel, factor, scale),
+        functools.partial(attend_back_kernel, factor, scale, key_rows),
         out_shape=[jax.ShapeDtypeStruct((line, count, width), jnp.bfloat16)]
         + [jax.ShapeDtypeStruct((line, 2, count, width), jnp.bfloat16)] * 2,
-        in_specs=[pl.BlockSpec(memory_space=pltpu.SMEM)] + vmem_specs(8),
+        in_specs=[pl.BlockSpec(memory_space=pltpu.SMEM)] + vmem_specs(7),
         out_specs=vmem_specs(3),
         scratch_shapes=[
             pltpu.VMEM((2 * line, count, width), f32),
             pltpu.VMEM((2 * line, count, width), f32),
             pltpu.VMEM((width, count), f32),
+            pltpu.VMEM((2 * line, count, width), jnp.bfloat16),
+            pltpu.VMEM((2 * line, count, width), jnp.int32),
         ],
         compiler_params=pltpu.CompilerParams(vmem_limit_bytes=40 << 20),
         cost_estimate=pl.CostEstimate(
@@ -723,7 +736,7 @@
             bytes_accessed=12 << 20,
             transcendentals=2 * line * line * count * count,
         ),
-    )(live, codes, rows, queries, keys, pairs, turned, log_total, grads)
+    )(live, notes, rows, queries, pairs, turned, log_total, grads)
 
 
 def block_kernel(
@@ -1839,44 +1852,51 @@
 
 
 def join_kernel(*refs):
-    sources, out_output, out_tokens = refs[:12], refs[12], refs[13]
-    outs, parts, sems = refs[14:21], refs[21:33], refs[33]
-    nears, fars = parts[:5], parts[5:10]
-    loads = [
-        pltpu.make_async_copy(source, part, sems.at[i])
-        for i, (source, part) in enumerate(zip(sources, parts))
-    ]
-    for load in loads[10:] + loads[:10]:
-        load.start()
-    copies = []
-    for i, target in ((10, out_output), (11, out_tokens)):
-        loads[i].wait()
-        copies.append(pltpu.make_async_copy(parts[i], target, sems.at[i + 2]))
-        copies[-1].start()
-    for load in loads[:10]:
-        load.wait()
+    nears, fars, whole = refs[:5], refs[5:10], refs[10:12]
+    outs, refs = refs[12:21], refs[21:]
+    stages, far_parts, whole_parts, sems = refs[:7], refs[7:12], refs[12:14], refs[14]
     spot = lax.axis_index("dp")
     x = lax.rem(spot, 2)
     z_low = lax.rem(spot // 2, 2)
-
-    def place(out, near, far, side, axis):
-        size = near.shape[axis]
-        for value, index in ((near, side), (far.astype(jnp.float32), 1 - side)):
-            cut = pl.ds(pl.multiple_of(index * size, size), size)
-            if axis == 0:
-                out[cut, :] = value
-            else:
-                out[:, cut] = value
-
-    place(outs[6], nears[0][...], fars[0][...], x, 0)
-    place(outs[4], nears[1][...], fars[1][...], z_low, 1)
-    place(outs[5], nears[2][...], fars[2][...], z_low, 1)
+    started = []
+
+    def move(source, target):
+        copy = pltpu.make_async_copy(source, target, sems.at[len(started)])
+        started.append(copy)
+        copy.start()
+        return copy
+
     width = nears[3].shape[1] // 3
-    for which in range(3):
-        cut = slice(which * width, (which + 1) * width)
-        place(outs[which], nears[3][:, cut], fars[3][:, cut], x, 1)
-    place(outs[3], nears[4][...], fars[4][...], x, 0)
-    for copy in copies:
+    plan = [(4, 1, None, z_low, 1), (5, 2, None, z_low, 1), (6, 0, None, x, 0)]
+    plan += [(i, 3, slice(i * width, (i + 1) * width), x, 1) for i in range(3)]
+    plan += [(3, 4, None, x, 0)]
+
+    def half(ref, side, axis):
+        size = ref.shape[axis] // 2
+        cut = pl.ds(pl.multiple_of(side * size, size), size)
+        return ref.at[cut, :] if axis == 0 else ref.at[:, cut]
+
+    whole_loads = [move(source, part) for source, part in zip(whole, whole_parts)]
+    far_loads, near_loads = {}, {}
+    for result, source, columns, side, axis in plan:
+        if source not in far_loads:
+            far_loads[source] = move(fars[source], far_parts[source])
+        near = nears[source] if columns is None else nears[source].at[:, columns]
+        near_loads[result] = move(near, half(stages[result], side, axis))
+    leaving = []
+    for load, part, out in zip(whole_loads, whole_parts, outs[:2]):
+        load.wait()
+        leaving.append(move(part, out))
+    waited = set()
+    for result, source, columns, side, axis in plan:
+        if source not in waited:
+            far_loads[source].wait()
+            waited.add(source)
+        far = far_parts[source][...] if columns is None else far_parts[source][:, columns]
+        half(stages[result], 1 - side, axis)[...] = far.astype(jnp.float32)
+        near_loads[result].wait()
+        leaving.append(move(stages[result], outs[2 + result]))
+    for copy in leaving:
         copy.wait()
 
 
@@ -1884,26 +1904,23 @@
     f32 = jnp.float32
     shape = jax.ShapeDtypeStruct
     any_spec = pl.BlockSpec(memory_space=pl.ANY)
-    far_spec = pl.BlockSpec(memory_space=pltpu.HBM)
     down, gate, up, raw, out = [part.shape for part in nears]
-    third = shape((raw[0], 2 * raw[1] // 3), f32)
+    third = (raw[0], 2 * raw[1] // 3)
+    results = [third] * 3 + [
+        (2 * out[0], out[1]),
+        (gate[0], 2 * gate[1]),
+        (up[0], 2 * up[1]),
+        (2 * down[0], down[1]),
+    ]
     return pl.pallas_call(
         join_kernel,
-        in_specs=[far_spec] * 12,
-        out_specs=[any_spec] * 2 + vmem_specs(7),
-        out_shape=[
-            shape(output.shape, output.dtype),
-            shape(tokens.shape, tokens.dtype),
-            third,
-            third,
-            third,
-            shape((2 * out[0], out[1]), f32),
-            shape((gate[0], 2 * gate[1]), f32),
-            shape((up[0], 2 * up[1]), f32),
-            shape((2 * down[0], down[1]), f32),
-        ],
-        scratch_shapes=[pltpu.VMEM(part.shape, part.dtype) for part in (*nears, *fars, output, tokens)]
-        + [pltpu.SemaphoreType.DMA((14,))],
+        in_specs=[any_spec] * 12,
+        out_specs=[any_spec] * 9,
+        out_shape=[shape(output.shape, output.dtype), shape(tokens.shape, tokens.dtype)]
+        + [shape(size, f32) for size in results],
+        scratch_shapes=[pltpu.VMEM(size, f32) for size in results]
+        + [pltpu.VMEM(part.shape, part.dtype) for part in (*fars, output, tokens)]
+        + [pltpu.SemaphoreType.DMA((24,))],
         compiler_params=pltpu.CompilerParams(vmem_limit_bytes=60 << 20),
     )(*nears, *fars, output, tokens)
 
@@ -1980,7 +1997,7 @@
         & (jnp.max(codes, axis=1)[None, :] >= jnp.min(lows, axis=1)[:, None])
     ).astype(jnp.int32)
 
-    turned, log_total, queries_n, keys_n, code_columns, code_rows, attended_out = attend(
+    turned, log_total, queries_n, code_rows, attended_out = attend(
         key_rows, live, notes, queries, pairs
     )
 
@@ -2020,7 +2037,7 @@
     )
     grad_up_z = line_flip(grad_up_far, 1)
     back = attend_back(
-        live, code_columns, code_rows, queries_n, keys_n, pairs, turned, log_total, grads
+        key_rows, live, notes, code_rows, queries_n, pairs, turned, log_total, grads
     )
     (
         own_down,

time: 495 us -> 491 us (level)
  local copies, waits for them, and re-layouts: 18.7 us -> 13.6 us
    unnamed x34 -> x26, local copies, waits for them, and re-layouts: 13.8 us -> 8.71 us
  transfers between devices with their start and end apart: 1 -> 1, of which waited for: 1 -> 1; matrix products, arithmetic and copies ran while one was open for 0% -> 0% of each run, Pallas kernels for 2% -> 3%
where the time goes in v8:
time: 491 us; the launch traced here: 485 us
  Pallas kernels  458 us (93%)
  local copies, waits for them, and re-layouts  13.6 us (3%)
  waiting for transfers between devices  5.72 us (1%)
    pallas_call x1, Pallas kernels, middle(): pl.pallas_call(middle_kernel, in_specs=[pl.BlockSpec(memory_space=pltpu.H...  153 us
    pallas_call x1, Pallas kernels, last(): pl.pallas_call(last_kernel, in_specs=vmem_specs(6) + [any_spec] * len(lar...  121 us
    pallas_call x1, Pallas kernels, block(): pl.pallas_call(block_kernel, out_shape=[jax.ShapeDtypeStruct((rows, colum...  107 us
    pallas_call x1, Pallas kernels, project(): pl.pallas_call(project_kernel, in_specs=[pl.BlockSpec(memory_space=pl.ANY...  46.2 us
    pallas_call x1, Pallas kernels, attend_back(): pl.pallas_call(functools.partial(attend_back_kernel, factor, scale, key_r...  12.3 us
    pallas_call x1, Pallas kernels, attend(): pl.pallas_call(functools.partial(attend_kernel, factor, key_rows), out_sh...  10.4 us
  transfers between devices with their start and end apart: 1, of which 1 were waited for; matrix products, arithmetic and copies ran while one was open for 0% of the time, Pallas kernels for 3%

profile of v8, /device:TPU:0, one launch (start us, length us, event | category | flops | bytes accessed | tf_op | source)
XLA Modules:
  0.0 484.7 jit_solution(3007322305082244394)
XLA Ops:
  0.6 0.0 copy-start.9
  0.7 0.0 copy-start.8
  2.0 0.7 broadcast_add_fusion
  2.7 0.1 fusion.5
  2.8 1.0 fusion
  3.8 0.1 pad_maximum_fusion.cosines
  4.0 0.0 copy-start.1
  4.0 0.1 pad_maximum_fusion.1.sines
  4.2 0.0 copy-start
  4.2 0.0 copy-done.9
  4.2 0.0 copy-done.8
  4.2 46.2 %shard_map.255 = (bf16[4,512,128]{2,1,0:T(8,128)(2,1)S(1)}, bf16[8,2,512,128]{3,2,1,0:T(8,128)(2,1)S(1)}, f32[8,4,512]{2,1,0:T(4,128)S(1)}, f32[512,512]{1,0:T(8,128)S(1)}, f32[512,512]{1,0:T(8,128)S(1)}) custom-call(bf16[512,2048]{1,0:T(8,128)(2,1)} %tokens.5, bf16[2048,512]{1,0:T(8,128)(2,1)} %w_query.1, bf16[2048,512]{1,0:T(8,128)(2,1)} %w_key.1, ...), custom_call_target="tpu_custom_call" | custom-call | tf_op jit(solution)/shard_map/pallas_call | solution.py:552
  50.4 0.0 copy-done.1
  50.4 0.0 copy-done
  50.4 0.0 copy-start.2
  50.5 1.0 copy-done.2
  51.4 0.0 copy-start.3
  51.4 1.0 copy-done.3
  52.4 0.2 multiply_reduce_fusion
  52.6 0.4 fusion.2
  53.0 0.2 slice_reduce_fusion
  53.1 0.1 and_convert_fusion.live
  53.2 10.4 %shard_map.256 = (f32[4,128,512]{2,1,0:T(8,128)S(1)}, f32[8,512]{1,0:T(8,128)S(1)}, bf16[4,512,128]{2,1,0:T(8,128)(2,1)S(1)}, s32[8,512]{1,0:T(8,128)S(1)}, bf16[4,512,128]{2,1,0:T(8,128)(2,1)S(1)}) custom-call(s32[4,8]{1,0:T(4,128)S(1)} %and_convert_fusion.live, f32[8,4,512]{2,1,0:T(4,128)S(1)} %get-tuple-element.74.notes, ...), custom_call_target="tpu_custom_call" | custom-call | tf_op jit(solution)/shard_map/pallas_call | solution.py:692
  63.6 0.0 copy-start.6
  63.6 0.8 copy-done.6
  64.4 0.0 copy-start.10
  64.4 1.0 copy-done.10
  65.4 106.6 %shard_map.257 = (bf16[512,512]{1,0:T(8,128)(2,1)}, bf16[512,2048]{1,0:T(8,128)(2,1)}, bf16[512,2048]{1,0:T(8,128)(2,1)}, bf16[512,2048]{1,0:T(8,128)(2,1)}, bf1...) custom-call(bf16[4,512,128]{2,1,0:T(8,128)(2,1)} %copy-done.6, ...), custom_call_target="tpu_custom_call" | custom-call | tf_op jit(solution)/shard_map/pallas_call | solution.py:1061
  172.0 2.6 collective-permute-start
  174.6 0.6 slice_bitcast_fusion.factors
  175.2 0.0 copy-start.11
  175.2 1.2 copy-done.11
  176.4 0.0 copy-start.12
  176.4 1.0 copy-done.12
  177.4 12.3 %shard_map.258 = (bf16[4,512,128]{2,1,0:T(8,128)(2,1)S(1)}, bf16[4,2,512,128]{3,2,1,0:T(8,128)(2,1)S(1)}, bf16[4,2,512,128]{3,2,1,0:T(8,128)(2,1)S(1)}) custom-call(s32[4,8]{1,0:T(4,128)S(1)} %and_convert_fusion.live, f32[8,4,512]{2,1,0:T(4,128)S(1)} %get-tuple-element.74.notes, s32[8,512]{1,0:T(8,128)S(1)} %get-tuple-element.77.rows, ...), custom_call_target="tpu_custom_call" | custom-call | flops 10737418240 | bytes 12582912 | tf_op jit(solution)/shard_map/pallas_call | solution.py:720
  189.7 0.0 copy-start.4
  189.7 1.0 copy-done.4
  190.7 0.0 copy-start.5
  190.7 1.0 copy-done.5
  191.7 0.0 copy-start.7
  191.7 0.8 copy-done.7
  192.5 5.7 %collective-permute-done.up_z = bf16[512,1024]{1,0:T(8,128)(2,1)} collective-permute-done((bf16[512,1024]{1,0:T(8,128)(2,1)}, bf16[512,1024]{1,0:T(8,128)(2,1)}, u32[]{:S(2)}, u32[]{:S(2)}) %collective-permute-start) | collective-permute-done | bytes 1048608 | tf_op jit(solution)/shard_map/ppermute | solution.py:340
  198.2 152.9 %shard_map.259 = (f32[1024,512]{1,0:T(8,128)}, bf16[1024,512]{1,0:T(8,128)(2,1)}, bf16[1024,1024]{1,0:T(8,128)(2,1)}, bf16[1024,1024]{1,0:T(8,128)(2,1)}, bf16[5...) custom-call(bf16[4,512,128]{2,1,0:T(8,128)(2,1)} %copy-done.7, ...), custom_call_target="tpu_custom_call" | custom-call | tf_op jit(solution)/shard_map/pallas_call | solution.py:1439
  351.1 120.9 %shard_map.260 = (f32[1024,256]{1,0:T(8,128)}, f32[256,1024]{1,0:T(8,128)}, f32[256,1024]{1,0:T(8,128)}, f32[256,768]{1,0:T(8,128)}, f32[256,256]{1,0:T(8,128)},...) custom-call(bf16[512,1536]{1,0:T(8,128)(2,1)} %get-tuple-element.98., ...), custom_call_target="tpu_custom_call" | custom-call | tf_op jit(solution)/shard_map/pallas_call | solution.py:1772
  472.0 0.8 fusion.4
  472.8 0.7 constant_dynamic-slice_fusion.2
  473.4 0.6 constant_dynamic-slice_fusion.3
  474.1 0.8 fusion.3
  474.9 0.7 constant_dynamic-slice_fusion
  475.6 0.7 constant_dynamic-slice_fusion.1
  476.2 8.2 %shard_map.261 = (bf16[512,2048]{1,0:T(8,128)(2,1)}, bf16[512,2048]{1,0:T(8,128)(2,1)}, f32[256,512]{1,0:T(8,128)}, f32[256,512]{1,0:T(8,128)}, f32[256,512]{1,0...) custom-call(f32[1024,256]{1,0:T(8,128)} %get-tuple-element.112.refs_0_, ...), custom_call_target="tpu_custom_call" | custom-call | tf_op jit(solution)/shard_map/pallas_call | solution.py:1915
  (9 shorter events, 0.1 us)
Async XLA Ops:
  0.6 3.5 copy-start.9
  0.7 3.5 copy-start.8
  4.0 46.5 %copy-start.1 = (f32[512,128]{1,0:T(8,128)}, f32[512,128]{1,0:T(8,128)S(1)}, u32[]{:S(2)}) copy-start(f32[512,128]{1,0:T(8,128)S(1)} %pad_maximum_fusion.cosines) | copy-start | bytes 786436
  4.2 46.3 %copy-start = (f32[512,128]{1,0:T(8,128)}, f32[512,128]{1,0:T(8,128)S(1)}, u32[]{:S(2)}) copy-start(f32[512,128]{1,0:T(8,128)S(1)} %pad_maximum_fusion.1.sines) | copy-start | bytes 786436
  50.4 1.0 copy-start.2
  51.4 1.0 copy-start.3
  63.6 0.8 copy-start.6
  64.4 1.0 copy-start.10
  172.0 26.2 %collective-permute-start = (bf16[512,1024]{1,0:T(8,128)(2,1)}, bf16[512,1024]{1,0:T(8,128)(2,1)}, u32[]{:S(2)}, u32[]{:S(2)}) collective-permute-start(bf16[512,1024]{1,0:T(8,128)(2,1)} %get-tuple-element.97), channel_id=1, source_target_pairs={{0,8},{4,12},{8,0},{12,4},{16,24},{20,28},{24,16},{28,20},{1,9},{5... | collective-permute-start | bytes 3145736 | tf_op jit(solution)/shard_map/ppermute | solution.py:340
  175.2 1.2 copy-start.11
  176.4 1.0 copy-start.12
  189.7 1.0 copy-start.4
  190.7 1.0 copy-start.5
  191.7 0.8 copy-start.7

commit v9 on v8

--- a/solution.py
+++ b/solution.py
@@ -762,7 +762,8 @@
     out_gate_far,
     out_gate_z,
     out_up,
-    out_up_far,
+    out_up_fa,
+    out_up_fb,
     out_attn,
     out_grads,
     out_grad_hidden,
@@ -978,12 +979,12 @@
         half = units // 2
         far = pl.ds(pl.multiple_of((1 - z_low) * half, half), half)
         flying["grads"] = [
-            keep_out(source, target.at[both(s)], waited=True)
+            keep_out(source, target, waited=True)
             for source, target in (
-                (grad_gate, out_gate),
-                (grad_gate.at[:, far], out_gate_far),
-                (grad_up, out_up),
-                (grad_up.at[:, far], out_up_far),
+                (grad_gate, out_gate.at[both(s)]),
+                (grad_gate.at[:, far], out_gate_far.at[both(s)]),
+                (grad_up, out_up.at[both(s)]),
+                (grad_up.at[:, far], (out_up_fa, out_up_fb)[s]),
             )
         ]
 
@@ -1074,14 +1075,15 @@
             jax.ShapeDtypeStruct((rows, units // 2), bf16),
             jax.ShapeDtypeStruct((rows, units // 2), bf16),
             tall,
-            jax.ShapeDtypeStruct((rows, units // 2), bf16),
+            jax.ShapeDtypeStruct((half, units // 2), bf16),
+            jax.ShapeDtypeStruct((half, units // 2), bf16),
             wide,
             jax.ShapeDtypeStruct((line, rows, width), bf16),
             jax.ShapeDtypeStruct((half, depth), f32),
             jax.ShapeDtypeStruct((2, depth), f32),
         ],
         in_specs=vmem_specs(4) + [any_spec] * 5,
-        out_specs=[any_spec] * 16 + vmem_specs(2),
+        out_specs=[any_spec] * 17 + vmem_specs(2),
         scratch_shapes=[
             pltpu.VMEM((depth, units), bf16),
             pltpu.VMEM((depth, units), bf16),
@@ -1249,12 +1251,14 @@
     gate,
     gate_z,
     up,
-    up_z,
+    up_za,
+    up_fb,
     out_own_down,
     out_r2_down,
     out_r1_gate,
     out_r1_up,
     out_r2_gate,
+    out_up_zb,
     out_raw_x,
     r1_down,
     out_raw,
@@ -1314,7 +1318,7 @@
         mail.move(gate.at[:, own_half], gate_v),
         mail.move(gate_z, gate_zv),
         mail.move(up.at[:, own_half], up_v),
-        mail.move(up_z, up_zv),
+        mail.move(up_za, up_zv.at[: count // 2]),
     ]
     small_loads = [mail.move(grad_queries_in, grad_queries), mail.move(near_in, near)]
     greet(spot.all)
@@ -1326,6 +1330,7 @@
         mail.send(grad_queries.at[d], query_home.at[:, my_head], spot.ahead[line - d])
         for d in range(1, line)
     ]
+    up_copy = mail.send(up_fb, up_zv.at[count // 2 :], spot.z_peer)
     query_home[:, my_head] = grad_queries[0]
     for load in loads[:4]:
         load.wait()
@@ -1345,6 +1350,8 @@
         for d in range(1, line)
     ]
     pair_home[:, :, my_head] = sums[0]
+    up_copy.wait()
+    keep_up = mail.move(up_zv.at[count // 2 :], out_up_zb)
     ups = Job(spot, False, hidden_v, hidden_zv, up_v, up_zv, True)
     up_first = ups.start_first(mail, send_up, out_r1_up)
 
@@ -1419,7 +1426,7 @@
         down.at(own_v, i)[...] = down.own_term(i, r1_own)
 
     keep_own = mail.move(own_v, out_own_down)
-    for copy in (gate_second, gate_first[1], *up_first, raw_copy, second_copy, keep_own):
+    for copy in (keep_up, gate_second, gate_first[1], *up_first, raw_copy, second_copy, keep_own):
         copy.wait()
 
 
@@ -1438,14 +1445,15 @@
     shape = jax.ShapeDtypeStruct
     return pl.pallas_call(
         middle_kernel,
-        in_specs=[pl.BlockSpec(memory_space=pltpu.HBM)] * 3 + vmem_specs(7) + [any_spec] * 10,
-        out_specs=[any_spec] * 7 + vmem_specs(3),
+        in_specs=[pl.BlockSpec(memory_space=pltpu.HBM)] * 3 + vmem_specs(7) + [any_spec] * 11,
+        out_specs=[any_spec] * 8 + vmem_specs(3),
         out_shape=[
             shape((half, cut // 2), f32),
             shape((half, cut // 2), bf16),
             shape((cut, half), bf16),
             shape((cut, half), bf16),
             shape((cut // 2, half), bf16),
+            shape((count // 2, half), bf16),
             shape((count, 3 * columns // 2), bf16),
             shape((half, cut), bf16),
             shape((count, 3 * columns), bf16),
@@ -1505,7 +1513,8 @@
     gate,
     gate_z,
     up,
-    up_z,
+    up_za,
+    up_zb,
     attn,
     tokens,
     tokens_x,
@@ -1606,7 +1615,7 @@
     r1_loads = []
     first_loads = [mail.move(hidden, hidden_v), mail.move(hidden_z, hidden_zv)]
     gate_loads = [mail.move(gate.at[:, own_half], gate_v), mail.move(gate_z, gate_zv)]
-    up_loads = [mail.move(up.at[:, own_half], up_v), mail.move(up_z, up_zv)]
+    up_loads = [mail.move(up.at[:, own_half], up_v), mail.move(up_za, up_zv.at[:rows]), mail.move(up_zb, up_zv.at[rows:])]
     ups = Job(spot, False, hidden_v, hidden_zv, up_v, up_zv, True)
     gates = Job(spot, False, hidden_v, hidden_zv, gate_v, gate_zv, True)
     raws = Job(spot, True, tokens_v, tokens_xv, raw_own, raw_x, True)
@@ -2027,7 +2036,8 @@
         _,
         grad_gate_z,
         grad_up,
-        grad_up_far,
+        grad_up_fa,
+        grad_up_fb,
         grad_attn,
         grads,
         grad_hidden,
@@ -2035,7 +2045,7 @@
     ) = block(
         attended_out, w_output, g_attn, g_mlp, tokens, cotangent, w_gate, w_up, w_down
     )
-    grad_up_z = line_flip(grad_up_far, 1)
+    grad_up_za = line_flip(grad_up_fa, 1)
     back = attend_back(
         key_rows, live, notes, code_rows, queries_n, pairs, turned, log_total, grads
     )
@@ -2045,6 +2055,7 @@
         r1_gate,
         r1_up,
         r2_gate,
+        grad_up_zb,
         raw_x,
         _,
         raw,
@@ -2062,7 +2073,8 @@
             grad_gate,
             grad_gate_z,
             grad_up,
-            grad_up_z,
+            grad_up_za,
+            grad_up_fb,
         ),
     )
     results = last(
@@ -2073,7 +2085,8 @@
             grad_gate,
             grad_gate_z,
             grad_up,
-            grad_up_z,
+            grad_up_za,
+            grad_up_zb,
             grad_attn,
             tokens,
             tokens_x,

time: 491 us -> 500 us (1.018)
  Pallas kernels: 458 us -> 470 us
  waiting for transfers between devices: 5.72 us -> 0.01 us
    pallas_call x1, Pallas kernels: 153 us -> 163 us  [middle(): pl.pallas_call(middle_kernel, in_specs=[pl.BlockSpec(memory_space=pltpu.H...]
    ppermute x1, waiting for transfers between devices: 5.72 us -> 0.01 us  [line_flip(): lax.ppermute(value, 'dp', [(z * pair + x, (z ^ bit) * pair + x) for z in...]
  transfers between devices with their start and end apart: 1 -> 1, of which waited for: 1 -> 0; matrix products, arithmetic and copies ran while one was open for 0% -> 0% of each run, Pallas kernels for 3% -> 3%
where the time goes in v9:
time: 500 us; the launch traced here: 493 us
  Pallas kernels  470 us (94%)
  local copies, waits for them, and re-layouts  14.4 us (3%)
    pallas_call x1, Pallas kernels, middle(): pl.pallas_call(middle_kernel, in_specs=[pl.BlockSpec(memory_space=pltpu.H...  163 us
    pallas_call x1, Pallas kernels, last(): pl.pallas_call(last_kernel, in_specs=vmem_specs(6) + [any_spec] * len(lar...  122 us
    pallas_call x1, Pallas kernels, block(): pl.pallas_call(block_kernel, out_shape=[jax.ShapeDtypeStruct((rows, colum...  107 us
    pallas_call x1, Pallas kernels, project(): pl.pallas_call(project_kernel, in_specs=[pl.BlockSpec(memory_space=pl.ANY...  46.2 us
    pallas_call x1, Pallas kernels, attend_back(): pl.pallas_call(functools.partial(attend_back_kernel, factor, scale, key_r...  13.1 us
    pallas_call x1, Pallas kernels, attend(): pl.pallas_call(functools.partial(attend_kernel, factor, key_rows), out_sh...  11 us
  transfers between devices with their start and end apart: 1, of which 0 were waited for; matrix products, arithmetic and copies ran while one was open for 0% of the time, Pallas kernels for 3%

profile of v9, /device:TPU:0, one launch (start us, length us, event | category | flops | bytes accessed | tf_op | source)
XLA Modules:
  0.0 492.6 jit_solution(7948841438718312874)
XLA Ops:
  0.6 0.0 copy-start.9
  0.7 0.0 copy-start.8
  2.0 0.7 broadcast_add_fusion
  2.7 0.1 fusion.5
  2.8 1.0 fusion
  3.8 0.1 pad_maximum_fusion.cosines
  4.0 0.0 copy-start.1
  4.0 0.1 pad_maximum_fusion.1.sines
  4.2 0.0 copy-start
  4.2 0.0 copy-done.9
  4.2 0.0 copy-done.8
  4.2 46.2 %shard_map.255 = (bf16[4,512,128]{2,1,0:T(8,128)(2,1)S(1)}, bf16[8,2,512,128]{3,2,1,0:T(8,128)(2,1)S(1)}, f32[8,4,512]{2,1,0:T(4,128)S(1)}, f32[512,512]{1,0:T(8,128)S(1)}, f32[512,512]{1,0:T(8,128)S(1)}) custom-call(bf16[512,2048]{1,0:T(8,128)(2,1)} %tokens.5, bf16[2048,512]{1,0:T(8,128)(2,1)} %w_query.1, bf16[2048,512]{1,0:T(8,128)(2,1)} %w_key.1, ...), custom_call_target="tpu_custom_call" | custom-call | tf_op jit(solution)/shard_map/pallas_call | solution.py:552
  50.4 0.0 copy-done.1
  50.4 0.0 copy-done
  50.4 0.0 copy-start.2
  50.4 1.0 copy-done.2
  51.4 0.0 copy-start.3
  51.4 1.0 copy-done.3
  52.4 0.2 multiply_reduce_fusion
  52.6 0.4 fusion.2
  53.0 0.2 slice_reduce_fusion
  53.1 0.1 and_convert_fusion.live
  53.2 11.0 %shard_map.256 = (f32[4,128,512]{2,1,0:T(8,128)S(1)}, f32[8,512]{1,0:T(8,128)S(1)}, bf16[4,512,128]{2,1,0:T(8,128)(2,1)S(1)}, s32[8,512]{1,0:T(8,128)S(1)}, bf16[4,512,128]{2,1,0:T(8,128)(2,1)S(1)}) custom-call(s32[4,8]{1,0:T(4,128)S(1)} %and_convert_fusion.live, f32[8,4,512]{2,1,0:T(4,128)S(1)} %get-tuple-element.76.notes, ...), custom_call_target="tpu_custom_call" | custom-call | tf_op jit(solution)/shard_map/pallas_call | solution.py:692
  64.2 0.0 copy-start.6
  64.3 0.8 copy-done.6
  65.0 0.0 copy-start.10
  65.0 1.0 copy-done.10
  66.0 106.6 %shard_map.257 = (bf16[512,512]{1,0:T(8,128)(2,1)}, bf16[512,2048]{1,0:T(8,128)(2,1)}, bf16[512,2048]{1,0:T(8,128)(2,1)}, bf16[512,2048]{1,0:T(8,128)(2,1)}, bf1...) custom-call(bf16[4,512,128]{2,1,0:T(8,128)(2,1)} %copy-done.6, ...), custom_call_target="tpu_custom_call" | custom-call | tf_op jit(solution)/shard_map/pallas_call | solution.py:1062
  172.6 2.6 collective-permute-start
  175.2 0.0 copy-start.11
  175.2 1.2 copy-done.11
  176.4 0.0 copy-start.12
  176.4 1.0 copy-done.12
  177.5 13.1 %shard_map.258 = (bf16[4,512,128]{2,1,0:T(8,128)(2,1)S(1)}, bf16[4,2,512,128]{3,2,1,0:T(8,128)(2,1)S(1)}, bf16[4,2,512,128]{3,2,1,0:T(8,128)(2,1)S(1)}) custom-call(s32[4,8]{1,0:T(4,128)S(1)} %and_convert_fusion.live, f32[8,4,512]{2,1,0:T(4,128)S(1)} %get-tuple-element.76.notes, s32[8,512]{1,0:T(8,128)S(1)} %get-tuple-element.79.rows, ...), custom_call_target="tpu_custom_call" | custom-call | flops 10737418240 | bytes 12582912 | tf_op jit(solution)/shard_map/pallas_call | solution.py:720
  190.5 0.0 copy-start.4
  190.6 1.0 copy-done.4
  191.5 0.0 copy-start.5
  191.5 1.0 copy-done.5
  192.5 0.0 copy-start.7
  192.5 0.8 copy-done.7
  193.3 0.6 slice_bitcast_fusion.factors
  193.9 0.0 collective-permute-done.up_za
  193.9 0.0 copy-start.13
  193.9 0.8 copy-done.13
  194.7 163.5 %shard_map.259 = (f32[1024,512]{1,0:T(8,128)}, bf16[1024,512]{1,0:T(8,128)(2,1)}, bf16[1024,1024]{1,0:T(8,128)(2,1)}, bf16[1024,1024]{1,0:T(8,128)(2,1)}, bf16[5...) custom-call(bf16[4,512,128]{2,1,0:T(8,128)(2,1)} %copy-done.7, ...), custom_call_target="tpu_custom_call" | custom-call | tf_op jit(solution)/shard_map/pallas_call | solution.py:1446
  358.1 121.8 %shard_map.260 = (f32[1024,256]{1,0:T(8,128)}, f32[256,1024]{1,0:T(8,128)}, f32[256,1024]{1,0:T(8,128)}, f32[256,768]{1,0:T(8,128)}, f32[256,256]{1,0:T(8,128)},...) custom-call(bf16[512,1536]{1,0:T(8,128)(2,1)} %get-tuple-element.101, ...), custom_call_target="tpu_custom_call" | custom-call | tf_op jit(solution)/shard_map/pallas_call | solution.py:1781
  479.9 0.8 fusion.4
  480.7 0.7 constant_dynamic-slice_fusion.2
  481.4 0.6 constant_dynamic-slice_fusion.3
  482.0 0.8 fusion.3
  482.8 0.7 constant_dynamic-slice_fusion
  483.5 0.7 constant_dynamic-slice_fusion.1
  484.2 8.2 %shard_map.261 = (bf16[512,2048]{1,0:T(8,128)(2,1)}, bf16[512,2048]{1,0:T(8,128)(2,1)}, f32[256,512]{1,0:T(8,128)}, f32[256,512]{1,0:T(8,128)}, f32[256,512]{1,0...) custom-call(f32[1024,256]{1,0:T(8,128)} %get-tuple-element.116.refs_0_, ...), custom_call_target="tpu_custom_call" | custom-call | tf_op jit(solution)/shard_map/pallas_call | solution.py:1924
  (9 shorter events, 0.1 us)
Async XLA Ops:
  0.6 3.5 copy-start.9
  0.7 3.5 copy-start.8
  4.0 46.4 %copy-start.1 = (f32[512,128]{1,0:T(8,128)}, f32[512,128]{1,0:T(8,128)S(1)}, u32[]{:S(2)}) copy-start(f32[512,128]{1,0:T(8,128)S(1)} %pad_maximum_fusion.cosines) | copy-start | bytes 786436
  4.2 46.3 %copy-start = (f32[512,128]{1,0:T(8,128)}, f32[512,128]{1,0:T(8,128)S(1)}, u32[]{:S(2)}) copy-start(f32[512,128]{1,0:T(8,128)S(1)} %pad_maximum_fusion.1.sines) | copy-start | bytes 786436
  50.4 1.0 copy-start.2
  51.4 1.0 copy-start.3
  64.2 0.8 copy-start.6
  65.0 1.0 copy-start.10
  172.6 21.2 %collective-permute-start = (bf16[256,1024]{1,0:T(8,128)(2,1)}, bf16[256,1024]{1,0:T(8,128)(2,1)S(1)}, u32[]{:S(2)}, u32[]{:S(2)}) collective-permute-start(bf16[256,1024]{1,0:T(8,128)(2,1)} %get-tuple-element.99), channel_id=1, source_target_pairs={{0,8},{4,12},{8,0},{12,4},{16,24},{20,28},{24,16},{28,20},{1,9},{5... | collective-permute-start | bytes 1572872 | tf_op jit(solution)/shard_map/ppermute | solution.py:340
  175.2 1.2 copy-start.11
  176.4 1.0 copy-start.12
  190.5 1.0 copy-start.4
  191.5 1.0 copy-start.5
  192.5 0.8 copy-start.7
  193.9 0.8 copy-start.13
